TPU v7x, 32 devices: a whole 2x2x4 slice. The times are simulated.
32 devices in a mesh: expert: 4 (over y, x), shard: 8 (over z, core).
Axes of the slice: x: 2, y: 2, z: 4, core: 2. Of those that a mesh axis runs over, the one named last changes fastest.
Arguments:
- tokens: bfloat16 [4096, 2304], P(('expert', 'shard')), may hold values from -6 to 6
- seq_lengths: int32 [32, 2], P(('expert', 'shard')), may hold values from 32 to 96, as said below
- routes: int32 [4096, 2], P(('expert', 'shard')), may hold values from 0 to 3, all different within a row; in each aligned block of 128 rows (0 to 127, 128 to 255, ...) at most 80 rows name the same one
- norm_attn: bfloat16 [2304], P('shard'), may hold values from 0.5 to 1.5
- w_query: bfloat16 [2304, 2304], P('shard'), may hold values from -0.125 to 0.125
- w_key: bfloat16 [2304, 2304], P('shard'), may hold values from -0.125 to 0.125
- w_value: bfloat16 [2304, 2304], P('shard'), may hold values from -0.125 to 0.125
- w_output: bfloat16 [2304, 2304], P('shard'), may hold values from -4 to 4
- norm_ffn: bfloat16 [2304], P('shard'), may hold values from 0.5 to 1.5
- w_router: bfloat16 [2304, 4], P('shard'), may hold values from -0.125 to 0.125
- w_in: bfloat16 [2304, 4, 11520], P('shard', 'expert'), may hold values from -0.125 to 0.125
- w_down: bfloat16 [5760, 4, 2304], P('shard', 'expert'), may hold values from -0.3125 to 0.3125
- cotangent: bfloat16 [4096, 2304], P(('expert', 'shard')), may hold values from -6 to 6
Outputs:
- activations: bfloat16 [4096, 2304], P(('expert', 'shard'))
- grad_tokens: float32 [4096, 2304], P(('expert', 'shard'))
- grad_norm_attn: float32 [2304], P('shard')
- grad_w_query: float32 [2304, 2304], P('shard')
- grad_w_key: float32 [2304, 2304], P('shard')
- grad_w_value: float32 [2304, 2304], P('shard')
- grad_w_output: float32 [2304, 2304], P('shard')
- grad_norm_ffn: float32 [2304], P('shard')
- grad_w_router: float32 [2304, 4], P('shard')
- grad_w_in: float32 [2304, 4, 11520], P('shard', 'expert')
- grad_w_down: float32 [5760, 4, 2304], P('shard', 'expert')
Inputs may be any that keep to these rules, and one draw needn't show every extreme that they name: `routes`: within the 128 rows of one device no expert is named by more than 80 rows; each row names two different experts. `seq_lengths`: the two lengths of a device add up to 128; its first sequence takes its first rows.
All inputs are finite; a program needn't handle non-finite values.
Results may differ from a plain program's by a relative error of at most 0.014.
The roundings to bfloat16 on the way count: a program that leaves them out, or rounds other values in their place, can miss the bound.
Values may be sent and summed in bfloat16 or wider, within the bound.
A program may use at most 704 MiB of HBM per device.

v0:
```python
import math

import jax
import jax.numpy as jnp
from jax import lax
from jax.sharding import PartitionSpec as P

HEADS = 36


eps_norm = 1e-05
branch_scale = 1.4 / math.sqrt(40.0)
rope_base = 10000.0
masked_score = -1e30


def rope_tables(positions, head_width):
    half_width = head_width // 2
    exponents = jnp.arange(half_width).astype(jnp.float32) * 2.0 / head_width
    frequency = rope_base ** (-exponents)
    angles = positions.astype(jnp.float32)[:, None] * frequency[None, :]
    return (jnp.cos(angles), jnp.sin(angles))


def rotate(values, cosine, sine_table):
    half_width = values.shape[-1] // 2
    leading = values[..., :half_width]
    trailing = values[..., half_width:]
    cos_rows = cosine[:, None, :]
    sin_rows = sine_table[:, None, :]
    return jnp.concatenate(
        [leading * cos_rows - trailing * sin_rows, trailing * cos_rows + leading * sin_rows],
        axis=-1,
    )


def rms_forward(values, norm_gain):
    inverse = lax.rsqrt(jnp.mean(values * values, axis=-1, keepdims=True) + eps_norm)
    return (values * inverse * norm_gain, inverse)


def rms_backward(values, inverse, norm_gain, upstream):
    weighted = upstream * norm_gain
    gain_grad = jnp.sum(upstream * values * inverse, axis=0)
    inner_mean = jnp.mean(weighted * values, axis=-1, keepdims=True)
    return (inverse * weighted - values * inverse * inverse * inverse * inner_mean, gain_grad)


def masked_scores(queries, keys_rot, allowed):
    head_width = queries.shape[-1]
    scores = jnp.einsum("qhd,khd->hqk", queries, keys_rot, preferred_element_type=jnp.float32) * (
        1.0 / math.sqrt(head_width)
    )
    return jnp.where(allowed[None], scores, masked_score)


def attend_forward(queries, keys_rot, values, allowed):
    scores = masked_scores(queries, keys_rot, allowed)
    row_peak = jnp.max(scores, axis=-1, keepdims=True)
    log_total = row_peak + jnp.log(jnp.sum(jnp.exp(scores - row_peak), axis=-1, keepdims=True))
    probs_half = jnp.exp(scores - log_total).astype(jnp.bfloat16)
    context = jnp.einsum("hqk,khd->qhd", probs_half, values, preferred_element_type=jnp.float32)
    return (context.astype(jnp.bfloat16), log_total)


def attend_backward(queries, keys_rot, values, allowed, log_total, context, context_grad):
    scale_factor = 1.0 / math.sqrt(queries.shape[-1])
    attn_probs = jnp.exp(masked_scores(queries, keys_rot, allowed) - log_total)
    probs_half = attn_probs.astype(jnp.bfloat16)
    row_delta = jnp.sum(context_grad * context.astype(jnp.float32), axis=-1)
    context_half = context_grad.astype(jnp.bfloat16)
    probs_grad = jnp.einsum(
        "qhd,khd->hqk", context_half, values, preferred_element_type=jnp.float32
    )
    scores_grad = (
        attn_probs * (probs_grad - jnp.transpose(row_delta)[:, :, None]) * scale_factor
    ).astype(jnp.bfloat16)
    queries_grad = jnp.einsum(
        "hqk,khd->qhd", scores_grad, keys_rot, preferred_element_type=jnp.float32
    )
    keys_grad = jnp.einsum("hqk,qhd->khd", scores_grad, queries, preferred_element_type=jnp.float32)
    values_grad = jnp.einsum(
        "hqk,qhd->khd", probs_half, context_half, preferred_element_type=jnp.float32
    )
    return (queries_grad, keys_grad, values_grad)


def expert_forward(arrived, weights_in, hidden_width):
    gate_up = jnp.einsum("secd,dez->secz", arrived, weights_in, preferred_element_type=jnp.float32)
    gate_part = gate_up[..., :hidden_width]
    up_part = gate_up[..., hidden_width:]
    activated = (jax.nn.silu(gate_part) * up_part).astype(jnp.bfloat16)
    return (gate_part, up_part, activated)


def on_device(
    tokens,
    seq_lengths,
    routes,
    norm_attn,
    w_query,
    w_key,
    w_value,
    w_output,
    norm_ffn,
    w_router,
    w_in,
    w_down,
    cotangent,
):
    tok_rows, model_width = tokens.shape
    head_width = model_width // HEADS
    head_shape = (tok_rows, HEADS, head_width)
    expert_axis = lax.axis_size("expert")
    expert_local = w_in.shape[1]
    expert_total = expert_local * expert_axis
    hidden_width = w_in.shape[2] // 2
    capacity = 10 * tok_rows // (4 * expert_total)
    highest = lax.Precision.HIGHEST
    gathered = (
        lax.all_gather(w_query, "shard", axis=0, tiled=True),
        lax.all_gather(w_key, "shard", axis=0, tiled=True),
        lax.all_gather(w_value, "shard", axis=0, tiled=True),
        lax.all_gather(w_output, "shard", axis=0, tiled=True),
        lax.all_gather(w_router, "shard", axis=0, tiled=True),
        lax.all_gather(norm_attn, "shard", axis=0, tiled=True),
        lax.all_gather(norm_ffn, "shard", axis=0, tiled=True),
    )
    full_query, full_key, full_value, full_output, full_router, gain_attn, gain_ffn = gathered
    gain_attn = gain_attn.astype(jnp.float32)
    gain_ffn = gain_ffn.astype(jnp.float32)
    row_index = jnp.arange(tok_rows)
    first_length = seq_lengths[0, 0]
    segment = (row_index >= first_length).astype(jnp.int32)
    positions = row_index - first_length * segment
    allowed = (segment[:, None] == segment[None, :]) & (row_index[None, :] <= row_index[:, None])
    cosine, sine_table = rope_tables(positions, head_width)
    residual_in = tokens.astype(jnp.float32)
    normed_in, inverse_in = rms_forward(residual_in, gain_attn)
    normed_half = normed_in.astype(jnp.bfloat16)
    queries = rotate(
        jnp.dot(normed_half, full_query, preferred_element_type=jnp.float32).reshape(head_shape),
        cosine,
        sine_table,
    ).astype(jnp.bfloat16)
    keys_rot = rotate(
        jnp.dot(normed_half, full_key, preferred_element_type=jnp.float32).reshape(head_shape),
        cosine,
        sine_table,
    ).astype(jnp.bfloat16)
    values = (
        jnp.dot(normed_half, full_value, preferred_element_type=jnp.float32)
        .astype(jnp.bfloat16)
        .reshape(head_shape)
    )
    context, log_total = attend_forward(queries, keys_rot, values, allowed)
    context_flat = context.reshape(tok_rows, model_width)
    residual_mid = residual_in + branch_scale * jnp.dot(
        context_flat, full_output, preferred_element_type=jnp.float32
    )
    normed_mid, inverse_mid = rms_forward(residual_mid, gain_ffn)
    normed_mid_half = normed_mid.astype(jnp.bfloat16)
    logits = jnp.dot(normed_mid_half, full_router, preferred_element_type=jnp.float32)
    expert_ids = jnp.arange(expert_total)
    route_mask = (routes[:, :, None] == expert_ids[None, None, :]).astype(jnp.float32)
    chosen = jnp.sum(logits[:, None, :] * route_mask, axis=-1)
    gate_probs = jax.nn.softmax(chosen, axis=-1)
    flat_routes = routes.reshape(2 * tok_rows)
    route_hits = (flat_routes[:, None] == expert_ids[None, :]).astype(jnp.int32)
    earlier = jnp.cumsum(route_hits, axis=0) - route_hits
    slot_index = jnp.sum(earlier * route_hits, axis=1)
    target_rows = flat_routes * capacity + slot_index
    buffer_shape = (expert_total * capacity, model_width)
    outgoing = (
        jnp.zeros(buffer_shape, jnp.bfloat16)
        .at[target_rows]
        .set(jnp.repeat(normed_mid_half, 2, axis=0))
    )
    arrived = lax.all_to_all(outgoing, "expert", split_axis=0, concat_axis=0, tiled=True).reshape(
        expert_axis, expert_local, capacity, model_width
    )
    full_in, full_down = (
        lax.all_gather(w_in, "shard", axis=0, tiled=True),
        lax.all_gather(w_down, "shard", axis=0, tiled=True),
    )
    gate_part, up_part, activated = expert_forward(arrived, full_in, hidden_width)
    expert_out = jnp.einsum(
        "secf,fed->secd", activated, full_down, preferred_element_type=jnp.float32
    ).astype(jnp.bfloat16)
    returned = lax.all_to_all(
        expert_out.reshape(buffer_shape), "expert", split_axis=0, concat_axis=0, tiled=True
    )
    expert_rows = returned[target_rows].reshape(tok_rows, 2, model_width).astype(jnp.float32)
    mixture = jnp.sum(gate_probs[:, :, None] * expert_rows, axis=1)
    activations = (residual_mid + branch_scale * mixture).astype(jnp.bfloat16)
    upstream = cotangent.astype(jnp.float32)
    mixture_grad = branch_scale * upstream
    gate_grad = jnp.sum(mixture_grad[:, None, :] * expert_rows, axis=-1)
    chosen_grad = gate_probs * (gate_grad - jnp.sum(gate_probs * gate_grad, axis=-1, keepdims=True))
    logit_grad = jnp.sum(chosen_grad[:, :, None] * route_mask, axis=1)
    row_grads = (
        (gate_probs[:, :, None] * mixture_grad[:, None, :])
        .astype(jnp.bfloat16)
        .reshape(2 * tok_rows, model_width)
    )
    grad_outgoing = jnp.zeros(buffer_shape, jnp.bfloat16).at[target_rows].set(row_grads)
    grad_arrived = lax.all_to_all(
        grad_outgoing, "expert", split_axis=0, concat_axis=0, tiled=True
    ).reshape(arrived.shape)
    again_in, again_down = (
        lax.all_gather(w_in, "shard", axis=0, tiled=True),
        lax.all_gather(w_down, "shard", axis=0, tiled=True),
    )
    gate_again, up_again, act_again = expert_forward(arrived, again_in, hidden_width)
    act_grad = jnp.einsum(
        "secd,fed->secf", grad_arrived, again_down, preferred_element_type=jnp.float32
    )
    sigmoid_gate = jax.nn.sigmoid(gate_again)
    pre_grad = jnp.concatenate(
        [
            act_grad * up_again * sigmoid_gate * (1.0 + gate_again * (1.0 - sigmoid_gate)),
            act_grad * jax.nn.silu(gate_again),
        ],
        axis=-1,
    ).astype(jnp.bfloat16)
    input_grad = jnp.einsum(
        "secz,dez->secd", pre_grad, again_in, preferred_element_type=jnp.float32
    ).astype(jnp.bfloat16)
    grad_back = lax.all_to_all(
        input_grad.reshape(buffer_shape), "expert", split_axis=0, concat_axis=0, tiled=True
    )
    in_term = jnp.einsum("secd,secz->dez", arrived, pre_grad, preferred_element_type=jnp.float32)
    down_term = jnp.einsum(
        "secf,secd->fed", act_again, grad_arrived, preferred_element_type=jnp.float32
    )
    grad_w_in, grad_w_down = (
        lax.psum_scatter(in_term, "shard", scatter_dimension=0, tiled=True),
        lax.psum_scatter(down_term, "shard", scatter_dimension=0, tiled=True),
    )
    normed_mid_grad = jnp.sum(
        grad_back[target_rows].reshape(tok_rows, 2, model_width).astype(jnp.float32), axis=1
    )
    normed_mid_grad = normed_mid_grad + jnp.dot(
        logit_grad, jnp.transpose(full_router.astype(jnp.float32)), precision=highest
    )
    router_grad = jnp.dot(
        jnp.transpose(normed_mid_half.astype(jnp.float32)), logit_grad, precision=highest
    )
    mid_norm_grad, gain_ffn_grad = rms_backward(
        residual_mid, inverse_mid, gain_ffn, normed_mid_grad
    )
    residual_grad = upstream + mid_norm_grad
    branch_grad = (branch_scale * residual_grad).astype(jnp.bfloat16)
    output_grad = jnp.dot(
        jnp.transpose(context_flat), branch_grad, preferred_element_type=jnp.float32
    )
    context_grad = jnp.dot(
        branch_grad, jnp.transpose(full_output), preferred_element_type=jnp.float32
    ).reshape(head_shape)
    queries_grad_rot, keys_grad_rot, values_grad = attend_backward(
        queries, keys_rot, values, allowed, log_total, context, context_grad
    )
    queries_grad = (
        rotate(queries_grad_rot, cosine, -sine_table)
        .reshape(tok_rows, model_width)
        .astype(jnp.bfloat16)
    )
    keys_grad = (
        rotate(keys_grad_rot, cosine, -sine_table)
        .reshape(tok_rows, model_width)
        .astype(jnp.bfloat16)
    )
    values_grad_half = values_grad.reshape(tok_rows, model_width).astype(jnp.bfloat16)
    query_weight_grad = jnp.dot(
        jnp.transpose(normed_half), queries_grad, preferred_element_type=jnp.float32
    )
    key_weight_grad = jnp.dot(
        jnp.transpose(normed_half), keys_grad, preferred_element_type=jnp.float32
    )
    value_weight_grad = jnp.dot(
        jnp.transpose(normed_half), values_grad_half, preferred_element_type=jnp.float32
    )
    normed_in_grad = jnp.dot(
        queries_grad, jnp.transpose(full_query), preferred_element_type=jnp.float32
    )
    normed_in_grad = normed_in_grad + jnp.dot(
        keys_grad, jnp.transpose(full_key), preferred_element_type=jnp.float32
    )
    normed_in_grad = normed_in_grad + jnp.dot(
        values_grad_half, jnp.transpose(full_value), preferred_element_type=jnp.float32
    )
    in_norm_grad, gain_attn_grad = rms_backward(residual_in, inverse_in, gain_attn, normed_in_grad)
    grad_tokens = residual_grad + in_norm_grad
    shard_sums = (
        lax.psum_scatter(query_weight_grad, "shard", scatter_dimension=0, tiled=True),
        lax.psum_scatter(key_weight_grad, "shard", scatter_dimension=0, tiled=True),
        lax.psum_scatter(value_weight_grad, "shard", scatter_dimension=0, tiled=True),
        lax.psum_scatter(output_grad, "shard", scatter_dimension=0, tiled=True),
        lax.psum_scatter(router_grad, "shard", scatter_dimension=0, tiled=True),
        lax.psum_scatter(gain_attn_grad, "shard", scatter_dimension=0, tiled=True),
        lax.psum_scatter(gain_ffn_grad, "shard", scatter_dimension=0, tiled=True),
    )
    totals = lax.psum(
        (
            shard_sums[0],
            shard_sums[1],
            shard_sums[2],
            shard_sums[3],
            shard_sums[4],
            shard_sums[5],
            shard_sums[6],
        ),
        "expert",
    )
    return (
        activations,
        grad_tokens,
        totals[5],
        totals[0],
        totals[1],
        totals[2],
        totals[3],
        totals[6],
        totals[4],
        grad_w_in,
        grad_w_down,
    )


def solution(mesh):
    in_specs = (
        P(("expert", "shard"), None),
        P(("expert", "shard"), None),
        P(("expert", "shard"), None),
        P("shard"),
        P("shard", None),
        P("shard", None),
        P("shard", None),
        P("shard", None),
        P("shard"),
        P("shard", None),
        P("shard", "expert", None),
        P("shard", "expert", None),
        P(("expert", "shard"), None),
    )
    out_specs = (
        P(("expert", "shard"), None),
        P(("expert", "shard"), None),
        P("shard"),
        P("shard", None),
        P("shard", None),
        P("shard", None),
        P("shard", None),
        P("shard"),
        P("shard", None),
        P("shard", "expert", None),
        P("shard", "expert", None),
    )
    return jax.shard_map(
        on_device, mesh=mesh, in_specs=in_specs, out_specs=out_specs, check_vma=False
    )
```

profile of v0, /device:TPU:16, one launch (start us, length us, event | category | flops | bytes accessed | tf_op | source)
XLA Modules:
  0.0 5365.5 jit_solution(13775798503771668990)
XLA Ops:
  13.4 25.8 all-reduce.9
  44.1 65.9 %all-gather.8.cloned.1.call-done = bf16[2304,2304]{1,0:T(8,128)(2,1)} async-done(((bf16[288,2304]{1,0:T(8,128)(2,1)}), bf16[2304,2304]{1,0:T(8,128)(2,1)}) %all-gather.8.cloned.1.call-update) | async-done | bytes 10616848 | tf_op jit(solution)/shard_map/all_gather | solution.py:123
  115.9 94.7 %all-gather.10.cloned.1.call-done = bf16[2304,2304]{1,0:T(8,128)(2,1)} async-done(((bf16[288,2304]{1,0:T(8,128)(2,1)}), bf16[2304,2304]{1,0:T(8,128)(2,1)}) %all-gather.10.cloned.1.call-update) | async-done | bytes 10616848 | tf_op jit(solution)/shard_map/all_gather | solution.py:121
  217.5 93.5 %all-gather.12.cloned.1.call-done = bf16[2304,2304]{1,0:T(8,128)(2,1)} async-done(((bf16[288,2304]{1,0:T(8,128)(2,1)}), bf16[2304,2304]{1,0:T(8,128)(2,1)}) %all-gather.12.cloned.1.call-update) | async-done | bytes 10616848 | tf_op jit(solution)/shard_map/all_gather | solution.py:122
  321.4 90.0 %all-gather.14.cloned.1.call-done = bf16[2304,2304]{1,0:T(8,128)(2,1)} async-done(((bf16[288,2304]{1,0:T(8,128)(2,1)}), bf16[2304,2304]{1,0:T(8,128)(2,1)}) %all-gather.14.cloned.1.call-update) | async-done | bytes 10616848 | tf_op jit(solution)/shard_map/all_gather | solution.py:124
  434.9 19.2 all-gather
  467.2 393.9 %all-gather.16.cloned.1.call-done = bf16[2304,1,11520]{2,0,1:T(8,128)(2,1)} async-done(((bf16[288,1,11520]{2,0,1:T(8,128)(2,1)}), bf16[2304,1,11520]{2,0,1:T(8,128)(2,1)}) %all-gather.16.cloned.1.call-update) | async-done | bytes 53084176 | tf_op jit(solution)/shard_map/all_gather | solution.py:183
  861.2 32.2 fusion.8
  893.3 198.7 %all-gather.18.cloned.1.call-done = bf16[5760,1,2304]{2,0,1:T(8,128)(2,1)} async-done(((bf16[720,1,2304]{2,0,1:T(8,128)(2,1)}), bf16[5760,1,2304]{2,0,1:T(8,128)(2,1)}) %all-gather.18.cloned.1.call-update) | async-done | bytes 26542096 | tf_op jit(solution)/shard_map/all_gather | solution.py:184
  1092.0 22.4 fusion.24
  1114.5 26.4 fusion.15
  1144.6 17.0 fusion.18
  1227.6 10.5 fusion.66
  1263.1 24.4 convolution_bitcast_fusion.1
  1287.5 107.0 %copy.119 = f32[5760,1,2304]{2,1,0:T(1,128)} copy(f32[5760,1,2304]{0,2,1:T(8,128)} %convolution_bitcast_fusion.1) | data formatting | bytes 106168320 | tf_op jit(solution)/shard_map/secf,secd->fed/transpose | solution.py:233
  1394.6 43.8 convolution_bitcast_fusion
  1438.4 212.8 %copy.118 = f32[2304,1,11520]{2,1,0:T(1,128)} copy(f32[2304,1,11520]{0,2,1:T(8,128)} %convolution_bitcast_fusion) | data formatting | bytes 212336640 | tf_op jit(solution)/shard_map/secd,secz->dez/transpose | solution.py:232
  1651.6 204.8 %reduce-scatter.12.cloned.1.call-done = f32[288,2304]{1,0:T(8,128)} async-done(((f32[2304,2304]{1,0:T(8,128)}), f32[288,2304]{1,0:T(8,128)}) %reduce-scatter.12.cloned.1.call-update) | async-done | bytes 2654224 | tf_op jit(solution)/shard_map/reduce_scatter | solution.py:297
  1856.4 210.9 %reduce-scatter.14.cloned.1.call-done = f32[288,2304]{1,0:T(8,128)} async-done(((f32[2304,2304]{1,0:T(8,128)}), f32[288,2304]{1,0:T(8,128)}) %reduce-scatter.14.cloned.1.call-update) | async-done | bytes 2654224 | tf_op jit(solution)/shard_map/reduce_scatter | solution.py:298
  2088.2 21.4 all-reduce.6
  2112.2 16.7 all-reduce.7
  2128.9 990.8 %all-reduce.16.cloned.1.call-done = f32[5760,1,2304]{2,1,0:T(1,128)} async-done(((f32[5760,1,2304]{2,1,0:T(1,128)}), f32[5760,1,2304]{2,1,0:T(1,128)}) %all-reduce.16.cloned.1.call-update) | async-done | bytes 53084176
  3125.2 2009.0 %all-reduce.14.cloned.1.call-done = f32[2304,1,11520]{2,1,0:T(1,128)} async-done(((f32[2304,1,11520]{2,1,0:T(1,128)}), f32[2304,1,11520]{2,1,0:T(1,128)}) %all-reduce.14.cloned.1.call-update) | async-done | bytes 106168336
  5144.3 204.0 %all-reduce.18.cloned.1.call-done = (f32[288,2304]{1,0:T(8,128)}, f32[288,2304]{1,0:T(8,128)}, f32[288,2304]{1,0:T(8,128)}, f32[288,2304]{1,0:T(8,128)}) async-done(((f32[288,2304]{1,0:T(8,128)}, f32[288,2304]{1,0:T(8,128)}, f32[288,2304]{1,0:T(8,128)}, f32[288,2304]{1,0:T(8,128)}), (f32[288,2304]{1,0:T(8,128)}, f32[288,2304]{1,0:T(8,128)}, f32[288,2304]{1,0:T(8,128)}, ...) | async-done | bytes 10616848 | tf_op jit(solution)/shard_map/psum | solution.py:303
  (288 shorter events, 212.6 us)
Async XLA Ops:
  7.2 102.8 %all-gather.8.cloned.1.call-start = ((), (), s32[]{:S(2)}) async-start(), calls=%async_computation.9 | async-start | bytes 11943936 | tf_op jit(solution)/shard_map/all_gather | solution.py:123
  7.9 202.6 %all-gather.10.cloned.1.call-start = ((), (), s32[]{:S(2)}) async-start(), calls=%async_computation.10 | async-start | bytes 11943936 | tf_op jit(solution)/shard_map/all_gather | solution.py:121
  8.7 302.4 %all-gather.12.cloned.1.call-start = ((), (), s32[]{:S(2)}) async-start(), calls=%async_computation.11 | async-start | bytes 11943936 | tf_op jit(solution)/shard_map/all_gather | solution.py:122
  9.4 402.1 %all-gather.14.cloned.1.call-start = ((), (), s32[]{:S(2)}) async-start(), calls=%async_computation.12 | async-start | bytes 11943936 | tf_op jit(solution)/shard_map/all_gather | solution.py:124
  10.0 851.2 %all-gather.16.cloned.1.call-start = ((), (), s32[]{:S(2)}) async-start(), calls=%async_computation.13 | async-start | bytes 59719680 | tf_op jit(solution)/shard_map/all_gather | solution.py:183
  10.6 1081.4 %all-gather.18.cloned.1.call-start = ((), (), s32[]{:S(2)}) async-start(), calls=%async_computation.14 | async-start | bytes 29859840 | tf_op jit(solution)/shard_map/all_gather | solution.py:184
  39.3 1201.2 %copy-start.29 = (f32[2304]{0:T(1024)}, f32[2304]{0:T(1024)S(1)}, u32[]{:S(2)}) copy-start(f32[2304]{0:T(1024)S(1)} %convert_element_type.142) | copy-start | bytes 27652
  42.1 1198.3 %copy-start.50 = (f32[128]{0:T(128)}, f32[128]{0:T(128)S(1)}, u32[]{:S(2)}) copy-start(f32[128]{0:T(128)S(1)} %add_rsqrt_fusion.1) | copy-start | bytes 1540
  115.9 204.1 %copy-start.21 = (bf16[128,2304]{0,1:T(8,128)(2,1)}, bf16[128,2304]{0,1:T(8,128)(2,1)S(1)}, u32[]{:S(2)}) copy-start(bf16[128,2304]{0,1:T(8,128)(2,1)S(1)} %copy.99) | copy-start | bytes 1769476
  217.5 100.5 %copy-start.48 = (f32[128,32]{0,1:T(8,128)S(1)}, f32[128,32]{0,1:T(8,128)}, u32[]{:S(2)}) copy-start(f32[128,32]{0,1:T(8,128)} %get-tuple-element.69) | copy-start | bytes 49156
  217.5 100.5 %copy-start.53 = (f32[128,32]{0,1:T(8,128)S(1)}, f32[128,32]{0,1:T(8,128)}, u32[]{:S(2)}) copy-start(f32[128,32]{0,1:T(8,128)} %get-tuple-element.68) | copy-start | bytes 49156
  423.4 39.7 all-to-all-start
  463.2 430.2 %all-to-all-start.2 = ((bf16[4,80,2304]{2,1,0:T(8,128)(2,1)}), bf16[4,80,2304]{2,1,0:T(8,128)(2,1)S(1)}, u32[]{:S(2)}, u32[]{:S(2)}) async-start(bf16[4,80,2304]{2,1,0:T(8,128)(2,1)} %bitcast.144), calls=%async_computation.2 | async-start | bytes 2949120 | tf_op jit(solution)/shard_map/all_to_all | solution.py:207
  893.3 221.1 %copy-start.31 = (bf16[4,80,2304]{2,1,0:T(8,128)(2,1)}, bf16[4,80,2304]{2,1,0:T(8,128)(2,1)S(1)}, u32[]{:S(2)}) copy-start(bf16[4,80,2304]{2,1,0:T(8,128)(2,1)S(1)} %all-to-all-done.2) | copy-start | bytes 4423684
  1140.8 22.6 all-to-all-start.3
  1163.4 21.5 all-to-all-start.1
  1167.0 484.6 %reduce-scatter.8.cloned.1.call-start = ((), (), s32[]{:S(2)}) async-start(), calls=%async_computation.15 | async-start | bytes 23887872 | tf_op jit(solution)/shard_map/reduce_scatter | solution.py:295
  1227.6 424.0 %reduce-scatter.10.cloned.1.call-start = ((), (), s32[]{:S(2)}) async-start(), calls=%async_computation.16 | async-start | bytes 23887872 | tf_op jit(solution)/shard_map/reduce_scatter | solution.py:296
  1238.1 618.3 %reduce-scatter.12.cloned.1.call-start = ((), (), s32[]{:S(2)}) async-start(), calls=%async_computation.17 | async-start | bytes 23887872 | tf_op jit(solution)/shard_map/reduce_scatter | solution.py:297
  1250.2 817.1 %reduce-scatter.14.cloned.1.call-start = ((), (), s32[]{:S(2)}) async-start(), calls=%async_computation.18 | async-start | bytes 23887872 | tf_op jit(solution)/shard_map/reduce_scatter | solution.py:298
  1260.2 850.9 %reduce-scatter.16.cloned.1.call-start = ((), (), s32[]{:S(2)}) async-start(), calls=%async_computation.19 | async-start | bytes 1327104
  1263.1 1856.7 %all-reduce.16.cloned.1.call-start = ((), (), s32[]{:S(2)}) async-start(), calls=%async_computation.21 | async-start | bytes 106168320
  1394.6 3739.7 %all-reduce.14.cloned.1.call-start = ((), (), s32[]{:S(2)}) async-start(), calls=%async_computation.20 | async-start | bytes 212336640
  1651.3 3697.0 %all-reduce.18.cloned.1.call-start = ((), (), s32[]{:S(2)}) async-start(), calls=%async_computation.22 | async-start | bytes 21233664 | tf_op jit(solution)/shard_map/psum | solution.py:303
  (69 other events, 449.0 us)
Sparse Core Ops, SparseCore 0:
  9.7 100.2 all-gather.7
  111.6 98.8 all-gather.9
  212.2 98.8 all-gather.11
  312.6 98.8 all-gather.13
  412.9 448.1 all-gather.15
  862.7 229.3 all-gather.17
  1227.7 206.6 reduce-scatter.7
  1436.9 208.5 reduce-scatter.9
  1647.8 208.5 reduce-scatter.11
  1858.7 208.5 reduce-scatter.13
  2070.2 27.2 reduce-scatter.15
  2099.9 1019.8 all-reduce.15
  3122.3 2011.9 all-reduce.13
  5138.5 209.7 all-reduce.17
where the time goes:
time: 5390 us; the launch traced here: 5370 us
  waiting for transfers between devices  4570 us (85%)
  local copies, waits for them, and re-layouts  385 us (7%)
  matrix products  264 us (5%)
  blocking collectives  83.2 us (2%)
    unnamed x17, waiting for transfers between devices  3000 us
    all_gather x1, waiting for transfers between devices, on_device(): lax.all_gather(w_in, 'shard', axis=0, tiled=True)  394 us
    transpose x1, local copies, waits for them, and re-layouts, on_device(): jnp.einsum('secd,secz->dez', arrived, pre_grad, preferred_element_type=jn...  213 us
    reduce_scatter x1, waiting for transfers between devices, on_device(): lax.psum_scatter(output_grad, 'shard', scatter_dimension=0, tiled=True)  211 us
    reduce_scatter x1, waiting for transfers between devices, on_device(): lax.psum_scatter(value_weight_grad, 'shard', scatter_dimension=0, tiled=T...  205 us
    psum x1, waiting for transfers between devices, on_device(): lax.psum((shard_sums[0], shard_sums[1], shard_sums[2], shard_sums[3], sha...  204 us
    all_gather x1, waiting for transfers between devices, on_device(): lax.all_gather(w_down, 'shard', axis=0, tiled=True)  199 us
  transfers between devices with their start and end apart: 18, of which 13 were waited for; matrix products, arithmetic and copies ran while one was open for 11% of the time, Pallas kernels for 0%

commit v1 on v0

v1 whole, which is shorter than its diff:
```python
import math

import jax
import jax.numpy as jnp
from jax import lax
from jax.sharding import Mesh, PartitionSpec as P

HEADS = 36

eps_norm = 1e-05
branch_scale = 1.4 / math.sqrt(40.0)
rope_base = 10000.0
masked_score = -1e30
bf16 = jnp.bfloat16
f32 = jnp.float32
SHARD = ("z", "core")
GRID = ("z", "expert")


def rope_tables(positions, head_width):
    half_width = head_width // 2
    exponents = jnp.arange(half_width).astype(f32) * 2.0 / head_width
    frequency = rope_base ** (-exponents)
    angles = positions.astype(f32)[..., None] * frequency
    return (jnp.cos(angles), jnp.sin(angles))


def rotate(values, cosine, sine_table):
    half_width = values.shape[-1] // 2
    leading = values[..., :half_width]
    trailing = values[..., half_width:]
    cos_rows = cosine[:, :, None, :]
    sin_rows = sine_table[:, :, None, :]
    return jnp.concatenate(
        [leading * cos_rows - trailing * sin_rows, trailing * cos_rows + leading * sin_rows],
        axis=-1,
    )


def rms_forward(values, norm_gain):
    inverse = lax.rsqrt(jnp.mean(values * values, axis=-1, keepdims=True) + eps_norm)
    return (values * inverse * norm_gain, inverse)


def rms_backward(values, inverse, norm_gain, upstream):
    weighted = upstream * norm_gain
    gain_grad = jnp.sum(upstream * values * inverse, axis=0)
    inner_mean = jnp.mean(weighted * values, axis=-1, keepdims=True)
    return (inverse * weighted - values * inverse * inverse * inverse * inner_mean, gain_grad)


def dot32(a, b):
    return jnp.dot(a, b, preferred_element_type=f32)


def dot_dims(a, b, da, db):
    return lax.dot_general(a, b, (((da,), (db,)), ((), ())), preferred_element_type=f32)


def ein32(spec, a, b):
    return jnp.einsum(spec, a, b, preferred_element_type=f32)


def swap_core(x, split, concat):
    return lax.all_to_all(x, "core", split_axis=split, concat_axis=concat, tiled=True)


def on_device(
    tokens,
    seq_lengths,
    routes,
    norm_attn,
    w_query,
    w_key,
    w_value,
    w_output,
    norm_ffn,
    w_router,
    w_in,
    w_down,
    cotangent,
):
    T, D = tokens.shape
    R = w_query.shape[0]
    H = D // 2
    head_width = D // HEADS
    heads = HEADS // 2
    n_exp = lax.axis_size("expert")
    n_shard = lax.axis_size("z") * lax.axis_size("core")
    experts = w_router.shape[1]
    local_experts = w_in.shape[1]
    F = w_down.shape[0]
    FF = F * n_shard
    capacity = 10 * T // (4 * experts)
    slots = experts * capacity
    highest = lax.Precision.HIGHEST
    e_index = lax.axis_index("expert")
    core = lax.axis_index("core")

    quarter = 2 * R // n_exp
    per_core = n_exp // 2
    first = (e_index % per_core) * quarter

    def column_half(weights):
        piece = [lax.dynamic_slice_in_dim(w, first, quarter, 0) for w in weights]
        mine = jnp.concatenate([lax.dynamic_slice_in_dim(p, core * H, H, 1) for p in piece], axis=1)
        other = jnp.concatenate(
            [lax.dynamic_slice_in_dim(p, (1 - core) * H, H, 1) for p in piece], axis=1
        )
        landed = lax.ppermute(other, "core", [(0, 1), (1, 0)])
        return jnp.where(core == e_index // per_core, mine, landed)

    full_qkv = lax.all_gather(
        column_half((w_query, w_key, w_value)), GRID, axis=0, tiled=True
    )
    full_output = lax.all_gather(column_half((w_output,)), GRID, axis=0, tiled=True)
    small = jnp.concatenate([w_router, norm_attn[:, None], norm_ffn[:, None]], axis=1)
    full_small = lax.all_gather(small, SHARD, axis=0, tiled=True)
    full_router = full_small[:, :experts]
    gain_attn = full_small[:, experts].astype(f32)
    gain_ffn = full_small[:, experts + 1].astype(f32)

    w_gate_cols = []
    for part in range(2):
        piece = w_in[:, :, part * FF : (part + 1) * FF].reshape(R, local_experts, n_shard, F)
        piece = piece.transpose(2, 1, 0, 3)
        w_gate_cols.append(piece)

    def reshard(piece):
        moved = lax.all_to_all(piece, SHARD, split_axis=0, concat_axis=0, tiled=True)
        return moved.transpose(1, 0, 2, 3).reshape(local_experts, n_shard * R, F)

    w_gate, w_up = reshard(w_gate_cols[0]), reshard(w_gate_cols[1])

    both = (2, T)
    residual_in = tokens.astype(f32)
    normed_in, inverse_in = rms_forward(residual_in, gain_attn)
    normed_own = normed_in.astype(bf16)
    normed_half = lax.all_gather(normed_own, "core", axis=0, tiled=True)
    lengths = lax.all_gather(seq_lengths[:, 0], "core", axis=0, tiled=True)
    row_index = jnp.arange(T)
    segment = (row_index[None, :] >= lengths[:, None]).astype(jnp.int32)
    positions = row_index[None, :] - lengths[:, None] * segment
    allowed = (segment[:, :, None] == segment[:, None, :]) & (
        row_index[None, None, :] <= row_index[None, :, None]
    )
    cosine, sine_table = rope_tables(positions, head_width)
    head_shape = both + (heads, head_width)
    qkv = dot32(normed_half, full_qkv)
    queries = rotate(qkv[:, :H].reshape(head_shape), cosine, sine_table).astype(bf16)
    keys_rot = rotate(qkv[:, H : 2 * H].reshape(head_shape), cosine, sine_table).astype(bf16)
    values = qkv[:, 2 * H :].astype(bf16).reshape(head_shape)
    score_scale = 1.0 / math.sqrt(head_width)
    scores = ein32("bqhd,bkhd->bhqk", queries, keys_rot) * score_scale
    scores = jnp.where(allowed[:, None], scores, masked_score)
    row_peak = jnp.max(scores, axis=-1, keepdims=True)
    log_total = row_peak + jnp.log(jnp.sum(jnp.exp(scores - row_peak), axis=-1, keepdims=True))
    attn_probs = jnp.exp(scores - log_total)
    probs_half = attn_probs.astype(bf16)
    context = ein32("bhqk,bkhd->bqhd", probs_half, values).astype(bf16)
    context_half = context.reshape(2 * T, H)
    context_full = lax.all_gather(context_half, "core", axis=1, tiled=True)
    mid_half = dot32(context_full, full_output)
    mid_own = swap_core(mid_half, 0, 1)
    residual_mid = residual_in + branch_scale * mid_own
    normed_mid, inverse_mid = rms_forward(residual_mid, gain_ffn)
    normed_mid_half = normed_mid.astype(bf16)

    logits = dot32(normed_mid_half, full_router)
    expert_ids = jnp.arange(experts)
    route_mask = (routes[:, :, None] == expert_ids[None, None, :]).astype(f32)
    chosen = jnp.sum(logits[:, None, :] * route_mask, axis=-1)
    gate_probs = jax.nn.softmax(chosen, axis=-1)
    flat_routes = routes.reshape(2 * T)
    hits = (flat_routes[:, None] == expert_ids[None, :]).astype(bf16)
    order = jnp.arange(2 * T)
    before = (order[:, None] > order[None, :]).astype(bf16)
    earlier = dot32(before, hits)
    slot_index = jnp.sum(earlier * hits.astype(f32), axis=1).astype(jnp.int32)
    target = (flat_routes * capacity + slot_index).reshape(T, 2)
    slot_ids = jnp.arange(slots)
    pick = [(target[:, k][:, None] == slot_ids[None, :]).astype(bf16) for k in range(2)]

    def send_rows(rows0, rows1):
        out = dot_dims(pick[0], rows0, 0, 0) + dot_dims(pick[1], rows1, 0, 0)
        out = out.astype(bf16)
        moved = lax.all_to_all(out, "expert", split_axis=0, concat_axis=0, tiled=True)
        return moved

    def spread(moved):
        rows = lax.all_gather(moved, SHARD, axis=0, tiled=True)
        if local_experts == 1:
            return rows[None]
        rows = rows.reshape(n_shard * n_exp, local_experts, capacity, D)
        return rows.transpose(1, 0, 2, 3).reshape(local_experts, -1, D)

    def bring_back(partial_rows):
        part = partial_rows.astype(bf16)
        if local_experts > 1:
            part = part.reshape(local_experts, n_shard * n_exp, capacity, D).transpose(1, 0, 2, 3)
        part = part.reshape(n_shard * slots, D)
        mine = lax.psum_scatter(part, SHARD, scatter_dimension=0, tiled=True)
        back = lax.all_to_all(mine, "expert", split_axis=0, concat_axis=0, tiled=True)
        return [dot32(pick[k], back) for k in range(2)]

    def per_expert(fn, *arrays):
        return jnp.stack([fn(*[a[i] for a in arrays]) for i in range(local_experts)])

    arrived = spread(send_rows(normed_mid_half, normed_mid_half))
    upstream = cotangent.astype(f32)
    mixture_grad = branch_scale * upstream
    row_grads = (gate_probs[:, :, None] * mixture_grad[:, None, :]).astype(bf16)
    grad_arrived = spread(send_rows(row_grads[:, 0], row_grads[:, 1]))
    down = w_down.transpose(1, 0, 2)
    gate_part = per_expert(dot32, arrived, w_gate)
    up_part = per_expert(dot32, arrived, w_up)
    sigmoid_gate = jax.nn.sigmoid(gate_part)
    silu_gate = gate_part * sigmoid_gate
    activated = (silu_gate * up_part).astype(bf16)
    expert_rows = bring_back(per_expert(dot32, activated, down))
    mixture = gate_probs[:, 0:1] * expert_rows[0] + gate_probs[:, 1:2] * expert_rows[1]
    activations = (residual_mid + branch_scale * mixture).astype(bf16)

    act_grad = per_expert(lambda a, b: dot_dims(a, b, 1, 1), grad_arrived, down)
    gate_grads = (
        act_grad * up_part * sigmoid_gate * (1.0 + gate_part * (1.0 - sigmoid_gate))
    ).astype(bf16)
    up_grads = (act_grad * silu_gate).astype(bf16)
    input_rows = bring_back(
        per_expert(
            lambda a, b, c, d: dot_dims(a, b, 1, 1) + dot_dims(c, d, 1, 1),
            gate_grads,
            w_gate,
            up_grads,
            w_up,
        )
    )
    grad_w_down = per_expert(lambda a, b: dot_dims(a, b, 0, 0), activated, grad_arrived)
    grad_w_down = grad_w_down.transpose(1, 0, 2)

    def reshard_grad(grads):
        term = per_expert(lambda a, b: dot_dims(a, b, 0, 0), arrived, grads).astype(bf16)
        term = term.reshape(local_experts, n_shard, R, F).transpose(1, 0, 2, 3)
        moved = lax.all_to_all(term, SHARD, split_axis=0, concat_axis=0, tiled=True)
        return moved.transpose(2, 1, 0, 3).reshape(R, local_experts, FF).astype(f32)

    grad_w_in = jnp.concatenate([reshard_grad(gate_grads), reshard_grad(up_grads)], axis=2)

    gate_grad = jnp.stack(
        [jnp.sum(mixture_grad * expert_rows[k], axis=-1) for k in range(2)], axis=1
    )
    chosen_grad = gate_probs * (gate_grad - jnp.sum(gate_probs * gate_grad, axis=-1, keepdims=True))
    logit_grad = jnp.sum(chosen_grad[:, :, None] * route_mask, axis=1)
    normed_mid_grad = input_rows[0] + input_rows[1]
    normed_mid_grad = normed_mid_grad + jnp.dot(
        logit_grad, jnp.transpose(full_router.astype(f32)), precision=highest
    )
    router_grad = jnp.dot(
        jnp.transpose(normed_mid_half.astype(f32)), logit_grad, precision=highest
    )
    mid_norm_grad, gain_ffn_grad = rms_backward(
        residual_mid, inverse_mid, gain_ffn, normed_mid_grad
    )
    residual_grad = upstream + mid_norm_grad
    branch_own = (branch_scale * residual_grad).astype(bf16)

    branch_half = swap_core(branch_own, 1, 0)
    output_grad = dot_dims(context_full, branch_half, 0, 0)
    context_grad = dot_dims(branch_half, full_output, 1, 1)
    context_grad = lax.psum_scatter(
        context_grad.reshape(2 * T, 2, H).transpose(1, 0, 2).reshape(4 * T, H),
        "core",
        scatter_dimension=0,
        tiled=True,
    ).reshape(head_shape)
    row_delta = jnp.sum(context_grad * context.astype(f32), axis=-1)
    context_grad_half = context_grad.astype(bf16)
    probs_grad = ein32("bqhd,bkhd->bhqk", context_grad_half, values)
    scores_grad = (
        attn_probs * (probs_grad - jnp.transpose(row_delta, (0, 2, 1))[..., None]) * score_scale
    ).astype(bf16)
    queries_grad = ein32("bhqk,bkhd->bqhd", scores_grad, keys_rot)
    keys_grad = ein32("bhqk,bqhd->bkhd", scores_grad, queries)
    values_grad = ein32("bhqk,bqhd->bkhd", probs_half, context_grad_half)
    qkv_grad = jnp.concatenate(
        [
            rotate(queries_grad, cosine, -sine_table).reshape(2 * T, H).astype(bf16),
            rotate(keys_grad, cosine, -sine_table).reshape(2 * T, H).astype(bf16),
            values_grad.reshape(2 * T, H).astype(bf16),
        ],
        axis=1,
    )
    qkv_weight_grad = dot_dims(normed_half, qkv_grad, 0, 0)
    normed_in_grad = lax.psum_scatter(
        dot_dims(qkv_grad, full_qkv, 1, 1), "core", scatter_dimension=0, tiled=True
    )
    in_norm_grad, gain_attn_grad = rms_backward(residual_in, inverse_in, gain_attn, normed_in_grad)
    grad_tokens = residual_grad + in_norm_grad

    def total(term):
        mine = lax.psum_scatter(term.astype(bf16), GRID, scatter_dimension=0, tiled=True)
        return lax.all_gather(mine, "expert", axis=0, tiled=True)

    out_sum = swap_core(total(output_grad), 0, 1).astype(f32)
    qkv_sum = total(qkv_weight_grad)
    qkv_sum = [
        swap_core(qkv_sum[:, i * H : (i + 1) * H], 0, 1).astype(f32) for i in range(3)
    ]
    small_grad = jnp.concatenate(
        [router_grad, gain_attn_grad[:, None], gain_ffn_grad[:, None]], axis=1
    )
    small_sum = lax.psum(
        lax.psum_scatter(small_grad, SHARD, scatter_dimension=0, tiled=True), "expert"
    )
    return (
        activations,
        grad_tokens,
        small_sum[:, experts],
        qkv_sum[0],
        qkv_sum[1],
        qkv_sum[2],
        out_sum,
        small_sum[:, experts + 1],
        small_sum[:, :experts],
        grad_w_in,
        grad_w_down,
    )


def solution(mesh):
    n_expert, n_shard = mesh.devices.shape
    chips = Mesh(mesh.devices.reshape(n_expert, n_shard // 2, 2), ("expert", "z", "core"))
    rows = P(("expert", "z", "core"), None)
    shard = P(SHARD)
    shard2 = P(SHARD, None)
    shard3 = P(SHARD, "expert", None)
    in_specs = (
        rows,
        rows,
        rows,
        shard,
        shard2,
        shard2,
        shard2,
        shard2,
        shard,
        shard2,
        shard3,
        shard3,
        rows,
    )
    out_specs = (
        rows,
        rows,
        shard,
        shard2,
        shard2,
        shard2,
        shard2,
        shard,
        shard2,
        shard3,
        shard3,
    )
    return jax.shard_map(
        on_device, mesh=chips, in_specs=in_specs, out_specs=out_specs, check_vma=False
    )
```

time: 5390 us -> 1820 us (0.34)
  waiting for transfers between devices: 4570 us -> 1280 us
  local copies, waits for them, and re-layouts: 385 us -> 155 us
  matrix products: 264 us -> 192 us
    unnamed x17 -> x16, waiting for transfers between devices: 3000 us -> 0.25 us
    all_gather x6 -> x8, waiting for transfers between devices: 937 us -> 369 us  [the longest x1 187 us: on_device(): lax.all_gather(column_half((w_query, w_key, w_value)), GRID, axis=0, tile...]
    transpose x2, local copies, waits for them, and re-layouts: 320 us -> 9.15 us  [on_device(): piece = piece.transpose(2, 1, 0, 3)]
    all_to_all x4 -> x8, waiting for transfers between devices: 12.3 us -> 320 us  [the longest x2 203 us: reshard(): lax.all_to_all(piece, SHARD, split_axis=0, concat_axis=0, tiled=True)]
    psum x1 -> x0, waiting for transfers between devices: 204 us -> none  [on_device(): lax.psum((shard_sums[0], shard_sums[1], shard_sums[2], shard_sums[3], sha...]
    reduce_scatter x4 -> x6, waiting for transfers between devices: 416 us -> 585 us  [the longest x2 337 us: total(): lax.psum_scatter(term.astype(bf16), GRID, scatter_dimension=0, tiled=True)]
    dot_general x26 -> x33, matrix products: 262 us -> 192 us  [the longest x14 120 us: dot_dims(): lax.dot_general(a, b, (((da,), (db,)), ((), ())), preferred_element_type=...]
    all_to_all x0 -> x6, blocking collectives: none -> 65.9 us  [the longest x2 45.5 us: send_rows(): lax.all_to_all(out, 'expert', split_axis=0, concat_axis=0, tiled=True)]
  transfers between devices with their start and end apart: 18 -> 25, of which waited for: 13 -> 17; matrix products, arithmetic and copies ran while one was open for 11% -> 13% of each run, Pallas kernels for 0% -> 0%
where the time goes in v1:
time: 1820 us; the launch traced here: 1810 us
  waiting for transfers between devices  1280 us (70%)
  matrix products  192 us (11%)
  local copies, waits for them, and re-layouts  155 us (9%)
  blocking collectives  96.7 us (5%)
  starting transfers between devices  44.9 us (2%)
  other arithmetic  32.1 us (2%)
    reduce_scatter x2, waiting for transfers between devices, total(): lax.psum_scatter(term.astype(bf16), GRID, scatter_dimension=0, tiled=True)  337 us
    reduce_scatter x2, waiting for transfers between devices, bring_back(): mine = lax.psum_scatter(part, SHARD, scatter_dimension=0, tiled=True)  239 us
    all_to_all x2, waiting for transfers between devices, reshard(): lax.all_to_all(piece, SHARD, split_axis=0, concat_axis=0, tiled=True)  203 us
    all_gather x1, waiting for transfers between devices, on_device(): lax.all_gather(column_half((w_query, w_key, w_value)), GRID, axis=0, tile...  187 us
    dot_general x14, matrix products, dot_dims(): lax.dot_general(a, b, (((da,), (db,)), ((), ())), preferred_element_type=...  120 us
    all_gather x2, waiting for transfers between devices, spread(): rows = lax.all_gather(moved, SHARD, axis=0, tiled=True)  107 us
    all_to_all x2, waiting for transfers between devices, reshard_grad(): moved = lax.all_to_all(term, SHARD, split_axis=0, concat_axis=0, tiled=True)  79.7 us
    dot_general x11, matrix products, dot32(): return jnp.dot(a, b, preferred_element_type=f32)  66.7 us
  transfers between devices with their start and end apart: 25, of which 17 were waited for; matrix products, arithmetic and copies ran while one was open for 13% of the time, Pallas kernels for 0%

profile of v1, /device:TPU:16, one launch (start us, length us, event | category | flops | bytes accessed | tf_op | source)
XLA Modules:
  0.0 1811.0 jit_solution(10325589774294244501)
XLA Ops:
  41.2 187.0 %all-gather.13.cloned.1.call-done = bf16[2304,3456]{1,0:T(8,128)(2,1)} async-done(((bf16[144,3456]{1,0:T(8,128)(2,1)}), bf16[2304,3456]{1,0:T(8,128)(2,1)}) %all-gather.13.cloned.1.call-update) | async-done | bytes 15925264 | tf_op jit(solution)/shard_map/all_gather | solution.py:113
  262.4 53.5 %all-gather.17.cloned.1.call-done = bf16[2304,1152]{1,0:T(8,128)(2,1)} async-done(((bf16[144,1152]{1,0:T(8,128)(2,1)}), bf16[2304,1152]{1,0:T(8,128)(2,1)}) %all-gather.17.cloned.1.call-update) | async-done | bytes 5308432 | tf_op jit(solution)/shard_map/all_gather | solution.py:116
  339.0 23.0 %all_to_all.153 = bf16[4,80,2304]{2,1,0:T(8,128)(2,1)} all-to-all(bf16[4,80,2304]{2,1,0:T(8,128)(2,1)S(1)} %bitcast.198), channel_id=1, replica_groups=mesh['expert'=4,'z'=4,'core'=2] {'expert'}, dimensions={0} | all-to-all | bytes 2949120 | tf_op jit(solution)/shard_map/all_to_all | solution.py:187
  399.7 141.2 %all-to-all-done.2 = bf16[8,1,288,720]{3,2,1,0:T(8,128)(2,1)} async-done(((bf16[8,1,288,720]{3,2,1,0:T(8,128)(2,1)}), bf16[8,1,288,720]{3,2,1,0:T(8,128)(2,1)}, u32[]{:S(2)}, u32[]{:S(2)}) %all-to-all-start.2) | async-done | bytes 3317792 | tf_op jit(solution)/shard_map/all_to_all | solution.py:130
  548.6 14.6 fusion.67
  563.3 62.1 %all-to-all-done.3 = bf16[8,1,288,720]{3,2,1,0:T(8,128)(2,1)} async-done(((bf16[8,1,288,720]{3,2,1,0:T(8,128)(2,1)}), bf16[8,1,288,720]{3,2,1,0:T(8,128)(2,1)}, u32[]{:S(2)}, u32[]{:S(2)}) %all-to-all-start.3) | async-done | bytes 3317792 | tf_op jit(solution)/shard_map/all_to_all | solution.py:130
  625.3 17.2 multiply_convert_fusion.2
  642.5 14.0 convolution_convert_fusion.1
  656.6 119.4 %reduce-scatter.10.cloned.1.call-done = bf16[320,2304]{1,0:T(8,128)(2,1)} async-done(((bf16[2560,2304]{1,0:T(8,128)(2,1)}), bf16[320,2304]{1,0:T(8,128)(2,1)}) %reduce-scatter.10.cloned.1.call-update) | async-done | bytes 1474576 | tf_op jit(solution)/shard_map/reduce_scatter | solution.py:202
  781.8 18.0 all-to-all-done.4
  806.8 22.5 %all_to_all.154 = bf16[4,80,2304]{2,1,0:T(8,128)(2,1)} all-to-all(bf16[4,80,2304]{2,1,0:T(8,128)(2,1)S(1)} %bitcast.197), channel_id=1, replica_groups=mesh['expert'=4,'z'=4,'core'=2] {'expert'}, dimensions={0} | all-to-all | bytes 2949120 | tf_op jit(solution)/shard_map/all_to_all | solution.py:187
  829.3 106.9 %all-gather.21.cloned.1.call-done = bf16[2560,2304]{1,0:T(8,128)(2,1)} async-done(((bf16[320,2304]{1,0:T(8,128)(2,1)}), bf16[2560,2304]{1,0:T(8,128)(2,1)}) %all-gather.21.cloned.1.call-update) | async-done | bytes 11796496 | tf_op jit(solution)/shard_map/all_gather | solution.py:191
  936.2 18.4 %multiply_convert_fusion = (bf16[2560,720]{0,1:T(8,128)(2,1)}, bf16[2560,720]{0,1:T(8,128)(2,1)S(1)}) fusion(f32[2560,720]{0,1:T(8,128)} %fusion.67, f32[2560,720]{0,1:T(8,128)} %get-tuple-element.146, bf16[2560,2304]{1,0:T(8,128)(2,1)} %all-gather.21.cloned.1.call-done, bf16[720,1,2304]{2,0,1:T(8,128)(2,1)S(1)} %copy-done), kind=kOutput, calls=%fused_computation.4 | convolution fusion | flops 8517427200 | bytes 37232640 | tf_op jit(solution)/shard_map/dot_general | solution.py:57
  954.6 16.1 fusion.68
  970.7 18.3 %add_convert_fusion = bf16[2560,2304]{1,0:T(8,128)(2,1)} fusion(f32[2560,2304]{1,0:T(8,128)} %fusion.68, bf16[2560,720]{0,1:T(8,128)(2,1)} %get-tuple-element.102, bf16[2304,720]{1,0:T(8,128)(2,1)} %bitcast.14), kind=kOutput, calls=%fused_computation | convolution fusion | flops 8505262080 | bytes 42393600 | tf_op jit(solution)/shard_map/dot_general | solution.py:57
  989.1 119.4 %reduce-scatter.12.cloned.1.call-done = bf16[320,2304]{1,0:T(8,128)(2,1)} async-done(((bf16[2560,2304]{1,0:T(8,128)(2,1)}), bf16[320,2304]{1,0:T(8,128)(2,1)}) %reduce-scatter.12.cloned.1.call-update) | async-done | bytes 1474576 | tf_op jit(solution)/shard_map/reduce_scatter | solution.py:202
  1112.4 19.1 %all-to-all-done.6 = bf16[4,80,2304]{2,1,0:T(8,128)(2,1)S(1)} async-done(((bf16[4,80,2304]{2,1,0:T(8,128)(2,1)}), bf16[4,80,2304]{2,1,0:T(8,128)(2,1)S(1)}, u32[]{:S(2)}, u32[]{:S(2)}) %all-to-all-start.6) | async-done | bytes 1474592 | tf_op jit(solution)/shard_map/all_to_all | solution.py:203
  1190.6 13.7 convolution_convert_fusion.4
  1213.0 13.8 convolution_convert_fusion.3
  1230.3 79.7 %all-to-all-done.12 = bf16[8,1,288,720]{3,2,1,0:T(8,128)(2,1)} async-done(((bf16[8,1,288,720]{3,2,1,0:T(8,128)(2,1)}), bf16[8,1,288,720]{3,2,1,0:T(8,128)(2,1)}, u32[]{:S(2)}, u32[]{:S(2)}) %all-to-all-start.12) | async-done | bytes 3317792 | tf_op jit(solution)/shard_map/all_to_all | solution.py:244
  1321.5 58.0 %reduce-scatter.20.cloned.1.call-done = bf16[144,1152]{1,0:T(8,128)(2,1)} async-done(((bf16[2304,1152]{1,0:T(8,128)(2,1)}), bf16[144,1152]{1,0:T(8,128)(2,1)}) %reduce-scatter.20.cloned.1.call-update) | async-done | bytes 331792 | tf_op jit(solution)/shard_map/reduce_scatter | solution.py:301
  1379.8 278.7 %reduce-scatter.18.cloned.1.call-done = bf16[144,3456]{1,0:T(8,128)(2,1)} async-done(((bf16[2304,3456]{1,0:T(8,128)(2,1)}), bf16[144,3456]{1,0:T(8,128)(2,1)}) %reduce-scatter.18.cloned.1.call-update) | async-done | bytes 995344 | tf_op jit(solution)/shard_map/reduce_scatter | solution.py:301
  1715.0 21.2 %copy.300 = f32[288,1,11520]{2,1,0:T(1,128)} copy(f32[288,1,11520]{2,0,1:T(8,128)} %maximum_convert_fusion) | data formatting | bytes 26542080
  1739.6 16.2 psum.7
  (312 shorter events, 343.8 us)
Async XLA Ops:
  7.2 34.0 %all-gather.11.cloned.1.call-start = ((), (), s32[]{:S(2)}) async-start(), calls=%async_computation.21 | async-start | bytes 1769472 | tf_op jit(solution)/shard_map/all_gather | solution.py:139
  13.4 15.5 collective-permute-start
  28.8 199.5 %all-gather.13.cloned.1.call-start = ((), (), s32[]{:S(2)}) async-start(), calls=%async_computation.22 | async-start | bytes 16920576 | tf_op jit(solution)/shard_map/all_gather | solution.py:113
  31.3 284.6 %all-gather.17.cloned.1.call-start = ((), (), s32[]{:S(2)}) async-start(), calls=%async_computation.24 | async-start | bytes 5640192 | tf_op jit(solution)/shard_map/all_gather | solution.py:116
  36.4 290.0 %all-gather.15.cloned.1.call-start = ((), (), s32[]{:S(2)}) async-start(), calls=%async_computation.23 | async-start | bytes 1769472 | tf_op jit(solution)/shard_map/all_gather | solution.py:162
  261.6 287.0 %all-gather.19.cloned.1.call-start = ((), (), s32[]{:S(2)}) async-start(), calls=%async_computation.25 | async-start | bytes 13271040 | tf_op jit(solution)/shard_map/all_gather | solution.py:191
  381.5 159.4 %all-to-all-start.2 = ((bf16[8,1,288,720]{3,2,1,0:T(8,128)(2,1)}), bf16[8,1,288,720]{3,2,1,0:T(8,128)(2,1)}, u32[]{:S(2)}, u32[]{:S(2)}) async-start(bf16[8,1,288,720]{3,2,1,0:T(8,128)(2,1)} %copy.275), calls=%async_computation.2 | async-start | bytes 7077888 | tf_op jit(solution)/shard_map/all_to_all | solution.py:130
  540.9 84.5 %all-to-all-start.3 = ((bf16[8,1,288,720]{3,2,1,0:T(8,128)(2,1)}), bf16[8,1,288,720]{3,2,1,0:T(8,128)(2,1)}, u32[]{:S(2)}, u32[]{:S(2)}) async-start(bf16[8,1,288,720]{3,2,1,0:T(8,128)(2,1)} %copy.276), calls=%async_computation.3 | async-start | bytes 7077888 | tf_op jit(solution)/shard_map/all_to_all | solution.py:130
  548.6 227.4 %reduce-scatter.10.cloned.1.call-start = ((), (), s32[]{:S(2)}) async-start(), calls=%async_computation.26 | async-start | bytes 13271040 | tf_op jit(solution)/shard_map/reduce_scatter | solution.py:202
  776.0 23.8 %all-to-all-start.4 = ((bf16[4,80,2304]{2,1,0:T(8,128)(2,1)}), bf16[4,80,2304]{2,1,0:T(8,128)(2,1)}, u32[]{:S(2)}, u32[]{:S(2)}) async-start(bf16[4,80,2304]{2,1,0:T(8,128)(2,1)} %bitcast.218), calls=%async_computation.5 | async-start | bytes 2949120 | tf_op jit(solution)/shard_map/all_to_all | solution.py:203
  780.4 155.9 %all-gather.21.cloned.1.call-start = ((), (), s32[]{:S(2)}) async-start(), calls=%async_computation.27 | async-start | bytes 13271040 | tf_op jit(solution)/shard_map/all_gather | solution.py:191
  829.3 279.2 %reduce-scatter.12.cloned.1.call-start = ((), (), s32[]{:S(2)}) async-start(), calls=%async_computation.28 | async-start | bytes 13271040 | tf_op jit(solution)/shard_map/reduce_scatter | solution.py:202
  1108.5 23.0 %all-to-all-start.6 = ((bf16[4,80,2304]{2,1,0:T(8,128)(2,1)}), bf16[4,80,2304]{2,1,0:T(8,128)(2,1)S(1)}, u32[]{:S(2)}, u32[]{:S(2)}) async-start(bf16[4,80,2304]{2,1,0:T(8,128)(2,1)} %bitcast.217), calls=%async_computation.8 | async-start | bytes 2949120 | tf_op jit(solution)/shard_map/all_to_all | solution.py:203
  1112.2 40.6 %reduce-scatter.14.cloned.1.call-start = ((), (), s32[]{:S(2)}) async-start(), calls=%async_computation.29 | async-start | bytes 3538944 | tf_op jit(solution)/shard_map/reduce_scatter | solution.py:270
  1143.4 175.0 %reduce-scatter.16.cloned.1.call-start = ((), (), s32[]{:S(2)}) async-start(), calls=%async_computation.30 | async-start | bytes 3538944 | tf_op jit(solution)/shard_map/reduce_scatter | solution.py:294
  1174.8 204.7 %reduce-scatter.20.cloned.1.call-start = ((), (), s32[]{:S(2)}) async-start(), calls=%async_computation.33 | async-start | bytes 5640192 | tf_op jit(solution)/shard_map/reduce_scatter | solution.py:301
  1181.2 477.3 %reduce-scatter.18.cloned.1.call-start = ((), (), s32[]{:S(2)}) async-start(), calls=%async_computation.31 | async-start | bytes 16920576 | tf_op jit(solution)/shard_map/reduce_scatter | solution.py:301
  1207.9 102.2 %all-to-all-start.12 = ((bf16[8,1,288,720]{3,2,1,0:T(8,128)(2,1)}), bf16[8,1,288,720]{3,2,1,0:T(8,128)(2,1)}, u32[]{:S(2)}, u32[]{:S(2)}) async-start(bf16[8,1,288,720]{3,2,1,0:T(8,128)(2,1)} %bitcast.190), calls=%async_computation.18 | async-start | bytes 7077888 | tf_op jit(solution)/shard_map/all_to_all | solution.py:244
  1310.0 383.5 %all-to-all-start.13 = ((bf16[8,1,288,720]{3,2,1,0:T(8,128)(2,1)}), bf16[8,1,288,720]{3,2,1,0:T(8,128)(2,1)}, u32[]{:S(2)}, u32[]{:S(2)}) async-start(bf16[8,1,288,720]{3,2,1,0:T(8,128)(2,1)} %bitcast.189), calls=%async_computation.19 | async-start | bytes 7077888 | tf_op jit(solution)/shard_map/all_to_all | solution.py:244
  1318.0 420.6 %reduce-scatter.22.cloned.1.call-start = ((), (), s32[]{:S(2)}) async-start(), calls=%async_computation.35 | async-start | bytes 1327104
  1321.5 435.5 %all-gather.25.cloned.1.call-start = ((), (), s32[]{:S(2)}) async-start(), calls=%async_computation.34 | async-start | bytes 1658880 | tf_op jit(solution)/shard_map/all_gather | solution.py:302
  1379.6 396.3 %all-gather.23.cloned.1.call-start = ((), (), s32[]{:S(2)}) async-start(), calls=%async_computation.32 | async-start | bytes 4976640 | tf_op jit(solution)/shard_map/all_gather | solution.py:302
  1785.4 7.8 all-to-all-start.10
  1793.2 7.7 all-to-all-start.9
  (61 other events, 1500.9 us)
Sparse Core Ops, SparseCore 0:
  28.9 12.2 all-gather.10
  44.6 183.6 all-gather.12
  231.7 84.1 all-gather.16
  317.8 8.5 all-gather.14
  362.2 180.4 all-gather.18
  656.7 119.2 reduce-scatter.9
  829.4 106.7 all-gather.20
  989.2 119.1 reduce-scatter.11
  1143.5 9.2 reduce-scatter.13
  1174.9 11.0 reduce-scatter.15
  1191.9 187.6 reduce-scatter.19
  1385.2 273.2 reduce-scatter.17
  1661.4 26.3 reduce-scatter.21
  1689.5 33.5 all-gather.24
  1724.8 51.0 all-gather.22

commit v2 on v1

--- a/solution.py
+++ b/solution.py
@@ -1,8 +1,11 @@
+import functools
 import math
 
 import jax
 import jax.numpy as jnp
 from jax import lax
+from jax.experimental import pallas as pl
+from jax.experimental.pallas import tpu as pltpu
 from jax.sharding import Mesh, PartitionSpec as P
 
 HEADS = 36
@@ -15,6 +18,609 @@
 f32 = jnp.float32
 SHARD = ("z", "core")
 GRID = ("z", "expert")
+ANY = pl.BlockSpec(memory_space=pl.ANY)
+
+
+def place():
+    e, z, c = lax.axis_index("expert"), lax.axis_index("z"), lax.axis_index("core")
+    across_x = e + 1 - 2 * (e % 2)
+    across_y = (e + 2) % 4
+    return e, z, c, across_x, across_y
+
+
+def remote(src, dst, send, recv, e, z, c):
+    return pltpu.make_async_remote_copy(
+        src_ref=src,
+        dst_ref=dst,
+        send_sem=send,
+        recv_sem=recv,
+        device_id=(e, z, c),
+        device_id_type=pl.DeviceIdType.MESH,
+    )
+
+
+def greet(nz, both_cores):
+    e, z, c, ex, ey = place()
+    barrier = pltpu.get_barrier_semaphore()
+
+    def hail(te, tz, tc):
+        pl.semaphore_signal(
+            barrier, inc=1, device_id=(te, tz, tc), device_id_type=pl.DeviceIdType.MESH
+        )
+
+    cores = (c, 1 - c) if both_cores[0] else (c,)
+    plane = (c, 1 - c) if both_cores[1] else (c,)
+    hail(e, z, 1 - c)
+    for t in plane:
+        hail(ex, z, t)
+        hail(ey, z, t)
+    for step in (-1, 1):
+
+        @pl.when((z + step >= 0) & (z + step < nz))
+        def _():
+            for t in cores:
+                hail(e, z + step, t)
+
+    ends = jnp.where(z > 0, 1, 0) + jnp.where(z < nz - 1, 1, 0)
+    pl.semaphore_wait(barrier, 1 + 2 * len(plane) + len(cores) * ends)
+
+
+def cut(k, Q):
+    big = (Q // 2 + 15) // 16 * 16
+    return big if k % 2 == 0 else Q - big
+
+
+def gather_kernel(
+    nz, Q, H,
+    q_ref, k_ref, v_ref, o_ref, s_ref, t_ref, l_ref,
+    qkv_out, o_out, s_out, t_out, l_out,
+    zrecv, zhop, zsend, near_recv, near_send, far_recv, far_send, own, sib_send, sib_recv,
+):
+    e, z, c, ex, ey = place()
+    holder, turn = e // 2, e % 2
+    sources = (q_ref, k_ref, v_ref, o_ref, s_ref)
+    K = len(sources)
+
+    def src(k, half, j, count=1):
+        rows = pl.ds(pl.multiple_of(j * Q, 16), count * Q)
+        if k == 4:
+            return sources[k].at[rows, :]
+        return sources[k].at[rows, pl.ds(pl.multiple_of(half * H, 128), H)]
+
+    def dst(k, zz, quarter, r0=0, n=Q):
+        rows = pl.ds(pl.multiple_of((zz * 4 + quarter) * Q + r0, 16), n)
+        if k < 3:
+            return qkv_out.at[rows, pl.ds(k * H, H)]
+        return (o_out if k == 3 else s_out).at[rows, :]
+
+    greet(nz, (True, False))
+
+    pairs = ((t_ref, t_out), (l_ref, l_out))
+    extra = []
+    for n, (a, b) in enumerate(pairs):
+        mine = pltpu.make_async_copy(a, b.at[c], own.at[K + n])
+        mine.start()
+        theirs = remote(a, b.at[c], sib_send.at[K + n], sib_recv.at[K + n], e, z, 1 - c)
+        theirs.start()
+        extra += [mine, theirs]
+
+    def first_hop(k, step, half):
+        side = 0 if step > 0 else 1
+        return remote(
+            src(k, half, turn), dst(k, z, e), zhop.at[k, side, half], zrecv.at[k, side, 0],
+            e, z + step, half,
+        )
+
+    for k in range(K):
+        for step in (1, -1):
+
+            @pl.when((c == holder) & (z + step >= 0) & (z + step < nz))
+            def _():
+                first_hop(k, step, 0).start()
+                first_hop(k, step, 1).start()
+
+    for k in range(K):
+        rows = src(k, c, 0, 2), dst(k, z, 2 * c, 0, 2 * Q)
+        mine = pltpu.make_async_copy(rows[0], rows[1], own.at[k])
+        mine.start()
+        theirs = remote(
+            src(k, 1 - c, 0, 2), rows[1], sib_send.at[k], sib_recv.at[k], e, z, 1 - c
+        )
+        theirs.start()
+        extra += [mine, theirs]
+
+    def where(side, i):
+        return z - 1 - i if side == 0 else z + 1 + i
+
+    def onward(k, side, i):
+        slab = dst(k, where(side, i), e)
+        step = 1 if side == 0 else -1
+        return remote(
+            slab, slab, zsend.at[k, side, i], zrecv.at[k, side, i + 1], e, z + step, c
+        )
+
+    def near(k, side, i, axis):
+        slab = dst(k, where(side, i), e)
+        return remote(
+            slab, slab, near_send.at[k, side, i, axis], near_recv.at[k, side, i, axis],
+            ex if axis == 0 else ey, z, c,
+        )
+
+    def near_wait(k, side, i, axis):
+        slab = dst(k, where(side, i), ex if axis == 0 else ey)
+        remote(
+            slab, slab, near_send.at[k, side, i, axis], near_recv.at[k, side, i, axis], ex, z, c
+        ).wait_recv()
+
+    def far(k, side, i, axis):
+        a = cut(k, Q)
+        if axis == 0:
+            slab = dst(k, where(side, i), ex, 0, a)
+        else:
+            slab = dst(k, where(side, i), ey, a, Q - a)
+        return remote(
+            slab, slab, far_send.at[k, side, i, axis], far_recv.at[k, side, i, axis],
+            ey if axis == 0 else ex, z, c,
+        )
+
+    def exists(side, i):
+        zz = where(side, i)
+        return (zz >= 0) & (zz < nz)
+
+    def inside(side):
+        return z < nz - 1 if side == 0 else z > 0
+
+    def arrive(k, side, i):
+        @pl.when(exists(side, i))
+        def _():
+            slab = dst(k, where(side, i), e)
+            remote(
+                slab, slab, zsend.at[k, side, i], zrecv.at[k, side, i], e, z, c
+            ).wait_recv()
+            if i < nz - 2:
+
+                @pl.when(inside(side))
+                def _():
+                    onward(k, side, i).start()
+
+            near(k, side, i, 0).start()
+            near(k, side, i, 1).start()
+
+    def relay(k, side, i):
+        @pl.when(exists(side, i))
+        def _():
+            for axis in range(2):
+                near_wait(k, side, i, axis)
+                far(k, side, i, axis).start()
+
+    steps = [(k, side, i) for i in range(nz - 1) for k in range(K) for side in range(2)]
+    lag = 2 * K
+    for n, step in enumerate(steps):
+        arrive(*step)
+        if n >= lag:
+            relay(*steps[n - lag])
+    for step in steps[len(steps) - lag :]:
+        relay(*step)
+
+    for k, side, i in steps:
+
+        @pl.when(exists(side, i))
+        def _():
+            if i < nz - 2:
+
+                @pl.when(inside(side))
+                def _():
+                    onward(k, side, i).wait_send()
+
+            a = cut(k, Q)
+            zz, diagonal = where(side, i), (ex + 2) % 4
+            for axis in range(2):
+                near(k, side, i, axis).wait_send()
+                far(k, side, i, axis).wait_send()
+                slab = dst(k, zz, diagonal, 0, a) if axis == 0 else dst(k, zz, diagonal, a, Q - a)
+                remote(
+                    slab, slab, far_send.at[k, side, i, axis], far_recv.at[k, side, i, axis],
+                    ex, z, c,
+                ).wait_recv()
+
+    for k in range(K):
+        for step in (1, -1):
+
+            @pl.when((c == holder) & (z + step >= 0) & (z + step < nz))
+            def _():
+                first_hop(k, step, 0).wait_send()
+                first_hop(k, step, 1).wait_send()
+
+    for copy in extra:
+        copy.wait()
+
+
+def gather_attention(nz, weights, small, tokens, lengths):
+    R, D = weights[0].shape
+    Q, H = R // 2, D // 2
+    K = len(weights) + 1
+    dma = pltpu.SemaphoreType.DMA
+    any_ = ANY
+    W = small.shape[1]
+    sd = jax.ShapeDtypeStruct
+    outs = pl.pallas_call(
+        functools.partial(gather_kernel, nz, Q, H),
+        out_shape=(
+            sd((nz * 4 * Q, 3 * H), bf16),
+            sd((nz * 4 * Q, H), bf16),
+            sd((nz * 4 * Q, W), bf16),
+            sd((2,) + tokens.shape, bf16),
+            sd((2,) + lengths.shape, lengths.dtype),
+        ),
+        in_specs=[any_] * 7,
+        out_specs=(any_,) * 5,
+        scratch_shapes=[
+            dma((K, 2, nz - 1)),
+            dma((K, 2, 2)),
+            dma((K, 2, nz - 1)),
+            dma((K, 2, nz - 1, 2)),
+            dma((K, 2, nz - 1, 2)),
+            dma((K, 2, nz - 1, 2)),
+            dma((K, 2, nz - 1, 2)),
+            dma((K + 2,)),
+            dma((K + 2,)),
+            dma((K + 2,)),
+        ],
+        compiler_params=pltpu.CompilerParams(collective_id=0, has_side_effects=True),
+        cost_estimate=pl.CostEstimate(
+            flops=10**11, bytes_accessed=8 * D * H * 2, transcendentals=0
+        ),
+        name="gather_attention",
+    )(*weights, small, tokens, lengths)
+    return outs
+
+
+def reduce_kernel(
+    nz, Q, widths,
+    *refs,
+):
+    K = len(widths)
+    parts, refs = refs[:K], refs[K:]
+    outs, refs = refs[:K], refs[K:]
+    (
+        mine, mine_x, mine_y, from_x, from_y, via_x, via_y, from_z, result,
+        load, via_send, via_recv, plain_send, plain_recv, sum_send, sum_recv,
+        zsend, zrecv, fin_send, fin_recv, far_send, far_recv, own,
+    ) = refs
+    e, z, c, ex, ey = place()
+    diagonal = (ex + 2) % 4
+    holder, turn = e // 2, e % 2
+    offs = [sum(widths[:k]) for k in range(K)]
+
+    def order(i):
+        code = 0
+        for zz in range(nz):
+            far_first = sorted(range(nz), key=lambda t: (-abs(t - zz), t))
+            code += far_first[i] * nz**zz
+        power = 1
+        for zz in range(nz):
+            power = power + (nz**zz - 1) * jnp.where(z == zz, 1, 0)
+        return (code // power) % nz
+
+    dest = [order(i) for i in range(nz)]
+
+    def cols(k):
+        return pl.ds(offs[k], widths[k])
+
+    greet(nz, (False, True))
+
+    def loads(k, i):
+        a = cut(k, Q)
+        zz = dest[i]
+        out = [
+            (parts[k].at[zz, e], mine.at[i, :, cols(k)]),
+            (parts[k].at[zz, ex, pl.ds(a, Q - a), :], mine_x.at[i, pl.ds(0, Q - a), cols(k)]),
+            (parts[k].at[zz, ey, pl.ds(0, a), :], mine_y.at[i, pl.ds(0, a), cols(k)]),
+        ]
+        return [pltpu.make_async_copy(s, d, load.at[k, i, n]) for n, (s, d) in enumerate(out)]
+
+    def via(k, i, axis):
+        a = cut(k, Q)
+        zz = dest[i]
+        if axis == 0:
+            return remote(
+                parts[k].at[zz, diagonal, pl.ds(0, a), :], via_x.at[i, pl.ds(0, a), cols(k)],
+                via_send.at[k, i, 0], via_recv.at[k, i, 0], ex, z, c,
+            )
+        return remote(
+            parts[k].at[zz, diagonal, pl.ds(a, Q - a), :], via_y.at[i, pl.ds(0, Q - a), cols(k)],
+            via_send.at[k, i, 1], via_recv.at[k, i, 1], ey, z, c,
+        )
+
+    def plain(k, i, axis):
+        a = cut(k, Q)
+        zz = dest[i]
+        if axis == 0:
+            return remote(
+                parts[k].at[zz, ex, pl.ds(0, a), :], from_x.at[i, pl.ds(0, a), cols(k)],
+                plain_send.at[k, i, 0], plain_recv.at[k, i, 0], ex, z, c,
+            )
+        return remote(
+            parts[k].at[zz, ey, pl.ds(a, Q - a), :], from_y.at[i, pl.ds(a, Q - a), cols(k)],
+            plain_send.at[k, i, 1], plain_recv.at[k, i, 1], ey, z, c,
+        )
+
+    def summed(k, i, axis):
+        a = cut(k, Q)
+        if axis == 0:
+            return remote(
+                mine_x.at[i, pl.ds(0, Q - a), cols(k)], from_x.at[i, pl.ds(a, Q - a), cols(k)],
+                sum_send.at[k, i, 0], sum_recv.at[k, i, 0], ex, z, c,
+            )
+        return remote(
+            mine_y.at[i, pl.ds(0, a), cols(k)], from_y.at[i, pl.ds(0, a), cols(k)],
+            sum_send.at[k, i, 1], sum_recv.at[k, i, 1], ey, z, c,
+        )
+
+    def add(target, others, n, k):
+        @pl.loop(0, n // 16)
+        def _(b):
+            rows = pl.ds(pl.multiple_of(b * 16, 16), 16)
+            acc = target[rows, cols(k)].astype(f32)
+            for o in others:
+                acc = acc + o[rows, cols(k)].astype(f32)
+            target[rows, cols(k)] = acc.astype(bf16)
+
+    pairs = [(k, i) for i in range(nz) for k in range(K)]
+    for k, i in pairs:
+        via(k, i, 0).start()
+        via(k, i, 1).start()
+        for copy in loads(k, i):
+            copy.start()
+        plain(k, i, 0).start()
+        plain(k, i, 1).start()
+
+    def combine(k, i):
+        a = cut(k, Q)
+        group = loads(k, i)
+        group[1].wait()
+        group[2].wait()
+        via(k, i, 0).wait_recv()
+        add(mine_y.at[i], [via_x.at[i]], a, k)
+        summed(k, i, 1).start()
+        via(k, i, 1).wait_recv()
+        add(mine_x.at[i], [via_y.at[i]], Q - a, k)
+        summed(k, i, 0).start()
+
+    def zcopy(k, i):
+        step = jnp.where(dest[i] > z, 1, -1)
+        side = jnp.where(dest[i] > z, 0, 1)
+        return remote(
+            mine.at[i, :, cols(k)], from_z.at[side, dest[i], :, cols(k)],
+            zsend.at[k, i], zrecv.at[k, side, dest[i]], e, z + step, c,
+        )
+
+    def zwait(k, side, zz):
+        slab = from_z.at[side, zz, :, cols(k)]
+        remote(slab, slab, zsend.at[k, 0], zrecv.at[k, side, zz], e, z, c).wait_recv()
+
+    def finish(k, i):
+        loads(k, i)[0].wait()
+        for axis in range(2):
+            plain(k, i, axis).wait_recv()
+            summed(k, i, axis).wait_recv()
+        add(mine.at[i], [from_x.at[i], from_y.at[i]], Q, k)
+        zz = dest[i]
+        if i < nz - 1:
+            for side in range(2):
+                going = zz > z if side == 0 else zz < z
+                behind = z > 0 if side == 0 else z < nz - 1
+
+                @pl.when(going & behind)
+                def _():
+                    zwait(k, side, zz)
+                    add(mine.at[i], [from_z.at[side, zz]], Q, k)
+
+            zcopy(k, i).start()
+
+    def fin(k, axis):
+        if widths[k] == widths[-1] and k == K - 1:
+            land = outs[k].at[turn, c]
+        else:
+            land = outs[k].at[turn, :, pl.ds(pl.multiple_of(c * widths[k], 128), widths[k])]
+        te = (ex, ey, e)[axis]
+        return remote(
+            result.at[:, cols(k)], land, fin_send.at[k, axis], fin_recv.at[k, axis, c],
+            te, z, holder,
+        )
+
+    def total(k):
+        last = nz - 1
+        for side in range(2):
+            behind = z > 0 if side == 0 else z < nz - 1
+
+            @pl.when(behind)
+            def _():
+                zwait(k, side, z)
+                add(mine.at[last], [from_z.at[side, z]], Q, k)
+
+        @pl.loop(0, Q // 16)
+        def _(b):
+            rows = pl.ds(pl.multiple_of(b * 16, 16), 16)
+            result[rows, cols(k)] = mine[last, rows, cols(k)]
+
+        fin(k, 0).start()
+        fin(k, 1).start()
+
+        @pl.when(c == holder)
+        def _():
+            pltpu.make_async_copy(result.at[:, cols(k)], fin_own(k), own.at[k]).start()
+
+        @pl.when(c != holder)
+        def _():
+            fin(k, 2).start()
+
+    def fin_own(k):
+        if k == K - 1:
+            return outs[k].at[turn, c]
+        return outs[k].at[turn, :, pl.ds(pl.multiple_of(c * widths[k], 128), widths[k])]
+
+    lag = K
+    for n, (k, i) in enumerate(pairs):
+        combine(k, i)
+        if n >= lag:
+            k2, i2 = pairs[n - lag]
+            finish(k2, i2)
+    for k2, i2 in pairs[len(pairs) - lag :]:
+        finish(k2, i2)
+    for k in range(K):
+        total(k)
+
+    def slot(k, j, half, r0=0, n=Q):
+        if k == K - 1:
+            return outs[k].at[j, half, pl.ds(r0, n), :]
+        return outs[k].at[j, pl.ds(r0, n), pl.ds(half * widths[k], widths[k])]
+
+    def got(k, axis, half):
+        j = (ex if axis == 0 else ey) % 2
+        view = slot(k, j, half)
+        return remote(
+            view, view, fin_send.at[k, axis], fin_recv.at[k, axis, half], e, z, c
+        )
+
+    def passed(k, axis, half, quarter):
+        a = cut(k, Q)
+        j = quarter % 2
+        view = slot(k, j, half, 0, a) if axis == 0 else slot(k, j, half, a, Q - a)
+        return remote(
+            view, view, far_send.at[k, half], far_recv.at[k, axis, half],
+            ey if axis == 0 else ex, z, c,
+        )
+
+    for k in range(K):
+        for axis in range(2):
+
+            @pl.when((c == holder) if axis == 0 else (c != holder))
+            def _():
+                for half in range(2):
+                    got(k, axis, half).wait_recv()
+                    passed(k, axis, half, ex if axis == 0 else ey).start()
+
+    for k in range(K):
+        for axis in range(2):
+
+            @pl.when((c == holder) if axis == 0 else (c != holder))
+            def _():
+                for half in range(2):
+                    passed(k, axis, half, ex if axis == 0 else ey).wait_send()
+
+        @pl.when(c != holder)
+        def _():
+            for half in range(2):
+                passed(k, 0, half, diagonal).wait_recv()
+                passed(k, 1, half, diagonal).wait_recv()
+            fin(k, 2).wait_send()
+
+        @pl.when(c == holder)
+        def _():
+            pltpu.make_async_copy(result.at[:, cols(k)], fin_own(k), own.at[k]).wait()
+            other = slot_of(outs, k, K, turn, 1 - c, widths)
+            remote(
+                other, other, fin_send.at[k, 2], fin_recv.at[k, 2, 1 - c], e, z, c
+            ).wait_recv()
+
+        fin(k, 0).wait_send()
+        fin(k, 1).wait_send()
+        for i in range(nz):
+            for axis in range(2):
+                via(k, i, axis).wait_send()
+                plain(k, i, axis).wait_send()
+                summed(k, i, axis).wait_send()
+            if i < nz - 1:
+                zcopy(k, i).wait_send()
+
+
+def slot_of(outs, k, K, j, half, widths):
+    if k == K - 1:
+        return outs[k].at[j, half]
+    return outs[k].at[j, :, pl.ds(pl.multiple_of(half * widths[k], 128), widths[k])]
+
+
+def reduce_attention(nz, parts):
+    Q = parts[0].shape[2]
+    widths = tuple(p.shape[3] for p in parts)
+    W, K = sum(widths), len(parts)
+    big = max(cut(0, Q), cut(1, Q))
+    dma = pltpu.SemaphoreType.DMA
+    sd = jax.ShapeDtypeStruct
+    vm = pltpu.VMEM
+    out_shape = tuple(sd((2, Q, 2 * w), bf16) for w in widths[:-1]) + (
+        sd((2, 2, Q, widths[-1]), bf16),
+    )
+    return pl.pallas_call(
+        functools.partial(reduce_kernel, nz, Q, widths),
+        out_shape=out_shape,
+        in_specs=[ANY] * K,
+        out_specs=(ANY,) * K,
+        scratch_shapes=[
+            vm((nz, Q, W), bf16),
+            vm((nz, big, W), bf16),
+            vm((nz, big, W), bf16),
+            vm((nz, Q, W), bf16),
+            vm((nz, Q, W), bf16),
+            vm((nz, big, W), bf16),
+            vm((nz, big, W), bf16),
+            vm((2, nz, Q, W), bf16),
+            vm((Q, W), bf16),
+            dma((K, nz, 3)),
+            dma((K, nz, 2)),
+            dma((K, nz, 2)),
+            dma((K, nz, 2)),
+            dma((K, nz, 2)),
+            dma((K, nz, 2)),
+            dma((K, nz, 2)),
+            dma((K, nz)),
+            dma((K, 2, nz)),
+            dma((K, 3)),
+            dma((K, 3, 2)),
+            dma((K, 2)),
+            dma((K, 2, 2)),
+            dma((K,)),
+        ],
+        compiler_params=pltpu.CompilerParams(
+            collective_id=1, has_side_effects=True, vmem_limit_bytes=60 << 20
+        ),
+        cost_estimate=pl.CostEstimate(
+            flops=10**11, bytes_accessed=nz * 4 * Q * W * 2, transcendentals=0
+        ),
+        name="reduce_attention",
+    )(*parts)
+
+
+def gather_plain(nz, weights, small, tokens, lengths):
+    core, H = lax.axis_index("core"), weights[0].shape[1] // 2
+    full = [
+        lax.all_gather(swap_core(w, 1, 0), "z", axis=0, tiled=True) for w in weights
+    ]
+    return (
+        jnp.concatenate(full[:3], axis=1),
+        full[3],
+        lax.all_gather(small, SHARD, axis=0, tiled=True),
+        lax.all_gather(tokens, "core", axis=0),
+        lax.all_gather(lengths, "core", axis=0),
+    )
+
+
+def reduce_plain(nz, parts):
+    n_exp = lax.axis_size("expert")
+    out = []
+    for k, part in enumerate(parts):
+        Q, w = part.shape[2:]
+        mine = lax.psum_scatter(part.reshape(nz * 4 * Q, w), "z", scatter_dimension=0, tiled=True)
+        mine = lax.psum(mine, "expert")
+        if k < len(parts) - 1:
+            out.append(swap_core(mine, 0, 1).reshape(2, Q, 2 * w))
+        else:
+            both = lax.all_to_all(
+                mine.reshape(2, 2 * Q, w), "core", split_axis=0, concat_axis=0, tiled=True
+            )
+            out.append(both.reshape(2, 2, Q, w).transpose(1, 0, 2, 3))
+    return out
 
 
 def rope_tables(positions, head_width):
@@ -97,25 +703,14 @@
     e_index = lax.axis_index("expert")
     core = lax.axis_index("core")
 
-    quarter = 2 * R // n_exp
-    per_core = n_exp // 2
-    first = (e_index % per_core) * quarter
-
-    def column_half(weights):
-        piece = [lax.dynamic_slice_in_dim(w, first, quarter, 0) for w in weights]
-        mine = jnp.concatenate([lax.dynamic_slice_in_dim(p, core * H, H, 1) for p in piece], axis=1)
-        other = jnp.concatenate(
-            [lax.dynamic_slice_in_dim(p, (1 - core) * H, H, 1) for p in piece], axis=1
-        )
-        landed = lax.ppermute(other, "core", [(0, 1), (1, 0)])
-        return jnp.where(core == e_index // per_core, mine, landed)
-
-    full_qkv = lax.all_gather(
-        column_half((w_query, w_key, w_value)), GRID, axis=0, tiled=True
-    )
-    full_output = lax.all_gather(column_half((w_output,)), GRID, axis=0, tiled=True)
+    nz = lax.axis_size("z")
     small = jnp.concatenate([w_router, norm_attn[:, None], norm_ffn[:, None]], axis=1)
-    full_small = lax.all_gather(small, SHARD, axis=0, tiled=True)
+    small = jnp.pad(small, ((0, 0), (0, 128 - small.shape[1])))
+    length_rows = jnp.broadcast_to(seq_lengths[:, :1], (8, 128))
+    gather = gather_attention if n_exp == 4 else gather_plain
+    full_qkv, full_output, full_small, chip_tokens, chip_lengths = gather(
+        nz, (w_query, w_key, w_value, w_output), small, tokens, length_rows
+    )
     full_router = full_small[:, :experts]
     gain_attn = full_small[:, experts].astype(f32)
     gain_ffn = full_small[:, experts + 1].astype(f32)
@@ -134,10 +729,9 @@
 
     both = (2, T)
     residual_in = tokens.astype(f32)
-    normed_in, inverse_in = rms_forward(residual_in, gain_attn)
-    normed_own = normed_in.astype(bf16)
-    normed_half = lax.all_gather(normed_own, "core", axis=0, tiled=True)
-    lengths = lax.all_gather(seq_lengths[:, 0], "core", axis=0, tiled=True)
+    inverse_in = rms_forward(residual_in, gain_attn)[1]
+    normed_half = rms_forward(chip_tokens.reshape(2 * T, D).astype(f32), gain_attn)[0].astype(bf16)
+    lengths = chip_lengths[:, 0, 0]
     row_index = jnp.arange(T)
     segment = (row_index[None, :] >= lengths[:, None]).astype(jnp.int32)
     positions = row_index[None, :] - lengths[:, None] * segment
@@ -265,7 +859,6 @@
     branch_own = (branch_scale * residual_grad).astype(bf16)
 
     branch_half = swap_core(branch_own, 1, 0)
-    output_grad = dot_dims(context_full, branch_half, 0, 0)
     context_grad = dot_dims(branch_half, full_output, 1, 1)
     context_grad = lax.psum_scatter(
         context_grad.reshape(2 * T, 2, H).transpose(1, 0, 2).reshape(4 * T, H),
@@ -282,44 +875,36 @@
     queries_grad = ein32("bhqk,bkhd->bqhd", scores_grad, keys_rot)
     keys_grad = ein32("bhqk,bqhd->bkhd", scores_grad, queries)
     values_grad = ein32("bhqk,bqhd->bkhd", probs_half, context_grad_half)
-    qkv_grad = jnp.concatenate(
-        [
-            rotate(queries_grad, cosine, -sine_table).reshape(2 * T, H).astype(bf16),
-            rotate(keys_grad, cosine, -sine_table).reshape(2 * T, H).astype(bf16),
-            values_grad.reshape(2 * T, H).astype(bf16),
-        ],
-        axis=1,
-    )
-    qkv_weight_grad = dot_dims(normed_half, qkv_grad, 0, 0)
+    parts = [
+        rotate(queries_grad, cosine, -sine_table).reshape(2 * T, H).astype(bf16),
+        rotate(keys_grad, cosine, -sine_table).reshape(2 * T, H).astype(bf16),
+        values_grad.reshape(2 * T, H).astype(bf16),
+    ]
+    weight_grads = [dot_dims(normed_half, p, 0, 0) for p in parts]
+    weight_grads.append(dot_dims(context_full, branch_half, 0, 0))
+    qkv_grad = jnp.concatenate(parts, axis=1)
     normed_in_grad = lax.psum_scatter(
         dot_dims(qkv_grad, full_qkv, 1, 1), "core", scatter_dimension=0, tiled=True
     )
     in_norm_grad, gain_attn_grad = rms_backward(residual_in, inverse_in, gain_attn, normed_in_grad)
     grad_tokens = residual_grad + in_norm_grad
 
-    def total(term):
-        mine = lax.psum_scatter(term.astype(bf16), GRID, scatter_dimension=0, tiled=True)
-        return lax.all_gather(mine, "expert", axis=0, tiled=True)
-
-    out_sum = swap_core(total(output_grad), 0, 1).astype(f32)
-    qkv_sum = total(qkv_weight_grad)
-    qkv_sum = [
-        swap_core(qkv_sum[:, i * H : (i + 1) * H], 0, 1).astype(f32) for i in range(3)
-    ]
     small_grad = jnp.concatenate(
         [router_grad, gain_attn_grad[:, None], gain_ffn_grad[:, None]], axis=1
     )
-    small_sum = lax.psum(
-        lax.psum_scatter(small_grad, SHARD, scatter_dimension=0, tiled=True), "expert"
-    )
+    weight_grads.append(jnp.pad(small_grad, ((0, 0), (0, 128 - small_grad.shape[1]))))
+    reduce = reduce_attention if n_exp == 4 else reduce_plain
+    sums = reduce(nz, [g.astype(bf16).reshape(nz, 4, -1, g.shape[1]) for g in weight_grads])
+    small_sum = jnp.sum(sums[4].astype(f32), axis=1).reshape(R, 128)
+    sums = [s.reshape(R, D).astype(f32) for s in sums[:4]]
     return (
         activations,
         grad_tokens,
         small_sum[:, experts],
-        qkv_sum[0],
-        qkv_sum[1],
-        qkv_sum[2],
-        out_sum,
+        sums[0],
+        sums[1],
+        sums[2],
+        sums[3],
         small_sum[:, experts + 1],
         small_sum[:, :experts],
         grad_w_in,

time: 1820 us -> 1550 us (0.85)
  waiting for transfers between devices: 1280 us -> 650 us
  Pallas kernels: 0 us -> 391 us
  blocking collectives: 96.7 us -> 54.4 us
    pallas_call x0 -> x2, Pallas kernels: none -> 391 us  [the longest x1 248 us: reduce_attention(): pl.pallas_call(functools.partial(reduce_kernel, nz, Q, widths), out_shape...]
    reduce_scatter x2 -> x0, waiting for transfers between devices: 337 us -> none  [total(): lax.psum_scatter(term.astype(bf16), GRID, scatter_dimension=0, tiled=True)]
    all_gather x5 -> x0, waiting for transfers between devices: 252 us -> none  [the longest x1 187 us: on_device(): lax.all_gather(column_half((w_query, w_key, w_value)), GRID, axis=0, tile...]
    all_to_all x2, waiting for transfers between devices: 37.1 us -> 17.8 us  [bring_back(): lax.all_to_all(mine, 'expert', split_axis=0, concat_axis=0, tiled=True)]
    dot_general x14 -> x16, matrix products: 120 us -> 130 us  [dot_dims(): lax.dot_general(a, b, (((da,), (db,)), ((), ())), preferred_element_type=...]
    unnamed x132 -> x131, local copies, waits for them, and re-layouts: 44.1 us -> 43.4 us
  transfers between devices with their start and end apart: 25 -> 13, of which waited for: 17 -> 9; matrix products, arithmetic and copies ran while one was open for 13% -> 14% of each run, Pallas kernels for 0% -> 0%
where the time goes in v2:
time: 1550 us; the launch traced here: 1530 us
  waiting for transfers between devices  650 us (42%)
  Pallas kernels  391 us (25%)
  matrix products  205 us (13%)
  local copies, waits for them, and re-layouts  146 us (9%)
  blocking collectives  54.4 us (4%)
  starting transfers between devices  37.2 us (2%)
  other arithmetic  35.8 us (2%)
  between operations  15.5 us (1%)
    pallas_call x1, Pallas kernels, reduce_attention(): pl.pallas_call(functools.partial(reduce_kernel, nz, Q, widths), out_shape...  248 us
    reduce_scatter x2, waiting for transfers between devices, bring_back(): mine = lax.psum_scatter(part, SHARD, scatter_dimension=0, tiled=True)  236 us
    all_to_all x2, waiting for transfers between devices, reshard(): lax.all_to_all(piece, SHARD, split_axis=0, concat_axis=0, tiled=True)  203 us
    pallas_call x1, Pallas kernels, gather_attention(): pl.pallas_call(functools.partial(gather_kernel, nz, Q, H), out_shape=(sd(...  142 us
    dot_general x16, matrix products, dot_dims(): lax.dot_general(a, b, (((da,), (db,)), ((), ())), preferred_element_type=...  130 us
    all_gather x2, waiting for transfers between devices, spread(): rows = lax.all_gather(moved, SHARD, axis=0, tiled=True)  107 us
    dot_general x11, matrix products, dot32(): return jnp.dot(a, b, preferred_element_type=f32)  66.8 us
    all_to_all x2, waiting for transfers between devices, reshard_grad(): moved = lax.all_to_all(term, SHARD, split_axis=0, concat_axis=0, tiled=True)  64.6 us
  transfers between devices with their start and end apart: 13, of which 9 were waited for; matrix products, arithmetic and copies ran while one was open for 14% of the time, Pallas kernels for 0%

profile of v2, /device:TPU:16, one launch (start us, length us, event | category | flops | bytes accessed | tf_op | source)
XLA Modules:
  0.0 1534.5 jit_solution(12054696304166653821)
XLA Ops:
  11.6 142.3 %gather_attention.1 = (bf16[2304,3456]{1,0:T(8,128)(2,1)}, bf16[2304,1152]{1,0:T(8,128)(2,1)}, bf16[2304,128]{1,0:T(8,128)(2,1)}, bf16[2,128,2304]{2,1,0:T(8,128)(2,1)}, s32[2,8,128]{2,1,0:T(8,128)}) custom-call(bf16[288,2304]{1,0:T(8,128)(2,1)} %q_ref.1, bf16[288,2304]{1,0:T(8,128)(2,1)} %k_ref.1, bf16[288,2304]{1,0:T(8,128)(2,1)} %v_ref.1, ...), custom_call_target="tpu_custom_call" | custom-call | flops 99999997952 | bytes 42467328 | tf_op jit(solution)/shard_map/gather_attention/pallas_call | solution.py:246
  196.9 21.6 %all-gather.4.cloned.1.call-done = bf16[256,2304]{0,1:T(8,128)(2,1)} async-done(((bf16[256,1152]{0,1:T(8,128)(2,1)}), bf16[256,2304]{0,1:T(8,128)(2,1)}) %all-gather.4.cloned.1.call-update) | async-done | bytes 1179664 | tf_op jit(solution)/shard_map/all_gather | solution.py:756
  231.4 22.8 %all_to_all.101 = bf16[4,80,2304]{2,1,0:T(8,128)(2,1)} all-to-all(bf16[4,80,2304]{2,1,0:T(8,128)(2,1)S(1)} %bitcast.210), channel_id=1, replica_groups=mesh['expert'=4,'z'=4,'core'=2] {'expert'}, dimensions={0} | all-to-all | bytes 2949120 | tf_op jit(solution)/shard_map/all_to_all | solution.py:781
  291.8 141.3 %all-to-all-done.2 = bf16[8,1,288,720]{3,2,1,0:T(8,128)(2,1)} async-done(((bf16[8,1,288,720]{3,2,1,0:T(8,128)(2,1)}), bf16[8,1,288,720]{3,2,1,0:T(8,128)(2,1)}, u32[]{:S(2)}, u32[]{:S(2)}) %all-to-all-start.2) | async-done | bytes 3317792 | tf_op jit(solution)/shard_map/all_to_all | solution.py:725
  441.3 14.6 fusion.71
  455.9 61.6 %all-to-all-done.3 = bf16[8,1,288,720]{3,2,1,0:T(8,128)(2,1)} async-done(((bf16[8,1,288,720]{3,2,1,0:T(8,128)(2,1)}), bf16[8,1,288,720]{3,2,1,0:T(8,128)(2,1)}, u32[]{:S(2)}, u32[]{:S(2)}) %all-to-all-start.3) | async-done | bytes 3317792 | tf_op jit(solution)/shard_map/all_to_all | solution.py:725
  517.5 17.0 %multiply_convert_fusion.2 = (bf16[2560,720]{0,1:T(8,128)(2,1)}, f32[2560,720]{0,1:T(8,128)}) fusion(f32[2560,720]{0,1:T(8,128)} %fusion.71, bf16[2560,2304]{1,0:T(8,128)(2,1)} %all-gather.6.cloned.1.call-done, bf16[2304,720]{1,0:T(8,128)(2,1)} %bitcast.14), kind=kOutput, calls=%fused_computation.8 | convolution fusion | flops 8504524800 | bytes 33546240 | tf_op jit(solution)/shard_map/dot_general | solution.py:659
  534.5 14.0 convolution_convert_fusion
  548.6 119.4 %reduce-scatter.5.cloned.1.call-done = bf16[320,2304]{1,0:T(8,128)(2,1)} async-done(((bf16[2560,2304]{1,0:T(8,128)(2,1)}), bf16[320,2304]{1,0:T(8,128)(2,1)}) %reduce-scatter.5.cloned.1.call-update) | async-done | bytes 1474576 | tf_op jit(solution)/shard_map/reduce_scatter | solution.py:796
  674.0 17.7 %all-to-all-done.4 = bf16[4,80,2304]{2,1,0:T(8,128)(2,1)} async-done(((bf16[4,80,2304]{2,1,0:T(8,128)(2,1)}), bf16[4,80,2304]{2,1,0:T(8,128)(2,1)}, u32[]{:S(2)}, u32[]{:S(2)}) %all-to-all-start.4) | async-done | bytes 1474592 | tf_op jit(solution)/shard_map/all_to_all | solution.py:797
  698.8 22.5 %all_to_all.102 = bf16[4,80,2304]{2,1,0:T(8,128)(2,1)} all-to-all(bf16[4,80,2304]{2,1,0:T(8,128)(2,1)S(1)} %bitcast.209), channel_id=1, replica_groups=mesh['expert'=4,'z'=4,'core'=2] {'expert'}, dimensions={0} | all-to-all | bytes 2949120 | tf_op jit(solution)/shard_map/all_to_all | solution.py:781
  721.3 106.9 %all-gather.8.cloned.1.call-done = bf16[2560,2304]{1,0:T(8,128)(2,1)} async-done(((bf16[320,2304]{1,0:T(8,128)(2,1)}), bf16[2560,2304]{1,0:T(8,128)(2,1)}) %all-gather.8.cloned.1.call-update) | async-done | bytes 11796496 | tf_op jit(solution)/shard_map/all_gather | solution.py:785
  828.2 18.1 %multiply_convert_fusion = (bf16[2560,720]{0,1:T(8,128)(2,1)}, bf16[2560,720]{0,1:T(8,128)(2,1)S(1)}) fusion(f32[2560,720]{0,1:T(8,128)} %fusion.71, f32[2560,720]{0,1:T(8,128)} %get-tuple-element.160, bf16[2560,2304]{1,0:T(8,128)(2,1)} %all-gather.8.cloned.1.call-done, bf16[720,1,2304]{2,0,1:T(8,128)(2,1)S(1)} %copy-done), kind=kOutput, calls=%fused_computation.6 | convolution fusion | flops 8517427200 | bytes 37232640 | tf_op jit(solution)/shard_map/dot_general | solution.py:663
  846.4 16.1 %fusion.72 = f32[2560,2304]{1,0:T(8,128)} fusion(bf16[2560,720]{0,1:T(8,128)(2,1)S(1)} %get-tuple-element.123, bf16[2304,720]{1,0:T(8,128)(2,1)} %bitcast.12), kind=kOutput, calls=%fused_computation.178 | convolution fusion | flops 8493465600 | bytes 30597120 | tf_op jit(solution)/shard_map/dot_general | solution.py:663
  862.5 18.3 %add_convert_fusion = bf16[2560,2304]{1,0:T(8,128)(2,1)} fusion(f32[2560,2304]{1,0:T(8,128)} %fusion.72, bf16[2560,720]{0,1:T(8,128)(2,1)} %get-tuple-element.122, bf16[2304,720]{1,0:T(8,128)(2,1)} %bitcast.14), kind=kOutput, calls=%fused_computation | convolution fusion | flops 8505262080 | bytes 42393600 | tf_op jit(solution)/shard_map/dot_general | solution.py:663
  883.6 116.6 %reduce-scatter.7.cloned.1.call-done = bf16[320,2304]{1,0:T(8,128)(2,1)} async-done(((bf16[2560,2304]{1,0:T(8,128)(2,1)}), bf16[320,2304]{1,0:T(8,128)(2,1)}) %reduce-scatter.7.cloned.1.call-update) | async-done | bytes 1474576 | tf_op jit(solution)/shard_map/reduce_scatter | solution.py:796
  1004.2 14.8 convolution_convert_fusion.6
  1047.7 15.0 convolution_convert_fusion.5
  1068.4 48.2 %all-to-all-done.8 = bf16[8,1,288,720]{3,2,1,0:T(8,128)(2,1)} async-done(((bf16[8,1,288,720]{3,2,1,0:T(8,128)(2,1)}), bf16[8,1,288,720]{3,2,1,0:T(8,128)(2,1)}, u32[]{:S(2)}, u32[]{:S(2)}) %all-to-all-start.8) | async-done | bytes 3317792 | tf_op jit(solution)/shard_map/all_to_all | solution.py:838
  1137.9 11.6 fusion.10
  1149.6 12.6 convolution_bitcast_fusion
  1184.8 16.4 %all-to-all-done.9 = bf16[8,1,288,720]{3,2,1,0:T(8,128)(2,1)} async-done(((bf16[8,1,288,720]{3,2,1,0:T(8,128)(2,1)}), bf16[8,1,288,720]{3,2,1,0:T(8,128)(2,1)}, u32[]{:S(2)}, u32[]{:S(2)}) %all-to-all-start.9) | async-done | bytes 3317792 | tf_op jit(solution)/shard_map/all_to_all | solution.py:838
  1222.6 21.4 %copy.290 = f32[288,1,11520]{2,1,0:T(1,128)} copy(f32[288,1,11520]{2,0,1:T(8,128)} %maximum_convert_fusion) | data formatting | bytes 26542080
  1263.3 248.4 %reduce_attention.1 = (bf16[2,144,2304]{2,1,0:T(8,128)(2,1)}, bf16[2,144,2304]{2,1,0:T(8,128)(2,1)}, bf16[2,144,2304]{2,1,0:T(8,128)(2,1)}, bf16[2,144,2304]{2,1,0:T(8,128)(2,1)}, bf16[2,2,144,128]{3,2,1,0:T(8,128)(2,1)}) custom-call(bf16[4,4,144,1152]{3,2,1,0:T(8,128)(2,1)} %bitcast.199, bf16[4,4,144,1152]{3,2,1,0:T(8,128)(2,1)} %bitcast.198, ...), custom_call_target="tpu_custom_call" | custom-call | flops 99999997952 | bytes 21823488 | tf_op jit(solution)/shard_map/reduce_attention/pallas_call | solution.py:555
  (270 shorter events, 259.6 us)
Async XLA Ops:
  7.2 527.4 %copy-start = (bf16[720,1,2304]{2,0,1:T(8,128)(2,1)S(1)}, bf16[720,1,2304]{2,0,1:T(8,128)(2,1)}, u32[]{:S(2)}) copy-start(bf16[720,1,2304]{2,0,1:T(8,128)(2,1)} %param.24) | copy-start | bytes 9953284
  7.2 211.3 %all-gather.4.cloned.1.call-start = ((), (), s32[]{:S(2)}) async-start(), calls=%async_computation.14 | async-start | bytes 1769472 | tf_op jit(solution)/shard_map/all_gather | solution.py:756
  153.9 5.3 copy-start.11
  157.1 72.6 %copy-start.41 = (f32[2304]{0:T(1024)}, f32[2304]{0:T(1024)S(1)}, u32[]{:S(2)}) copy-start(f32[2304]{0:T(1024)S(1)} %get-tuple-element.114) | copy-start | bytes 27652
  186.6 6.9 copy-start.39
  195.9 245.4 %all-gather.6.cloned.1.call-start = ((), (), s32[]{:S(2)}) async-start(), calls=%async_computation.15 | async-start | bytes 13271040 | tf_op jit(solution)/shard_map/all_gather | solution.py:785
  273.6 159.4 %all-to-all-start.2 = ((bf16[8,1,288,720]{3,2,1,0:T(8,128)(2,1)}), bf16[8,1,288,720]{3,2,1,0:T(8,128)(2,1)}, u32[]{:S(2)}, u32[]{:S(2)}) async-start(bf16[8,1,288,720]{3,2,1,0:T(8,128)(2,1)} %copy.267), calls=%async_computation.2 | async-start | bytes 7077888 | tf_op jit(solution)/shard_map/all_to_all | solution.py:725
  433.0 84.5 %all-to-all-start.3 = ((bf16[8,1,288,720]{3,2,1,0:T(8,128)(2,1)}), bf16[8,1,288,720]{3,2,1,0:T(8,128)(2,1)}, u32[]{:S(2)}, u32[]{:S(2)}) async-start(bf16[8,1,288,720]{3,2,1,0:T(8,128)(2,1)} %copy.268), calls=%async_computation.3 | async-start | bytes 7077888 | tf_op jit(solution)/shard_map/all_to_all | solution.py:725
  440.8 227.1 %reduce-scatter.5.cloned.1.call-start = ((), (), s32[]{:S(2)}) async-start(), calls=%async_computation.16 | async-start | bytes 13271040 | tf_op jit(solution)/shard_map/reduce_scatter | solution.py:796
  668.0 23.8 %all-to-all-start.4 = ((bf16[4,80,2304]{2,1,0:T(8,128)(2,1)}), bf16[4,80,2304]{2,1,0:T(8,128)(2,1)}, u32[]{:S(2)}, u32[]{:S(2)}) async-start(bf16[4,80,2304]{2,1,0:T(8,128)(2,1)} %bitcast.229), calls=%async_computation.5 | async-start | bytes 2949120 | tf_op jit(solution)/shard_map/all_to_all | solution.py:797
  672.3 155.9 %all-gather.8.cloned.1.call-start = ((), (), s32[]{:S(2)}) async-start(), calls=%async_computation.17 | async-start | bytes 13271040 | tf_op jit(solution)/shard_map/all_gather | solution.py:785
  721.3 278.9 %reduce-scatter.7.cloned.1.call-start = ((), (), s32[]{:S(2)}) async-start(), calls=%async_computation.18 | async-start | bytes 13271040 | tf_op jit(solution)/shard_map/reduce_scatter | solution.py:796
  846.4 16.1 %copy-start.60 = (bf16[2560,720]{0,1:T(8,128)(2,1)}, bf16[2560,720]{0,1:T(8,128)(2,1)S(1)}, u32[]{:S(2)}) copy-start(bf16[2560,720]{0,1:T(8,128)(2,1)S(1)} %get-tuple-element.123) | copy-start | bytes 11059204
  1000.2 24.6 %all-to-all-start.6 = ((bf16[4,80,2304]{2,1,0:T(8,128)(2,1)}), bf16[4,80,2304]{2,1,0:T(8,128)(2,1)S(1)}, u32[]{:S(2)}, u32[]{:S(2)}) async-start(bf16[4,80,2304]{2,1,0:T(8,128)(2,1)} %bitcast.228), calls=%async_computation.8 | async-start | bytes 2949120 | tf_op jit(solution)/shard_map/all_to_all | solution.py:797
  1032.6 7.3 copy-start.25
  1032.6 84.0 %all-to-all-start.8 = ((bf16[8,1,288,720]{3,2,1,0:T(8,128)(2,1)}), bf16[8,1,288,720]{3,2,1,0:T(8,128)(2,1)}, u32[]{:S(2)}, u32[]{:S(2)}) async-start(bf16[8,1,288,720]{3,2,1,0:T(8,128)(2,1)} %bitcast.201), calls=%async_computation.12 | async-start | bytes 7077888 | tf_op jit(solution)/shard_map/all_to_all | solution.py:838
  1039.9 85.6 %reduce-scatter.9.cloned.1.call-start = ((), (), s32[]{:S(2)}) async-start(), calls=%async_computation.19 | async-start | bytes 3538944 | tf_op jit(solution)/shard_map/reduce_scatter | solution.py:863
  1116.6 7.9 copy-start.59
  1116.6 8.5 copy-start.7
  1116.6 84.6 %all-to-all-start.9 = ((bf16[8,1,288,720]{3,2,1,0:T(8,128)(2,1)}), bf16[8,1,288,720]{3,2,1,0:T(8,128)(2,1)}, u32[]{:S(2)}, u32[]{:S(2)}) async-start(bf16[8,1,288,720]{3,2,1,0:T(8,128)(2,1)} %bitcast.200), calls=%async_computation.13 | async-start | bytes 7077888 | tf_op jit(solution)/shard_map/all_to_all | solution.py:838
  1124.5 135.8 %reduce-scatter.11.cloned.1.call-start = ((), (), s32[]{:S(2)}) async-start(), calls=%async_computation.20 | async-start | bytes 3538944 | tf_op jit(solution)/shard_map/reduce_scatter | solution.py:886
  1222.6 21.5 %copy-start.8 = (bf16[256,2304]{0,1:T(8,128)(2,1)S(1)}, bf16[256,2304]{0,1:T(8,128)(2,1)}, u32[]{:S(2)}) copy-start(bf16[256,2304]{0,1:T(8,128)(2,1)} %all-gather.4.cloned.1.call-done) | copy-start | bytes 3538948
  1222.6 21.5 %copy-start.26 = (bf16[128,2,1152]{2,0,1:T(8,128)(2,1)S(1)}, bf16[128,2,1152]{2,0,1:T(8,128)(2,1)}, u32[]{:S(2)}) copy-start(bf16[128,2,1152]{2,0,1:T(8,128)(2,1)} %copy-done.25) | copy-start | bytes 1769476
  1521.8 5.4 copy-start.1
  (50 other events, 97.7 us)
Sparse Core Ops, SparseCore 0:
  196.0 22.4 all-gather.3
  254.4 180.4 all-gather.5
  548.7 119.2 reduce-scatter.4
  721.4 106.7 all-gather.7
  881.0 119.1 reduce-scatter.6
  1046.3 11.5 reduce-scatter.8
  1149.7 11.5 reduce-scatter.10

commit v3 on v2

--- a/solution.py
+++ b/solution.py
@@ -18,6 +18,7 @@
 f32 = jnp.float32
 SHARD = ("z", "core")
 GRID = ("z", "expert")
+AHEAD = 2
 ANY = pl.BlockSpec(memory_space=pl.ANY)
 
 
@@ -72,9 +73,10 @@
 
 def gather_kernel(
     nz, Q, H,
-    q_ref, k_ref, v_ref, o_ref, s_ref, t_ref, l_ref,
-    qkv_out, o_out, s_out, t_out, l_out,
+    q_ref, k_ref, v_ref, o_ref, s_ref, t_ref, l_ref, p_ref,
+    qkv_out, o_out, s_out, t_out, l_out, p_out,
     zrecv, zhop, zsend, near_recv, near_send, far_recv, far_send, own, sib_send, sib_recv,
+    *payload,
 ):
     e, z, c, ex, ey = place()
     holder, turn = e // 2, e % 2
@@ -119,6 +121,8 @@
                 first_hop(k, step, 0).start()
                 first_hop(k, step, 1).start()
 
+    stream = payload_stream(nz, p_ref, p_out, payload, p_ref.shape[0] // 2)
+    stream[0]()
     for k in range(K):
         rows = src(k, c, 0, 2), dst(k, z, 2 * c, 0, 2 * Q)
         mine = pltpu.make_async_copy(rows[0], rows[1], own.at[k])
@@ -195,12 +199,27 @@
 
     steps = [(k, side, i) for i in range(nz - 1) for k in range(K) for side in range(2)]
     lag = 2 * K
+    blocks = 2 * nz - 1
+    beat = len(steps) // blocks
+    p_begin, p_arrive, p_relay, p_close, p_end = stream
     for n, step in enumerate(steps):
         arrive(*step)
         if n >= lag:
             relay(*steps[n - lag])
+        if n % beat == beat - 1 and n // beat < blocks:
+            s = n // beat
+            p_arrive(s)
+            if s >= 1:
+                p_relay(s - 1)
+            if s >= 2:
+                p_close(s - 2)
     for step in steps[len(steps) - lag :]:
         relay(*step)
+    p_relay(blocks - 1)
+    p_close(blocks - 2)
+    p_close(blocks - 1)
+    for s in range(blocks):
+        p_end(s)
 
     for k, side, i in steps:
 
@@ -235,7 +254,7 @@
         copy.wait()
 
 
-def gather_attention(nz, weights, small, tokens, lengths):
+def gather_attention(nz, weights, small, tokens, lengths, block):
     R, D = weights[0].shape
     Q, H = R // 2, D // 2
     K = len(weights) + 1
@@ -251,9 +270,10 @@
             sd((nz * 4 * Q, W), bf16),
             sd((2,) + tokens.shape, bf16),
             sd((2,) + lengths.shape, lengths.dtype),
+            sd((nz, 2, 4) + block.shape, block.dtype),
         ),
-        in_specs=[any_] * 7,
-        out_specs=(any_,) * 5,
+        in_specs=[any_] * 8,
+        out_specs=(any_,) * 6,
         scratch_shapes=[
             dma((K, 2, nz - 1)),
             dma((K, 2, 2)),
@@ -265,13 +285,14 @@
             dma((K + 2,)),
             dma((K + 2,)),
             dma((K + 2,)),
+            *payload_sems(nz),
         ],
         compiler_params=pltpu.CompilerParams(collective_id=0, has_side_effects=True),
         cost_estimate=pl.CostEstimate(
             flops=10**11, bytes_accessed=8 * D * H * 2, transcendentals=0
         ),
         name="gather_attention",
-    )(*weights, small, tokens, lengths)
+    )(*weights, small, tokens, lengths, block)
     return outs
 
 
@@ -367,13 +388,17 @@
             target[rows, cols(k)] = acc.astype(bf16)
 
     pairs = [(k, i) for i in range(nz) for k in range(K)]
-    for k, i in pairs:
+    def begin(k, i):
         via(k, i, 0).start()
         via(k, i, 1).start()
         for copy in loads(k, i):
             copy.start()
         plain(k, i, 0).start()
         plain(k, i, 1).start()
+
+    ahead = AHEAD * K
+    for k, i in pairs[:ahead]:
+        begin(k, i)
 
     def combine(k, i):
         a = cut(k, Q)
@@ -463,6 +488,8 @@
     lag = K
     for n, (k, i) in enumerate(pairs):
         combine(k, i)
+        if n + ahead < len(pairs):
+            begin(*pairs[n + ahead])
         if n >= lag:
             k2, i2 = pairs[n - lag]
             finish(k2, i2)
@@ -592,7 +619,294 @@
     )(*parts)
 
 
-def gather_plain(nz, weights, small, tokens, lengths):
+def payload_stream(nz, ref, out, sems, split):
+    zrecv, zsend, near_recv, near_send, far_recv, far_send, sib_recv, sib_send, own = sems
+    e, z, c, ex, ey = place()
+    diagonal = (ex + 2) % 4
+    T = ref.shape[0]
+    S = 2 * nz - 1
+
+    def split_step(s):
+        return (s - 1) % 2, (s - 1) // 2
+
+    def where(s):
+        if s == 0:
+            return z
+        side, i = split_step(s)
+        return z - 1 - i if side == 0 else z + 1 + i
+
+    def exists(s):
+        if s == 0:
+            return z >= 0
+        zz = where(s)
+        return (zz >= 0) & (zz < nz)
+
+    def slab(s, quarter, r0=0, n=T):
+        return out.at[where(s), c, quarter, pl.ds(r0, n), :]
+
+    def first(step):
+        side = 0 if step > 0 else 1
+        return remote(ref, slab(0, e), zsend.at[side, nz - 1], zrecv.at[side, 0], e, z + step, c)
+
+    def onward(s):
+        side, i = split_step(s)
+        step = 1 if side == 0 else -1
+        return remote(
+            slab(s, e), slab(s, e), zsend.at[side, i], zrecv.at[side, i + 1], e, z + step, c
+        )
+
+    def near(s, axis):
+        source = ref if s == 0 else slab(s, e)
+        return remote(
+            source, slab(s, e), near_send.at[s, axis], near_recv.at[s, axis],
+            ex if axis == 0 else ey, z, c,
+        )
+
+    def near_wait(s, axis):
+        view = slab(s, ex if axis == 0 else ey)
+        remote(view, view, near_send.at[s, axis], near_recv.at[s, axis], ex, z, c).wait_recv()
+
+    axes = range(2) if split else range(1)
+
+    def far_view(s, quarter, axis):
+        if not split:
+            return slab(s, quarter)
+        return slab(s, quarter, 0, split) if axis == 0 else slab(s, quarter, split, T - split)
+
+    def far(s, axis):
+        view = far_view(s, ex if axis == 0 else ey, axis)
+        return remote(
+            view, view, far_send.at[s, axis], far_recv.at[s, axis],
+            ey if axis == 0 else ex, z, c,
+        )
+
+    def far_wait(s, axis):
+        view = far_view(s, diagonal, axis)
+        remote(view, view, far_send.at[s, axis], far_recv.at[s, axis], ex, z, c).wait_recv()
+
+    def beside(s, n):
+        quarter = (e, ex, ey, diagonal)[n]
+        source = ref if s == 0 and n == 0 else slab(s, quarter)
+        return remote(
+            source, slab(s, quarter), sib_send.at[s, n], sib_recv.at[s, n], e, z, 1 - c
+        )
+
+    def beside_wait(s, n):
+        view = out.at[where(s), 1 - c, (e, ex, ey, diagonal)[n]]
+        remote(view, view, sib_send.at[s, n], sib_recv.at[s, n], e, z, c).wait_recv()
+
+    def inside(side):
+        return z < nz - 1 if side == 0 else z > 0
+
+    def begin():
+        for step in (1, -1):
+
+            @pl.when((z + step >= 0) & (z + step < nz))
+            def _():
+                first(step).start()
+
+        near(0, 0).start()
+        near(0, 1).start()
+        beside(0, 0).start()
+        pltpu.make_async_copy(ref, slab(0, e), own).start()
+
+    def arrive(s):
+        if s == 0:
+            return
+
+        @pl.when(exists(s))
+        def _():
+            side, i = split_step(s)
+            remote(
+                slab(s, e), slab(s, e), zsend.at[side, i], zrecv.at[side, i], e, z, c
+            ).wait_recv()
+            if i < nz - 2:
+
+                @pl.when(inside(side))
+                def _():
+                    onward(s).start()
+
+            near(s, 0).start()
+            near(s, 1).start()
+            beside(s, 0).start()
+
+    def relay(s):
+        @pl.when(exists(s))
+        def _():
+            near_wait(s, 0)
+            far(s, 0).start()
+            beside(s, 1).start()
+            near_wait(s, 1)
+            if split:
+                far(s, 1).start()
+            beside(s, 2).start()
+
+    def close(s):
+        @pl.when(exists(s))
+        def _():
+            for axis in axes:
+                far_wait(s, axis)
+            beside(s, 3).start()
+
+    def end(s):
+        @pl.when(exists(s))
+        def _():
+            for axis in range(2):
+                near(s, axis).wait_send()
+            for axis in axes:
+                far(s, axis).wait_send()
+            for n in range(4):
+                beside(s, n).wait_send()
+                beside_wait(s, n)
+            if s > 0 and split_step(s)[1] < nz - 2:
+
+                @pl.when(inside(split_step(s)[0]))
+                def _():
+                    onward(s).wait_send()
+
+        if s == 0:
+            for step in (1, -1):
+
+                @pl.when((z + step >= 0) & (z + step < nz))
+                def _():
+                    first(step).wait_send()
+
+            pltpu.make_async_copy(ref, slab(0, e), own).wait()
+
+    return begin, arrive, relay, close, end
+
+
+def payload_sems(nz):
+    dma = pltpu.SemaphoreType.DMA
+    S = 2 * nz - 1
+    return [
+        dma((2, nz)), dma((2, nz)), dma((S, 2)), dma((S, 2)), dma((S, 2)), dma((S, 2)),
+        dma((S, 4)), dma((S, 4)), dma(()),
+    ]
+
+
+def spread_kernel(nz, splits, *refs):
+    n = len(splits)
+    ins, outs, sems = refs[:n], refs[n : 2 * n], refs[2 * n :]
+    greet(nz, (False, False))
+    streams = [
+        payload_stream(nz, ins[i], outs[i], sems[9 * i : 9 * i + 9], splits[i]) for i in range(n)
+    ]
+    for t in streams:
+        t[0]()
+    S = 2 * nz - 1
+    for s in range(S):
+        for t in streams:
+            t[1](s)
+        if s >= 1:
+            for t in streams:
+                t[2](s - 1)
+        if s >= 2:
+            for t in streams:
+                t[3](s - 2)
+    for t in streams:
+        t[2](S - 1)
+    for s in (S - 2, S - 1):
+        for t in streams:
+            t[3](s)
+    for s in range(S):
+        for t in streams:
+            t[4](s)
+
+
+def spread_blocks(nz, blocks, collective):
+    sd = jax.ShapeDtypeStruct
+    splits = tuple(b.shape[0] // 2 if b.shape[0] % 32 == 0 else 0 for b in blocks)
+    return pl.pallas_call(
+        functools.partial(spread_kernel, nz, splits),
+        out_shape=tuple(sd((nz, 2, 4) + b.shape, b.dtype) for b in blocks),
+        in_specs=[ANY] * len(blocks),
+        out_specs=(ANY,) * len(blocks),
+        scratch_shapes=[s for _ in blocks for s in payload_sems(nz)],
+        compiler_params=pltpu.CompilerParams(collective_id=collective, has_side_effects=True),
+        cost_estimate=pl.CostEstimate(
+            flops=5 * 10**10, bytes_accessed=sum(b.size for b in blocks) * 128, transcendentals=0
+        ),
+        name="spread_blocks",
+    )(*blocks)
+
+
+def pack_kernel(n, F, Fp, x_ref, o_ref):
+    half = n * F
+    rows = x_ref.shape[0]
+    for i in range(n):
+        for part in range(2):
+            cols = x_ref[:, part * half + i * F : part * half + (i + 1) * F]
+            if Fp > F:
+                cols = jnp.concatenate([cols, jnp.zeros((rows, Fp - F), cols.dtype)], axis=1)
+            o_ref[i, :, part * Fp : (part + 1) * Fp] = cols
+
+
+def pack_columns(w, n, F, Fp):
+    rows = w.shape[0]
+    block = 16
+    return pl.pallas_call(
+        functools.partial(pack_kernel, n, F, Fp),
+        grid=(rows // block,),
+        in_specs=[pl.BlockSpec((block, w.shape[1]), lambda i: (i, 0))],
+        out_specs=pl.BlockSpec((n, block, 2 * Fp), lambda i: (0, i, 0)),
+        out_shape=jax.ShapeDtypeStruct((n, rows, 2 * Fp), w.dtype),
+        name="pack_columns",
+    )(w)
+
+
+def unpack_kernel(n, F, Fp, x_ref, o_ref, line):
+    half = n * F
+    rows = line.shape[0]
+    for i in range(n):
+        for part in range(2):
+            cols = x_ref[i, :, part * Fp : part * Fp + F].astype(f32)
+            line[:, part * half + i * F : part * half + (i + 1) * F] = cols
+    tiles = 2 * half // 128
+    for j in range(tiles):
+        o_ref[pl.ds(j, rows, stride=tiles), :] = line[:, j * 128 : (j + 1) * 128]
+
+
+def unpack_columns(x, F):
+    n, rows, Fp2 = x.shape
+    block = 16
+    width = 2 * n * F
+    tiles = width // 128
+    flat = pl.pallas_call(
+        functools.partial(unpack_kernel, n, F, Fp2 // 2),
+        grid=(rows // block,),
+        in_specs=[pl.BlockSpec((n, block, Fp2), lambda i: (0, i, 0))],
+        out_specs=pl.BlockSpec((block * tiles, 128), lambda i: (i, 0)),
+        out_shape=jax.ShapeDtypeStruct((rows * tiles, 128), f32),
+        scratch_shapes=[pltpu.VMEM((block, width), f32)],
+        name="unpack_columns",
+    )(x)
+    return flat.reshape(rows, 1, width)
+
+
+def line_kernel(x_ref, o_ref):
+    rows, width = x_ref.shape
+    tiles = width // 128
+    for j in range(tiles):
+        o_ref[pl.ds(j, rows, stride=tiles), :] = x_ref[:, j * 128 : (j + 1) * 128]
+
+
+def lined_up(x):
+    rows, width = x.shape
+    tiles = width // 128
+    block = 80 if rows % 80 == 0 else 8
+    flat = pl.pallas_call(
+        line_kernel,
+        grid=(rows // block,),
+        in_specs=[pl.BlockSpec((block, width), lambda i: (i, 0))],
+        out_specs=pl.BlockSpec((block * tiles, 128), lambda i: (i, 0)),
+        out_shape=jax.ShapeDtypeStruct((rows * tiles, 128), x.dtype),
+        name="lined_up",
+    )(x)
+    return flat.reshape(rows, 1, width)
+
+
+def gather_plain(nz, weights, small, tokens, lengths, block):
     core, H = lax.axis_index("core"), weights[0].shape[1] // 2
     full = [
         lax.all_gather(swap_core(w, 1, 0), "z", axis=0, tiled=True) for w in weights
@@ -603,7 +917,17 @@
         lax.all_gather(small, SHARD, axis=0, tiled=True),
         lax.all_gather(tokens, "core", axis=0),
         lax.all_gather(lengths, "core", axis=0),
-    )
+        spread_plain(nz, (block,), 0)[0],
+    )
+
+
+def spread_plain(nz, blocks, collective):
+    out = []
+    for block in blocks:
+        for axis in ("expert", "core", "z"):
+            block = lax.all_gather(block, axis, axis=0)
+        out.append(block)
+    return out
 
 
 def reduce_plain(nz, parts):
@@ -694,7 +1018,6 @@
     n_exp = lax.axis_size("expert")
     n_shard = lax.axis_size("z") * lax.axis_size("core")
     experts = w_router.shape[1]
-    local_experts = w_in.shape[1]
     F = w_down.shape[0]
     FF = F * n_shard
     capacity = 10 * T // (4 * experts)
@@ -703,29 +1026,23 @@
     e_index = lax.axis_index("expert")
     core = lax.axis_index("core")
 
+    Fp = -(-F // 128) * 128
+    packed = pack_columns(w_in.reshape(R, 2 * FF), n_shard, F, Fp)
+    moved = lax.all_to_all(packed, SHARD, split_axis=0, concat_axis=0, tiled=True)
+    w_pair = moved.reshape(n_shard * R, 2 * Fp)
+    down = jnp.pad(w_down.reshape(F, D), ((0, Fp - F), (0, 0)))
+
     nz = lax.axis_size("z")
     small = jnp.concatenate([w_router, norm_attn[:, None], norm_ffn[:, None]], axis=1)
     small = jnp.pad(small, ((0, 0), (0, 128 - small.shape[1])))
     length_rows = jnp.broadcast_to(seq_lengths[:, :1], (8, 128))
     gather = gather_attention if n_exp == 4 else gather_plain
-    full_qkv, full_output, full_small, chip_tokens, chip_lengths = gather(
-        nz, (w_query, w_key, w_value, w_output), small, tokens, length_rows
+    full_qkv, full_output, full_small, chip_tokens, chip_lengths, all_cotangent = gather(
+        nz, (w_query, w_key, w_value, w_output), small, tokens, length_rows, cotangent
     )
     full_router = full_small[:, :experts]
     gain_attn = full_small[:, experts].astype(f32)
     gain_ffn = full_small[:, experts + 1].astype(f32)
-
-    w_gate_cols = []
-    for part in range(2):
-        piece = w_in[:, :, part * FF : (part + 1) * FF].reshape(R, local_experts, n_shard, F)
-        piece = piece.transpose(2, 1, 0, 3)
-        w_gate_cols.append(piece)
-
-    def reshard(piece):
-        moved = lax.all_to_all(piece, SHARD, split_axis=0, concat_axis=0, tiled=True)
-        return moved.transpose(1, 0, 2, 3).reshape(local_experts, n_shard * R, F)
-
-    w_gate, w_up = reshard(w_gate_cols[0]), reshard(w_gate_cols[1])
 
     both = (2, T)
     residual_in = tokens.astype(f32)
@@ -775,70 +1092,68 @@
     slot_ids = jnp.arange(slots)
     pick = [(target[:, k][:, None] == slot_ids[None, :]).astype(bf16) for k in range(2)]
 
-    def send_rows(rows0, rows1):
-        out = dot_dims(pick[0], rows0, 0, 0) + dot_dims(pick[1], rows1, 0, 0)
-        out = out.astype(bf16)
-        moved = lax.all_to_all(out, "expert", split_axis=0, concat_axis=0, tiled=True)
-        return moved
-
-    def spread(moved):
-        rows = lax.all_gather(moved, SHARD, axis=0, tiled=True)
-        if local_experts == 1:
-            return rows[None]
-        rows = rows.reshape(n_shard * n_exp, local_experts, capacity, D)
-        return rows.transpose(1, 0, 2, 3).reshape(local_experts, -1, D)
-
     def bring_back(partial_rows):
-        part = partial_rows.astype(bf16)
-        if local_experts > 1:
-            part = part.reshape(local_experts, n_shard * n_exp, capacity, D).transpose(1, 0, 2, 3)
-        part = part.reshape(n_shard * slots, D)
-        mine = lax.psum_scatter(part, SHARD, scatter_dimension=0, tiled=True)
+        mine = lax.psum_scatter(
+            partial_rows.astype(bf16), SHARD, scatter_dimension=0, tiled=True
+        )
+        return at_home(mine)
+
+    def at_home(mine):
         back = lax.all_to_all(mine, "expert", split_axis=0, concat_axis=0, tiled=True)
         return [dot32(pick[k], back) for k in range(2)]
 
-    def per_expert(fn, *arrays):
-        return jnp.stack([fn(*[a[i] for a in arrays]) for i in range(local_experts)])
-
-    arrived = spread(send_rows(normed_mid_half, normed_mid_half))
-    upstream = cotangent.astype(f32)
-    mixture_grad = branch_scale * upstream
-    row_grads = (gate_probs[:, :, None] * mixture_grad[:, None, :]).astype(bf16)
-    grad_arrived = spread(send_rows(row_grads[:, 0], row_grads[:, 1]))
-    down = w_down.transpose(1, 0, 2)
-    gate_part = per_expert(dot32, arrived, w_gate)
-    up_part = per_expert(dot32, arrived, w_up)
+    notes = jnp.concatenate([gate_probs, target.astype(f32), jnp.zeros((T, 4), f32)], axis=1)
+    notes = jnp.pad(jnp.transpose(notes), ((0, 0), (0, -T % 128)))
+    spread = spread_blocks if n_exp == 4 else spread_plain
+    all_normed, all_notes = spread(nz, (normed_mid_half, notes), 2)
+    devices = n_shard * n_exp
+    all_notes = all_notes.reshape(devices, 8, -1)[:, :, :T]
+    wanted = (e_index * capacity + jnp.arange(capacity)).astype(f32)
+    found = [
+        all_notes[:, 2 + k, None, :] == wanted[None, :, None] for k in range(2)
+    ]
+    gate_rows = jnp.sum(
+        jnp.where(found[0], all_notes[:, 0, None, :], 0.0)
+        + jnp.where(found[1], all_notes[:, 1, None, :], 0.0),
+        axis=-1,
+    ).reshape(devices * capacity, 1)
+    chosen_rows = (found[0] | found[1]).astype(bf16)
+
+    def take(blocks):
+        rows = ein32("spt,std->spd", chosen_rows, blocks.reshape(devices, T, D))
+        return rows.astype(bf16).reshape(devices * capacity, D)
+
+    arrived = take(all_normed)
+    grad_arrived = (gate_rows * (branch_scale * take(all_cotangent).astype(f32))).astype(bf16)
+    pre = dot32(arrived, w_pair)
+    gate_part, up_part = pre[:, :Fp], pre[:, Fp:]
     sigmoid_gate = jax.nn.sigmoid(gate_part)
     silu_gate = gate_part * sigmoid_gate
     activated = (silu_gate * up_part).astype(bf16)
-    expert_rows = bring_back(per_expert(dot32, activated, down))
+    expert_rows = bring_back(dot32(activated, down))
+    upstream = cotangent.astype(f32)
+    mixture_grad = branch_scale * upstream
     mixture = gate_probs[:, 0:1] * expert_rows[0] + gate_probs[:, 1:2] * expert_rows[1]
     activations = (residual_mid + branch_scale * mixture).astype(bf16)
 
-    act_grad = per_expert(lambda a, b: dot_dims(a, b, 1, 1), grad_arrived, down)
-    gate_grads = (
-        act_grad * up_part * sigmoid_gate * (1.0 + gate_part * (1.0 - sigmoid_gate))
+    act_grad = dot_dims(grad_arrived, down, 1, 1)
+    pre_grad = jnp.concatenate(
+        [
+            act_grad * up_part * sigmoid_gate * (1.0 + gate_part * (1.0 - sigmoid_gate)),
+            act_grad * silu_gate,
+        ],
+        axis=1,
     ).astype(bf16)
-    up_grads = (act_grad * silu_gate).astype(bf16)
-    input_rows = bring_back(
-        per_expert(
-            lambda a, b, c, d: dot_dims(a, b, 1, 1) + dot_dims(c, d, 1, 1),
-            gate_grads,
-            w_gate,
-            up_grads,
-            w_up,
-        )
-    )
-    grad_w_down = per_expert(lambda a, b: dot_dims(a, b, 0, 0), activated, grad_arrived)
-    grad_w_down = grad_w_down.transpose(1, 0, 2)
-
-    def reshard_grad(grads):
-        term = per_expert(lambda a, b: dot_dims(a, b, 0, 0), arrived, grads).astype(bf16)
-        term = term.reshape(local_experts, n_shard, R, F).transpose(1, 0, 2, 3)
-        moved = lax.all_to_all(term, SHARD, split_axis=0, concat_axis=0, tiled=True)
-        return moved.transpose(2, 1, 0, 3).reshape(R, local_experts, FF).astype(f32)
-
-    grad_w_in = jnp.concatenate([reshard_grad(gate_grads), reshard_grad(up_grads)], axis=2)
+    in_sum = lax.psum_scatter(
+        dot_dims(pre_grad, w_pair, 1, 1).astype(bf16), SHARD, scatter_dimension=0, tiled=True
+    )
+    in_term = dot_dims(arrived, pre_grad, 0, 0).astype(bf16).reshape(n_shard, R, 2 * Fp)
+    down_term = dot_dims(activated[:, :F], grad_arrived, 0, 0)
+    in_sum, in_term, down_term = lax.optimization_barrier((in_sum, in_term, down_term))
+    input_rows = at_home(in_sum)
+    in_term = lax.all_to_all(in_term, SHARD, split_axis=0, concat_axis=0, tiled=True)
+    grad_w_in = unpack_columns(in_term, F)
+    grad_w_down = lined_up(down_term)
 
     gate_grad = jnp.stack(
         [jnp.sum(mixture_grad * expert_rows[k], axis=-1) for k in range(2)], axis=1

time: 1550 us -> 1270 us (0.82)
  waiting for transfers between devices: 650 us -> 220 us
  Pallas kernels: 391 us -> 711 us
  local copies, waits for them, and re-layouts: 146 us -> 35.3 us
  blocking collectives: 54.4 us -> 8.89 us
    pallas_call x0 -> x4, Pallas kernels: none -> 269 us  [the longest x1 232 us: spread_blocks(): pl.pallas_call(functools.partial(spread_kernel, nz, splits), out_shape=tu...]
    all_to_all x6 -> x4, waiting for transfers between devices: 285 us -> 17.9 us  [the longest x2 17.9 us: at_home(): lax.all_to_all(mine, 'expert', split_axis=0, concat_axis=0, tiled=True)]
    all_gather x2 -> x0, waiting for transfers between devices: 107 us -> none  [spread(): rows = lax.all_gather(moved, SHARD, axis=0, tiled=True)]
    pallas_call x1, Pallas kernels: 142 us -> 214 us  [gather_attention(): pl.pallas_call(functools.partial(gather_kernel, nz, Q, H), out_shape=(sd(...]
    reduce_scatter x2, waiting for transfers between devices: 236 us -> 185 us  [the longest x1 119 us: bring_back(): lax.psum_scatter(partial_rows.astype(bf16), SHARD, scatter_dimension=0, t...]
    all_to_all x2 -> x0, blocking collectives: 45.3 us -> none  [send_rows(): lax.all_to_all(out, 'expert', split_axis=0, concat_axis=0, tiled=True)]
    convert_element_type x6 -> x0, local copies, waits for them, and re-layouts: 37 us -> none  [the longest x4 25.6 us: reshard_grad(): return moved.transpose(2, 1, 0, 3).reshape(R, local_experts, FF).astype(f32)]
    unnamed x131 -> x157, local copies, waits for them, and re-layouts: 43.4 us -> 12 us
  transfers between devices with their start and end apart: 13 -> 9, of which waited for: 9 -> 5; matrix products, arithmetic and copies ran while one was open for 14% -> 10% of each run, Pallas kernels for 0% -> 38%
where the time goes in v3:
time: 1270 us; the launch traced here: 1260 us
  Pallas kernels  711 us (56%)
  waiting for transfers between devices  220 us (17%)
  matrix products  202 us (16%)
  other arithmetic  38.8 us (3%)
  local copies, waits for them, and re-layouts  35.3 us (3%)
  starting transfers between devices  26.7 us (2%)
  between operations  15 us (1%)
    pallas_call x1, Pallas kernels, spread_blocks(): pl.pallas_call(functools.partial(spread_kernel, nz, splits), out_shape=tu...  232 us
    pallas_call x1, Pallas kernels, reduce_attention(): pl.pallas_call(functools.partial(reduce_kernel, nz, Q, widths), out_shape...  228 us
    pallas_call x1, Pallas kernels, gather_attention(): pl.pallas_call(functools.partial(gather_kernel, nz, Q, H), out_shape=(sd(...  214 us
    reduce_scatter x1, waiting for transfers between devices, bring_back(): lax.psum_scatter(partial_rows.astype(bf16), SHARD, scatter_dimension=0, t...  119 us
    dot_general x10, matrix products, dot_dims(): lax.dot_general(a, b, (((da,), (db,)), ((), ())), preferred_element_type=...  114 us
    reduce_scatter x1, waiting for transfers between devices, on_device(): lax.psum_scatter(dot_dims(pre_grad, w_pair, 1, 1).astype(bf16), SHARD, sc...  66.4 us
    dot_general x10, matrix products, dot32(): return jnp.dot(a, b, preferred_element_type=f32)  60.2 us
    dot_general x8, matrix products, ein32(): return jnp.einsum(spec, a, b, preferred_element_type=f32)  25.6 us
  transfers between devices with their start and end apart: 9, of which 5 were waited for; matrix products, arithmetic and copies ran while one was open for 10% of the time, Pallas kernels for 38%

profile of v3, /device:TPU:16, one launch (start us, length us, event | category | flops | bytes accessed | tf_op | source)
XLA Modules:
  0.0 1258.3 jit_solution(12899596104547815212)
XLA Ops:
  12.5 213.6 %gather_attention.1 = (bf16[2304,3456]{1,0:T(8,128)(2,1)}, bf16[2304,1152]{1,0:T(8,128)(2,1)}, bf16[2304,128]{1,0:T(8,128)(2,1)}, bf16[2,128,2304]{2,1,0:T(8,128...) custom-call(bf16[288,2304]{1,0:T(8,128)(2,1)} %q_ref.1, bf16[288,2304]{1,0:T(8,128)(2,1)} %k_ref.1, ...), custom_call_target="tpu_custom_call" | custom-call | flops 99999997952 | bytes 42467328 | tf_op jit(solution)/shard_map/gather_attention/pallas_call | solution.py:265
  232.5 8.4 fusion.80
  255.1 13.3 %pack_columns.1 = bf16[8,288,1536]{2,1,0:T(8,128)(2,1)} custom-call(bf16[288,11520]{1,0:T(8,128)(2,1)} %bitcast.179), custom_call_target="tpu_custom_call" | custom-call | tf_op jit(solution)/shard_map/pack_columns/pallas_call | solution.py:848
  269.1 7.9 all-gather.2.cloned.1.call-done
  286.3 13.1 %all-to-all-start.1 = ((bf16[8,288,1536]{2,1,0:T(8,128)(2,1)}), bf16[8,288,1536]{2,1,0:T(8,128)(2,1)}, u32[]{:S(2)}, u32[]{:S(2)}) async-start(bf16[8,288,1536]{2,1,0:T(8,128)(2,1)} %pack_columns.1), calls=%async_computation.1 | async-start | bytes 14155776 | tf_op jit(solution)/shard_map/all_to_all | solution.py:1031
  304.0 232.1 %spread_blocks.1 = (bf16[4,2,4,128,2304]{4,3,2,1,0:T(8,128)(2,1)}, f32[4,2,4,8,128]{4,3,2,1,0:T(8,128)}) custom-call(bf16[128,2304]{1,0:T(8,128)(2,1)} %copy-done.20, f32[8,128]{1,0:T(8,128)} %maximum_bitcast_fusion.refs_1_), custom_call_target="tpu_custom_call" | custom-call | flops 49999998976 | bytes 37879808 | tf_op jit(solution)/shard_map/spread_blocks/pallas_call | solution.py:820
  538.1 10.7 convolution_convert_fusion.7
  548.8 10.7 convolution_convert_fusion.8
  559.5 10.8 fusion
  570.4 25.0 %fusion.82 = f32[2560,1536]{0,1:T(8,128)} fusion(bf16[2560,2304]{1,0:T(8,128)(2,1)} %bitcast.168, bf16[2304,1536]{1,0:T(8,128)(2,1)} %bitcast.15), kind=kOutput, calls=%fused_computation.189 | convolution fusion | flops 18119393280 | bytes 34603008 | tf_op jit(solution)/shard_map/dot_general | solution.py:983
  595.3 19.6 %multiply_convert_fusion.1 = (bf16[2560,768]{0,1:T(8,128)(2,1)}, bf16[2560,768]{0,1:T(8,128)(2,1)}, bf16[2560,768]{0,1:T(8,128)(2,1)}) fusion(f32[2560,1536]{0,1:T(8,128)} %fusion.82, bf16[2560,2304]{1,0:T(8,128)(2,1)} %fusion, bf16[720,2304]{1,0:T(8,128)(2,1)S(1)} %bitcast.218), kind=kOutput, calls=%fused_computation.13 | convolution fusion | flops 9089187840 | bytes 42639360 | tf_op jit(solution)/shard_map/dot_general | solution.py:987
  615.0 25.4 %convolution_convert_fusion = bf16[2560,2304]{1,0:T(8,128)(2,1)} fusion(bf16[2304,1536]{1,0:T(8,128)(2,1)} %bitcast.15, bf16[2560,768]{0,1:T(8,128)(2,1)} %get-tuple-element.113, bf16[2560,768]{0,1:T(8,128)(2,1)} %get-tuple-element.112), kind=kOutput, calls=%fused_computation.2 | convolution fusion | flops 18141020160 | bytes 26738688 | tf_op jit(solution)/shard_map/dot_general | solution.py:987
  640.4 13.9 %convolution_convert_fusion.1 = bf16[2560,2304]{1,0:T(8,128)(2,1)} fusion(bf16[2560,768]{0,1:T(8,128)(2,1)} %get-tuple-element.114, bf16[720,2304]{1,0:T(8,128)(2,1)S(1)} %bitcast.219), kind=kOutput, calls=%fused_computation.3 | convolution fusion | flops 9065594880 | bytes 19046400 | tf_op jit(solution)/shard_map/dot_general | solution.py:983
  654.4 15.6 %fusion.3.x_ref = f32[720,2304]{1,0:T(8,128)} fusion(bf16[2560,2304]{1,0:T(8,128)(2,1)} %fusion, bf16[2560,768]{0,1:T(8,128)(2,1)} %get-tuple-element.114), kind=kOutput, calls=%fused_computation.19 | convolution fusion | flops 8493465600 | bytes 22118400 | tf_op jit(solution)/shard_map/dot_general | solution.py:987
  670.0 22.7 %convolution_convert_fusion.2 = bf16[2304,1536]{1,0:T(8,128)(2,1)} fusion(bf16[2560,2304]{1,0:T(8,128)(2,1)} %bitcast.169, bf16[2560,768]{0,1:T(8,128)(2,1)S(1)} %copy-done.72, bf16[2560,768]{0,1:T(8,128)(2,1)S(1)} %copy-done.71), kind=kOutput, calls=%fused_computation.4 | convolution fusion | flops 18138660864 | bytes 26738688 | tf_op jit(solution)/shard_map/dot_general | solution.py:987
  692.7 66.4 %reduce-scatter.7.cloned.1.call-done = bf16[320,2304]{1,0:T(8,128)(2,1)} async-done(((bf16[2560,2304]{1,0:T(8,128)(2,1)}), bf16[320,2304]{1,0:T(8,128)(2,1)}) %reduce-scatter.7.cloned.1.call-update) | async-done | bytes 1474576 | tf_op jit(solution)/shard_map/reduce_scatter | solution.py:1147
  762.7 118.8 %reduce-scatter.5.cloned.1.call-done = bf16[320,2304]{1,0:T(8,128)(2,1)} async-done(((bf16[2560,2304]{1,0:T(8,128)(2,1)}), bf16[320,2304]{1,0:T(8,128)(2,1)}) %reduce-scatter.5.cloned.1.call-update) | async-done | bytes 1474576 | tf_op jit(solution)/shard_map/reduce_scatter | solution.py:1096
  887.6 17.9 %all-to-all-done.2 = bf16[4,80,2304]{2,1,0:T(8,128)(2,1)} async-done(((bf16[4,80,2304]{2,1,0:T(8,128)(2,1)}), bf16[4,80,2304]{2,1,0:T(8,128)(2,1)}, u32[]{:S(2)}, u32[]{:S(2)}) %all-to-all-start.2) | async-done | bytes 1474592 | tf_op jit(solution)/shard_map/all_to_all | solution.py:1102
  922.2 9.3 reduce-scatter.9.cloned.1.call-done
  942.5 11.4 fusion.11
  956.8 5.3 all-to-all-start.5
  962.1 9.2 lined_up.1
  995.0 228.2 %reduce_attention.1 = (bf16[2,144,2304]{2,1,0:T(8,128)(2,1)}, bf16[2,144,2304]{2,1,0:T(8,128)(2,1)}, bf16[2,144,2304]{2,1,0:T(8,128)(2,1)}, bf16[2,144,2304]{2,1,0:T(8,128)(2,1)}, bf16[2,2,144,128]{3,2,1,0:T(8,128)(2,1)}) custom-call(bf16[4,4,144,1152]{3,2,1,0:T(8,128)(2,1)} %bitcast.171, bf16[4,4,144,1152]{3,2,1,0:T(8,128)(2,1)} %bitcast.170, ...), custom_call_target="tpu_custom_call" | custom-call | flops 99999997952 | bytes 21823488 | tf_op jit(solution)/shard_map/reduce_attention/pallas_call | solution.py:582
  1237.0 14.5 %unpack_columns.1 = f32[25920,128]{1,0:T(8,128)} custom-call(bf16[8,288,1536]{2,1,0:T(8,128)(2,1)} %all-to-all-done.5.x_ref), custom_call_target="tpu_custom_call" | custom-call | tf_op jit(solution)/shard_map/unpack_columns/pallas_call | solution.py:875
  (281 shorter events, 119.4 us)
Async XLA Ops:
  7.2 269.8 %all-gather.2.cloned.1.call-start = ((), (), s32[]{:S(2)}) async-start(), calls=%async_computation.10 | async-start | bytes 1769472 | tf_op jit(solution)/shard_map/all_gather | solution.py:1073
  231.9 69.5 %copy-start.39 = (f32[2304]{0:T(1024)}, f32[2304]{0:T(1024)S(1)}, u32[]{:S(2)}) copy-start(f32[2304]{0:T(1024)S(1)} %get-tuple-element.104) | copy-start | bytes 27652
  243.6 7.7 copy-start.12
  286.3 284.0 %all-to-all-start.1 = ((bf16[8,288,1536]{2,1,0:T(8,128)(2,1)}), bf16[8,288,1536]{2,1,0:T(8,128)(2,1)}, u32[]{:S(2)}, u32[]{:S(2)}) async-start(bf16[8,288,1536]{2,1,0:T(8,128)(2,1)} %pack_columns.1), calls=%async_computation.1 | async-start | bytes 14155776 | tf_op jit(solution)/shard_map/all_to_all | solution.py:1031
  299.4 459.6 %reduce-scatter.7.cloned.1.call-start = ((), (), s32[]{:S(2)}) async-start(), calls=%async_computation.12 | async-start | bytes 13271040 | tf_op jit(solution)/shard_map/reduce_scatter | solution.py:1147
  303.3 232.8 %copy-start.50 = (f32[128,2]{0,1:T(2,128)}, f32[128,2]{0,1:T(2,128)S(1)}, u32[]{:S(2)}) copy-start(f32[128,2]{0,1:T(2,128)S(1)} %select_reduce_fusion.1) | copy-start | bytes 3076
  303.3 232.8 %copy-start.54 = (f32[128]{0:T(128)}, f32[128]{0:T(128)S(1)}, u32[]{:S(2)}) copy-start(f32[128]{0:T(128)S(1)} %reduce_max.19) | copy-start | bytes 1540
  303.3 232.8 %copy-start.58 = (f32[128]{0:T(128)}, f32[128]{0:T(128)S(1)}, u32[]{:S(2)}) copy-start(f32[128]{0:T(128)S(1)} %fusion.64) | copy-start | bytes 1540
  303.4 232.8 %copy-start.56 = (f32[128,2]{0,1:T(2,128)}, f32[128,2]{0,1:T(2,128)S(1)}, u32[]{:S(2)}) copy-start(f32[128,2]{0,1:T(2,128)S(1)} %fusion.63) | copy-start | bytes 3076
  570.3 25.0 %copy-start.70 = (bf16[720,1,2304]{2,0,1:T(8,128)(2,1)S(1)}, bf16[720,1,2304]{2,0,1:T(8,128)(2,1)}, u32[]{:S(2)}) copy-start(bf16[720,1,2304]{2,0,1:T(8,128)(2,1)} %param.24) | copy-start | bytes 9953284
  640.4 241.2 %reduce-scatter.5.cloned.1.call-start = ((), (), s32[]{:S(2)}) async-start(), calls=%async_computation.11 | async-start | bytes 13271040 | tf_op jit(solution)/shard_map/reduce_scatter | solution.py:1096
  654.3 15.6 %copy-start.71 = (bf16[2560,768]{0,1:T(8,128)(2,1)S(1)}, bf16[2560,768]{0,1:T(8,128)(2,1)}, u32[]{:S(2)}) copy-start(bf16[2560,768]{0,1:T(8,128)(2,1)} %get-tuple-element.112) | copy-start | bytes 11796484
  654.3 15.6 %copy-start.72 = (bf16[2560,768]{0,1:T(8,128)(2,1)S(1)}, bf16[2560,768]{0,1:T(8,128)(2,1)}, u32[]{:S(2)}) copy-start(bf16[2560,768]{0,1:T(8,128)(2,1)} %get-tuple-element.113) | copy-start | bytes 11796484
  759.1 122.5 %all-to-all-start.3 = ((bf16[4,80,2304]{2,1,0:T(8,128)(2,1)}), bf16[4,80,2304]{2,1,0:T(8,128)(2,1)S(1)}, u32[]{:S(2)}, u32[]{:S(2)}) async-start(bf16[4,80,2304]{2,1,0:T(8,128)(2,1)} %bitcast.198), calls=%async_computation.5 | async-start | bytes 2949120 | tf_op jit(solution)/shard_map/all_to_all | solution.py:1102
  881.5 23.9 %all-to-all-start.2 = ((bf16[4,80,2304]{2,1,0:T(8,128)(2,1)}), bf16[4,80,2304]{2,1,0:T(8,128)(2,1)}, u32[]{:S(2)}, u32[]{:S(2)}) async-start(bf16[4,80,2304]{2,1,0:T(8,128)(2,1)} %bitcast.197), calls=%async_computation.3 | async-start | bytes 2949120 | tf_op jit(solution)/shard_map/all_to_all | solution.py:1102
  886.0 45.5 %reduce-scatter.9.cloned.1.call-start = ((), (), s32[]{:S(2)}) async-start(), calls=%async_computation.13 | async-start | bytes 3538944 | tf_op jit(solution)/shard_map/reduce_scatter | solution.py:1178
  887.6 19.8 %copy-start.1 = (f32[128,2304]{1,0:T(8,128)S(1)}, f32[128,2304]{1,0:T(8,128)}, u32[]{:S(2)}) copy-start(f32[128,2304]{1,0:T(8,128)} %copy-done) | copy-start | bytes 3538948
  887.6 19.8 %copy-start.14 = (bf16[128,2304]{1,0:T(8,128)(2,1)S(1)}, bf16[128,2304]{1,0:T(8,128)(2,1)}, u32[]{:S(2)}) copy-start(bf16[128,2304]{1,0:T(8,128)(2,1)} %p_ref.1) | copy-start | bytes 1769476
  907.4 10.9 slice-start
  911.8 6.6 slice-start.1
  922.1 11.6 copy-start.19
  922.1 69.8 %reduce-scatter.11.cloned.1.call-start = ((), (), s32[]{:S(2)}) async-start(), calls=%async_computation.14 | async-start | bytes 3538944 | tf_op jit(solution)/shard_map/reduce_scatter | solution.py:1201
  956.8 280.3 %all-to-all-start.5 = ((bf16[8,288,1536]{2,1,0:T(8,128)(2,1)}), bf16[8,288,1536]{2,1,0:T(8,128)(2,1)}, u32[]{:S(2)}, u32[]{:S(2)}) async-start(bf16[8,288,1536]{2,1,0:T(8,128)(2,1)} %bitcast.177), calls=%async_computation.9 | async-start | bytes 14155776 | tf_op jit(solution)/shard_map/all_to_all | solution.py:1154
  962.1 12.5 copy-start.5
  (60 other events, 118.3 us)
Sparse Core Ops, SparseCore 0:
  254.5 22.4 all-gather.1
  640.5 118.5 reduce-scatter.6
  761.4 120.0 reduce-scatter.4
  922.2 9.2 reduce-scatter.8
  954.1 11.0 reduce-scatter.10

commit v4 on v3

--- a/solution.py
+++ b/solution.py
@@ -17,7 +17,6 @@
 bf16 = jnp.bfloat16
 f32 = jnp.float32
 SHARD = ("z", "core")
-GRID = ("z", "expert")
 AHEAD = 2
 ANY = pl.BlockSpec(memory_space=pl.ANY)
 
@@ -51,10 +50,17 @@
 
     cores = (c, 1 - c) if both_cores[0] else (c,)
     plane = (c, 1 - c) if both_cores[1] else (c,)
-    hail(e, z, 1 - c)
     for t in plane:
         hail(ex, z, t)
         hail(ey, z, t)
+    if both_cores[0]:
+        n = 2 * nz
+        for d in range(1, n):
+            to = (2 * z + c + d) % n
+            hail(e, to // 2, to % 2)
+        pl.semaphore_wait(barrier, n - 1 + 2 * len(plane))
+        return
+    hail(e, z, 1 - c)
     for step in (-1, 1):
 
         @pl.when((z + step >= 0) & (z + step < nz))
@@ -73,9 +79,10 @@
 
 def gather_kernel(
     nz, Q, H,
-    q_ref, k_ref, v_ref, o_ref, s_ref, t_ref, l_ref, p_ref,
-    qkv_out, o_out, s_out, t_out, l_out, p_out,
+    q_ref, k_ref, v_ref, o_ref, s_ref, t_ref, l_ref, p_ref, w_ref,
+    qkv_out, o_out, s_out, t_out, l_out, p_out, w_out,
     zrecv, zhop, zsend, near_recv, near_send, far_recv, far_send, own, sib_send, sib_recv,
+    w_send, w_recv, w_own,
     *payload,
 ):
     e, z, c, ex, ey = place()
@@ -213,6 +220,8 @@
                 p_relay(s - 1)
             if s >= 2:
                 p_close(s - 2)
+    w_begin, w_end = scatter_stream(nz, w_ref, w_out, w_send, w_recv, w_own)
+    w_begin()
     for step in steps[len(steps) - lag :]:
         relay(*step)
     p_relay(blocks - 1)
@@ -220,6 +229,7 @@
     p_close(blocks - 1)
     for s in range(blocks):
         p_end(s)
+    w_end()
 
     for k, side, i in steps:
 
@@ -254,7 +264,7 @@
         copy.wait()
 
 
-def gather_attention(nz, weights, small, tokens, lengths, block):
+def gather_attention(nz, weights, small, tokens, lengths, block, columns):
     R, D = weights[0].shape
     Q, H = R // 2, D // 2
     K = len(weights) + 1
@@ -271,9 +281,10 @@
             sd((2,) + tokens.shape, bf16),
             sd((2,) + lengths.shape, lengths.dtype),
             sd((nz, 2, 4) + block.shape, block.dtype),
+            sd(columns.shape, columns.dtype),
         ),
-        in_specs=[any_] * 8,
-        out_specs=(any_,) * 6,
+        in_specs=[any_] * 9,
+        out_specs=(any_,) * 7,
         scratch_shapes=[
             dma((K, 2, nz - 1)),
             dma((K, 2, 2)),
@@ -285,6 +296,9 @@
             dma((K + 2,)),
             dma((K + 2,)),
             dma((K + 2,)),
+            dma((2 * nz,)),
+            dma((2 * nz,)),
+            dma(()),
             *payload_sems(nz),
         ],
         compiler_params=pltpu.CompilerParams(collective_id=0, has_side_effects=True),
@@ -292,7 +306,7 @@
             flops=10**11, bytes_accessed=8 * D * H * 2, transcendentals=0
         ),
         name="gather_attention",
-    )(*weights, small, tokens, lengths, block)
+    )(*weights, small, tokens, lengths, block, columns)
     return outs
 
 
@@ -613,7 +627,7 @@
             collective_id=1, has_side_effects=True, vmem_limit_bytes=60 << 20
         ),
         cost_estimate=pl.CostEstimate(
-            flops=10**11, bytes_accessed=nz * 4 * Q * W * 2, transcendentals=0
+            flops=10**6, bytes_accessed=10**6, transcendentals=0
         ),
         name="reduce_attention",
     )(*parts)
@@ -825,13 +839,308 @@
         scratch_shapes=[s for _ in blocks for s in payload_sems(nz)],
         compiler_params=pltpu.CompilerParams(collective_id=collective, has_side_effects=True),
         cost_estimate=pl.CostEstimate(
-            flops=5 * 10**10, bytes_accessed=sum(b.size for b in blocks) * 128, transcendentals=0
+            flops=10**6, bytes_accessed=10**6, transcendentals=0
         ),
         name="spread_blocks",
     )(*blocks)
 
 
-def pack_kernel(n, F, Fp, x_ref, o_ref):
+def scatter_stream(nz, ref, out, send, recv, own):
+    e, z, c, ex, ey = place()
+    n = 2 * nz
+    me = 2 * z + c
+
+    def copy(d):
+        to = (me + d) % n
+        return remote(ref.at[to], out.at[me], send.at[d], recv.at[d], e, to // 2, to % 2)
+
+    def kept():
+        return pltpu.make_async_copy(ref.at[me], out.at[me], own)
+
+    def begin():
+        kept().start()
+        for d in range(1, n):
+            copy(d).start()
+
+    def end():
+        kept().wait()
+        for d in range(1, n):
+            view = out.at[(me + n - d) % n]
+            remote(view, view, send.at[d], recv.at[d], e, z, c).wait_recv()
+            copy(d).wait_send()
+
+    return begin, end
+
+
+def line_order(nz, z):
+    def order(i):
+        code = 0
+        for zz in range(nz):
+            far_first = sorted(range(nz), key=lambda t: (-abs(t - zz), t))
+            code += far_first[i] * nz**zz
+        power = 1
+        for zz in range(nz):
+            power = power + (nz**zz - 1) * jnp.where(z == zz, 1, 0)
+        return (code // power) % nz
+
+    return [order(i) for i in range(nz)]
+
+
+def collect_kernel(
+    nz, cap,
+    rows_ref, notes_ref, dots_ref,
+    out_ref, dots_out,
+    dots, notes, mine, theirs, block, from_x, from_y, via_x, via_y, from_z,
+    note_sem, load, sib_send, sib_recv, via_send, via_recv, plain_send, plain_recv,
+    sum_send, sum_recv, zsend, zrecv, dot_send, dot_recv, dot_own,
+):
+    e, z, c, ex, ey = place()
+    diagonal = (ex + 2) % 4
+    T, D = out_ref.shape
+    h = T // 2
+    dest = line_order(nz, z)
+    who = (diagonal, ex, ey, e)
+
+    def others():
+        for d in range(1, 8 * nz):
+            to = ((e * nz + z) * 2 + c + d) % (8 * nz)
+            yield d, to // (2 * nz), to // 2 % nz, to % 2
+
+    barrier = pltpu.get_barrier_semaphore()
+    for _, te, tz, tc in others():
+        pl.semaphore_signal(
+            barrier, inc=1, device_id=(te, tz, tc), device_id_type=pl.DeviceIdType.MESH
+        )
+    pl.semaphore_wait(barrier, 8 * nz - 1)
+
+    def dot(d, te, tz, tc):
+        return remote(
+            dots_ref.at[tz, tc, te], dots.at[d], dot_send.at[d], dot_recv.at[d], te, tz, tc
+        )
+
+    dot_kept = pltpu.make_async_copy(dots_ref.at[z, c, e], dots.at[0], dot_own)
+    dot_kept.start()
+    for d, te, tz, tc in others():
+        dot(d, te, tz, tc).start()
+
+    note_copy = pltpu.make_async_copy(notes_ref, notes, note_sem)
+    note_copy.start()
+
+    def fetch(i, q):
+        return pltpu.make_async_copy(
+            rows_ref.at[dest[i], c, who[q]], mine.at[i, q], load.at[i, q]
+        )
+
+    def hand(i, q):
+        return remote(
+            rows_ref.at[dest[i], 1 - c, who[q]], theirs.at[i, q],
+            sib_send.at[i, q], sib_recv.at[i, q], e, z, 1 - c,
+        )
+
+    for i in range(nz):
+        for q in range(4):
+            hand(i, q).start()
+            fetch(i, q).start()
+    note_copy.wait()
+
+    def open_out(i, q):
+        fetch(i, q).wait()
+        hand(i, q).wait_recv()
+        places = (lax.broadcasted_iota(jnp.int32, (cap, T), 0) + e * cap).astype(f32)
+        note = notes[dest[i], c, who[q]]
+        pick = ((note[2:3, :] == places) | (note[3:4, :] == places)).astype(bf16)
+        wide = 768 if D % 768 == 0 else 128
+
+        @pl.loop(0, D // wide)
+        def _(b):
+            cols = pl.ds(pl.multiple_of(b * wide, 128), wide)
+            both = mine[i, q, :, cols].astype(f32) + theirs[i, q, :, cols].astype(f32)
+            block[i, q, :, cols] = lax.dot_general(
+                pick, both.astype(bf16), (((0,), (0,)), ((), ())), preferred_element_type=f32
+            ).astype(bf16)
+
+    def via(i, axis):
+        if axis == 0:
+            return remote(
+                block.at[i, 0, pl.ds(0, h), :], via_x.at[i],
+                via_send.at[i, 0], via_recv.at[i, 0], ex, z, c,
+            )
+        return remote(
+            block.at[i, 0, pl.ds(h, h), :], via_y.at[i],
+            via_send.at[i, 1], via_recv.at[i, 1], ey, z, c,
+        )
+
+    def plain(i, axis):
+        if axis == 0:
+            return remote(
+                block.at[i, 1, pl.ds(0, h), :], from_x.at[i, pl.ds(0, h), :],
+                plain_send.at[i, 0], plain_recv.at[i, 0], ex, z, c,
+            )
+        return remote(
+            block.at[i, 2, pl.ds(h, h), :], from_y.at[i, pl.ds(h, h), :],
+            plain_send.at[i, 1], plain_recv.at[i, 1], ey, z, c,
+        )
+
+    def summed(i, axis):
+        if axis == 0:
+            return remote(
+                block.at[i, 1, pl.ds(h, h), :], from_x.at[i, pl.ds(h, h), :],
+                sum_send.at[i, 0], sum_recv.at[i, 0], ex, z, c,
+            )
+        return remote(
+            block.at[i, 2, pl.ds(0, h), :], from_y.at[i, pl.ds(0, h), :],
+            sum_send.at[i, 1], sum_recv.at[i, 1], ey, z, c,
+        )
+
+    def add(target, others, n):
+        @pl.loop(0, n // 16)
+        def _(b):
+            rows = pl.ds(pl.multiple_of(b * 16, 16), 16)
+            acc = target[rows, :].astype(f32)
+            for o in others:
+                acc = acc + o[rows, :].astype(f32)
+            target[rows, :] = acc.astype(target.dtype)
+
+    def start(i):
+        open_out(i, 0)
+        via(i, 0).start()
+        via(i, 1).start()
+        open_out(i, 1)
+        plain(i, 0).start()
+        open_out(i, 2)
+        plain(i, 1).start()
+        open_out(i, 3)
+
+    def combine(i):
+        via(i, 0).wait_recv()
+        add(block.at[i, 2, pl.ds(0, h), :], [via_x.at[i]], h)
+        summed(i, 1).start()
+        via(i, 1).wait_recv()
+        add(block.at[i, 1, pl.ds(h, h), :], [via_y.at[i]], h)
+        summed(i, 0).start()
+
+    def zcopy(i):
+        step = jnp.where(dest[i] > z, 1, -1)
+        side = jnp.where(dest[i] > z, 0, 1)
+        return remote(
+            block.at[i, 3], from_z.at[side, dest[i]],
+            zsend.at[i], zrecv.at[side, dest[i]], e, z + step, c,
+        )
+
+    def zwait(side, zz):
+        slab = from_z.at[side, zz]
+        remote(slab, slab, zsend.at[0], zrecv.at[side, zz], e, z, c).wait_recv()
+
+    def finish(i):
+        for axis in range(2):
+            plain(i, axis).wait_recv()
+            summed(i, axis).wait_recv()
+        zz = dest[i]
+        if i < nz - 1:
+            add(block.at[i, 3], [from_x.at[i], from_y.at[i]], T)
+            for side in range(2):
+                going = zz > z if side == 0 else zz < z
+                behind = z > 0 if side == 0 else z < nz - 1
+
+                @pl.when(going & behind)
+                def _():
+                    zwait(side, zz)
+                    add(block.at[i, 3], [from_z.at[side, zz]], T)
+
+            zcopy(i).start()
+            return
+
+        @pl.loop(0, T // 16)
+        def _(b):
+            rows = pl.ds(pl.multiple_of(b * 16, 16), 16)
+            acc = block[i, 3, rows, :].astype(f32) + from_x[i, rows, :].astype(f32)
+            out_ref[rows, :] = acc + from_y[i, rows, :].astype(f32)
+
+        for side in range(2):
+
+            @pl.when(z > 0 if side == 0 else z < nz - 1)
+            def _():
+                zwait(side, z)
+                add(out_ref, [from_z.at[side, z]], T)
+
+    for i in range(nz):
+        start(i)
+        if i >= 1:
+            combine(i - 1)
+        if i >= 2:
+            finish(i - 2)
+    combine(nz - 1)
+    if nz >= 2:
+        finish(nz - 2)
+    finish(nz - 1)
+
+    dot_kept.wait()
+    for d, te, tz, tc in others():
+        dot(d, te, tz, tc).wait_recv()
+        dot(d, te, tz, tc).wait_send()
+    dots_out[...] = jnp.sum(dots[...], axis=0)
+
+    for i in range(nz):
+        for q in range(4):
+            hand(i, q).wait_send()
+        for axis in range(2):
+            via(i, axis).wait_send()
+            plain(i, axis).wait_send()
+            summed(i, axis).wait_send()
+        if i < nz - 1:
+            zcopy(i).wait_send()
+
+
+def collect_rows(nz, rows, notes, dots, T):
+    cap, D = rows.shape[3:]
+    dma = pltpu.SemaphoreType.DMA
+    vm = pltpu.VMEM
+    return pl.pallas_call(
+        functools.partial(collect_kernel, nz, cap),
+        out_shape=(
+            jax.ShapeDtypeStruct((T, D), f32),
+            jax.ShapeDtypeStruct(dots.shape[3:], f32),
+        ),
+        in_specs=[ANY] * 3,
+        out_specs=(pl.BlockSpec(memory_space=pltpu.VMEM),) * 2,
+        scratch_shapes=[
+            vm((8 * nz,) + dots.shape[3:], f32),
+            vm(notes.shape, f32),
+            vm((nz, 4, cap, D), bf16),
+            vm((nz, 4, cap, D), bf16),
+            vm((nz, 4, T, D), bf16),
+            vm((nz, T, D), bf16),
+            vm((nz, T, D), bf16),
+            vm((nz, T // 2, D), bf16),
+            vm((nz, T // 2, D), bf16),
+            vm((2, nz, T, D), bf16),
+            dma(()),
+            dma((nz, 4)),
+            dma((nz, 4)),
+            dma((nz, 4)),
+            dma((nz, 2)),
+            dma((nz, 2)),
+            dma((nz, 2)),
+            dma((nz, 2)),
+            dma((nz, 2)),
+            dma((nz, 2)),
+            dma((nz,)),
+            dma((2, nz)),
+            dma((8 * nz,)),
+            dma((8 * nz,)),
+            dma(()),
+        ],
+        compiler_params=pltpu.CompilerParams(
+            collective_id=3, has_side_effects=True, vmem_limit_bytes=56 << 20
+        ),
+        cost_estimate=pl.CostEstimate(
+            flops=5 * 10**10, bytes_accessed=2 * rows.size, transcendentals=0
+        ),
+        name="collect_rows",
+    )(rows, notes, dots)
+
+
+def pack_kernel(n, F, Fp, x_ref, *o_refs):
     half = n * F
     rows = x_ref.shape[0]
     for i in range(n):
@@ -839,7 +1148,7 @@
             cols = x_ref[:, part * half + i * F : part * half + (i + 1) * F]
             if Fp > F:
                 cols = jnp.concatenate([cols, jnp.zeros((rows, Fp - F), cols.dtype)], axis=1)
-            o_ref[i, :, part * Fp : (part + 1) * Fp] = cols
+            o_refs[part][i] = cols
 
 
 def pack_columns(w, n, F, Fp):
@@ -849,8 +1158,8 @@
         functools.partial(pack_kernel, n, F, Fp),
         grid=(rows // block,),
         in_specs=[pl.BlockSpec((block, w.shape[1]), lambda i: (i, 0))],
-        out_specs=pl.BlockSpec((n, block, 2 * Fp), lambda i: (0, i, 0)),
-        out_shape=jax.ShapeDtypeStruct((n, rows, 2 * Fp), w.dtype),
+        out_specs=(pl.BlockSpec((n, block, Fp), lambda i: (0, i, 0)),) * 2,
+        out_shape=(jax.ShapeDtypeStruct((n, rows, Fp), w.dtype),) * 2,
         name="pack_columns",
     )(w)
 
@@ -906,7 +1215,7 @@
     return flat.reshape(rows, 1, width)
 
 
-def gather_plain(nz, weights, small, tokens, lengths, block):
+def gather_plain(nz, weights, small, tokens, lengths, block, columns):
     core, H = lax.axis_index("core"), weights[0].shape[1] // 2
     full = [
         lax.all_gather(swap_core(w, 1, 0), "z", axis=0, tiled=True) for w in weights
@@ -918,6 +1227,7 @@
         lax.all_gather(tokens, "core", axis=0),
         lax.all_gather(lengths, "core", axis=0),
         spread_plain(nz, (block,), 0)[0],
+        lax.all_to_all(columns, SHARD, split_axis=0, concat_axis=0, tiled=True),
     )
 
 
@@ -928,6 +1238,21 @@
             block = lax.all_gather(block, axis, axis=0)
         out.append(block)
     return out
+
+
+def collect_plain(nz, rows, notes, dots, T):
+    n_exp, cap, D = rows.shape[2:]
+    places = (lax.axis_index("expert") * cap + jnp.arange(cap)).astype(f32)
+    notes = notes[..., :T]
+    pick = (notes[..., 2, None, :] == places[:, None]) | (notes[..., 3, None, :] == places[:, None])
+    part = jnp.einsum(
+        "zceps,zcepd->zcesd", pick.astype(bf16), rows, preferred_element_type=f32
+    ).astype(bf16)
+    part = part.transpose(2, 0, 1, 3, 4).reshape(n_exp * nz * 2 * T, D)
+    part = lax.psum_scatter(part, "expert", scatter_dimension=0, tiled=True)
+    part = lax.psum_scatter(part, SHARD, scatter_dimension=0, tiled=True).astype(f32)
+    z, core, e = lax.axis_index("z"), lax.axis_index("core"), lax.axis_index("expert")
+    return part, lax.psum(dots, ("expert",) + SHARD)[z, core, e]
 
 
 def reduce_plain(nz, parts):
@@ -1027,9 +1352,8 @@
     core = lax.axis_index("core")
 
     Fp = -(-F // 128) * 128
-    packed = pack_columns(w_in.reshape(R, 2 * FF), n_shard, F, Fp)
-    moved = lax.all_to_all(packed, SHARD, split_axis=0, concat_axis=0, tiled=True)
-    w_pair = moved.reshape(n_shard * R, 2 * Fp)
+    packed_gate, packed_up = pack_columns(w_in.reshape(R, 2 * FF), n_shard, F, Fp)
+    moved_up = lax.all_to_all(packed_up, SHARD, split_axis=0, concat_axis=0, tiled=True)
     down = jnp.pad(w_down.reshape(F, D), ((0, Fp - F), (0, 0)))
 
     nz = lax.axis_size("z")
@@ -1037,9 +1361,10 @@
     small = jnp.pad(small, ((0, 0), (0, 128 - small.shape[1])))
     length_rows = jnp.broadcast_to(seq_lengths[:, :1], (8, 128))
     gather = gather_attention if n_exp == 4 else gather_plain
-    full_qkv, full_output, full_small, chip_tokens, chip_lengths, all_cotangent = gather(
-        nz, (w_query, w_key, w_value, w_output), small, tokens, length_rows, cotangent
+    full_qkv, full_output, full_small, chip_tokens, chip_lengths, all_cotangent, moved_gate = gather(
+        nz, (w_query, w_key, w_value, w_output), small, tokens, length_rows, cotangent, packed_gate
     )
+    w_gate, w_up = moved_gate.reshape(n_shard * R, Fp), moved_up.reshape(n_shard * R, Fp)
     full_router = full_small[:, :experts]
     gain_attn = full_small[:, experts].astype(f32)
     gain_ffn = full_small[:, experts + 1].astype(f32)
@@ -1070,9 +1395,24 @@
     probs_half = attn_probs.astype(bf16)
     context = ein32("bhqk,bkhd->bqhd", probs_half, values).astype(bf16)
     context_half = context.reshape(2 * T, H)
-    context_full = lax.all_gather(context_half, "core", axis=1, tiled=True)
+    core = lax.axis_index("core")
+
+    def beside(x):
+        return lax.ppermute(x, "core", [(0, 1), (1, 0)])
+
+    def side_by_side(mine, theirs, axis):
+        first = jnp.where(core == 0, mine, theirs)
+        return jnp.concatenate([first, jnp.where(core == 0, theirs, mine)], axis=axis)
+
+    def halves(x, axis):
+        size = x.shape[axis] // 2
+        mine = lax.dynamic_slice_in_dim(x, core * size, size, axis)
+        return mine, lax.dynamic_slice_in_dim(x, (1 - core) * size, size, axis)
+
+    context_full = side_by_side(context_half, beside(context_half), 1)
     mid_half = dot32(context_full, full_output)
-    mid_own = swap_core(mid_half, 0, 1)
+    mid_mine, mid_other = halves(mid_half, 0)
+    mid_own = side_by_side(mid_mine, beside(mid_other), 1)
     residual_mid = residual_in + branch_scale * mid_own
     normed_mid, inverse_mid = rms_forward(residual_mid, gain_ffn)
     normed_mid_half = normed_mid.astype(bf16)
@@ -1107,36 +1447,42 @@
     spread = spread_blocks if n_exp == 4 else spread_plain
     all_normed, all_notes = spread(nz, (normed_mid_half, notes), 2)
     devices = n_shard * n_exp
-    all_notes = all_notes.reshape(devices, 8, -1)[:, :, :T]
+    flat_notes = all_notes.reshape(devices, 8, -1)[:, :, :T]
     wanted = (e_index * capacity + jnp.arange(capacity)).astype(f32)
     found = [
-        all_notes[:, 2 + k, None, :] == wanted[None, :, None] for k in range(2)
+        flat_notes[:, 2 + k, None, :] == wanted[None, :, None] for k in range(2)
     ]
     gate_rows = jnp.sum(
-        jnp.where(found[0], all_notes[:, 0, None, :], 0.0)
-        + jnp.where(found[1], all_notes[:, 1, None, :], 0.0),
+        jnp.where(found[0], flat_notes[:, 0, None, :], 0.0)
+        + jnp.where(found[1], flat_notes[:, 1, None, :], 0.0),
         axis=-1,
     ).reshape(devices * capacity, 1)
     chosen_rows = (found[0] | found[1]).astype(bf16)
 
     def take(blocks):
         rows = ein32("spt,std->spd", chosen_rows, blocks.reshape(devices, T, D))
-        return rows.astype(bf16).reshape(devices * capacity, D)
-
-    arrived = take(all_normed)
-    grad_arrived = (gate_rows * (branch_scale * take(all_cotangent).astype(f32))).astype(bf16)
-    pre = dot32(arrived, w_pair)
-    gate_part, up_part = pre[:, :Fp], pre[:, Fp:]
+        return rows.reshape(devices * capacity, D)
+
+    arrived = take(all_normed).astype(bf16)
+    cotangent_rows = take(all_cotangent)
+    grad_scale = gate_rows * branch_scale
+    grad_arrived = (gate_rows * (branch_scale * cotangent_rows)).astype(bf16)
+    gate_part, up_part = dot32(arrived, w_gate), dot32(arrived, w_up)
     sigmoid_gate = jax.nn.sigmoid(gate_part)
     silu_gate = gate_part * sigmoid_gate
     activated = (silu_gate * up_part).astype(bf16)
     expert_rows = bring_back(dot32(activated, down))
     upstream = cotangent.astype(f32)
-    mixture_grad = branch_scale * upstream
     mixture = gate_probs[:, 0:1] * expert_rows[0] + gate_probs[:, 1:2] * expert_rows[1]
     activations = (residual_mid + branch_scale * mixture).astype(bf16)
 
-    act_grad = dot_dims(grad_arrived, down, 1, 1)
+    raw_grad = dot_dims(cotangent_rows.astype(bf16), down, 1, 1)
+    row_dots = branch_scale * jnp.sum(raw_grad * activated.astype(f32), axis=1)
+    row_dots = row_dots.reshape(devices, capacity, 1)
+    token_dots = [jnp.sum(jnp.where(found[k], row_dots, 0.0), axis=1) for k in range(2)]
+    token_dots = jnp.stack(token_dots, axis=1).reshape(nz, 2, n_exp, 2, T)
+    token_dots = jnp.pad(token_dots, ((0, 0),) * 3 + ((0, 6), (0, -T % 128)))
+    act_grad = grad_scale * raw_grad
     pre_grad = jnp.concatenate(
         [
             act_grad * up_part * sigmoid_gate * (1.0 + gate_part * (1.0 - sigmoid_gate)),
@@ -1144,23 +1490,21 @@
         ],
         axis=1,
     ).astype(bf16)
-    in_sum = lax.psum_scatter(
-        dot_dims(pre_grad, w_pair, 1, 1).astype(bf16), SHARD, scatter_dimension=0, tiled=True
-    )
+    w_pair = jnp.concatenate([w_gate, w_up], axis=1)
+    in_rows = dot_dims(pre_grad, w_pair, 1, 1).astype(bf16)
+    in_rows = in_rows.reshape(nz, 2, n_exp, capacity, D)
+    collect = collect_rows if n_exp == 4 else collect_plain
+    normed_mid_grad, gate_grad = collect(nz, in_rows, all_notes, token_dots, T)
+    gate_grad = jnp.transpose(gate_grad[:2, :T])
     in_term = dot_dims(arrived, pre_grad, 0, 0).astype(bf16).reshape(n_shard, R, 2 * Fp)
+    in_term, normed_mid_grad = lax.optimization_barrier((in_term, normed_mid_grad))
+    in_term = lax.all_to_all(in_term, SHARD, split_axis=0, concat_axis=0, tiled=True)
     down_term = dot_dims(activated[:, :F], grad_arrived, 0, 0)
-    in_sum, in_term, down_term = lax.optimization_barrier((in_sum, in_term, down_term))
-    input_rows = at_home(in_sum)
-    in_term = lax.all_to_all(in_term, SHARD, split_axis=0, concat_axis=0, tiled=True)
     grad_w_in = unpack_columns(in_term, F)
     grad_w_down = lined_up(down_term)
 
-    gate_grad = jnp.stack(
-        [jnp.sum(mixture_grad * expert_rows[k], axis=-1) for k in range(2)], axis=1
-    )
     chosen_grad = gate_probs * (gate_grad - jnp.sum(gate_probs * gate_grad, axis=-1, keepdims=True))
     logit_grad = jnp.sum(chosen_grad[:, :, None] * route_mask, axis=1)
-    normed_mid_grad = input_rows[0] + input_rows[1]
     normed_mid_grad = normed_mid_grad + jnp.dot(
         logit_grad, jnp.transpose(full_router.astype(f32)), precision=highest
     )
@@ -1173,14 +1517,11 @@
     residual_grad = upstream + mid_norm_grad
     branch_own = (branch_scale * residual_grad).astype(bf16)
 
-    branch_half = swap_core(branch_own, 1, 0)
+    branch_mine, branch_other = halves(branch_own, 1)
+    branch_half = side_by_side(branch_mine, beside(branch_other), 0)
     context_grad = dot_dims(branch_half, full_output, 1, 1)
-    context_grad = lax.psum_scatter(
-        context_grad.reshape(2 * T, 2, H).transpose(1, 0, 2).reshape(4 * T, H),
-        "core",
-        scatter_dimension=0,
-        tiled=True,
-    ).reshape(head_shape)
+    grad_mine, grad_other = halves(context_grad, 1)
+    context_grad = (grad_mine + beside(grad_other)).reshape(head_shape)
     row_delta = jnp.sum(context_grad * context.astype(f32), axis=-1)
     context_grad_half = context_grad.astype(bf16)
     probs_grad = ein32("bqhd,bkhd->bhqk", context_grad_half, values)
@@ -1198,9 +1539,8 @@
     weight_grads = [dot_dims(normed_half, p, 0, 0) for p in parts]
     weight_grads.append(dot_dims(context_full, branch_half, 0, 0))
     qkv_grad = jnp.concatenate(parts, axis=1)
-    normed_in_grad = lax.psum_scatter(
-        dot_dims(qkv_grad, full_qkv, 1, 1), "core", scatter_dimension=0, tiled=True
-    )
+    grad_mine, grad_other = halves(dot_dims(qkv_grad, full_qkv, 1, 1), 0)
+    normed_in_grad = grad_mine + beside(grad_other)
     in_norm_grad, gain_attn_grad = rms_backward(residual_in, inverse_in, gain_attn, normed_in_grad)
     grad_tokens = residual_grad + in_norm_grad
 

time: 1270 us -> 1130 us (0.89)
  waiting for transfers between devices: 220 us -> 0.57 us
  Pallas kernels: 711 us -> 776 us
  other arithmetic: 38.8 us -> 69.6 us
    pallas_call x1, Pallas kernels: 232 us -> 91.1 us  [spread_blocks(): pl.pallas_call(functools.partial(spread_kernel, nz, splits), out_shape=tu...]
    reduce_scatter x1, waiting for transfers between devices: 119 us -> 0.01 us  [bring_back(): lax.psum_scatter(partial_rows.astype(bf16), SHARD, scatter_dimension=0, t...]
    pallas_call x0 -> x1, Pallas kernels: none -> 114 us  [collect_rows(): pl.pallas_call(functools.partial(collect_kernel, nz, cap), out_shape=(jax...]
    pallas_call x1, Pallas kernels: 214 us -> 307 us  [gather_attention(): pl.pallas_call(functools.partial(gather_kernel, nz, Q, H), out_shape=(sd(...]
    reduce_scatter x3 -> x0, waiting for transfers between devices: 75.7 us -> none  [the longest x1 66.4 us: on_device(): lax.psum_scatter(dot_dims(pre_grad, w_pair, 1, 1).astype(bf16), SHARD, sc...]
    all_to_all x2 -> x1, waiting for transfers between devices: 17.9 us -> 0.01 us  [at_home(): lax.all_to_all(mine, 'expert', split_axis=0, concat_axis=0, tiled=True)]
    convert_element_type x1 -> x2, other arithmetic: 10.8 us -> 25.5 us  [the longest x1 12.9 us: on_device(): grad_arrived = (gate_rows * (branch_scale * cotangent_rows)).astype(bf16)]
    dot_general x10 -> x9, matrix products: 60.2 us -> 60.4 us  [dot32(): return jnp.dot(a, b, preferred_element_type=f32)]
  transfers between devices with their start and end apart: 9 -> 9, of which waited for: 5 -> 2; matrix products, arithmetic and copies ran while one was open for 10% -> 22% of each run, Pallas kernels for 38% -> 68%
where the time goes in v4:
time: 1130 us; the launch traced here: 1120 us
  Pallas kernels  776 us (69%)
  matrix products  203 us (18%)
  other arithmetic  69.6 us (6%)
  local copies, waits for them, and re-layouts  35.5 us (3%)
  starting transfers between devices  19.9 us (2%)
  between operations  15.6 us (1%)
    pallas_call x1, Pallas kernels, gather_attention(): pl.pallas_call(functools.partial(gather_kernel, nz, Q, H), out_shape=(sd(...  307 us
    pallas_call x1, Pallas kernels, reduce_attention(): pl.pallas_call(functools.partial(reduce_kernel, nz, Q, widths), out_shape...  227 us
    pallas_call x1, Pallas kernels, collect_rows(): pl.pallas_call(functools.partial(collect_kernel, nz, cap), out_shape=(jax...  114 us
    dot_general x10, matrix products, dot_dims(): lax.dot_general(a, b, (((da,), (db,)), ((), ())), preferred_element_type=...  110 us
    pallas_call x1, Pallas kernels, spread_blocks(): pl.pallas_call(functools.partial(spread_kernel, nz, splits), out_shape=tu...  91.1 us
    dot_general x9, matrix products, dot32(): return jnp.dot(a, b, preferred_element_type=f32)  60.4 us
    dot_general x8, matrix products, ein32(): return jnp.einsum(spec, a, b, preferred_element_type=f32)  29.2 us
  transfers between devices with their start and end apart: 9, of which 2 were waited for; matrix products, arithmetic and copies ran while one was open for 22% of the time, Pallas kernels for 68%

profile of v4, /device:TPU:16, one launch (start us, length us, event | category | flops | bytes accessed | tf_op | source)
XLA Modules:
  0.0 1120.9 jit_solution(12691110202056380685)
XLA Ops:
  7.2 13.4 %pack_columns.1 = (bf16[8,288,768]{2,1,0:T(8,128)(2,1)}, bf16[8,288,768]{2,1,0:T(8,128)(2,1)}) custom-call(bf16[288,11520]{1,0:T(8,128)(2,1)} %bitcast.167), custom_call_target="tpu_custom_call" | custom-call | tf_op jit(solution)/shard_map/pack_columns/pallas_call | solution.py:1157
  20.6 5.4 all-to-all-start
  28.5 307.1 %gather_attention.1 = (bf16[2304,3456]{1,0:T(8,128)(2,1)}, bf16[2304,1152]{1,0:T(8,128)(2,1)}, bf16[2304,128]{1,0:T(8,128)(2,1)}, bf16[2,128,2304]{2,1,0:T(8,128...) custom-call(bf16[288,2304]{1,0:T(8,128)(2,1)} %q_ref.1, ...), custom_call_target="tpu_custom_call" | custom-call | flops 99999997952 | bytes 42467328 | tf_op jit(solution)/shard_map/gather_attention/pallas_call | solution.py:275
  342.5 8.5 fusion.86
  370.2 4.7 fusion.41
  379.9 91.1 %spread_blocks.1 = (bf16[4,2,4,128,2304]{4,3,2,1,0:T(8,128)(2,1)}, f32[4,2,4,8,128]{4,3,2,1,0:T(8,128)}) custom-call(bf16[128,2304]{1,0:T(8,128)(2,1)} %copy-done.11, f32[8,128]{1,0:T(8,128)} %maximum_bitcast_fusion.refs_1_), custom_call_target="tpu_custom_call" | custom-call | flops 1000000 | bytes 1000000 | tf_op jit(solution)/shard_map/spread_blocks/pallas_call | solution.py:834
  472.3 13.2 %fusion.40 = f32[32,80,2304]{2,1,0:T(8,128)} fusion(bf16[32,128,2304]{2,1,0:T(8,128)(2,1)} %bitcast.157, f32[32,128]{1,0:T(8,128)S(1)} %bitcast.184, f32[32,128]{1,0:T(8,128)S(1)} %bitcast.187, f32[80]{0:T(128)S(1)} %add_convert_fusion.2), kind=kOutput, calls=%fused_computation.102 | convolution fusion | flops 1510932480 | bytes 42500416 | tf_op jit(solution)/shard_map/spt,std->spd/dot_general | solution.py:1316
  485.5 10.8 convolution_convert_fusion.7
  497.5 14.5 %fusion.87 = f32[2560,768]{0,1:T(8,128)} fusion(bf16[2560,2304]{1,0:T(8,128)(2,1)} %bitcast.159, bf16[2304,768]{1,0:T(8,128)(2,1)S(1)} %bitcast.201), kind=kOutput, calls=%fused_computation.212 | convolution fusion | flops 9059696640 | bytes 23199744 | tf_op jit(solution)/shard_map/dot_general | solution.py:1308
  511.9 12.5 %bitcast_convert_fusion = bf16[2560,2304]{1,0:T(8,128)(2,1)} fusion(f32[32,80,2304]{2,1,0:T(8,128)} %fusion.40), kind=kLoop, calls=%fused_computation.1 | loop fusion | flops 5898240 | bytes 35389440 | tf_op jit(solution)/shard_map/convert_element_type | solution.py:1479
  524.5 15.6 %fusion.88 = f32[2560,768]{0,1:T(8,128)} fusion(bf16[2560,2304]{1,0:T(8,128)(2,1)} %bitcast.160, bf16[2304,768]{1,0:T(8,128)(2,1)} %bitcast.14), kind=kOutput, calls=%fused_computation.213 | convolution fusion | flops 9059696640 | bytes 23199744 | tf_op jit(solution)/shard_map/dot_general | solution.py:1308
  540.1 18.4 %multiply_reduce_fusion = (f32[2560]{0:T(1024)S(1)}, bf16[2560,768]{0,1:T(8,128)(2,1)}, f32[2560,768]{0,1:T(8,128)}) fusion(f32[2560,768]{0,1:T(8,128)} %fusion.88, f32[2560,768]{0,1:T(8,128)} %fusion.87, bf16[2560,2304]{1,0:T(8,128)(2,1)} %bitcast_convert_fusion, bf16[720,2304]{1,0:T(8,128)(2,1)S(1)} %bitcast.198), kind=kOutput, calls=%fused_computation.12 | convolution fusion | flops 9077389312 | bytes 42649600 | tf_op jit(solution)/shard_map/dot_general | solution.py:1312
  560.0 14.8 %convolution_convert_fusion.1 = bf16[2560,2304]{1,0:T(8,128)(2,1)} fusion(bf16[2560,768]{0,1:T(8,128)(2,1)} %get-tuple-element.119, bf16[720,2304]{1,0:T(8,128)(2,1)} %bitcast.197), kind=kOutput, calls=%fused_computation.4 | convolution fusion | flops 9065594880 | bytes 19046400 | tf_op jit(solution)/shard_map/dot_general | solution.py:1308
  574.9 9.7 multiply_convert_fusion.1
  584.6 22.5 %convolution_convert_fusion.2 = bf16[2304,1536]{1,0:T(8,128)(2,1)} fusion(bf16[2560,2304]{1,0:T(8,128)(2,1)} %bitcast.161, bf16[2560,768]{0,1:T(8,128)(2,1)S(1)} %get-tuple-element.125, bf16[2560,768]{0,1:T(8,128)(2,1)S(1)} %get-tuple-element.124), kind=kOutput, calls=%fused_computation.5 | convolution fusion | flops 18138660864 | bytes 26738688 | tf_op jit(solution)/shard_map/dot_general | solution.py:1312
  607.1 24.3 %convolution_convert_fusion = bf16[2560,2304]{1,0:T(8,128)(2,1)} fusion(bf16[2304,768]{1,0:T(8,128)(2,1)} %bitcast.14, bf16[2304,768]{1,0:T(8,128)(2,1)} %bitcast.200, bf16[2560,768]{0,1:T(8,128)(2,1)S(1)} %get-tuple-element.125, bf16[2560,768]{0,1:T(8,128)(2,1)S(1)} %get-tuple-element.124), kind=kOutput, calls=%fused_computation.3 | convolution fusion | flops 18155175936 | bytes 26738688 | tf_op jit(solution)/shard_map/dot_general | solution.py:1312
  632.1 113.8 %collect_rows.1 = (f32[128,2304]{1,0:T(8,128)}, f32[8,128]{1,0:T(8,128)}) custom-call(bf16[4,2,4,80,2304]{4,3,2,1,0:T(8,128)(2,1)} %bitcast.199, f32[4,2,4,8,128]{4,3,2,1,0:T(8,128)} %get-tuple-element.37.notes_ref, f32[4,2,4,8,128]{4,3,2,1,0:T(8,128)} %select_maximum_fusion.dots_ref), custom_call_target="tpu_custom_call" | custom-call | flops 49999998976 | bytes 11796480 | tf_op jit(solution)/shard_map/collect_rows/pallas_call | solution.py:1098
  752.0 12.9 %fusion = bf16[2560,2304]{1,0:T(8,128)(2,1)} fusion(f32[32,80,2304]{2,1,0:T(8,128)} %fusion.40, f32[2560]{0:T(1024)S(1)} %mul.498), kind=kLoop, calls=%fused_computation.2 | loop fusion | flops 11796480 | bytes 35399680 | tf_op jit(solution)/shard_map/convert_element_type | solution.py:1469
  765.0 5.6 all-to-all-start.2
  777.8 12.2 %fusion.8.x_ref = f32[720,2304]{1,0:T(8,128)} fusion(bf16[2560,2304]{1,0:T(8,128)(2,1)S(1)} %copy-done.5, bf16[2560,768]{0,1:T(8,128)(2,1)} %get-tuple-element.119), kind=kOutput, calls=%fused_computation.27 | convolution fusion | flops 8493465600 | bytes 22118400 | tf_op jit(solution)/shard_map/dot_general | solution.py:1312
  789.9 9.2 lined_up.1
  822.2 11.6 %fusion.17 = f32[256,2304]{1,0:T(8,128)} fusion(bf16[2304,3456]{1,0:T(8,128)(2,1)} %get-tuple-element.34, bf16[256,1152]{0,1:T(8,128)(2,1)S(1)} %bitcast.181, bf16[256,1152]{0,1:T(8,128)(2,1)} %bitcast.183, bf16[256,1152]{0,1:T(8,128)(2,1)S(1)} %bitcast.182), kind=kOutput, calls=%fused_computation.54 | convolution fusion | flops 4082171904 | bytes 20054016 | tf_op jit(solution)/shard_map/dot_general | solution.py:1312
  851.0 227.1 %reduce_attention.1 = (bf16[2,144,2304]{2,1,0:T(8,128)(2,1)}, bf16[2,144,2304]{2,1,0:T(8,128)(2,1)}, bf16[2,144,2304]{2,1,0:T(8,128)(2,1)}, bf16[2,144,2304]{2,1,0:T(8,128)(2,1)}, bf16[2,2,144,128]{3,2,1,0:T(8,128)(2,1)}) custom-call(bf16[4,4,144,1152]{3,2,1,0:T(8,128)(2,1)} %bitcast.154, bf16[4,4,144,1152]{3,2,1,0:T(8,128)(2,1)} %bitcast.153, ...), custom_call_target="tpu_custom_call" | custom-call | flops 1000000 | bytes 1000000 | tf_op jit(solution)/shard_map/reduce_attention/pallas_call | solution.py:596
  1097.0 14.5 %unpack_columns.1 = f32[25920,128]{1,0:T(8,128)} custom-call(bf16[8,288,1536]{2,1,0:T(8,128)(2,1)} %all-to-all-done.2.x_ref), custom_call_target="tpu_custom_call" | custom-call | tf_op jit(solution)/shard_map/unpack_columns/pallas_call | solution.py:1184
  (296 shorter events, 111.9 us)
Async XLA Ops:
  20.6 503.9 %all-to-all-start = ((bf16[8,288,768]{2,1,0:T(8,128)(2,1)}), bf16[8,288,768]{2,1,0:T(8,128)(2,1)}, u32[]{:S(2)}, u32[]{:S(2)}) async-start(bf16[8,288,768]{2,1,0:T(8,128)(2,1)} %get-tuple-element.40), calls=%async_computation | async-start | bytes 7077888 | tf_op jit(solution)/shard_map/all_to_all | solution.py:1356
  25.9 1061.5 %reduce-scatter.2.cloned.1.call-start = ((), (), s32[]{:S(2)}) async-start(), calls=%async_computation.4 | async-start | bytes 13271040 | tf_op jit(solution)/shard_map/reduce_scatter | solution.py:1436
  342.2 33.3 %copy-start.44 = (f32[2304]{0:T(1024)}, f32[2304]{0:T(1024)S(1)}, u32[]{:S(2)}) copy-start(f32[2304]{0:T(1024)S(1)} %get-tuple-element.111) | copy-start | bytes 27652
  365.0 5.1 collective-permute-start
  375.0 2.1 collective-permute-start.1
  379.2 91.9 %copy-start.54 = (f32[128,2]{0,1:T(2,128)}, f32[128,2]{0,1:T(2,128)S(1)}, u32[]{:S(2)}) copy-start(f32[128,2]{0,1:T(2,128)S(1)} %select_reduce_fusion.1) | copy-start | bytes 3076
  379.2 91.8 %copy-start.58 = (f32[128]{0:T(128)}, f32[128]{0:T(128)S(1)}, u32[]{:S(2)}) copy-start(f32[128]{0:T(128)S(1)} %reduce_max.19) | copy-start | bytes 1540
  379.2 91.8 %copy-start.60 = (f32[128]{0:T(128)}, f32[128]{0:T(128)S(1)}, u32[]{:S(2)}) copy-start(f32[128]{0:T(128)S(1)} %fusion.67) | copy-start | bytes 1540
  524.5 15.6 %copy-start.79 = (bf16[720,1,2304]{2,0,1:T(8,128)(2,1)S(1)}, bf16[720,1,2304]{2,0,1:T(8,128)(2,1)}, u32[]{:S(2)}) copy-start(bf16[720,1,2304]{2,0,1:T(8,128)(2,1)} %param.24) | copy-start | bytes 9953284
  632.1 113.9 %copy-start.55 = (f32[128,2]{0,1:T(2,128)S(1)}, f32[128,2]{0,1:T(2,128)}, u32[]{:S(2)}) copy-start(f32[128,2]{0,1:T(2,128)} %copy-done.54) | copy-start | bytes 3076
  632.1 113.9 %copy-start.59 = (f32[128]{0:T(128)S(1)}, f32[128]{0:T(128)}, u32[]{:S(2)}) copy-start(f32[128]{0:T(128)} %copy-done.58) | copy-start | bytes 1540
  632.1 113.9 %copy-start.61 = (f32[128]{0:T(128)S(1)}, f32[128]{0:T(128)}, u32[]{:S(2)}) copy-start(f32[128]{0:T(128)} %copy-done.60) | copy-start | bytes 1540
  632.1 115.4 %copy-start.57 = (s32[128,2]{0,1:T(2,128)S(1)}, s32[128,2]{0,1:T(2,128)}, u32[]{:S(2)}) copy-start(s32[128,2]{0,1:T(2,128)} %param.15) | copy-start | bytes 3076
  632.1 115.4 %copy-start.1 = (f32[128,2304]{1,0:T(8,128)S(1)}, f32[128,2304]{1,0:T(8,128)}, u32[]{:S(2)}) copy-start(f32[128,2304]{1,0:T(8,128)} %copy-done) | copy-start | bytes 3538948
  632.1 115.4 %copy-start.10 = (bf16[2304,128]{1,0:T(8,128)(2,1)S(1)}, bf16[2304,128]{1,0:T(8,128)(2,1)}, u32[]{:S(2)}) copy-start(bf16[2304,128]{1,0:T(8,128)(2,1)} %get-tuple-element.33) | copy-start | bytes 1769476
  632.1 115.4 %copy-start.47 = (f32[2304]{0:T(1024)S(1)}, f32[2304]{0:T(1024)}, u32[]{:S(2)}) copy-start(f32[2304]{0:T(1024)} %get-tuple-element.110) | copy-start | bytes 27652
  632.1 115.4 %copy-start.63 = (f32[128]{0:T(128)S(1)}, f32[128]{0:T(128)}, u32[]{:S(2)}) copy-start(f32[128]{0:T(128)} %copy-done.62) | copy-start | bytes 1540
  750.4 14.6 %copy-start.72 = (f32[128]{0:T(128)}, f32[128]{0:T(128)S(1)}, u32[]{:S(2)}) copy-start(f32[128]{0:T(128)S(1)} %broadcast_multiply_fusion.3) | copy-start | bytes 1540
  752.0 18.6 %collective-permute-start.2 = (bf16[128,1152]{1,0:T(8,128)(2,1)S(1)}, bf16[128,1152]{1,0:T(8,128)(2,1)S(1)}, u32[]{:S(2)}, u32[]{:S(2)}) collective-permute-start(bf16[128,1152]{1,0:T(8,128)(2,1)S(1)} %constant_dynamic-slice_fusion.2), channel_id=1, source_target_pairs={{0,1},{1,0},{2,3},{3,2},{4,5},{5,4},{6,7},{7,6},{8,9},{9,8},{10,11... | collective-permute-start | bytes 884744 | tf_op jit(solution)/shard_map/ppermute | solution.py:1401
  765.0 322.5 %all-to-all-start.2 = ((bf16[8,288,1536]{2,1,0:T(8,128)(2,1)}), bf16[8,288,1536]{2,1,0:T(8,128)(2,1)}, u32[]{:S(2)}, u32[]{:S(2)}) async-start(bf16[8,288,1536]{2,1,0:T(8,128)(2,1)} %bitcast.165), calls=%async_computation.3 | async-start | bytes 14155776 | tf_op jit(solution)/shard_map/all_to_all | solution.py:1501
  777.6 27.9 %collective-permute-start.3 = (f32[256,1152]{1,0:T(8,128)}, f32[256,1152]{1,0:T(8,128)}, u32[]{:S(2)}, u32[]{:S(2)}) collective-permute-start(f32[256,1152]{1,0:T(8,128)} %constant_dynamic-slice_fusion.1), channel_id=1, source_target_pairs={{0,1},{1,0},{2,3},{3,2},{4,5},{5,4},{6,7},{7,6},{8,9},{9,8},{10,11... | collective-permute-start | bytes 3538952 | tf_op jit(solution)/shard_map/ppermute | solution.py:1401
  835.3 13.0 %collective-permute-start.4 = (f32[128,2304]{1,0:T(8,128)S(1)}, f32[128,2304]{1,0:T(8,128)S(1)}, u32[]{:S(2)}, u32[]{:S(2)}) collective-permute-start(f32[128,2304]{1,0:T(8,128)S(1)} %constant_dynamic-slice_fusion), channel_id=1, source_target_pairs={{0,1},{1,0},{2,3},{3,2},{4,5},{5,4},{6,7},{7,6},{8,9},{9,8},{10,11... | collective-permute-start | bytes 3538952 | tf_op jit(solution)/shard_map/ppermute | solution.py:1401
  1087.5 24.1 %all-to-all-start.1 = ((bf16[4,80,2304]{2,1,0:T(8,128)(2,1)}), bf16[4,80,2304]{2,1,0:T(8,128)(2,1)S(1)}, u32[]{:S(2)}, u32[]{:S(2)}) async-start(bf16[4,80,2304]{2,1,0:T(8,128)(2,1)} %bitcast.179), calls=%async_computation.2 | async-start | bytes 2949120 | tf_op jit(solution)/shard_map/all_to_all | solution.py:1442
  1097.0 14.5 %copy-start.70 = (f32[128]{0:T(128)S(1)}, f32[128]{0:T(128)}, u32[]{:S(2)}) copy-start(f32[128]{0:T(128)} %get-tuple-element.163) | copy-start | bytes 1540
  (66 other events, 241.1 us)
Sparse Core Ops, SparseCore 0:
  575.0 122.1 reduce-scatter.1

commit v5 on v4

v5 whole, which is shorter than its diff:
```python
import functools
import math

import jax
import jax.numpy as jnp
from jax import lax
from jax.experimental import pallas as pl
from jax.experimental.pallas import tpu as pltpu
from jax.sharding import Mesh, PartitionSpec as P

HEADS = 36

eps_norm = 1e-05
branch_scale = 1.4 / math.sqrt(40.0)
rope_base = 10000.0
masked_score = -1e30
bf16 = jnp.bfloat16
f32 = jnp.float32
SHARD = ("z", "core")
ANY = pl.BlockSpec(memory_space=pl.ANY)


def place():
    e, z, c = lax.axis_index("expert"), lax.axis_index("z"), lax.axis_index("core")
    across_x = e + 1 - 2 * (e % 2)
    across_y = (e + 2) % 4
    return e, z, c, across_x, across_y


def remote(src, dst, send, recv, e, z, c):
    return pltpu.make_async_remote_copy(
        src_ref=src,
        dst_ref=dst,
        send_sem=send,
        recv_sem=recv,
        device_id=(e, z, c),
        device_id_type=pl.DeviceIdType.MESH,
    )


def payload_stream(nz, ref, out, sems, split):
    zrecv, zsend, near_recv, near_send, far_recv, far_send, sib_recv, sib_send, own = sems
    e, z, c, ex, ey = place()
    diagonal = (ex + 2) % 4
    T = ref.shape[0]
    S = 2 * nz - 1

    def split_step(s):
        return (s - 1) % 2, (s - 1) // 2

    def where(s):
        if s == 0:
            return z
        side, i = split_step(s)
        return z - 1 - i if side == 0 else z + 1 + i

    def exists(s):
        if s == 0:
            return z >= 0
        zz = where(s)
        return (zz >= 0) & (zz < nz)

    def slab(s, quarter, r0=0, n=T):
        return out.at[where(s), c, quarter, pl.ds(r0, n), :]

    def first(step):
        side = 0 if step > 0 else 1
        return remote(ref, slab(0, e), zsend.at[side, nz - 1], zrecv.at[side, 0], e, z + step, c)

    def onward(s):
        side, i = split_step(s)
        step = 1 if side == 0 else -1
        return remote(
            slab(s, e), slab(s, e), zsend.at[side, i], zrecv.at[side, i + 1], e, z + step, c
        )

    def near(s, axis):
        source = ref if s == 0 else slab(s, e)
        return remote(
            source, slab(s, e), near_send.at[s, axis], near_recv.at[s, axis],
            ex if axis == 0 else ey, z, c,
        )

    def near_wait(s, axis):
        view = slab(s, ex if axis == 0 else ey)
        remote(view, view, near_send.at[s, axis], near_recv.at[s, axis], ex, z, c).wait_recv()

    axes = range(2) if split else range(1)

    def far_view(s, quarter, axis):
        if not split:
            return slab(s, quarter)
        return slab(s, quarter, 0, split) if axis == 0 else slab(s, quarter, split, T - split)

    def far(s, axis):
        view = far_view(s, ex if axis == 0 else ey, axis)
        return remote(
            view, view, far_send.at[s, axis], far_recv.at[s, axis],
            ey if axis == 0 else ex, z, c,
        )

    def far_wait(s, axis):
        view = far_view(s, diagonal, axis)
        remote(view, view, far_send.at[s, axis], far_recv.at[s, axis], ex, z, c).wait_recv()

    def beside(s, n):
        quarter = (e, ex, ey, diagonal)[n]
        source = ref if s == 0 and n == 0 else slab(s, quarter)
        return remote(
            source, slab(s, quarter), sib_send.at[s, n], sib_recv.at[s, n], e, z, 1 - c
        )

    def beside_wait(s, n):
        view = out.at[where(s), 1 - c, (e, ex, ey, diagonal)[n]]
        remote(view, view, sib_send.at[s, n], sib_recv.at[s, n], e, z, c).wait_recv()

    def inside(side):
        return z < nz - 1 if side == 0 else z > 0

    def begin():
        for step in (1, -1):

            @pl.when((z + step >= 0) & (z + step < nz))
            def _():
                first(step).start()

        near(0, 0).start()
        near(0, 1).start()
        beside(0, 0).start()
        pltpu.make_async_copy(ref, slab(0, e), own).start()

    def arrive(s):
        if s == 0:
            return

        @pl.when(exists(s))
        def _():
            side, i = split_step(s)
            remote(
                slab(s, e), slab(s, e), zsend.at[side, i], zrecv.at[side, i], e, z, c
            ).wait_recv()
            if i < nz - 2:

                @pl.when(inside(side))
                def _():
                    onward(s).start()

            near(s, 0).start()
            near(s, 1).start()
            beside(s, 0).start()

    def relay(s):
        @pl.when(exists(s))
        def _():
            near_wait(s, 0)
            far(s, 0).start()
            beside(s, 1).start()
            near_wait(s, 1)
            if split:
                far(s, 1).start()
            beside(s, 2).start()

    def close(s):
        @pl.when(exists(s))
        def _():
            for axis in axes:
                far_wait(s, axis)
            beside(s, 3).start()

    def end(s):
        @pl.when(exists(s))
        def _():
            for axis in range(2):
                near(s, axis).wait_send()
            for axis in axes:
                far(s, axis).wait_send()
            for n in range(4):
                beside(s, n).wait_send()
                beside_wait(s, n)
            if s > 0 and split_step(s)[1] < nz - 2:

                @pl.when(inside(split_step(s)[0]))
                def _():
                    onward(s).wait_send()

        if s == 0:
            for step in (1, -1):

                @pl.when((z + step >= 0) & (z + step < nz))
                def _():
                    first(step).wait_send()

            pltpu.make_async_copy(ref, slab(0, e), own).wait()

    return begin, arrive, relay, close, end


def payload_sems(nz):
    dma = pltpu.SemaphoreType.DMA
    S = 2 * nz - 1
    return [
        dma((2, nz)), dma((2, nz)), dma((S, 2)), dma((S, 2)), dma((S, 2)), dma((S, 2)),
        dma((S, 4)), dma((S, 4)), dma(()),
    ]


def spread_kernel(nz, splits, *refs):
    n = len(splits)
    ins, outs, sems = refs[:n], refs[n : 2 * n], refs[2 * n :]
    greet_cross(nz)
    streams = [
        payload_stream(nz, ins[i], outs[i], sems[9 * i : 9 * i + 9], splits[i]) for i in range(n)
    ]
    for t in streams:
        t[0]()
    S = 2 * nz - 1
    for s in range(S):
        for t in streams:
            t[1](s)
        if s >= 1:
            for t in streams:
                t[2](s - 1)
        if s >= 2:
            for t in streams:
                t[3](s - 2)
    for t in streams:
        t[2](S - 1)
    for s in (S - 2, S - 1):
        for t in streams:
            t[3](s)
    for s in range(S):
        for t in streams:
            t[4](s)


def spread_blocks(nz, blocks, collective):
    sd = jax.ShapeDtypeStruct
    splits = tuple(b.shape[0] // 2 if b.shape[0] % 32 == 0 else 0 for b in blocks)
    return pl.pallas_call(
        functools.partial(spread_kernel, nz, splits),
        out_shape=tuple(sd((nz, 2, 4) + b.shape, b.dtype) for b in blocks),
        in_specs=[ANY] * len(blocks),
        out_specs=(ANY,) * len(blocks),
        scratch_shapes=[s for _ in blocks for s in payload_sems(nz)],
        compiler_params=pltpu.CompilerParams(collective_id=collective, has_side_effects=True),
        cost_estimate=pl.CostEstimate(
            flops=10**6, bytes_accessed=10**6, transcendentals=0
        ),
        name="spread_blocks",
    )(*blocks)


def line_order(nz, z):
    def order(i):
        code = 0
        for zz in range(nz):
            far_first = sorted(range(nz), key=lambda t: (-abs(t - zz), t))
            code += far_first[i] * nz**zz
        power = 1
        for zz in range(nz):
            power = power + (nz**zz - 1) * jnp.where(z == zz, 1, 0)
        return (code // power) % nz

    return [order(i) for i in range(nz)]


def collect_kernel(
    nz, cap,
    rows_ref, notes_ref, dots_ref,
    out_ref, dots_out,
    dots, notes, mine, theirs, block, from_x, from_y, via_x, via_y, from_z,
    note_sem, load, sib_send, sib_recv, via_send, via_recv, plain_send, plain_recv,
    sum_send, sum_recv, zsend, zrecv, dot_send, dot_recv, dot_own,
):
    e, z, c, ex, ey = place()
    diagonal = (ex + 2) % 4
    T, D = out_ref.shape
    h = T // 2
    dest = line_order(nz, z)
    who = (diagonal, ex, ey, e)

    def others():
        for d in range(1, 8 * nz):
            to = ((e * nz + z) * 2 + c + d) % (8 * nz)
            yield d, to // (2 * nz), to // 2 % nz, to % 2

    barrier = pltpu.get_barrier_semaphore()
    for _, te, tz, tc in others():
        pl.semaphore_signal(
            barrier, inc=1, device_id=(te, tz, tc), device_id_type=pl.DeviceIdType.MESH
        )
    pl.semaphore_wait(barrier, 8 * nz - 1)

    def dot(d, te, tz, tc):
        return remote(
            dots_ref.at[tz, tc, te], dots.at[d], dot_send.at[d], dot_recv.at[d], te, tz, tc
        )

    dot_kept = pltpu.make_async_copy(dots_ref.at[z, c, e], dots.at[0], dot_own)
    dot_kept.start()
    for d, te, tz, tc in others():
        dot(d, te, tz, tc).start()

    note_copy = pltpu.make_async_copy(notes_ref, notes, note_sem)
    note_copy.start()

    def fetch(i, q):
        return pltpu.make_async_copy(
            rows_ref.at[dest[i], c, who[q]], mine.at[i, q], load.at[i, q]
        )

    def hand(i, q):
        return remote(
            rows_ref.at[dest[i], 1 - c, who[q]], theirs.at[i, q],
            sib_send.at[i, q], sib_recv.at[i, q], e, z, 1 - c,
        )

    for i in range(nz):
        for q in range(4):
            hand(i, q).start()
            fetch(i, q).start()
    note_copy.wait()

    def open_out(i, q):
        fetch(i, q).wait()
        hand(i, q).wait_recv()
        places = (lax.broadcasted_iota(jnp.int32, (cap, T), 0) + e * cap).astype(f32)
        note = notes[dest[i], c, who[q]]
        pick = ((note[2:3, :] == places) | (note[3:4, :] == places)).astype(bf16)
        wide = 768 if D % 768 == 0 else 128

        @pl.loop(0, D // wide)
        def _(b):
            cols = pl.ds(pl.multiple_of(b * wide, 128), wide)
            both = mine[i, q, :, cols].astype(f32) + theirs[i, q, :, cols].astype(f32)
            block[i, q, :, cols] = lax.dot_general(
                pick, both.astype(bf16), (((0,), (0,)), ((), ())), preferred_element_type=f32
            ).astype(bf16)

    def via(i, axis):
        if axis == 0:
            return remote(
                block.at[i, 0, pl.ds(0, h), :], via_x.at[i],
                via_send.at[i, 0], via_recv.at[i, 0], ex, z, c,
            )
        return remote(
            block.at[i, 0, pl.ds(h, h), :], via_y.at[i],
            via_send.at[i, 1], via_recv.at[i, 1], ey, z, c,
        )

    def plain(i, axis):
        if axis == 0:
            return remote(
                block.at[i, 1, pl.ds(0, h), :], from_x.at[i, pl.ds(0, h), :],
                plain_send.at[i, 0], plain_recv.at[i, 0], ex, z, c,
            )
        return remote(
            block.at[i, 2, pl.ds(h, h), :], from_y.at[i, pl.ds(h, h), :],
            plain_send.at[i, 1], plain_recv.at[i, 1], ey, z, c,
        )

    def summed(i, axis):
        if axis == 0:
            return remote(
                block.at[i, 1, pl.ds(h, h), :], from_x.at[i, pl.ds(h, h), :],
                sum_send.at[i, 0], sum_recv.at[i, 0], ex, z, c,
            )
        return remote(
            block.at[i, 2, pl.ds(0, h), :], from_y.at[i, pl.ds(0, h), :],
            sum_send.at[i, 1], sum_recv.at[i, 1], ey, z, c,
        )

    def add(target, others, n):
        @pl.loop(0, n // 16)
        def _(b):
            rows = pl.ds(pl.multiple_of(b * 16, 16), 16)
            acc = target[rows, :].astype(f32)
            for o in others:
                acc = acc + o[rows, :].astype(f32)
            target[rows, :] = acc.astype(target.dtype)

    def start(i):
        open_out(i, 0)
        via(i, 0).start()
        via(i, 1).start()
        open_out(i, 1)
        plain(i, 0).start()
        open_out(i, 2)
        plain(i, 1).start()
        open_out(i, 3)

    def combine(i):
        via(i, 0).wait_recv()
        add(block.at[i, 2, pl.ds(0, h), :], [via_x.at[i]], h)
        summed(i, 1).start()
        via(i, 1).wait_recv()
        add(block.at[i, 1, pl.ds(h, h), :], [via_y.at[i]], h)
        summed(i, 0).start()

    def zcopy(i):
        step = jnp.where(dest[i] > z, 1, -1)
        side = jnp.where(dest[i] > z, 0, 1)
        return remote(
            block.at[i, 3], from_z.at[side, dest[i]],
            zsend.at[i], zrecv.at[side, dest[i]], e, z + step, c,
        )

    def zwait(side, zz):
        slab = from_z.at[side, zz]
        remote(slab, slab, zsend.at[0], zrecv.at[side, zz], e, z, c).wait_recv()

    def finish(i):
        for axis in range(2):
            plain(i, axis).wait_recv()
            summed(i, axis).wait_recv()
        zz = dest[i]
        if i < nz - 1:
            add(block.at[i, 3], [from_x.at[i], from_y.at[i]], T)
            for side in range(2):
                going = zz > z if side == 0 else zz < z
                behind = z > 0 if side == 0 else z < nz - 1

                @pl.when(going & behind)
                def _():
                    zwait(side, zz)
                    add(block.at[i, 3], [from_z.at[side, zz]], T)

            zcopy(i).start()
            return

        @pl.loop(0, T // 16)
        def _(b):
            rows = pl.ds(pl.multiple_of(b * 16, 16), 16)
            acc = block[i, 3, rows, :].astype(f32) + from_x[i, rows, :].astype(f32)
            out_ref[rows, :] = acc + from_y[i, rows, :].astype(f32)

        for side in range(2):

            @pl.when(z > 0 if side == 0 else z < nz - 1)
            def _():
                zwait(side, z)
                add(out_ref, [from_z.at[side, z]], T)

    for i in range(nz):
        start(i)
        if i >= 1:
            combine(i - 1)
        if i >= 2:
            finish(i - 2)
    combine(nz - 1)
    if nz >= 2:
        finish(nz - 2)
    finish(nz - 1)

    dot_kept.wait()
    for d, te, tz, tc in others():
        dot(d, te, tz, tc).wait_recv()
        dot(d, te, tz, tc).wait_send()
    dots_out[...] = jnp.sum(dots[...], axis=0)

    for i in range(nz):
        for q in range(4):
            hand(i, q).wait_send()
        for axis in range(2):
            via(i, axis).wait_send()
            plain(i, axis).wait_send()
            summed(i, axis).wait_send()
        if i < nz - 1:
            zcopy(i).wait_send()


def collect_rows(nz, rows, notes, dots, T):
    cap, D = rows.shape[3:]
    dma = pltpu.SemaphoreType.DMA
    vm = pltpu.VMEM
    return pl.pallas_call(
        functools.partial(collect_kernel, nz, cap),
        out_shape=(
            jax.ShapeDtypeStruct((T, D), f32),
            jax.ShapeDtypeStruct(dots.shape[3:], f32),
        ),
        in_specs=[ANY] * 3,
        out_specs=(pl.BlockSpec(memory_space=pltpu.VMEM),) * 2,
        scratch_shapes=[
            vm((8 * nz,) + dots.shape[3:], f32),
            vm(notes.shape, f32),
            vm((nz, 4, cap, D), bf16),
            vm((nz, 4, cap, D), bf16),
            vm((nz, 4, T, D), bf16),
            vm((nz, T, D), bf16),
            vm((nz, T, D), bf16),
            vm((nz, T // 2, D), bf16),
            vm((nz, T // 2, D), bf16),
            vm((2, nz, T, D), bf16),
            dma(()),
            dma((nz, 4)),
            dma((nz, 4)),
            dma((nz, 4)),
            dma((nz, 2)),
            dma((nz, 2)),
            dma((nz, 2)),
            dma((nz, 2)),
            dma((nz, 2)),
            dma((nz, 2)),
            dma((nz,)),
            dma((2, nz)),
            dma((8 * nz,)),
            dma((8 * nz,)),
            dma(()),
        ],
        compiler_params=pltpu.CompilerParams(
            collective_id=3, has_side_effects=True, vmem_limit_bytes=56 << 20
        ),
        cost_estimate=pl.CostEstimate(
            flops=5 * 10**10, bytes_accessed=2 * rows.size, transcendentals=0
        ),
        name="collect_rows",
    )(rows, notes, dots)


def pack_kernel(n, F, Fp, x_ref, o_ref):
    half = n * F
    rows = x_ref.shape[0]
    for i in range(n):
        for part in range(2):
            cols = x_ref[:, part * half + i * F : part * half + (i + 1) * F]
            if Fp > F:
                cols = jnp.concatenate([cols, jnp.zeros((rows, Fp - F), cols.dtype)], axis=1)
            o_ref[i, :, part * Fp : (part + 1) * Fp] = cols


def pack_columns(w, n, F, Fp):
    rows = w.shape[0]
    block = 16
    return pl.pallas_call(
        functools.partial(pack_kernel, n, F, Fp),
        grid=(rows // block,),
        in_specs=[pl.BlockSpec((block, w.shape[1]), lambda i: (i, 0))],
        out_specs=pl.BlockSpec((n, block, 2 * Fp), lambda i: (0, i, 0)),
        out_shape=jax.ShapeDtypeStruct((n, rows, 2 * Fp), w.dtype),
        name="pack_columns",
    )(w)


def unpack_kernel(n, F, Fp, x_ref, o_ref, line):
    half = n * F
    rows = line.shape[0]
    for i in range(n):
        for part in range(2):
            cols = x_ref[i, :, part * Fp : part * Fp + F].astype(f32)
            line[:, part * half + i * F : part * half + (i + 1) * F] = cols
    tiles = 2 * half // 128
    for j in range(tiles):
        o_ref[pl.ds(j, rows, stride=tiles), :] = line[:, j * 128 : (j + 1) * 128]


def unpack_columns(x, F):
    n, rows, Fp2 = x.shape
    block = 16
    width = 2 * n * F
    tiles = width // 128
    flat = pl.pallas_call(
        functools.partial(unpack_kernel, n, F, Fp2 // 2),
        grid=(rows // block,),
        in_specs=[pl.BlockSpec((n, block, Fp2), lambda i: (0, i, 0))],
        out_specs=pl.BlockSpec((block * tiles, 128), lambda i: (i, 0)),
        out_shape=jax.ShapeDtypeStruct((rows * tiles, 128), f32),
        scratch_shapes=[pltpu.VMEM((block, width), f32)],
        name="unpack_columns",
    )(x)
    return flat.reshape(rows, 1, width)


def line_kernel(x_ref, o_ref):
    rows, width = x_ref.shape
    tiles = width // 128
    for j in range(tiles):
        o_ref[pl.ds(j, rows, stride=tiles), :] = x_ref[:, j * 128 : (j + 1) * 128]


def lined_up(x):
    rows, width = x.shape
    tiles = width // 128
    block = 80 if rows % 80 == 0 else 8
    flat = pl.pallas_call(
        line_kernel,
        grid=(rows // block,),
        in_specs=[pl.BlockSpec((block, width), lambda i: (i, 0))],
        out_specs=pl.BlockSpec((block * tiles, 128), lambda i: (i, 0)),
        out_shape=jax.ShapeDtypeStruct((rows * tiles, 128), x.dtype),
        name="lined_up",
    )(x)
    return flat.reshape(rows, 1, width)


def greet_cross(nz):
    e, z, c, ex, ey = place()
    barrier = pltpu.get_barrier_semaphore()

    def hail(te, tz, tc):
        pl.semaphore_signal(
            barrier, inc=1, device_id=(te, tz, tc), device_id_type=pl.DeviceIdType.MESH
        )

    hail(e, z, 1 - c)
    for te in (ex, ey, (ex + 2) % 4):
        hail(te, z, c)
    for step in (-1, 1):

        @pl.when((z + step >= 0) & (z + step < nz))
        def _():
            hail(e, z + step, c)

    pl.semaphore_wait(barrier, 4 + jnp.where(z > 0, 1, 0) + jnp.where(z < nz - 1, 1, 0))


def line_stream(nz, ref, out, zrecv, zsend, sib_recv, sib_send, own):
    e, z, c, _, _ = place()

    def split_step(s):
        return (s - 1) % 2, (s - 1) // 2

    def where(s):
        if s == 0:
            return z
        side, i = split_step(s)
        return z - 1 - i if side == 0 else z + 1 + i

    def exists(s):
        return (where(s) >= 0) & (where(s) < nz)

    def inside(side):
        return z < nz - 1 if side == 0 else z > 0

    def slab(s):
        return out.at[where(s), c]

    def first(side):
        step = 1 if side == 0 else -1
        return remote(ref, slab(0), zsend.at[side, nz - 1], zrecv.at[side, 0], e, z + step, c)

    def onward(s):
        side, i = split_step(s)
        step = 1 if side == 0 else -1
        return remote(
            slab(s), slab(s), zsend.at[side, i], zrecv.at[side, i + 1], e, z + step, c
        )

    def beside(s):
        return remote(
            ref if s == 0 else slab(s), slab(s), sib_send.at[s], sib_recv.at[s], e, z, 1 - c
        )

    def begin():
        for side in range(2):

            @pl.when(inside(side))
            def _():
                first(side).start()

        beside(0).start()
        pltpu.make_async_copy(ref, slab(0), own).start()

    def arrive(s):
        side, i = split_step(s)

        @pl.when(exists(s))
        def _():
            remote(slab(s), slab(s), zsend.at[side, i], zrecv.at[side, i], e, z, c).wait_recv()
            if i < nz - 2:

                @pl.when(inside(side))
                def _():
                    onward(s).start()

            beside(s).start()

    def end():
        for s in range(2 * nz - 1):

            @pl.when(exists(s))
            def _():
                beside(s).wait_send()
                view = out.at[where(s), 1 - c]
                remote(view, view, sib_send.at[s], sib_recv.at[s], e, z, c).wait_recv()
                if s > 0 and split_step(s)[1] < nz - 2:

                    @pl.when(inside(split_step(s)[0]))
                    def _():
                        onward(s).wait_send()

        for side in range(2):

            @pl.when(inside(side))
            def _():
                first(side).wait_send()

        pltpu.make_async_copy(ref, slab(0), own).wait()

    return begin, arrive, end


def line_sems(nz):
    dma = pltpu.SemaphoreType.DMA
    S = 2 * nz - 1
    return [dma((2, nz)), dma((2, nz)), dma((S,)), dma((S,)), dma(())]


def plane_stream(source, views, send, recv, own):
    e, z, c, ex, ey = place()
    peers = (ex, ey, (ex + 2) % 4)

    def copy(n):
        return remote(source, views(e), send.at[n], recv.at[n], peers[n], z, c)

    def kept():
        return pltpu.make_async_copy(source, views(e), own)

    def begin():
        for n in range(3):
            copy(n).start()
        kept().start()

    def end():
        kept().wait()
        for n in range(3):
            view = views(peers[n])
            remote(view, view, send.at[n], recv.at[n], e, z, c).wait_recv()
            copy(n).wait_send()

    return begin, end


def plane_sems():
    dma = pltpu.SemaphoreType.DMA
    return [dma((3,)), dma((3,)), dma(())]


def fetch_kernel(
    nz,
    w_ref, s_ref, o_ref, t_ref, l_ref, p_ref,
    w_out, s_out, o_out, t_out, l_out, p_out,
    *sems,
):
    e, z, c, ex, ey = place()
    w_sems, sems = sems[:5], sems[5:]
    s_sems, sems = sems[:5], sems[5:]
    t_sems, sems = sems[:3], sems[3:]
    l_sems, sems = sems[:3], sems[3:]
    p_sems, sems = sems[:9], sems[9:]
    orecv, osend, sib_recv, sib_send, own = sems
    greet_cross(nz)
    w_begin, w_arrive, w_end = line_stream(nz, w_ref, w_out, *w_sems)
    s_begin, s_arrive, s_end = line_stream(nz, s_ref, s_out, *s_sems)
    t_begin, t_end = plane_stream(t_ref, lambda q: t_out.at[q], *t_sems)
    l_begin, l_end = plane_stream(l_ref, lambda q: l_out.at[q], *l_sems)
    p_begin, p_arrive, p_relay, p_close, p_end = payload_stream(
        nz, p_ref, p_out, p_sems, p_ref.shape[0] // 2
    )

    def o_copy(side, source):
        step = 1 if side == 0 else -1
        return remote(source, o_out.at[c], osend.at[side], orecv, e, z + step, c)

    def o_beside(source):
        return remote(source, o_out.at[c], sib_send, sib_recv, e, z, 1 - c)

    def o_goes(side):
        return (z >= e) & (z < nz - 1) if side == 0 else (z <= e) & (z > 0)

    w_begin()
    s_begin()

    @pl.when(z == e)
    def _():
        for side in range(2):

            @pl.when(o_goes(side))
            def _():
                o_copy(side, o_ref).start()

        o_beside(o_ref).start()
        pltpu.make_async_copy(o_ref, o_out.at[c], own).start()

    t_begin()
    l_begin()
    p_begin()

    def o_arrive():
        @pl.when(z != e)
        def _():
            remote(o_out.at[c], o_out.at[c], sib_send, orecv, e, z, c).wait_recv()
            for side in range(2):

                @pl.when(o_goes(side))
                def _():
                    o_copy(side, o_out.at[c]).start()

            o_beside(o_out.at[c]).start()

    blocks = 2 * nz - 1
    for s in range(1, blocks):
        w_arrive(s)
        s_arrive(s)
        p_arrive(s)
        p_relay(s - 1)
        if s >= 2:
            p_close(s - 2)
        if s == 4:
            o_arrive()
    p_relay(blocks - 1)
    p_close(blocks - 2)
    p_close(blocks - 1)
    for s in range(blocks):
        p_end(s)
    w_end()
    s_end()
    t_end()
    l_end()
    view = o_out.at[1 - c]
    remote(view, view, sib_send, sib_recv, e, z, c).wait_recv()
    o_beside(o_out.at[c]).wait_send()
    for side in range(2):

        @pl.when(o_goes(side))
        def _():
            o_copy(side, o_out.at[c]).wait_send()

    @pl.when(z == e)
    def _():
        pltpu.make_async_copy(o_ref, o_out.at[c], own).wait()


def fetch_weights(nz, columns, small, rows, tokens, lengths, block):
    dma = pltpu.SemaphoreType.DMA
    sd = jax.ShapeDtypeStruct
    return pl.pallas_call(
        functools.partial(fetch_kernel, nz),
        out_shape=(
            sd((nz, 2) + columns.shape, bf16),
            sd((nz, 2) + small.shape, bf16),
            sd((2,) + rows.shape, bf16),
            sd((4,) + tokens.shape, bf16),
            sd((4,) + lengths.shape, lengths.dtype),
            sd((nz, 2, 4) + block.shape, block.dtype),
        ),
        in_specs=[ANY] * 6,
        out_specs=(ANY,) * 6,
        scratch_shapes=[
            *line_sems(nz), *line_sems(nz), *plane_sems(), *plane_sems(), *payload_sems(nz),
            dma(()), dma((2,)), dma(()), dma(()), dma(()),
        ],
        compiler_params=pltpu.CompilerParams(collective_id=0, has_side_effects=True),
        cost_estimate=pl.CostEstimate(
            flops=10**11, bytes_accessed=8 * columns.size, transcendentals=0
        ),
        name="fetch_weights",
    )(columns, small, rows, tokens, lengths, block)


def plane_gather_kernel(x_ref, out_ref, send, recv, own):
    e, z, c, ex, ey = place()
    greet_plane()
    begin, end = plane_stream(x_ref, lambda q: out_ref.at[q], send, recv, own)
    begin()
    end()


def greet_plane():
    e, z, c, ex, ey = place()
    barrier = pltpu.get_barrier_semaphore()
    for te in (ex, ey, (ex + 2) % 4):
        pl.semaphore_signal(
            barrier, inc=1, device_id=(te, z, c), device_id_type=pl.DeviceIdType.MESH
        )
    pl.semaphore_wait(barrier, 3)


def plane_gather(x, collective):
    return pl.pallas_call(
        plane_gather_kernel,
        out_shape=jax.ShapeDtypeStruct((4,) + x.shape, x.dtype),
        in_specs=[ANY],
        out_specs=ANY,
        scratch_shapes=plane_sems(),
        compiler_params=pltpu.CompilerParams(collective_id=collective, has_side_effects=True),
        cost_estimate=pl.CostEstimate(flops=10**6, bytes_accessed=10**6, transcendentals=0),
        name="plane_gather",
    )(x)


def plane_sum_kernel(x_ref, out_ref, held, send, recv, own):
    e, z, c, ex, ey = place()
    peers = (ex, ey, (ex + 2) % 4)
    greet_plane()

    def copy(n):
        return remote(x_ref.at[peers[n]], held.at[n], send.at[n], recv.at[n], peers[n], z, c)

    for n in (2, 0, 1):
        copy(n).start()
    kept = pltpu.make_async_copy(x_ref.at[e], held.at[3], own)
    kept.start()
    kept.wait()
    for n in range(3):
        copy(n).wait_recv()

    @pl.loop(0, out_ref.shape[0] // 16)
    def _(b):
        rows = pl.ds(pl.multiple_of(b * 16, 16), 16)
        acc = held[3, rows, :].astype(f32) + held[0, rows, :].astype(f32)
        acc = acc + held[1, rows, :].astype(f32)
        out_ref[rows, :] = acc + held[2, rows, :].astype(f32)

    for n in range(3):
        copy(n).wait_send()


def plane_sum(x, collective):
    vm = pltpu.VMEM
    return pl.pallas_call(
        plane_sum_kernel,
        out_shape=jax.ShapeDtypeStruct(x.shape[1:], f32),
        in_specs=[ANY],
        out_specs=pl.BlockSpec(memory_space=vm),
        scratch_shapes=[vm(x.shape, bf16), *plane_sems()],
        compiler_params=pltpu.CompilerParams(collective_id=collective, has_side_effects=True),
        cost_estimate=pl.CostEstimate(flops=10**6, bytes_accessed=10**6, transcendentals=0),
        name="plane_sum",
    )(x)


def settle_kernel(
    nz,
    g_ref, s_ref, o_ref,
    g_out, s_out, o_out,
    g_mine, g_sib, g_z, s_mine, s_sib, s_z, o_mine, o_sib, o_z,
    load, sib_send, sib_recv, zsend, zrecv,
    o_load, o_sib_send, o_sib_recv, o_zsend, o_zrecv,
    o_send, o_recv, o_own,
    *sems,
):
    e, z, c, ex, ey = place()
    peers = (ex, ey, (ex + 2) % 4)
    dest = line_order(nz, z)
    greet_cross(nz)
    groups = ((g_ref, g_mine, g_sib, g_z, g_out), (s_ref, s_mine, s_sib, s_z, s_out))

    def fetch(k, i):
        ref, mine = groups[k][0], groups[k][1]
        return pltpu.make_async_copy(ref.at[dest[i], c], mine.at[i], load.at[k, i])

    def hand(k, i):
        ref, theirs = groups[k][0], groups[k][2]
        return remote(
            ref.at[dest[i], 1 - c], theirs.at[i], sib_send.at[k, i], sib_recv.at[k, i], e, z, 1 - c
        )

    def zcopy(k, i):
        mine, from_z = groups[k][1], groups[k][3]
        step = jnp.where(dest[i] > z, 1, -1)
        side = jnp.where(dest[i] > z, 0, 1)
        return remote(
            mine.at[i], from_z.at[side, dest[i]],
            zsend.at[k, i], zrecv.at[k, side, dest[i]], e, z + step, c,
        )

    def zwait(k, side, zz):
        slab = groups[k][3].at[side, zz]
        remote(slab, slab, zsend.at[k, 0], zrecv.at[k, side, zz], e, z, c).wait_recv()

    def add(target, others):
        @pl.loop(0, target.shape[0] // 16)
        def _(b):
            rows = pl.ds(pl.multiple_of(b * 16, 16), 16)
            acc = target[rows, :].astype(f32)
            for o in others:
                acc = acc + o[rows, :].astype(f32)
            target[rows, :] = acc.astype(target.dtype)

    def o_fetch():
        return pltpu.make_async_copy(o_ref.at[c], o_mine, o_load)

    def o_hand():
        return remote(o_ref.at[1 - c], o_sib, o_sib_send, o_sib_recv, e, z, 1 - c)

    def o_line():
        step, side = jnp.where(z < e, 1, -1), jnp.where(z < e, 0, 1)
        return remote(o_mine, o_z.at[side], o_zsend, o_zrecv.at[side], e, z + step, c)

    def o_wait(side):
        slab = o_z.at[side]
        remote(slab, slab, o_zsend, o_zrecv.at[side], e, z, c).wait_recv()
        add(o_mine, [slab])

    def o_peer(n):
        return remote(o_mine, o_out, o_send.at[n], o_recv, peers[n], z, c)

    def o_kept():
        return pltpu.make_async_copy(o_mine, o_out, o_own)

    o_fetch().start()
    o_hand().start()
    for i in range(nz):
        for k in range(2):
            hand(k, i).start()
            fetch(k, i).start()

    def finish(k, i):
        mine, theirs, from_z = groups[k][1:4]
        fetch(k, i).wait()
        hand(k, i).wait_recv()
        zz = dest[i]
        add(mine.at[i], [theirs.at[i]])
        if i < nz - 1:
            for side in range(2):
                going = zz > z if side == 0 else zz < z
                behind = z > 0 if side == 0 else z < nz - 1

                @pl.when(going & behind)
                def _():
                    zwait(k, side, zz)
                    add(mine.at[i], [from_z.at[side, zz]])

            zcopy(k, i).start()
            return
        for side in range(2):

            @pl.when(z > 0 if side == 0 else z < nz - 1)
            def _():
                zwait(k, side, z)
                add(mine.at[i], [from_z.at[side, z]])

    def o_flow():
        o_fetch().wait()
        o_hand().wait_recv()
        add(o_mine, [o_sib])
        for side in range(2):
            behind = (z > 0) & (z <= e) if side == 0 else (z < nz - 1) & (z >= e)

            @pl.when(behind)
            def _():
                o_wait(side)

        @pl.when(z != e)
        def _():
            o_line().start()

        @pl.when(z == e)
        def _():
            for n in range(3):
                o_peer(n).start()
            o_kept().start()

    for i in range(nz - 1):
        for k in range(2):
            finish(k, i)
        if i == 0:
            o_flow()
    for k in range(2):
        finish(k, nz - 1)
    spread = [
        plane_stream(
            groups[k][1].at[nz - 1], lambda q, k=k: groups[k][4].at[q], *sems[3 * k : 3 * k + 3]
        )
        for k in range(2)
    ]
    for begin, _ in spread:
        begin()

    @pl.when(z == e)
    def _():
        o_kept().wait()
        for n in range(3):
            o_peer(n).wait_send()

    @pl.when(z != e)
    def _():
        remote(o_out, o_out, o_send.at[0], o_recv, e, z, c).wait_recv()
        o_line().wait_send()

    o_hand().wait_send()
    for i in range(nz):
        for k in range(2):
            hand(k, i).wait_send()
            if i < nz - 1:
                zcopy(k, i).wait_send()
    for _, end in spread:
        end()


def settle_weights(nz, grads, small, rows):
    R, W = grads.shape[2:]
    D = rows.shape[2]
    dma = pltpu.SemaphoreType.DMA
    sd = jax.ShapeDtypeStruct
    vm = pltpu.VMEM
    Ws = small.shape[3]
    return pl.pallas_call(
        functools.partial(settle_kernel, nz),
        out_shape=(sd((4, R, W), bf16), sd((4, R, Ws), bf16), sd((R, D), bf16)),
        in_specs=[ANY] * 3,
        out_specs=(ANY,) * 3,
        scratch_shapes=[
            vm((nz, R, W), bf16), vm((nz, R, W), bf16), vm((2, nz, R, W), bf16),
            vm((nz, R, Ws), bf16), vm((nz, R, Ws), bf16), vm((2, nz, R, Ws), bf16),
            vm((R, D), bf16), vm((R, D), bf16), vm((2, R, D), bf16),
            dma((2, nz)), dma((2, nz)), dma((2, nz)), dma((2, nz)), dma((2, 2, nz)),
            dma(()), dma(()), dma(()), dma(()), dma((2,)),
            dma((3,)), dma(()), dma(()),
            *plane_sems(), *plane_sems(),
        ],
        compiler_params=pltpu.CompilerParams(
            collective_id=1, has_side_effects=True, vmem_limit_bytes=56 << 20
        ),
        cost_estimate=pl.CostEstimate(flops=10**6, bytes_accessed=10**6, transcendentals=0),
        name="settle_weights",
    )(grads, small, rows)


def pick_kernel(width, q_ref, k_ref, v_ref, o_ref):
    e = lax.axis_index("expert")
    for n in range(4):

        @pl.when(e == n)
        def _():
            for i, ref in enumerate((q_ref, k_ref, v_ref)):
                o_ref[:, i * width : (i + 1) * width] = ref[:, n * width : (n + 1) * width]


def pick_columns(weights, width):
    vm = pl.BlockSpec(memory_space=pltpu.VMEM)
    return pl.pallas_call(
        functools.partial(pick_kernel, width),
        in_specs=[vm] * 3,
        out_specs=vm,
        out_shape=jax.ShapeDtypeStruct((weights[0].shape[0], 3 * width), bf16),
        name="pick_columns",
    )(*weights)


def assemble_kernel(width, x_ref, *o_refs):
    for n in range(4):
        for i in range(3):
            cols = x_ref[n, :, i * width : (i + 1) * width]
            o_refs[i][:, n * width : (n + 1) * width] = cols.astype(f32)


def assemble_columns(x, width):
    R = x.shape[1]
    block = 32
    return pl.pallas_call(
        functools.partial(assemble_kernel, width),
        grid=(R // block,),
        in_specs=[pl.BlockSpec((4, block, 3 * width), lambda i: (0, i, 0))],
        out_specs=(pl.BlockSpec((block, 4 * width), lambda i: (i, 0)),) * 3,
        out_shape=(jax.ShapeDtypeStruct((R, 4 * width), f32),) * 3,
        name="assemble_columns",
    )(x)


def sum_shard(x, axis=0):
    mine = lax.psum_scatter(x, SHARD, scatter_dimension=axis, tiled=True)
    return lax.psum(mine, "expert")


def fetch(nz, fast, weights, w_output, small, tokens, lengths, block):
    D = tokens.shape[1]
    if fast:
        width = D // 4
        columns, full_small, rows, tokens, lengths, blocks = fetch_weights(
            nz, pick_columns(weights, width), small, w_output, tokens, lengths, block
        )
        columns, rows = columns.reshape(D, 3 * width), rows.reshape(width, D)
        return columns, rows, full_small.reshape(D, -1), tokens, lengths, blocks
    full = [lax.all_gather(w, SHARD, axis=0, tiled=True) for w in weights + (w_output, small)]
    blocks = spread_plain(nz, (block,), 0)[0]
    return jnp.concatenate(full[:3], axis=1), full[3], full[4], tokens[None], lengths[None], blocks


def settle(nz, fast, columns, rows, small):
    D, width = rows.shape[1], rows.shape[0]
    if fast:
        R = D // (2 * nz)
        parts = [x.astype(bf16).reshape(nz, 2, R, -1) for x in (columns, small)]
        sums, small, out = settle_weights(nz, *parts, rows.astype(bf16).reshape(2, R, D))
        return *assemble_columns(sums, width), out.astype(f32), jnp.sum(small.astype(f32), axis=0)
    parts = [columns[:, i * width : (i + 1) * width] for i in range(3)] + [rows, small]
    return [sum_shard(x) for x in parts]


def spread_plain(nz, blocks, collective):
    out = []
    for block in blocks:
        for axis in ("expert", "core", "z"):
            block = lax.all_gather(block, axis, axis=0)
        out.append(block)
    return out


def collect_plain(nz, rows, notes, dots, T):
    n_exp, cap, D = rows.shape[2:]
    places = (lax.axis_index("expert") * cap + jnp.arange(cap)).astype(f32)
    notes = notes[..., :T]
    pick = (notes[..., 2, None, :] == places[:, None]) | (notes[..., 3, None, :] == places[:, None])
    part = jnp.einsum(
        "zceps,zcepd->zcesd", pick.astype(bf16), rows, preferred_element_type=f32
    ).astype(bf16)
    part = part.transpose(2, 0, 1, 3, 4).reshape(n_exp * nz * 2 * T, D)
    part = lax.psum_scatter(part, "expert", scatter_dimension=0, tiled=True)
    part = lax.psum_scatter(part, SHARD, scatter_dimension=0, tiled=True).astype(f32)
    z, core, e = lax.axis_index("z"), lax.axis_index("core"), lax.axis_index("expert")
    return part, lax.psum(dots, ("expert",) + SHARD)[z, core, e]


def rope_tables(positions, head_width):
    half_width = head_width // 2
    exponents = jnp.arange(half_width).astype(f32) * 2.0 / head_width
    frequency = rope_base ** (-exponents)
    angles = positions.astype(f32)[..., None] * frequency
    return (jnp.cos(angles), jnp.sin(angles))


def rotate(values, cosine, sine_table):
    half_width = values.shape[-1] // 2
    leading = values[..., :half_width]
    trailing = values[..., half_width:]
    cos_rows = cosine[:, :, None, :]
    sin_rows = sine_table[:, :, None, :]
    return jnp.concatenate(
        [leading * cos_rows - trailing * sin_rows, trailing * cos_rows + leading * sin_rows],
        axis=-1,
    )


def rms_forward(values, norm_gain):
    inverse = lax.rsqrt(jnp.mean(values * values, axis=-1, keepdims=True) + eps_norm)
    return (values * inverse * norm_gain, inverse)


def rms_backward(values, inverse, norm_gain, upstream):
    weighted = upstream * norm_gain
    gain_grad = jnp.sum(upstream * values * inverse, axis=0)
    inner_mean = jnp.mean(weighted * values, axis=-1, keepdims=True)
    return (inverse * weighted - values * inverse * inverse * inverse * inner_mean, gain_grad)


def dot32(a, b):
    return jnp.dot(a, b, preferred_element_type=f32)


def dot_dims(a, b, da, db):
    return lax.dot_general(a, b, (((da,), (db,)), ((), ())), preferred_element_type=f32)


def ein32(spec, a, b):
    return jnp.einsum(spec, a, b, preferred_element_type=f32)


def on_device(
    tokens,
    seq_lengths,
    routes,
    norm_attn,
    w_query,
    w_key,
    w_value,
    w_output,
    norm_ffn,
    w_router,
    w_in,
    w_down,
    cotangent,
):
    T, D = tokens.shape
    R = w_query.shape[0]
    head_width = D // HEADS
    n_exp = lax.axis_size("expert")
    nz = lax.axis_size("z")
    n_shard = nz * lax.axis_size("core")
    experts = w_router.shape[1]
    F = w_down.shape[0]
    FF = F * n_shard
    capacity = 10 * T // (4 * experts)
    slots = experts * capacity
    highest = lax.Precision.HIGHEST
    e_index = lax.axis_index("expert")
    fast = n_exp == 4 and nz == 4

    small = jnp.concatenate([w_router, norm_attn[:, None], norm_ffn[:, None]], axis=1)
    small = jnp.pad(small, ((0, 0), (0, 128 - small.shape[1])))
    length_rows = jnp.broadcast_to(seq_lengths[:, :1], (8, 128))
    full_qkv, full_output, full_small, near_tokens, near_lengths, all_cotangent = fetch(
        nz, fast, (w_query, w_key, w_value), w_output, small, tokens, length_rows, cotangent
    )
    full_router = full_small[:, :experts]
    gain_attn = full_small[:, experts].astype(f32)
    gain_ffn = full_small[:, experts + 1].astype(f32)

    Fp = -(-F // 128) * 128
    packed = pack_columns(w_in.reshape(R, 2 * FF), n_shard, F, Fp)
    packed, full_qkv = lax.optimization_barrier((packed, full_qkv))
    moved = lax.all_to_all(packed, SHARD, split_axis=0, concat_axis=0, tiled=True)
    w_pair = moved.reshape(n_shard * R, 2 * Fp)
    down = jnp.pad(w_down.reshape(F, D), ((0, Fp - F), (0, 0)))

    B, H = near_tokens.shape[0], full_output.shape[0]
    heads = H // head_width
    residual_in = tokens.astype(f32)
    inverse_in = rms_forward(residual_in, gain_attn)[1]
    near_in = near_tokens.reshape(B * T, D).astype(f32)
    near_normed, near_inverse = rms_forward(near_in, gain_attn)
    normed_half = near_normed.astype(bf16)
    lengths = near_lengths[:, 0, 0]
    row_index = jnp.arange(T)
    segment = (row_index[None, :] >= lengths[:, None]).astype(jnp.int32)
    positions = row_index[None, :] - lengths[:, None] * segment
    allowed = (segment[:, :, None] == segment[:, None, :]) & (
        row_index[None, None, :] <= row_index[None, :, None]
    )
    cosine, sine_table = rope_tables(positions, head_width)
    head_shape = (B, T, heads, head_width)
    qkv = dot32(normed_half, full_qkv)
    queries = rotate(qkv[:, :H].reshape(head_shape), cosine, sine_table).astype(bf16)
    keys_rot = rotate(qkv[:, H : 2 * H].reshape(head_shape), cosine, sine_table).astype(bf16)
    values = qkv[:, 2 * H :].astype(bf16).reshape(head_shape)
    score_scale = 1.0 / math.sqrt(head_width)
    scores = ein32("bqhd,bkhd->bhqk", queries, keys_rot) * score_scale
    scores = jnp.where(allowed[:, None], scores, masked_score)
    row_peak = jnp.max(scores, axis=-1, keepdims=True)
    log_total = row_peak + jnp.log(jnp.sum(jnp.exp(scores - row_peak), axis=-1, keepdims=True))
    attn_probs = jnp.exp(scores - log_total)
    probs_half = attn_probs.astype(bf16)
    context = ein32("bhqk,bkhd->bqhd", probs_half, values).astype(bf16)
    context_flat = context.reshape(B * T, H)

    def at_home(partial_rows, collective):
        if not fast:
            return partial_rows
        return plane_sum(partial_rows.astype(bf16).reshape(B, T, D), collective)

    residual_mid = residual_in + branch_scale * at_home(dot32(context_flat, full_output), 4)
    normed_mid, inverse_mid = rms_forward(residual_mid, gain_ffn)
    normed_mid_half = normed_mid.astype(bf16)

    logits = dot32(normed_mid_half, full_router)
    expert_ids = jnp.arange(experts)
    route_mask = (routes[:, :, None] == expert_ids[None, None, :]).astype(f32)
    chosen = jnp.sum(logits[:, None, :] * route_mask, axis=-1)
    gate_probs = jax.nn.softmax(chosen, axis=-1)
    flat_routes = routes.reshape(2 * T)
    hits = (flat_routes[:, None] == expert_ids[None, :]).astype(bf16)
    order = jnp.arange(2 * T)
    before = (order[:, None] > order[None, :]).astype(bf16)
    earlier = dot32(before, hits)
    slot_index = jnp.sum(earlier * hits.astype(f32), axis=1).astype(jnp.int32)
    target = (flat_routes * capacity + slot_index).reshape(T, 2)
    slot_ids = jnp.arange(slots)
    pick = [(target[:, k][:, None] == slot_ids[None, :]).astype(bf16) for k in range(2)]

    notes = jnp.concatenate([gate_probs, target.astype(f32), jnp.zeros((T, 4), f32)], axis=1)
    notes = jnp.pad(jnp.transpose(notes), ((0, 0), (0, -T % 128)))
    spread = spread_blocks if fast else spread_plain
    all_normed, all_notes = spread(nz, (normed_mid_half, notes), 2)
    devices = n_shard * n_exp
    flat_notes = all_notes.reshape(devices, 8, -1)[:, :, :T]
    wanted = (e_index * capacity + jnp.arange(capacity)).astype(f32)
    found = [flat_notes[:, 2 + k, None, :] == wanted[None, :, None] for k in range(2)]
    gate_rows = jnp.sum(
        jnp.where(found[0], flat_notes[:, 0, None, :], 0.0)
        + jnp.where(found[1], flat_notes[:, 1, None, :], 0.0),
        axis=-1,
    ).reshape(devices * capacity, 1)
    chosen_rows = (found[0] | found[1]).astype(bf16)

    def take(blocks):
        rows = ein32("spt,std->spd", chosen_rows, blocks.reshape(devices, T, D))
        return rows.astype(bf16).reshape(devices * capacity, D)

    arrived = take(all_normed)
    cotangent_rows = take(all_cotangent)
    grad_scale = gate_rows * branch_scale
    pre = dot32(arrived, w_pair)
    gate_part, up_part = pre[:, :Fp], pre[:, Fp:]
    sigmoid_gate = jax.nn.sigmoid(gate_part)
    silu_gate = gate_part * sigmoid_gate
    activated = (silu_gate * up_part).astype(bf16)
    out_sum = lax.psum_scatter(
        dot32(activated, down).astype(bf16), SHARD, scatter_dimension=0, tiled=True
    )
    back = lax.all_to_all(out_sum, "expert", split_axis=0, concat_axis=0, tiled=True)
    mixture = gate_probs[:, 0:1] * dot32(pick[0], back) + gate_probs[:, 1:2] * dot32(pick[1], back)
    activations = (residual_mid + branch_scale * mixture).astype(bf16)

    raw_grad = dot_dims(cotangent_rows, down, 1, 1)
    row_dots = branch_scale * jnp.sum(raw_grad * activated.astype(f32), axis=1)
    row_dots = row_dots.reshape(devices, capacity, 1)
    token_dots = [jnp.sum(jnp.where(found[k], row_dots, 0.0), axis=1) for k in range(2)]
    token_dots = jnp.stack(token_dots, axis=1).reshape(nz, 2, n_exp, 2, T)
    token_dots = jnp.pad(token_dots, ((0, 0),) * 3 + ((0, 6), (0, -T % 128)))
    act_grad = grad_scale * raw_grad
    pre_grad = jnp.concatenate(
        [
            act_grad * up_part * sigmoid_gate * (1.0 + gate_part * (1.0 - sigmoid_gate)),
            act_grad * silu_gate,
        ],
        axis=1,
    ).astype(bf16)
    in_rows = dot_dims(pre_grad, w_pair, 1, 1).astype(bf16)
    in_rows = in_rows.reshape(nz, 2, n_exp, capacity, D)
    collect = collect_rows if fast else collect_plain
    normed_mid_grad, gate_grad = collect(nz, in_rows, all_notes, token_dots, T)
    gate_grad = jnp.transpose(gate_grad[:2, :T])
    in_term = dot_dims(arrived, pre_grad, 0, 0).astype(bf16).reshape(n_shard, R, 2 * Fp)
    in_term, normed_mid_grad = lax.optimization_barrier((in_term, normed_mid_grad))
    in_term = lax.all_to_all(in_term, SHARD, split_axis=0, concat_axis=0, tiled=True)
    grad_w_in = unpack_columns(in_term, F)
    scaled = (grad_scale * activated.astype(f32)).astype(bf16)
    grad_w_down = lined_up(dot_dims(scaled[:, :F], cotangent_rows, 0, 0))

    upstream = cotangent.astype(f32)
    chosen_grad = gate_probs * (gate_grad - jnp.sum(gate_probs * gate_grad, axis=-1, keepdims=True))
    logit_grad = jnp.sum(chosen_grad[:, :, None] * route_mask, axis=1)
    normed_mid_grad = normed_mid_grad + jnp.dot(
        logit_grad, jnp.transpose(full_router.astype(f32)), precision=highest
    )
    router_grad = jnp.dot(
        jnp.transpose(normed_mid_half.astype(f32)), logit_grad, precision=highest
    )
    mid_norm_grad, gain_ffn_grad = rms_backward(
        residual_mid, inverse_mid, gain_ffn, normed_mid_grad
    )
    residual_grad = upstream + mid_norm_grad
    branch_grad = (branch_scale * residual_grad).astype(bf16)

    if fast:
        branch_grad = plane_gather(branch_grad, 5).reshape(B * T, D)
    output_grad = dot_dims(context_flat, branch_grad, 0, 0)
    context_grad = dot_dims(branch_grad, full_output, 1, 1).reshape(head_shape)
    row_delta = jnp.sum(context_grad * context.astype(f32), axis=-1)
    context_grad_half = context_grad.astype(bf16)
    probs_grad = ein32("bqhd,bkhd->bhqk", context_grad_half, values)
    scores_grad = (
        attn_probs * (probs_grad - jnp.transpose(row_delta, (0, 2, 1))[..., None]) * score_scale
    ).astype(bf16)
    queries_grad = ein32("bhqk,bkhd->bqhd", scores_grad, keys_rot)
    keys_grad = ein32("bhqk,bqhd->bkhd", scores_grad, queries)
    values_grad = ein32("bhqk,bqhd->bkhd", probs_half, context_grad_half)
    qkv_grad = jnp.concatenate(
        [
            rotate(queries_grad, cosine, -sine_table).reshape(B * T, H).astype(bf16),
            rotate(keys_grad, cosine, -sine_table).reshape(B * T, H).astype(bf16),
            values_grad.reshape(B * T, H).astype(bf16),
        ],
        axis=1,
    )
    qkv_weight_grad = dot_dims(normed_half, qkv_grad, 0, 0)
    near_grad = dot_dims(qkv_grad, full_qkv, 1, 1)
    gain_attn_grad = jnp.sum(near_grad * near_in * near_inverse, axis=0)
    in_norm_grad = rms_backward(residual_in, inverse_in, gain_attn, at_home(near_grad, 6))[0]
    grad_tokens = residual_grad + in_norm_grad

    small_grad = jnp.concatenate(
        [router_grad, gain_attn_grad[:, None], gain_ffn_grad[:, None]], axis=1
    )
    small_grad = jnp.pad(small_grad, ((0, 0), (0, 128 - small_grad.shape[1])))
    sum_query, sum_key, sum_value, sum_output, small_sum = settle(
        nz, fast, qkv_weight_grad, output_grad, small_grad
    )
    return (
        activations,
        grad_tokens,
        small_sum[:, experts],
        sum_query,
        sum_key,
        sum_value,
        sum_output,
        small_sum[:, experts + 1],
        small_sum[:, :experts],
        grad_w_in,
        grad_w_down,
    )


def solution(mesh):
    n_expert, n_shard = mesh.devices.shape
    chips = Mesh(mesh.devices.reshape(n_expert, n_shard // 2, 2), ("expert", "z", "core"))
    rows = P(("expert", "z", "core"), None)
    shard = P(SHARD)
    shard2 = P(SHARD, None)
    shard3 = P(SHARD, "expert", None)
    in_specs = (
        rows,
        rows,
        rows,
        shard,
        shard2,
        shard2,
        shard2,
        shard2,
        shard,
        shard2,
        shard3,
        shard3,
        rows,
    )
    out_specs = (
        rows,
        rows,
        shard,
        shard2,
        shard2,
        shard2,
        shard2,
        shard,
        shard2,
        shard3,
        shard3,
    )
    return jax.shard_map(
        on_device, mesh=chips, in_specs=in_specs, out_specs=out_specs, check_vma=False
    )
```

time: 1130 us -> 1160 us (1.027)
  starting transfers between devices: 19.9 us -> 67.9 us
  other arithmetic: 69.6 us -> 35.2 us
  matrix products: 203 us -> 185 us
  Pallas kernels: 776 us -> 794 us
    pallas_call x1, Pallas kernels: 91.1 us -> 168 us  [spread_blocks(): pl.pallas_call(functools.partial(spread_kernel, nz, splits), out_shape=tu...]
    pallas_call x2 -> x7, Pallas kernels: 534 us -> 481 us  [the longest x1 221 us: settle_weights(): pl.pallas_call(functools.partial(settle_kernel, nz), out_shape=(sd((4, R,...]
    all_to_all x2, starting transfers between devices: 9.73 us -> 62.5 us  [the longest x1 58.9 us: on_device(): lax.all_to_all(packed, SHARD, split_axis=0, concat_axis=0, tiled=True)]
    convert_element_type x12 -> x5, other arithmetic: 37.8 us -> 10.5 us  [the longest x1 5.5 us: on_device(): row_dots = branch_scale * jnp.sum(raw_grad * activated.astype(f32), axis=1)]
    dot_general x9 -> x8, matrix products: 60.4 us -> 53.5 us  [dot32(): return jnp.dot(a, b, preferred_element_type=f32)]
    dot_general x10 -> x8, matrix products: 110 us -> 104 us  [dot_dims(): lax.dot_general(a, b, (((da,), (db,)), ((), ())), preferred_element_type=...]
  transfers between devices with their start and end apart: 9 -> 4, of which waited for: 2 -> 0; matrix products, arithmetic and copies ran while one was open for 22% -> 17% of each run, Pallas kernels for 68% -> 54%
where the time goes in v5:
time: 1160 us; the launch traced here: 1140 us
  Pallas kernels  794 us (68%)
  matrix products  185 us (16%)
  starting transfers between devices  67.9 us (6%)
  local copies, waits for them, and re-layouts  45.9 us (4%)
  other arithmetic  35.2 us (3%)
  between operations  15.4 us (1%)
    pallas_call x1, Pallas kernels, settle_weights(): pl.pallas_call(functools.partial(settle_kernel, nz), out_shape=(sd((4, R,...  221 us
    pallas_call x1, Pallas kernels, spread_blocks(): pl.pallas_call(functools.partial(spread_kernel, nz, splits), out_shape=tu...  168 us
    pallas_call x1, Pallas kernels, fetch_weights(): pl.pallas_call(functools.partial(fetch_kernel, nz), out_shape=(sd((nz, 2)...  160 us
    pallas_call x1, Pallas kernels, collect_rows(): pl.pallas_call(functools.partial(collect_kernel, nz, cap), out_shape=(jax...  108 us
    dot_general x8, matrix products, dot_dims(): lax.dot_general(a, b, (((da,), (db,)), ((), ())), preferred_element_type=...  104 us
    pallas_call x2, Pallas kernels, plane_sum(): pl.pallas_call(plane_sum_kernel, out_shape=jax.ShapeDtypeStruct(x.shape[1...  59.3 us
    all_to_all x1, starting transfers between devices, on_device(): lax.all_to_all(packed, SHARD, split_axis=0, concat_axis=0, tiled=True)  58.9 us
    dot_general x8, matrix products, dot32(): return jnp.dot(a, b, preferred_element_type=f32)  53.5 us
  transfers between devices with their start and end apart: 4, of which 0 were waited for; matrix products, arithmetic and copies ran while one was open for 17% of the time, Pallas kernels for 54%

profile of v5, /device:TPU:16, one launch (start us, length us, event | category | flops | bytes accessed | tf_op | source)
XLA Modules:
  0.0 1144.1 jit_solution(3181012503216770829)
XLA Ops:
  9.4 13.3 %pack_columns.1 = bf16[8,288,1536]{2,1,0:T(8,128)(2,1)} custom-call(bf16[288,11520]{1,0:T(8,128)(2,1)} %bitcast.158), custom_call_target="tpu_custom_call" | custom-call | tf_op jit(solution)/shard_map/pack_columns/pallas_call | solution.py:535
  27.3 160.0 %fetch_weights.1 = (bf16[4,2,288,1728]{3,2,1,0:T(8,128)(2,1)}, bf16[4,2,288,128]{3,2,1,0:T(8,128)(2,1)}, bf16[2,288,2304]{2,1,0:T(8,128)(2,1)}, bf16[4,128,2304]...) custom-call(bf16[288,1728]{1,0:T(8,128)(2,1)} %pick_columns.1.w_ref, ...), custom_call_target="tpu_custom_call" | custom-call | flops 99999997952 | bytes 3981312 | tf_op jit(solution)/shard_map/fetch_weights/pallas_call | solution.py:837
  187.3 58.9 %all-to-all-start = ((bf16[8,288,1536]{2,1,0:T(8,128)(2,1)}), bf16[8,288,1536]{2,1,0:T(8,128)(2,1)}, u32[]{:S(2)}, u32[]{:S(2)}) async-start(bf16[8,288,1536]{2,1,0:T(8,128)(2,1)} %pack_columns.1), calls=%async_computation | async-start | bytes 14155776 | tf_op jit(solution)/shard_map/all_to_all | solution.py:1303
  277.2 29.7 %plane_sum.2 = f32[128,2304]{1,0:T(8,128)} custom-call(bf16[4,128,2304]{2,1,0:T(8,128)(2,1)} %bitcast.155), custom_call_target="tpu_custom_call" | custom-call | flops 1000000 | bytes 1000000 | tf_op jit(solution)/shard_map/plane_sum/pallas_call | solution.py:921
  311.5 168.2 %spread_blocks.1 = (bf16[4,2,4,128,2304]{4,3,2,1,0:T(8,128)(2,1)}, f32[4,2,4,8,128]{4,3,2,1,0:T(8,128)}) custom-call(bf16[128,2304]{1,0:T(8,128)(2,1)} %copy-done.11, f32[8,128]{1,0:T(8,128)} %maximum_bitcast_fusion.refs_1_), custom_call_target="tpu_custom_call" | custom-call | flops 1000000 | bytes 1000000 | tf_op jit(solution)/shard_map/spread_blocks/pallas_call | solution.py:239
  481.0 10.6 convolution_convert_fusion.4
  491.6 10.7 convolution_convert_fusion.5
  502.3 24.0 %fusion.79 = f32[2560,1536]{0,1:T(8,128)S(1)} fusion(bf16[2560,2304]{1,0:T(8,128)(2,1)} %bitcast.147, bf16[2304,1536]{1,0:T(8,128)(2,1)} %bitcast.17), kind=kOutput, calls=%fused_computation.181 | convolution fusion | flops 18119393280 | bytes 34603008 | tf_op jit(solution)/shard_map/dot_general | solution.py:1249
  536.2 14.2 %convolution_convert_fusion.1 = bf16[2560,2304]{1,0:T(8,128)(2,1)} fusion(bf16[2560,768]{0,1:T(8,128)(2,1)} %get-tuple-element.116, bf16[720,2304]{1,0:T(8,128)(2,1)S(1)} %bitcast.185), kind=kOutput, calls=%fused_computation.1 | convolution fusion | flops 9065594880 | bytes 19046400 | tf_op jit(solution)/shard_map/dot_general | solution.py:1249
  550.4 14.8 %multiply_reduce_fusion = (f32[2560]{0:T(1024)S(1)}, f32[2560,768]{0,1:T(8,128)}) fusion(bf16[2560,768]{0,1:T(8,128)(2,1)} %get-tuple-element.116, bf16[2560,2304]{1,0:T(8,128)(2,1)} %bitcast.145, bf16[720,2304]{1,0:T(8,128)(2,1)S(1)} %bitcast.186), kind=kOutput, calls=%fused_computation.7 | convolution fusion | flops 9065592832 | bytes 26920960 | tf_op jit(solution)/shard_map/dot_general | solution.py:1253
  567.4 10.2 multiply_convert_fusion.1
  577.6 24.0 %convolution_convert_fusion = bf16[2560,2304]{1,0:T(8,128)(2,1)} fusion(bf16[2304,1536]{1,0:T(8,128)(2,1)} %bitcast.17, bf16[2560,768]{0,1:T(8,128)(2,1)S(1)} %get-tuple-element.122, bf16[2560,768]{0,1:T(8,128)(2,1)S(1)} %get-tuple-element.121), kind=kOutput, calls=%fused_computation | convolution fusion | flops 18141020160 | bytes 26738688 | tf_op jit(solution)/shard_map/dot_general | solution.py:1253
  601.5 23.0 %convolution_convert_fusion.2 = bf16[2304,1536]{1,0:T(8,128)(2,1)} fusion(bf16[2560,2304]{1,0:T(8,128)(2,1)} %bitcast.148, bf16[2560,768]{0,1:T(8,128)(2,1)S(1)} %get-tuple-element.122, bf16[2560,768]{0,1:T(8,128)(2,1)S(1)} %get-tuple-element.121), kind=kOutput, calls=%fused_computation.2 | convolution fusion | flops 18138660864 | bytes 26738688 | tf_op jit(solution)/shard_map/dot_general | solution.py:1253
  624.5 108.0 %collect_rows.1 = (f32[128,2304]{1,0:T(8,128)}, f32[8,128]{1,0:T(8,128)}) custom-call(bf16[4,2,4,80,2304]{4,3,2,1,0:T(8,128)(2,1)} %bitcast.187, f32[4,2,4,8,128]{4,3,2,1,0:T(8,128)} %get-tuple-element.37.notes_ref, f32[4,2,4,8,128]{4,3,2,1,0:T(8,128)} %select_maximum_fusion.dots_ref), custom_call_target="tpu_custom_call" | custom-call | flops 49999998976 | bytes 11796480 | tf_op jit(solution)/shard_map/collect_rows/pallas_call | solution.py:476
  743.1 29.2 %plane_gather.1 = bf16[4,128,2304]{2,1,0:T(8,128)(2,1)} custom-call(bf16[128,2304]{1,0:T(8,128)(2,1)} %multiply_convert_fusion.4.x_ref), custom_call_target="tpu_custom_call" | custom-call | flops 1000000 | bytes 1000000 | tf_op jit(solution)/shard_map/plane_gather/pallas_call | solution.py:880
  783.9 9.7 fusion.6
  798.6 8.6 convolution_convert_fusion.3
  807.1 11.9 %copy.148 = bf16[2304,1728]{1,0:T(8,128)(2,1)} copy(bf16[2304,1728]{0,1:T(8,128)(2,1)} %convolution_convert_fusion.3) | data formatting | bytes 15925248 | tf_op jit(solution)/shard_map/convert_element_type | solution.py:1185
  819.0 29.7 %plane_sum.3 = f32[128,2304]{1,0:T(8,128)} custom-call(bf16[4,128,2304]{2,1,0:T(8,128)(2,1)} %bitcast.165), custom_call_target="tpu_custom_call" | custom-call | flops 1000000 | bytes 1000000 | tf_op jit(solution)/shard_map/plane_sum/pallas_call | solution.py:921
  852.8 221.3 %settle_weights.1 = (bf16[4,288,1728]{2,1,0:T(8,128)(2,1)}, bf16[4,288,128]{2,1,0:T(8,128)(2,1)}, bf16[288,2304]{1,0:T(8,128)(2,1)}) custom-call(bf16[4,2,288,1728]{3,2,1,0:T(8,128)(2,1)} %bitcast.142, bf16[4,2,288,128]{3,2,1,0:T(8,128)(2,1)} %bitcast.162, bf16[2,288,2304]{2,1,0:T(8,128)(2,1)} %bitcast.161), custom_call_target="tpu_custom_call" | custom-call | flops 1000000 | bytes 1000000 | tf_op jit(solution)/shard_map/settle_weights/pallas_call | solution.py:1099
  1075.5 16.1 %fusion.10.x_ref = f32[720,2304]{1,0:T(8,128)} fusion(bf16[2560,2304]{1,0:T(8,128)(2,1)} %bitcast.146, f32[2560,768]{0,1:T(8,128)} %get-tuple-element.115, f32[2560]{0:T(1024)S(1)} %copy-done.44), kind=kOutput, calls=%fused_computation.31 | convolution fusion | flops 8497152000 | bytes 25815040 | tf_op jit(solution)/shard_map/dot_general | solution.py:1253
  1096.1 9.1 lined_up.1
  1105.1 8.1 assemble_columns.1
  1120.5 14.5 %unpack_columns.1 = f32[25920,128]{1,0:T(8,128)} custom-call(bf16[8,288,1536]{2,1,0:T(8,128)(2,1)} %all-to-all-done.2.x_ref), custom_call_target="tpu_custom_call" | custom-call | tf_op jit(solution)/shard_map/unpack_columns/pallas_call | solution.py:562
  (252 shorter events, 101.1 us)
Async XLA Ops:
  187.3 59.1 %copy-start.9 = (bf16[4,2,288,128]{3,2,1,0:T(8,128)(2,1)S(1)}, bf16[4,2,288,128]{3,2,1,0:T(8,128)(2,1)}, u32[]{:S(2)}) copy-start(bf16[4,2,288,128]{3,2,1,0:T(8,128)(2,1)} %get-tuple-element.32) | copy-start | bytes 1769476
  187.3 315.0 %all-to-all-start = ((bf16[8,288,1536]{2,1,0:T(8,128)(2,1)}), bf16[8,288,1536]{2,1,0:T(8,128)(2,1)}, u32[]{:S(2)}, u32[]{:S(2)}) async-start(bf16[8,288,1536]{2,1,0:T(8,128)(2,1)} %pack_columns.1), calls=%async_computation | async-start | bytes 14155776 | tf_op jit(solution)/shard_map/all_to_all | solution.py:1303
  246.2 845.4 %reduce-scatter.2.cloned.1.call-start = ((), (), s32[]{:S(2)}) async-start(), calls=%async_computation.4 | async-start | bytes 13271040 | tf_op jit(solution)/shard_map/reduce_scatter | solution.py:1388
  250.6 7.8 copy-start.17
  277.2 29.7 %copy-start.15 = (bf16[128,2304]{1,0:T(8,128)(2,1)S(1)}, bf16[128,2304]{1,0:T(8,128)(2,1)}, u32[]{:S(2)}) copy-start(bf16[128,2304]{1,0:T(8,128)(2,1)} %t_ref.1) | copy-start | bytes 1769476
  310.1 181.4 %copy-start.45 = (f32[128,2]{0,1:T(2,128)}, f32[128,2]{0,1:T(2,128)S(1)}, u32[]{:S(2)}) copy-start(f32[128,2]{0,1:T(2,128)S(1)} %select_reduce_fusion.1) | copy-start | bytes 3076
  310.2 181.4 %copy-start.50 = (f32[128]{0:T(128)}, f32[128]{0:T(128)S(1)}, u32[]{:S(2)}) copy-start(f32[128]{0:T(128)S(1)} %reduce_max.19) | copy-start | bytes 1540
  310.3 181.3 %copy-start.56 = (f32[128]{0:T(128)}, f32[128]{0:T(128)S(1)}, u32[]{:S(2)}) copy-start(f32[128]{0:T(128)S(1)} %fusion.62) | copy-start | bytes 1540
  310.3 181.3 %copy-start.52 = (f32[128,2]{0,1:T(2,128)}, f32[128,2]{0,1:T(2,128)S(1)}, u32[]{:S(2)}) copy-start(f32[128,2]{0,1:T(2,128)S(1)} %fusion.61) | copy-start | bytes 3076
  526.2 10.0 copy-start
  526.3 9.9 copy-start.70
  732.7 358.9 %all-to-all-start.2 = ((bf16[8,288,1536]{2,1,0:T(8,128)(2,1)}), bf16[8,288,1536]{2,1,0:T(8,128)(2,1)}, u32[]{:S(2)}, u32[]{:S(2)}) async-start(bf16[8,288,1536]{2,1,0:T(8,128)(2,1)} %bitcast.156), calls=%async_computation.3 | async-start | bytes 14155776 | tf_op jit(solution)/shard_map/all_to_all | solution.py:1416
  740.8 31.5 %copy-start.66 = (f32[128]{0:T(128)}, f32[128]{0:T(128)S(1)}, u32[]{:S(2)}) copy-start(f32[128]{0:T(128)S(1)} %broadcast_multiply_fusion.3) | copy-start | bytes 1540
  743.1 29.2 %copy-start.20 = (bf16[4,128,9,64]{1,3,2,0:T(8,128)(2,1)S(1)}, bf16[4,128,9,64]{1,3,2,0:T(8,128)(2,1)}, u32[]{:S(2)}) copy-start(bf16[4,128,9,64]{1,3,2,0:T(8,128)(2,1)} %copy-done.19) | copy-start | bytes 1769476
  783.9 9.8 copy-start.47
  783.9 9.8 copy-start.12
  819.0 29.7 %copy-start.21 = (bf16[4,128,2304]{2,1,0:T(8,128)(2,1)S(1)}, bf16[4,128,2304]{2,1,0:T(8,128)(2,1)}, u32[]{:S(2)}) copy-start(bf16[4,128,2304]{2,1,0:T(8,128)(2,1)} %plane_gather.1) | copy-start | bytes 7077892
  852.8 222.3 %copy-start.5 = (f32[128,2304]{1,0:T(8,128)S(1)}, f32[128,2304]{1,0:T(8,128)}, u32[]{:S(2)}) copy-start(f32[128,2304]{1,0:T(8,128)} %plane_sum.3) | copy-start | bytes 3538948
  852.8 222.3 %copy-start.16 = (bf16[128,2304]{1,0:T(8,128)(2,1)S(1)}, bf16[128,2304]{1,0:T(8,128)(2,1)}, u32[]{:S(2)}) copy-start(bf16[128,2304]{1,0:T(8,128)(2,1)} %t_ref.1) | copy-start | bytes 1769476
  852.8 222.3 %copy-start.42 = (f32[2304]{0:T(1024)S(1)}, f32[2304]{0:T(1024)}, u32[]{:S(2)}) copy-start(f32[2304]{0:T(1024)} %copy-done.41) | copy-start | bytes 27652
  852.8 222.7 %copy-start.44 = (f32[2560]{0:T(1024)S(1)}, f32[2560]{0:T(1024)}, u32[]{:S(2)}) copy-start(f32[2560]{0:T(1024)} %copy-done.43) | copy-start | bytes 30724
  1091.6 43.4 %all-to-all-start.1 = ((bf16[4,80,2304]{2,1,0:T(8,128)(2,1)}), bf16[4,80,2304]{2,1,0:T(8,128)(2,1)S(1)}, u32[]{:S(2)}, u32[]{:S(2)}) async-start(bf16[4,80,2304]{2,1,0:T(8,128)(2,1)} %bitcast.171), calls=%async_computation.2 | async-start | bytes 2949120 | tf_op jit(solution)/shard_map/all_to_all | solution.py:1391
  1120.5 14.5 %copy-start.63 = (f32[128]{0:T(128)S(1)}, f32[128]{0:T(128)}, u32[]{:S(2)}) copy-start(f32[128]{0:T(128)} %get-tuple-element.155) | copy-start | bytes 1540
  1120.5 14.5 %copy-start.65 = (s32[128]{0:T(128)S(1)}, s32[128]{0:T(128)}, u32[]{:S(2)}) copy-start(s32[128]{0:T(128)} %get-tuple-element.153) | copy-start | bytes 1540
  (51 other events, 154.5 us)
Sparse Core Ops, SparseCore 0:
  566.8 117.9 reduce-scatter.1

commit v6 on v5

--- a/solution.py
+++ b/solution.py
@@ -758,56 +758,66 @@
         nz, p_ref, p_out, p_sems, p_ref.shape[0] // 2
     )
 
-    def o_copy(side, source):
+    pieces = orecv.shape[0]
+    height = o_ref.shape[0] // pieces
+
+    def o_part(n):
+        return pl.ds(n * height, height)
+
+    def o_view(n):
+        return o_out.at[c, o_part(n), :]
+
+    def o_copy(side, n, source):
         step = 1 if side == 0 else -1
-        return remote(source, o_out.at[c], osend.at[side], orecv, e, z + step, c)
-
-    def o_beside(source):
-        return remote(source, o_out.at[c], sib_send, sib_recv, e, z, 1 - c)
+        return remote(source, o_view(n), osend.at[side, n], orecv.at[n], e, z + step, c)
+
+    def o_beside(n, source):
+        return remote(source, o_view(n), sib_send.at[n], sib_recv.at[n], e, z, 1 - c)
 
     def o_goes(side):
         return (z >= e) & (z < nz - 1) if side == 0 else (z <= e) & (z > 0)
 
-    w_begin()
-    s_begin()
+    def o_pass(n, source):
+        for side in range(2):
+
+            @pl.when(o_goes(side))
+            def _():
+                o_copy(side, n, source).start()
+
+        o_beside(n, source).start()
+
+    def o_arrive(n):
+        @pl.when(z != e)
+        def _():
+            remote(o_view(n), o_view(n), sib_send.at[n], orecv.at[n], e, z, c).wait_recv()
+            o_pass(n, o_view(n))
+
+    p_begin()
 
     @pl.when(z == e)
     def _():
-        for side in range(2):
-
-            @pl.when(o_goes(side))
-            def _():
-                o_copy(side, o_ref).start()
-
-        o_beside(o_ref).start()
+        for n in range(pieces):
+            o_pass(n, o_ref.at[o_part(n), :])
         pltpu.make_async_copy(o_ref, o_out.at[c], own).start()
 
+    s_begin()
+    w_begin()
     t_begin()
     l_begin()
-    p_begin()
-
-    def o_arrive():
-        @pl.when(z != e)
-        def _():
-            remote(o_out.at[c], o_out.at[c], sib_send, orecv, e, z, c).wait_recv()
-            for side in range(2):
-
-                @pl.when(o_goes(side))
-                def _():
-                    o_copy(side, o_out.at[c]).start()
-
-            o_beside(o_out.at[c]).start()
 
     blocks = 2 * nz - 1
     for s in range(1, blocks):
+        p_arrive(s)
+        s_arrive(s)
+        if s <= pieces:
+            o_arrive(s - 1)
+    for n in range(blocks - 1, pieces):
+        o_arrive(n)
+    for s in range(1, blocks):
+        p_relay(s - 1)
         w_arrive(s)
-        s_arrive(s)
-        p_arrive(s)
-        p_relay(s - 1)
         if s >= 2:
             p_close(s - 2)
-        if s == 4:
-            o_arrive()
     p_relay(blocks - 1)
     p_close(blocks - 2)
     p_close(blocks - 1)
@@ -817,14 +827,15 @@
     s_end()
     t_end()
     l_end()
-    view = o_out.at[1 - c]
-    remote(view, view, sib_send, sib_recv, e, z, c).wait_recv()
-    o_beside(o_out.at[c]).wait_send()
-    for side in range(2):
-
-        @pl.when(o_goes(side))
-        def _():
-            o_copy(side, o_out.at[c]).wait_send()
+    for n in range(pieces):
+        view = o_out.at[1 - c, o_part(n), :]
+        remote(view, view, sib_send.at[n], sib_recv.at[n], e, z, c).wait_recv()
+        o_beside(n, o_view(n)).wait_send()
+        for side in range(2):
+
+            @pl.when(o_goes(side))
+            def _():
+                o_copy(side, n, o_view(n)).wait_send()
 
     @pl.when(z == e)
     def _():
@@ -848,7 +859,7 @@
         out_specs=(ANY,) * 6,
         scratch_shapes=[
             *line_sems(nz), *line_sems(nz), *plane_sems(), *plane_sems(), *payload_sems(nz),
-            dma(()), dma((2,)), dma(()), dma(()), dma(()),
+            dma((6,)), dma((2, 6)), dma((6,)), dma((6,)), dma(()),
         ],
         compiler_params=pltpu.CompilerParams(collective_id=0, has_side_effects=True),
         cost_estimate=pl.CostEstimate(
@@ -944,29 +955,39 @@
     peers = (ex, ey, (ex + 2) % 4)
     dest = line_order(nz, z)
     greet_cross(nz)
-    groups = ((g_ref, g_mine, g_sib, g_z, g_out), (s_ref, s_mine, s_sib, s_z, s_out))
+    W = g_ref.shape[3]
+    first = W // 256 * 128
+    groups = (
+        (g_ref, g_mine, g_sib, g_z, g_out, pl.ds(0, first)),
+        (g_ref, g_mine, g_sib, g_z, g_out, pl.ds(first, W - first)),
+        (s_ref, s_mine, s_sib, s_z, s_out, pl.ds(0, s_ref.shape[3])),
+    )
+    K = len(groups)
+
+    def part(k, which, *index):
+        return groups[k][which].at[(*index, slice(None), groups[k][5])]
 
     def fetch(k, i):
-        ref, mine = groups[k][0], groups[k][1]
-        return pltpu.make_async_copy(ref.at[dest[i], c], mine.at[i], load.at[k, i])
+        return pltpu.make_async_copy(
+            part(k, 0, dest[i], c), part(k, 1, i), load.at[k, i]
+        )
 
     def hand(k, i):
-        ref, theirs = groups[k][0], groups[k][2]
-        return remote(
-            ref.at[dest[i], 1 - c], theirs.at[i], sib_send.at[k, i], sib_recv.at[k, i], e, z, 1 - c
+        return remote(
+            part(k, 0, dest[i], 1 - c), part(k, 2, i),
+            sib_send.at[k, i], sib_recv.at[k, i], e, z, 1 - c,
         )
 
     def zcopy(k, i):
-        mine, from_z = groups[k][1], groups[k][3]
         step = jnp.where(dest[i] > z, 1, -1)
         side = jnp.where(dest[i] > z, 0, 1)
         return remote(
-            mine.at[i], from_z.at[side, dest[i]],
+            part(k, 1, i), part(k, 3, side, dest[i]),
             zsend.at[k, i], zrecv.at[k, side, dest[i]], e, z + step, c,
         )
 
     def zwait(k, side, zz):
-        slab = groups[k][3].at[side, zz]
+        slab = part(k, 3, side, zz)
         remote(slab, slab, zsend.at[k, 0], zrecv.at[k, side, zz], e, z, c).wait_recv()
 
     def add(target, others):
@@ -978,40 +999,56 @@
                 acc = acc + o[rows, :].astype(f32)
             target[rows, :] = acc.astype(target.dtype)
 
-    def o_fetch():
-        return pltpu.make_async_copy(o_ref.at[c], o_mine, o_load)
-
-    def o_hand():
-        return remote(o_ref.at[1 - c], o_sib, o_sib_send, o_sib_recv, e, z, 1 - c)
-
-    def o_line():
+    pieces = o_load.shape[0]
+    height = o_mine.shape[0] // pieces
+
+    def o_part(n):
+        return pl.ds(n * height, height)
+
+    def o_fetch(n):
+        return pltpu.make_async_copy(o_ref.at[c, o_part(n), :], o_mine.at[o_part(n), :], o_load.at[n])
+
+    def o_hand(n):
+        return remote(
+            o_ref.at[1 - c, o_part(n), :], o_sib.at[o_part(n), :],
+            o_sib_send.at[n], o_sib_recv.at[n], e, z, 1 - c,
+        )
+
+    def o_line(n):
         step, side = jnp.where(z < e, 1, -1), jnp.where(z < e, 0, 1)
-        return remote(o_mine, o_z.at[side], o_zsend, o_zrecv.at[side], e, z + step, c)
-
-    def o_wait(side):
-        slab = o_z.at[side]
-        remote(slab, slab, o_zsend, o_zrecv.at[side], e, z, c).wait_recv()
-        add(o_mine, [slab])
-
-    def o_peer(n):
-        return remote(o_mine, o_out, o_send.at[n], o_recv, peers[n], z, c)
+        return remote(
+            o_mine.at[o_part(n), :], o_z.at[side, o_part(n), :],
+            o_zsend.at[n], o_zrecv.at[side, n], e, z + step, c,
+        )
+
+    def o_wait(side, n):
+        slab = o_z.at[side, o_part(n), :]
+        remote(slab, slab, o_zsend.at[n], o_zrecv.at[side, n], e, z, c).wait_recv()
+        add(o_mine.at[o_part(n), :], [slab])
+
+    def o_peer(p, n):
+        view = o_out.at[o_part(n), :]
+        return remote(
+            o_mine.at[o_part(n), :], view, o_send.at[p, n], o_recv.at[n], peers[p], z, c
+        )
 
     def o_kept():
         return pltpu.make_async_copy(o_mine, o_out, o_own)
 
-    o_fetch().start()
-    o_hand().start()
     for i in range(nz):
-        for k in range(2):
+        for k in range(K):
             hand(k, i).start()
             fetch(k, i).start()
+        if i == 0:
+            for n in range(pieces):
+                o_fetch(n).start()
+                o_hand(n).start()
 
     def finish(k, i):
-        mine, theirs, from_z = groups[k][1:4]
         fetch(k, i).wait()
         hand(k, i).wait_recv()
         zz = dest[i]
-        add(mine.at[i], [theirs.at[i]])
+        add(part(k, 1, i), [part(k, 2, i)])
         if i < nz - 1:
             for side in range(2):
                 going = zz > z if side == 0 else zz < z
@@ -1020,7 +1057,7 @@
                 @pl.when(going & behind)
                 def _():
                     zwait(k, side, zz)
-                    add(mine.at[i], [from_z.at[side, zz]])
+                    add(part(k, 1, i), [part(k, 3, side, zz)])
 
             zcopy(k, i).start()
             return
@@ -1029,63 +1066,71 @@
             @pl.when(z > 0 if side == 0 else z < nz - 1)
             def _():
                 zwait(k, side, z)
-                add(mine.at[i], [from_z.at[side, z]])
-
-    def o_flow():
-        o_fetch().wait()
-        o_hand().wait_recv()
-        add(o_mine, [o_sib])
+                add(part(k, 1, i), [part(k, 3, side, z)])
+
+        streams[k][0]()
+
+    def o_flow(n):
+        o_fetch(n).wait()
+        o_hand(n).wait_recv()
+        add(o_mine.at[o_part(n), :], [o_sib.at[o_part(n), :]])
         for side in range(2):
             behind = (z > 0) & (z <= e) if side == 0 else (z < nz - 1) & (z >= e)
 
             @pl.when(behind)
             def _():
-                o_wait(side)
+                o_wait(side, n)
 
         @pl.when(z != e)
         def _():
-            o_line().start()
+            o_line(n).start()
 
         @pl.when(z == e)
         def _():
-            for n in range(3):
-                o_peer(n).start()
-            o_kept().start()
-
-    for i in range(nz - 1):
-        for k in range(2):
-            finish(k, i)
-        if i == 0:
-            o_flow()
-    for k in range(2):
-        finish(k, nz - 1)
-    spread = [
+            for p in range(3):
+                o_peer(p, n).start()
+
+    streams = [
         plane_stream(
-            groups[k][1].at[nz - 1], lambda q, k=k: groups[k][4].at[q], *sems[3 * k : 3 * k + 3]
-        )
-        for k in range(2)
+            part(k, 1, nz - 1), lambda q, k=k: part(k, 4, q), *sems[3 * k : 3 * k + 3]
+        )
+        for k in range(K)
     ]
-    for begin, _ in spread:
-        begin()
+    order = []
+    for k in range(K):
+        order += [(k, i) for i in range(1 if k else 0, nz - 1)]
+        if k + 1 < K:
+            order.append((k + 1, 0))
+        order.append((k, nz - 1))
+    for n, (k, i) in enumerate(order):
+        finish(k, i)
+        if n == 0:
+            for m in range(pieces):
+                o_flow(m)
 
     @pl.when(z == e)
     def _():
+        o_kept().start()
         o_kept().wait()
-        for n in range(3):
-            o_peer(n).wait_send()
+        for n in range(pieces):
+            for p in range(3):
+                o_peer(p, n).wait_send()
 
     @pl.when(z != e)
     def _():
-        remote(o_out, o_out, o_send.at[0], o_recv, e, z, c).wait_recv()
-        o_line().wait_send()
-
-    o_hand().wait_send()
+        for n in range(pieces):
+            view = o_out.at[o_part(n), :]
+            remote(view, view, o_send.at[0, n], o_recv.at[n], e, z, c).wait_recv()
+            o_line(n).wait_send()
+
+    for n in range(pieces):
+        o_hand(n).wait_send()
     for i in range(nz):
-        for k in range(2):
+        for k in range(K):
             hand(k, i).wait_send()
             if i < nz - 1:
                 zcopy(k, i).wait_send()
-    for _, end in spread:
+    for _, end in streams:
         end()
 
 
@@ -1105,10 +1150,10 @@
             vm((nz, R, W), bf16), vm((nz, R, W), bf16), vm((2, nz, R, W), bf16),
             vm((nz, R, Ws), bf16), vm((nz, R, Ws), bf16), vm((2, nz, R, Ws), bf16),
             vm((R, D), bf16), vm((R, D), bf16), vm((2, R, D), bf16),
-            dma((2, nz)), dma((2, nz)), dma((2, nz)), dma((2, nz)), dma((2, 2, nz)),
-            dma(()), dma(()), dma(()), dma(()), dma((2,)),
-            dma((3,)), dma(()), dma(()),
-            *plane_sems(), *plane_sems(),
+            dma((3, nz)), dma((3, nz)), dma((3, nz)), dma((3, nz)), dma((3, 2, nz)),
+            dma((6,)), dma((6,)), dma((6,)), dma((6,)), dma((2, 6)),
+            dma((3, 6)), dma((6,)), dma(()),
+            *plane_sems(), *plane_sems(), *plane_sems(),
         ],
         compiler_params=pltpu.CompilerParams(
             collective_id=1, has_side_effects=True, vmem_limit_bytes=56 << 20
@@ -1120,6 +1165,9 @@
 
 def pick_kernel(width, q_ref, k_ref, v_ref, o_ref):
     e = lax.axis_index("expert")
+    spare = o_ref.shape[1] - 3 * width
+    if spare:
+        o_ref[:, 3 * width :] = jnp.zeros((o_ref.shape[0], spare), o_ref.dtype)
     for n in range(4):
 
         @pl.when(e == n)
@@ -1134,7 +1182,7 @@
         functools.partial(pick_kernel, width),
         in_specs=[vm] * 3,
         out_specs=vm,
-        out_shape=jax.ShapeDtypeStruct((weights[0].shape[0], 3 * width), bf16),
+        out_shape=jax.ShapeDtypeStruct((weights[0].shape[0], -(-3 * width // 128) * 128), bf16),
         name="pick_columns",
     )(*weights)
 
@@ -1152,7 +1200,7 @@
     return pl.pallas_call(
         functools.partial(assemble_kernel, width),
         grid=(R // block,),
-        in_specs=[pl.BlockSpec((4, block, 3 * width), lambda i: (0, i, 0))],
+        in_specs=[pl.BlockSpec((4, block, x.shape[2]), lambda i: (0, i, 0))],
         out_specs=(pl.BlockSpec((block, 4 * width), lambda i: (i, 0)),) * 3,
         out_shape=(jax.ShapeDtypeStruct((R, 4 * width), f32),) * 3,
         name="assemble_columns",
@@ -1171,7 +1219,7 @@
         columns, full_small, rows, tokens, lengths, blocks = fetch_weights(
             nz, pick_columns(weights, width), small, w_output, tokens, lengths, block
         )
-        columns, rows = columns.reshape(D, 3 * width), rows.reshape(width, D)
+        columns, rows = columns.reshape(D, -1), rows.reshape(width, D)
         return columns, rows, full_small.reshape(D, -1), tokens, lengths, blocks
     full = [lax.all_gather(w, SHARD, axis=0, tiled=True) for w in weights + (w_output, small)]
     blocks = spread_plain(nz, (block,), 0)[0]
@@ -1323,7 +1371,7 @@
     qkv = dot32(normed_half, full_qkv)
     queries = rotate(qkv[:, :H].reshape(head_shape), cosine, sine_table).astype(bf16)
     keys_rot = rotate(qkv[:, H : 2 * H].reshape(head_shape), cosine, sine_table).astype(bf16)
-    values = qkv[:, 2 * H :].astype(bf16).reshape(head_shape)
+    values = qkv[:, 2 * H : 3 * H].astype(bf16).reshape(head_shape)
     score_scale = 1.0 / math.sqrt(head_width)
     scores = ein32("bqhd,bkhd->bhqk", queries, keys_rot) * score_scale
     scores = jnp.where(allowed[:, None], scores, masked_score)
@@ -1451,6 +1499,7 @@
             rotate(queries_grad, cosine, -sine_table).reshape(B * T, H).astype(bf16),
             rotate(keys_grad, cosine, -sine_table).reshape(B * T, H).astype(bf16),
             values_grad.reshape(B * T, H).astype(bf16),
+            jnp.zeros((B * T, full_qkv.shape[1] - 3 * H), bf16),
         ],
         axis=1,
     )

time: 1160 us -> 1060 us (0.914)
  Pallas kernels: 794 us -> 738 us
  starting transfers between devices: 67.9 us -> 34.8 us
    pallas_call x1, Pallas kernels: 221 us -> 185 us  [settle_weights(): pl.pallas_call(functools.partial(settle_kernel, nz), out_shape=(sd((4, R,...]
    all_to_all x1, starting transfers between devices: 58.9 us -> 26 us  [on_device(): lax.all_to_all(packed, SHARD, split_axis=0, concat_axis=0, tiled=True)]
    convert_element_type x1 -> x0, local copies, waits for them, and re-layouts: 11.9 us -> none  [settle(): parts = [x.astype(bf16).reshape(nz, 2, R, -1) for x in (columns, small)]]
    pallas_call x1, Pallas kernels: 160 us -> 148 us  [fetch_weights(): pl.pallas_call(functools.partial(fetch_kernel, nz), out_shape=(sd((nz, 2)...]
  transfers between devices with their start and end apart: 4 -> 4, of which waited for: 0 -> 0; matrix products, arithmetic and copies ran while one was open for 17% -> 18% of each run, Pallas kernels for 54% -> 54%
where the time goes in v6:
time: 1060 us; the launch traced here: 1050 us
  Pallas kernels  738 us (70%)
  matrix products  189 us (18%)
  local copies, waits for them, and re-layouts  39.7 us (4%)
  other arithmetic  35.1 us (3%)
  starting transfers between devices  34.8 us (3%)
  between operations  15.7 us (1%)
    pallas_call x1, Pallas kernels, settle_weights(): pl.pallas_call(functools.partial(settle_kernel, nz), out_shape=(sd((4, R,...  185 us
    pallas_call x1, Pallas kernels, spread_blocks(): pl.pallas_call(functools.partial(spread_kernel, nz, splits), out_shape=tu...  161 us
    pallas_call x1, Pallas kernels, fetch_weights(): pl.pallas_call(functools.partial(fetch_kernel, nz), out_shape=(sd((nz, 2)...  148 us
    pallas_call x1, Pallas kernels, collect_rows(): pl.pallas_call(functools.partial(collect_kernel, nz, cap), out_shape=(jax...  107 us
    dot_general x8, matrix products, dot_dims(): lax.dot_general(a, b, (((da,), (db,)), ((), ())), preferred_element_type=...  107 us
    pallas_call x2, Pallas kernels, plane_sum(): pl.pallas_call(plane_sum_kernel, out_shape=jax.ShapeDtypeStruct(x.shape[1...  59.4 us
    dot_general x8, matrix products, dot32(): return jnp.dot(a, b, preferred_element_type=f32)  54.2 us
    pallas_call x1, Pallas kernels, plane_gather(): pl.pallas_call(plane_gather_kernel, out_shape=jax.ShapeDtypeStruct((4,) +...  28.7 us
  transfers between devices with their start and end apart: 4, of which 0 were waited for; matrix products, arithmetic and copies ran while one was open for 18% of the time, Pallas kernels for 54%

profile of v6, /device:TPU:16, one launch (start us, length us, event | category | flops | bytes accessed | tf_op | source)
XLA Modules:
  0.0 1052.1 jit_solution(8007190558179001)
XLA Ops:
  9.4 13.3 %pack_columns.1 = bf16[8,288,1536]{2,1,0:T(8,128)(2,1)} custom-call(bf16[288,11520]{1,0:T(8,128)(2,1)} %bitcast.159), custom_call_target="tpu_custom_call" | custom-call | tf_op jit(solution)/shard_map/pack_columns/pallas_call | solution.py:535
  27.3 148.3 %fetch_weights.1 = (bf16[4,2,288,1792]{3,2,1,0:T(8,128)(2,1)}, bf16[4,2,288,128]{3,2,1,0:T(8,128)(2,1)}, bf16[2,288,2304]{2,1,0:T(8,128)(2,1)}, bf16[4,128,2304]...) custom-call(bf16[288,1792]{1,0:T(8,128)(2,1)} %pick_columns.1.w_ref, ...), custom_call_target="tpu_custom_call" | custom-call | flops 99999997952 | bytes 4128768 | tf_op jit(solution)/shard_map/fetch_weights/pallas_call | solution.py:848
  175.6 26.0 %all-to-all-start = ((bf16[8,288,1536]{2,1,0:T(8,128)(2,1)}), bf16[8,288,1536]{2,1,0:T(8,128)(2,1)}, u32[]{:S(2)}, u32[]{:S(2)}) async-start(bf16[8,288,1536]{2,1,0:T(8,128)(2,1)} %pack_columns.1), calls=%async_computation | async-start | bytes 14155776 | tf_op jit(solution)/shard_map/all_to_all | solution.py:1351
  206.0 8.6 fusion.79
  240.7 29.7 %plane_sum.2 = f32[128,2304]{1,0:T(8,128)} custom-call(bf16[4,128,2304]{2,1,0:T(8,128)(2,1)} %bitcast.155), custom_call_target="tpu_custom_call" | custom-call | flops 1000000 | bytes 1000000 | tf_op jit(solution)/shard_map/plane_sum/pallas_call | solution.py:932
  275.0 160.7 %spread_blocks.1 = (bf16[4,2,4,128,2304]{4,3,2,1,0:T(8,128)(2,1)}, f32[4,2,4,8,128]{4,3,2,1,0:T(8,128)}) custom-call(bf16[128,2304]{1,0:T(8,128)(2,1)} %copy-done.11, f32[8,128]{1,0:T(8,128)} %maximum_bitcast_fusion.refs_1_), custom_call_target="tpu_custom_call" | custom-call | flops 1000000 | bytes 1000000 | tf_op jit(solution)/shard_map/spread_blocks/pallas_call | solution.py:239
  437.0 11.0 %convolution_convert_fusion.4 = bf16[32,80,2304]{2,1,0:T(8,128)(2,1)} fusion(bf16[32,128,2304]{2,1,0:T(8,128)(2,1)} %bitcast.143, f32[32,128]{1,0:T(8,128)S(1)} %bitcast.179, f32[32,128]{1,0:T(8,128)S(1)} %bitcast.182, f32[80]{0:T(128)S(1)} %add_convert_fusion.4), kind=kOutput, calls=%fused_computation.4 | convolution fusion | flops 1516830720 | bytes 30703936 | tf_op jit(solution)/shard_map/spt,std->spd/dot_general | solution.py:1305
  448.0 10.7 %convolution_convert_fusion.5 = bf16[32,80,2304]{2,1,0:T(8,128)(2,1)} fusion(bf16[32,128,2304]{2,1,0:T(8,128)(2,1)} %bitcast.144, f32[32,128]{1,0:T(8,128)S(1)} %bitcast.180, f32[32,128]{1,0:T(8,128)S(1)} %bitcast.183, f32[80]{0:T(128)S(1)} %add_convert_fusion.4), kind=kOutput, calls=%fused_computation.5 | convolution fusion | flops 1516830720 | bytes 30703936 | tf_op jit(solution)/shard_map/spt,std->spd/dot_general | solution.py:1305
  458.7 24.0 %fusion.80 = f32[2560,1536]{0,1:T(8,128)S(1)} fusion(bf16[2560,2304]{1,0:T(8,128)(2,1)} %bitcast.147, bf16[2304,1536]{1,0:T(8,128)(2,1)} %bitcast.17), kind=kOutput, calls=%fused_computation.183 | convolution fusion | flops 18119393280 | bytes 34603008 | tf_op jit(solution)/shard_map/dot_general | solution.py:1297
  492.6 14.0 %convolution_convert_fusion.1 = bf16[2560,2304]{1,0:T(8,128)(2,1)} fusion(bf16[2560,768]{0,1:T(8,128)(2,1)} %get-tuple-element.116, bf16[720,2304]{1,0:T(8,128)(2,1)S(1)} %bitcast.192), kind=kOutput, calls=%fused_computation.1 | convolution fusion | flops 9065594880 | bytes 19046400 | tf_op jit(solution)/shard_map/dot_general | solution.py:1297
  506.7 14.8 %multiply_reduce_fusion = (f32[2560]{0:T(1024)S(1)}, f32[2560,768]{0,1:T(8,128)}) fusion(bf16[2560,768]{0,1:T(8,128)(2,1)} %get-tuple-element.116, bf16[2560,2304]{1,0:T(8,128)(2,1)} %bitcast.145, bf16[720,2304]{1,0:T(8,128)(2,1)S(1)} %bitcast.193), kind=kOutput, calls=%fused_computation.7 | convolution fusion | flops 9065592832 | bytes 26920960 | tf_op jit(solution)/shard_map/dot_general | solution.py:1301
  523.7 10.7 %multiply_convert_fusion.1 = (bf16[2560,768]{0,1:T(8,128)(2,1)S(1)}, bf16[2560,768]{0,1:T(8,128)(2,1)S(1)}) fusion(f32[2560,1536]{0,1:T(8,128)} %copy-done, f32[2560,768]{0,1:T(8,128)} %get-tuple-element.159, f32[2560]{0:T(1024)S(1)} %mul.462), kind=kLoop, calls=%fused_computation.9 | loop fusion | flops 27525120 | bytes 31467520 | tf_op jit(solution)/shard_map/convert.14
  534.4 24.2 %convolution_convert_fusion = bf16[2560,2304]{1,0:T(8,128)(2,1)} fusion(bf16[2304,1536]{1,0:T(8,128)(2,1)} %bitcast.17, bf16[2560,768]{0,1:T(8,128)(2,1)S(1)} %get-tuple-element.122, bf16[2560,768]{0,1:T(8,128)(2,1)S(1)} %get-tuple-element.121), kind=kOutput, calls=%fused_computation | convolution fusion | flops 18141020160 | bytes 26738688 | tf_op jit(solution)/shard_map/dot_general | solution.py:1301
  558.6 22.8 %convolution_convert_fusion.2 = bf16[2304,1536]{1,0:T(8,128)(2,1)} fusion(bf16[2560,2304]{1,0:T(8,128)(2,1)} %bitcast.148, bf16[2560,768]{0,1:T(8,128)(2,1)S(1)} %get-tuple-element.122, bf16[2560,768]{0,1:T(8,128)(2,1)S(1)} %get-tuple-element.121), kind=kOutput, calls=%fused_computation.2 | convolution fusion | flops 18138660864 | bytes 26738688 | tf_op jit(solution)/shard_map/dot_general | solution.py:1301
  581.4 107.3 %collect_rows.1 = (f32[128,2304]{1,0:T(8,128)}, f32[8,128]{1,0:T(8,128)}) custom-call(bf16[4,2,4,80,2304]{4,3,2,1,0:T(8,128)(2,1)} %bitcast.194, f32[4,2,4,8,128]{4,3,2,1,0:T(8,128)} %get-tuple-element.37.notes_ref, f32[4,2,4,8,128]{4,3,2,1,0:T(8,128)} %select_maximum_fusion.dots_ref), custom_call_target="tpu_custom_call" | custom-call | flops 49999998976 | bytes 11796480 | tf_op jit(solution)/shard_map/collect_rows/pallas_call | solution.py:476
  698.7 28.7 %plane_gather.1 = bf16[4,128,2304]{2,1,0:T(8,128)(2,1)} custom-call(bf16[128,2304]{1,0:T(8,128)(2,1)} %multiply_convert_fusion.4.x_ref), custom_call_target="tpu_custom_call" | custom-call | flops 1000000 | bytes 1000000 | tf_op jit(solution)/shard_map/plane_gather/pallas_call | solution.py:891
  737.9 10.5 fusion.6
  752.1 29.7 %plane_sum.3 = f32[128,2304]{1,0:T(8,128)} custom-call(bf16[4,128,2304]{2,1,0:T(8,128)(2,1)} %bitcast.166), custom_call_target="tpu_custom_call" | custom-call | flops 1000000 | bytes 1000000 | tf_op jit(solution)/shard_map/plane_sum/pallas_call | solution.py:932
  786.1 10.2 convolution_convert_fusion.3
  796.4 185.4 %settle_weights.1 = (bf16[4,288,1792]{2,1,0:T(8,128)(2,1)}, bf16[4,288,128]{2,1,0:T(8,128)(2,1)}, bf16[288,2304]{1,0:T(8,128)(2,1)}) custom-call(bf16[4,2,288,1792]{3,2,1,0:T(8,128)(2,1)} %bitcast.156, bf16[4,2,288,128]{3,2,1,0:T(8,128)(2,1)} %bitcast.163, bf16[2,288,2304]{2,1,0:T(8,128)(2,1)} %bitcast.162), custom_call_target="tpu_custom_call" | custom-call | flops 1000000 | bytes 1000000 | tf_op jit(solution)/shard_map/settle_weights/pallas_call | solution.py:1144
  983.1 16.4 %fusion.10.x_ref = f32[720,2304]{1,0:T(8,128)} fusion(bf16[2560,2304]{1,0:T(8,128)(2,1)} %bitcast.146, f32[2560,768]{0,1:T(8,128)} %get-tuple-element.115, f32[2560]{0:T(1024)S(1)} %copy-done.50), kind=kOutput, calls=%fused_computation.31 | convolution fusion | flops 8497152000 | bytes 25815040 | tf_op jit(solution)/shard_map/dot_general | solution.py:1301
  1003.9 9.1 lined_up.1
  1013.0 8.1 assemble_columns.1
  1028.4 14.5 %unpack_columns.1 = f32[25920,128]{1,0:T(8,128)} custom-call(bf16[8,288,1536]{2,1,0:T(8,128)(2,1)} %all-to-all-done.2.x_ref), custom_call_target="tpu_custom_call" | custom-call | tf_op jit(solution)/shard_map/unpack_columns/pallas_call | solution.py:562
  (268 shorter events, 97.8 us)
Async XLA Ops:
  175.6 26.0 %copy-start.9 = (bf16[4,2,288,128]{3,2,1,0:T(8,128)(2,1)S(1)}, bf16[4,2,288,128]{3,2,1,0:T(8,128)(2,1)}, u32[]{:S(2)}) copy-start(bf16[4,2,288,128]{3,2,1,0:T(8,128)(2,1)} %get-tuple-element.32) | copy-start | bytes 1769476
  175.6 283.1 %all-to-all-start = ((bf16[8,288,1536]{2,1,0:T(8,128)(2,1)}), bf16[8,288,1536]{2,1,0:T(8,128)(2,1)}, u32[]{:S(2)}, u32[]{:S(2)}) async-start(bf16[8,288,1536]{2,1,0:T(8,128)(2,1)} %pack_columns.1), calls=%async_computation | async-start | bytes 14155776 | tf_op jit(solution)/shard_map/all_to_all | solution.py:1351
  201.6 797.9 %reduce-scatter.2.cloned.1.call-start = ((), (), s32[]{:S(2)}) async-start(), calls=%async_computation.4 | async-start | bytes 13271040 | tf_op jit(solution)/shard_map/reduce_scatter | solution.py:1436
  240.7 29.7 %copy-start.15 = (bf16[128,2304]{1,0:T(8,128)(2,1)S(1)}, bf16[128,2304]{1,0:T(8,128)(2,1)}, u32[]{:S(2)}) copy-start(bf16[128,2304]{1,0:T(8,128)(2,1)} %t_ref.1) | copy-start | bytes 1769476
  273.6 174.4 %copy-start.51 = (f32[128,2]{0,1:T(2,128)}, f32[128,2]{0,1:T(2,128)S(1)}, u32[]{:S(2)}) copy-start(f32[128,2]{0,1:T(2,128)S(1)} %select_reduce_fusion.1) | copy-start | bytes 3076
  273.6 174.4 %copy-start.55 = (f32[128]{0:T(128)}, f32[128]{0:T(128)S(1)}, u32[]{:S(2)}) copy-start(f32[128]{0:T(128)S(1)} %reduce_max.19) | copy-start | bytes 1540
  273.7 174.3 %copy-start.61 = (f32[128]{0:T(128)}, f32[128]{0:T(128)S(1)}, u32[]{:S(2)}) copy-start(f32[128]{0:T(128)S(1)} %fusion.62) | copy-start | bytes 1540
  273.7 174.3 %copy-start.57 = (f32[128,2]{0,1:T(2,128)}, f32[128,2]{0,1:T(2,128)S(1)}, u32[]{:S(2)}) copy-start(f32[128,2]{0,1:T(2,128)S(1)} %fusion.61) | copy-start | bytes 3076
  482.7 10.0 copy-start
  482.7 9.9 copy-start.76
  688.9 310.6 %all-to-all-start.2 = ((bf16[8,288,1536]{2,1,0:T(8,128)(2,1)}), bf16[8,288,1536]{2,1,0:T(8,128)(2,1)}, u32[]{:S(2)}, u32[]{:S(2)}) async-start(bf16[8,288,1536]{2,1,0:T(8,128)(2,1)} %bitcast.157), calls=%async_computation.3 | async-start | bytes 14155776 | tf_op jit(solution)/shard_map/all_to_all | solution.py:1464
  694.2 43.4 %copy-start.65 = (bf16[1792]{0:T(1024)(128)(2,1)}, bf16[1792]{0:T(1024)(128)(2,1)S(1)}, u32[]{:S(2)}) copy-start(bf16[1792]{0:T(1024)(128)(2,1)S(1)} %pad.27.clone) | copy-start | bytes 10756
  696.4 31.1 %copy-start.72 = (f32[128]{0:T(128)}, f32[128]{0:T(128)S(1)}, u32[]{:S(2)}) copy-start(f32[128]{0:T(128)S(1)} %broadcast_multiply_fusion.3) | copy-start | bytes 1540
  698.7 28.7 %copy-start.21 = (bf16[4,128,9,64]{1,3,2,0:T(8,128)(2,1)S(1)}, bf16[4,128,9,64]{1,3,2,0:T(8,128)(2,1)}, u32[]{:S(2)}) copy-start(bf16[4,128,9,64]{1,3,2,0:T(8,128)(2,1)} %copy-done.20) | copy-start | bytes 1769476
  737.5 10.8 %copy-start.40 = (bf16[72,8,4,128]{3,1,2,0:T(8,128)(2,1)}, bf16[72,8,4,128]{3,1,2,0:T(8,128)(2,1)S(1)}, u32[]{:S(2)}) copy-start(bf16[72,8,4,128]{3,1,2,0:T(8,128)(2,1)S(1)} %copy.200) | copy-start | bytes 1769476
  737.9 10.5 copy-start.12
  749.9 31.9 %copy-start.22 = (bf16[4,128,2304]{2,1,0:T(8,128)(2,1)S(1)}, bf16[4,128,2304]{2,1,0:T(8,128)(2,1)}, u32[]{:S(2)}) copy-start(bf16[4,128,2304]{2,1,0:T(8,128)(2,1)} %plane_gather.1) | copy-start | bytes 7077892
  796.3 186.4 %copy-start.5 = (f32[128,2304]{1,0:T(8,128)S(1)}, f32[128,2304]{1,0:T(8,128)}, u32[]{:S(2)}) copy-start(f32[128,2304]{1,0:T(8,128)} %plane_sum.3) | copy-start | bytes 3538948
  796.3 186.4 %copy-start.16 = (bf16[128,2304]{1,0:T(8,128)(2,1)S(1)}, bf16[128,2304]{1,0:T(8,128)(2,1)}, u32[]{:S(2)}) copy-start(bf16[128,2304]{1,0:T(8,128)(2,1)} %t_ref.1) | copy-start | bytes 1769476
  796.3 186.4 %copy-start.48 = (f32[2304]{0:T(1024)S(1)}, f32[2304]{0:T(1024)}, u32[]{:S(2)}) copy-start(f32[2304]{0:T(1024)} %copy-done.47) | copy-start | bytes 27652
  796.3 186.8 %copy-start.50 = (f32[2560]{0:T(1024)S(1)}, f32[2560]{0:T(1024)}, u32[]{:S(2)}) copy-start(f32[2560]{0:T(1024)} %copy-done.49) | copy-start | bytes 30724
  999.5 43.4 %all-to-all-start.1 = ((bf16[4,80,2304]{2,1,0:T(8,128)(2,1)}), bf16[4,80,2304]{2,1,0:T(8,128)(2,1)S(1)}, u32[]{:S(2)}, u32[]{:S(2)}) async-start(bf16[4,80,2304]{2,1,0:T(8,128)(2,1)} %bitcast.172), calls=%async_computation.2 | async-start | bytes 2949120 | tf_op jit(solution)/shard_map/all_to_all | solution.py:1439
  1028.4 14.5 %copy-start.69 = (f32[128]{0:T(128)S(1)}, f32[128]{0:T(128)}, u32[]{:S(2)}) copy-start(f32[128]{0:T(128)} %get-tuple-element.155) | copy-start | bytes 1540
  1028.4 14.5 %copy-start.71 = (s32[128]{0:T(128)S(1)}, s32[128]{0:T(128)}, u32[]{:S(2)}) copy-start(s32[128]{0:T(128)} %get-tuple-element.153) | copy-start | bytes 1540
  (57 other events, 187.2 us)
Sparse Core Ops, SparseCore 0:
  523.1 117.5 reduce-scatter.1

commit v7 on v6

--- a/solution.py
+++ b/solution.py
@@ -512,13 +512,13 @@
             collective_id=3, has_side_effects=True, vmem_limit_bytes=56 << 20
         ),
         cost_estimate=pl.CostEstimate(
-            flops=5 * 10**10, bytes_accessed=2 * rows.size, transcendentals=0
+            flops=10**6, bytes_accessed=10**6, transcendentals=0
         ),
         name="collect_rows",
     )(rows, notes, dots)
 
 
-def pack_kernel(n, F, Fp, x_ref, o_ref):
+def pack_rows(n, F, Fp, x_ref, o_ref):
     half = n * F
     rows = x_ref.shape[0]
     for i in range(n):
@@ -533,7 +533,7 @@
     rows = w.shape[0]
     block = 16
     return pl.pallas_call(
-        functools.partial(pack_kernel, n, F, Fp),
+        functools.partial(pack_rows, n, F, Fp),
         grid=(rows // block,),
         in_specs=[pl.BlockSpec((block, w.shape[1]), lambda i: (i, 0))],
         out_specs=pl.BlockSpec((n, block, 2 * Fp), lambda i: (0, i, 0)),
@@ -738,8 +738,9 @@
 
 def fetch_kernel(
     nz,
-    w_ref, s_ref, o_ref, t_ref, l_ref, p_ref,
-    w_out, s_out, o_out, t_out, l_out, p_out,
+    F, w_ref, s_ref, o_ref, t_ref, l_ref, p_ref, x_ref,
+    w_out, s_out, o_out, t_out, l_out, p_out, x_out,
+    wide, packed, wide_sem, packed_sem,
     *sems,
 ):
     e, z, c, ex, ey = place()
@@ -749,6 +750,8 @@
     l_sems, sems = sems[:3], sems[3:]
     p_sems, sems = sems[:9], sems[9:]
     orecv, osend, sib_recv, sib_send, own = sems
+    wide_copy = pltpu.make_async_copy(x_ref, wide, wide_sem)
+    wide_copy.start()
     greet_cross(nz)
     w_begin, w_arrive, w_end = line_stream(nz, w_ref, w_out, *w_sems)
     s_begin, s_arrive, s_end = line_stream(nz, s_ref, s_out, *s_sems)
@@ -804,6 +807,16 @@
     w_begin()
     t_begin()
     l_begin()
+
+    wide_copy.wait()
+
+    @pl.loop(0, wide.shape[0] // 16)
+    def _(b):
+        rows = pl.ds(pl.multiple_of(b * 16, 16), 16)
+        pack_rows(packed.shape[0], F, packed.shape[2] // 2, wide.at[rows, :], packed.at[:, rows, :])
+
+    packed_copy = pltpu.make_async_copy(packed, x_out, packed_sem)
+    packed_copy.start()
 
     blocks = 2 * nz - 1
     for s in range(1, blocks):
@@ -841,12 +854,15 @@
     def _():
         pltpu.make_async_copy(o_ref, o_out.at[c], own).wait()
 
-
-def fetch_weights(nz, columns, small, rows, tokens, lengths, block):
+    packed_copy.wait()
+
+
+def fetch_weights(nz, columns, small, rows, tokens, lengths, block, wide, F):
     dma = pltpu.SemaphoreType.DMA
+    packed = (2 * nz, wide.shape[0], 2 * (-(-F // 128) * 128))
     sd = jax.ShapeDtypeStruct
     return pl.pallas_call(
-        functools.partial(fetch_kernel, nz),
+        functools.partial(fetch_kernel, nz, F),
         out_shape=(
             sd((nz, 2) + columns.shape, bf16),
             sd((nz, 2) + small.shape, bf16),
@@ -854,19 +870,23 @@
             sd((4,) + tokens.shape, bf16),
             sd((4,) + lengths.shape, lengths.dtype),
             sd((nz, 2, 4) + block.shape, block.dtype),
+            sd(packed, wide.dtype),
         ),
-        in_specs=[ANY] * 6,
-        out_specs=(ANY,) * 6,
+        in_specs=[ANY] * 7,
+        out_specs=(ANY,) * 7,
         scratch_shapes=[
+            pltpu.VMEM(wide.shape, wide.dtype), pltpu.VMEM(packed, wide.dtype), dma(()), dma(()),
             *line_sems(nz), *line_sems(nz), *plane_sems(), *plane_sems(), *payload_sems(nz),
             dma((6,)), dma((2, 6)), dma((6,)), dma((6,)), dma(()),
         ],
-        compiler_params=pltpu.CompilerParams(collective_id=0, has_side_effects=True),
+        compiler_params=pltpu.CompilerParams(
+            collective_id=0, has_side_effects=True, vmem_limit_bytes=32 << 20
+        ),
         cost_estimate=pl.CostEstimate(
             flops=10**11, bytes_accessed=8 * columns.size, transcendentals=0
         ),
         name="fetch_weights",
-    )(columns, small, rows, tokens, lengths, block)
+    )(columns, small, rows, tokens, lengths, block, wide)
 
 
 def plane_gather_kernel(x_ref, out_ref, send, recv, own):
@@ -900,29 +920,37 @@
     )(x)
 
 
-def plane_sum_kernel(x_ref, out_ref, held, send, recv, own):
+def plane_sum_parts(x_ref, out_ref, held, send, recv, own):
     e, z, c, ex, ey = place()
     peers = (ex, ey, (ex + 2) % 4)
-    greet_plane()
 
     def copy(n):
         return remote(x_ref.at[peers[n]], held.at[n], send.at[n], recv.at[n], peers[n], z, c)
 
+    kept = pltpu.make_async_copy(x_ref.at[e], held.at[3], own)
+
+    def total():
+        kept.wait()
+        for n in range(3):
+            copy(n).wait_recv()
+
+        @pl.loop(0, out_ref.shape[0] // 16)
+        def _(b):
+            rows = pl.ds(pl.multiple_of(b * 16, 16), 16)
+            acc = held[3, rows, :].astype(f32) + held[0, rows, :].astype(f32)
+            acc = acc + held[1, rows, :].astype(f32)
+            out_ref[rows, :] = acc + held[2, rows, :].astype(f32)
+
+    return copy, kept, total
+
+
+def plane_sum_kernel(x_ref, out_ref, held, send, recv, own):
+    greet_plane()
+    copy, kept, total = plane_sum_parts(x_ref, out_ref, held, send, recv, own)
     for n in (2, 0, 1):
         copy(n).start()
-    kept = pltpu.make_async_copy(x_ref.at[e], held.at[3], own)
     kept.start()
-    kept.wait()
-    for n in range(3):
-        copy(n).wait_recv()
-
-    @pl.loop(0, out_ref.shape[0] // 16)
-    def _(b):
-        rows = pl.ds(pl.multiple_of(b * 16, 16), 16)
-        acc = held[3, rows, :].astype(f32) + held[0, rows, :].astype(f32)
-        acc = acc + held[1, rows, :].astype(f32)
-        out_ref[rows, :] = acc + held[2, rows, :].astype(f32)
-
+    total()
     for n in range(3):
         copy(n).wait_send()
 
@@ -943,8 +971,9 @@
 
 def settle_kernel(
     nz,
-    g_ref, s_ref, o_ref,
-    g_out, s_out, o_out,
+    g_ref, s_ref, o_ref, x_ref, y_ref,
+    g_out, s_out, o_out, x_out, y_out,
+    x_held, x_send, x_recv, x_own, y_send, y_recv, y_own,
     g_mine, g_sib, g_z, s_mine, s_sib, s_z, o_mine, o_sib, o_z,
     load, sib_send, sib_recv, zsend, zrecv,
     o_load, o_sib_send, o_sib_recv, o_zsend, o_zrecv,
@@ -1070,6 +1099,21 @@
 
         streams[k][0]()
 
+    x_copy, x_kept, x_total = plane_sum_parts(x_ref, x_out, x_held, x_send, x_recv, x_own)
+    for p in (2, 0, 1):
+        x_copy(p).start()
+    x_kept.start()
+
+    def y_copy(p):
+        return remote(
+            y_ref.at[peers[p]], y_out.at[e], y_send.at[p], y_recv.at[p], peers[p], z, c
+        )
+
+    y_kept = pltpu.make_async_copy(y_ref.at[e], y_out.at[e], y_own)
+    y_kept.start()
+    for p in range(3):
+        y_copy(p).start()
+
     def o_flow(n):
         o_fetch(n).wait()
         o_hand(n).wait_recv()
@@ -1096,6 +1140,7 @@
         )
         for k in range(K)
     ]
+    turn = K * nz // 2
     order = []
     for k in range(K):
         order += [(k, i) for i in range(1 if k else 0, nz - 1)]
@@ -1107,6 +1152,8 @@
         if n == 0:
             for m in range(pieces):
                 o_flow(m)
+        if n == turn:
+            x_total()
 
     @pl.when(z == e)
     def _():
@@ -1123,6 +1170,12 @@
             remote(view, view, o_send.at[0, n], o_recv.at[n], e, z, c).wait_recv()
             o_line(n).wait_send()
 
+    y_kept.wait()
+    for p in range(3):
+        x_copy(p).wait_send()
+        view = y_out.at[peers[p]]
+        remote(view, view, y_send.at[p], y_recv.at[p], e, z, c).wait_recv()
+        y_copy(p).wait_send()
     for n in range(pieces):
         o_hand(n).wait_send()
     for i in range(nz):
@@ -1134,7 +1187,7 @@
         end()
 
 
-def settle_weights(nz, grads, small, rows):
+def settle_weights(nz, grads, small, rows, near, blocks):
     R, W = grads.shape[2:]
     D = rows.shape[2]
     dma = pltpu.SemaphoreType.DMA
@@ -1143,10 +1196,17 @@
     Ws = small.shape[3]
     return pl.pallas_call(
         functools.partial(settle_kernel, nz),
-        out_shape=(sd((4, R, W), bf16), sd((4, R, Ws), bf16), sd((R, D), bf16)),
-        in_specs=[ANY] * 3,
-        out_specs=(ANY,) * 3,
+        out_shape=(
+            sd((4, R, W), bf16),
+            sd((4, R, Ws), bf16),
+            sd((R, D), bf16),
+            sd(near.shape[1:], f32),
+            sd(blocks.shape, bf16),
+        ),
+        in_specs=[ANY] * 5,
+        out_specs=(ANY,) * 3 + (pl.BlockSpec(memory_space=vm), ANY),
         scratch_shapes=[
+            vm(near.shape, bf16), *plane_sems(), *plane_sems(),
             vm((nz, R, W), bf16), vm((nz, R, W), bf16), vm((2, nz, R, W), bf16),
             vm((nz, R, Ws), bf16), vm((nz, R, Ws), bf16), vm((2, nz, R, Ws), bf16),
             vm((R, D), bf16), vm((R, D), bf16), vm((2, R, D), bf16),
@@ -1160,7 +1220,7 @@
         ),
         cost_estimate=pl.CostEstimate(flops=10**6, bytes_accessed=10**6, transcendentals=0),
         name="settle_weights",
-    )(grads, small, rows)
+    )(grads, small, rows, near, blocks)
 
 
 def pick_kernel(width, q_ref, k_ref, v_ref, o_ref):
@@ -1212,29 +1272,37 @@
     return lax.psum(mine, "expert")
 
 
-def fetch(nz, fast, weights, w_output, small, tokens, lengths, block):
+def fetch(nz, fast, weights, w_output, small, tokens, lengths, block, wide, F):
     D = tokens.shape[1]
     if fast:
         width = D // 4
-        columns, full_small, rows, tokens, lengths, blocks = fetch_weights(
-            nz, pick_columns(weights, width), small, w_output, tokens, lengths, block
+        columns, full_small, rows, tokens, lengths, blocks, packed = fetch_weights(
+            nz, pick_columns(weights, width), small, w_output, tokens, lengths, block, wide, F
         )
         columns, rows = columns.reshape(D, -1), rows.reshape(width, D)
-        return columns, rows, full_small.reshape(D, -1), tokens, lengths, blocks
+        return columns, rows, full_small.reshape(D, -1), tokens, lengths, blocks, packed
     full = [lax.all_gather(w, SHARD, axis=0, tiled=True) for w in weights + (w_output, small)]
     blocks = spread_plain(nz, (block,), 0)[0]
-    return jnp.concatenate(full[:3], axis=1), full[3], full[4], tokens[None], lengths[None], blocks
-
-
-def settle(nz, fast, columns, rows, small):
+    packed = pack_columns(wide, 2 * nz, F, -(-F // 128) * 128)
+    columns = jnp.concatenate(full[:3], axis=1)
+    return columns, full[3], full[4], tokens[None], lengths[None], blocks, packed
+
+
+def settle(nz, fast, columns, rows, small, near, blocks):
     D, width = rows.shape[1], rows.shape[0]
     if fast:
         R = D // (2 * nz)
         parts = [x.astype(bf16).reshape(nz, 2, R, -1) for x in (columns, small)]
-        sums, small, out = settle_weights(nz, *parts, rows.astype(bf16).reshape(2, R, D))
-        return *assemble_columns(sums, width), out.astype(f32), jnp.sum(small.astype(f32), axis=0)
+        near = near.astype(bf16).reshape(4, -1, D)
+        blocks = blocks.reshape(4, -1, D)
+        sums, small, out, near, blocks = settle_weights(
+            nz, *parts, rows.astype(bf16).reshape(2, R, D), near, blocks
+        )
+        small, blocks = jnp.sum(small.astype(f32), axis=0), blocks.reshape(-1, D)
+        return *assemble_columns(sums, width), out.astype(f32), small, near, blocks
     parts = [columns[:, i * width : (i + 1) * width] for i in range(3)] + [rows, small]
-    return [sum_shard(x) for x in parts]
+    blocks = lax.all_to_all(blocks, "expert", split_axis=0, concat_axis=0, tiled=True)
+    return [sum_shard(x) for x in parts] + [near, blocks]
 
 
 def spread_plain(nz, blocks, collective):
@@ -1338,16 +1406,23 @@
     small = jnp.concatenate([w_router, norm_attn[:, None], norm_ffn[:, None]], axis=1)
     small = jnp.pad(small, ((0, 0), (0, 128 - small.shape[1])))
     length_rows = jnp.broadcast_to(seq_lengths[:, :1], (8, 128))
-    full_qkv, full_output, full_small, near_tokens, near_lengths, all_cotangent = fetch(
-        nz, fast, (w_query, w_key, w_value), w_output, small, tokens, length_rows, cotangent
+    full_qkv, full_output, full_small, near_tokens, near_lengths, all_cotangent, packed = fetch(
+        nz,
+        fast,
+        (w_query, w_key, w_value),
+        w_output,
+        small,
+        tokens,
+        length_rows,
+        cotangent,
+        w_in.reshape(R, 2 * FF),
+        F,
     )
     full_router = full_small[:, :experts]
     gain_attn = full_small[:, experts].astype(f32)
     gain_ffn = full_small[:, experts + 1].astype(f32)
 
     Fp = -(-F // 128) * 128
-    packed = pack_columns(w_in.reshape(R, 2 * FF), n_shard, F, Fp)
-    packed, full_qkv = lax.optimization_barrier((packed, full_qkv))
     moved = lax.all_to_all(packed, SHARD, split_axis=0, concat_axis=0, tiled=True)
     w_pair = moved.reshape(n_shard * R, 2 * Fp)
     down = jnp.pad(w_down.reshape(F, D), ((0, Fp - F), (0, 0)))
@@ -1436,9 +1511,6 @@
     out_sum = lax.psum_scatter(
         dot32(activated, down).astype(bf16), SHARD, scatter_dimension=0, tiled=True
     )
-    back = lax.all_to_all(out_sum, "expert", split_axis=0, concat_axis=0, tiled=True)
-    mixture = gate_probs[:, 0:1] * dot32(pick[0], back) + gate_probs[:, 1:2] * dot32(pick[1], back)
-    activations = (residual_mid + branch_scale * mixture).astype(bf16)
 
     raw_grad = dot_dims(cotangent_rows, down, 1, 1)
     row_dots = branch_scale * jnp.sum(raw_grad * activated.astype(f32), axis=1)
@@ -1455,16 +1527,19 @@
         axis=1,
     ).astype(bf16)
     in_rows = dot_dims(pre_grad, w_pair, 1, 1).astype(bf16)
+    scaled = (grad_scale * activated.astype(f32)).astype(bf16)
+    grad_w_down = lined_up(dot_dims(scaled[:, :F], cotangent_rows, 0, 0))
+    in_term = dot_dims(arrived, pre_grad, 0, 0).astype(bf16).reshape(n_shard, R, 2 * Fp)
+    in_rows, in_term, grad_w_down = lax.optimization_barrier((in_rows, in_term, grad_w_down))
     in_rows = in_rows.reshape(nz, 2, n_exp, capacity, D)
     collect = collect_rows if fast else collect_plain
     normed_mid_grad, gate_grad = collect(nz, in_rows, all_notes, token_dots, T)
     gate_grad = jnp.transpose(gate_grad[:2, :T])
-    in_term = dot_dims(arrived, pre_grad, 0, 0).astype(bf16).reshape(n_shard, R, 2 * Fp)
-    in_term, normed_mid_grad = lax.optimization_barrier((in_term, normed_mid_grad))
+    in_term, normed_mid_grad, out_sum = lax.optimization_barrier(
+        (in_term, normed_mid_grad, out_sum)
+    )
     in_term = lax.all_to_all(in_term, SHARD, split_axis=0, concat_axis=0, tiled=True)
     grad_w_in = unpack_columns(in_term, F)
-    scaled = (grad_scale * activated.astype(f32)).astype(bf16)
-    grad_w_down = lined_up(dot_dims(scaled[:, :F], cotangent_rows, 0, 0))
 
     upstream = cotangent.astype(f32)
     chosen_grad = gate_probs * (gate_grad - jnp.sum(gate_probs * gate_grad, axis=-1, keepdims=True))
@@ -1506,16 +1581,18 @@
     qkv_weight_grad = dot_dims(normed_half, qkv_grad, 0, 0)
     near_grad = dot_dims(qkv_grad, full_qkv, 1, 1)
     gain_attn_grad = jnp.sum(near_grad * near_in * near_inverse, axis=0)
-    in_norm_grad = rms_backward(residual_in, inverse_in, gain_attn, at_home(near_grad, 6))[0]
-    grad_tokens = residual_grad + in_norm_grad
 
     small_grad = jnp.concatenate(
         [router_grad, gain_attn_grad[:, None], gain_ffn_grad[:, None]], axis=1
     )
     small_grad = jnp.pad(small_grad, ((0, 0), (0, 128 - small_grad.shape[1])))
-    sum_query, sum_key, sum_value, sum_output, small_sum = settle(
-        nz, fast, qkv_weight_grad, output_grad, small_grad
-    )
+    sum_query, sum_key, sum_value, sum_output, small_sum, normed_in_grad, back = settle(
+        nz, fast, qkv_weight_grad, output_grad, small_grad, near_grad, out_sum
+    )
+    mixture = gate_probs[:, 0:1] * dot32(pick[0], back) + gate_probs[:, 1:2] * dot32(pick[1], back)
+    activations = (residual_mid + branch_scale * mixture).astype(bf16)
+    in_norm_grad = rms_backward(residual_in, inverse_in, gain_attn, normed_in_grad)[0]
+    grad_tokens = residual_grad + in_norm_grad
     return (
         activations,
         grad_tokens,

time: 1060 us -> 1050 us (level)
  Pallas kernels: 738 us -> 707 us
  local copies, waits for them, and re-layouts: 39.7 us -> 67.1 us
    pallas_call x2 -> x1, Pallas kernels: 59.4 us -> 29.7 us  [plane_sum(): pl.pallas_call(plane_sum_kernel, out_shape=jax.ShapeDtypeStruct(x.shape[1...]
    unnamed x162 -> x183, local copies, waits for them, and re-layouts: 12.1 us -> 34.3 us
    pallas_call x1, Pallas kernels: 185 us -> 205 us  [settle_weights(): pl.pallas_call(functools.partial(settle_kernel, nz), out_shape=(sd((4, R,...]
    pallas_call x2 -> x1, Pallas kernels: 162 us -> 148 us  [fetch_weights(): pl.pallas_call(functools.partial(fetch_kernel, nz, F), out_shape=(sd((nz,...]
  transfers between devices with their start and end apart: 4 -> 3, of which waited for: 0 -> 0; matrix products, arithmetic and copies ran while one was open for 18% -> 21% of each run, Pallas kernels for 54% -> 52%
where the time goes in v7:
time: 1050 us; the launch traced here: 1040 us
  Pallas kernels  707 us (67%)
  matrix products  188 us (18%)
  local copies, waits for them, and re-layouts  67.1 us (6%)
  other arithmetic  34.9 us (3%)
  starting transfers between devices  31 us (3%)
  between operations  15.5 us (1%)
    pallas_call x1, Pallas kernels, settle_weights(): pl.pallas_call(functools.partial(settle_kernel, nz), out_shape=(sd((4, R,...  205 us
    pallas_call x1, Pallas kernels, spread_blocks(): pl.pallas_call(functools.partial(spread_kernel, nz, splits), out_shape=tu...  161 us
    pallas_call x1, Pallas kernels, fetch_weights(): pl.pallas_call(functools.partial(fetch_kernel, nz, F), out_shape=(sd((nz,...  148 us
    dot_general x8, matrix products, dot_dims(): lax.dot_general(a, b, (((da,), (db,)), ((), ())), preferred_element_type=...  107 us
    pallas_call x1, Pallas kernels, collect_rows(): pl.pallas_call(functools.partial(collect_kernel, nz, cap), out_shape=(jax...  99.3 us
    dot_general x8, matrix products, dot32(): return jnp.dot(a, b, preferred_element_type=f32)  53.4 us
    unnamed x183, local copies, waits for them, and re-layouts  34.3 us
    pallas_call x1, Pallas kernels, plane_sum(): pl.pallas_call(plane_sum_kernel, out_shape=jax.ShapeDtypeStruct(x.shape[1...  29.7 us
  transfers between devices with their start and end apart: 3, of which 0 were waited for; matrix products, arithmetic and copies ran while one was open for 21% of the time, Pallas kernels for 52%

profile of v7, /device:TPU:16, one launch (start us, length us, event | category | flops | bytes accessed | tf_op | source)
XLA Modules:
  0.0 1043.9 jit_solution(17962876389280321951)
XLA Ops:
  20.8 148.4 %fetch_weights.1 = (bf16[4,2,288,1792]{3,2,1,0:T(8,128)(2,1)}, bf16[4,2,288,128]{3,2,1,0:T(8,128)(2,1)S(1)}, bf16[2,288,2304]{2,1,0:T(8,128)(2,1)S(1)}, bf16[4,1...) custom-call(bf16[288,1792]{1,0:T(8,128)(2,1)S(1)} %copy-done.11, ...), custom_call_target="tpu_custom_call" | custom-call | flops 99999997952 | bytes 4128768 | tf_op jit(solution)/shard_map/fetch_weights/pallas_call | solution.py:864
  173.6 26.2 %all-to-all-start = ((bf16[8,288,1536]{2,1,0:T(8,128)(2,1)}), bf16[8,288,1536]{2,1,0:T(8,128)(2,1)}, u32[]{:S(2)}, u32[]{:S(2)}) async-start(bf16[8,288,1536]{2,1,0:T(8,128)(2,1)} %copy-done.4), calls=%async_computation | async-start | bytes 14155776 | tf_op jit(solution)/shard_map/all_to_all | solution.py:1426
  205.6 7.8 fusion.83
  239.3 29.7 %plane_sum.1 = f32[128,2304]{1,0:T(8,128)} custom-call(bf16[4,128,2304]{2,1,0:T(8,128)(2,1)} %bitcast.157), custom_call_target="tpu_custom_call" | custom-call | flops 1000000 | bytes 1000000 | tf_op jit(solution)/shard_map/plane_sum/pallas_call | solution.py:960
  273.2 160.7 %spread_blocks.1 = (bf16[4,2,4,128,2304]{4,3,2,1,0:T(8,128)(2,1)}, f32[4,2,4,8,128]{4,3,2,1,0:T(8,128)}) custom-call(bf16[128,2304]{1,0:T(8,128)(2,1)} %copy-done.23, f32[8,128]{1,0:T(8,128)} %maximum_bitcast_fusion.refs_1_), custom_call_target="tpu_custom_call" | custom-call | flops 1000000 | bytes 1000000 | tf_op jit(solution)/shard_map/spread_blocks/pallas_call | solution.py:239
  435.2 10.9 %convolution_convert_fusion.4 = bf16[32,80,2304]{2,1,0:T(8,128)(2,1)} fusion(bf16[32,128,2304]{2,1,0:T(8,128)(2,1)} %bitcast.150, f32[32,128]{1,0:T(8,128)S(1)} %bitcast.180, f32[32,128]{1,0:T(8,128)S(1)} %bitcast.183, f32[80]{0:T(128)S(1)} %add_convert_fusion.4), kind=kOutput, calls=%fused_computation.4 | convolution fusion | flops 1516830720 | bytes 30703936 | tf_op jit(solution)/shard_map/spt,std->spd/dot_general | solution.py:1373
  446.0 24.0 %fusion.84 = f32[2560,1536]{0,1:T(8,128)S(1)} fusion(bf16[2560,2304]{1,0:T(8,128)(2,1)} %bitcast.151, bf16[2304,1536]{1,0:T(8,128)(2,1)} %bitcast.23), kind=kOutput, calls=%fused_computation.188 | convolution fusion | flops 18119393280 | bytes 34603008 | tf_op jit(solution)/shard_map/dot_general | solution.py:1365
  480.0 14.0 %convolution_convert_fusion = bf16[2560,2304]{1,0:T(8,128)(2,1)} fusion(bf16[2560,768]{0,1:T(8,128)(2,1)} %get-tuple-element.126, bf16[720,2304]{1,0:T(8,128)(2,1)S(1)} %bitcast.193), kind=kOutput, calls=%fused_computation | convolution fusion | flops 9065594880 | bytes 19046400 | tf_op jit(solution)/shard_map/dot_general | solution.py:1365
  494.0 11.2 %convolution_convert_fusion.5 = bf16[32,80,2304]{2,1,0:T(8,128)(2,1)} fusion(bf16[32,128,2304]{2,1,0:T(8,128)(2,1)} %bitcast.149, f32[32,128]{1,0:T(8,128)S(1)} %bitcast.181, f32[32,128]{1,0:T(8,128)S(1)} %bitcast.184, f32[80]{0:T(128)S(1)} %add_convert_fusion.4), kind=kOutput, calls=%fused_computation.5 | convolution fusion | flops 1516830720 | bytes 30703936 | tf_op jit(solution)/shard_map/spt,std->spd/dot_general | solution.py:1373
  505.2 14.2 %multiply_reduce_fusion = (f32[2560]{0:T(1024)S(1)}, f32[2560,768]{0,1:T(8,128)}) fusion(bf16[2560,768]{0,1:T(8,128)(2,1)S(1)} %copy-done.30, bf16[2560,2304]{1,0:T(8,128)(2,1)} %bitcast.153, bf16[720,2304]{1,0:T(8,128)(2,1)S(1)} %bitcast.194), kind=kOutput, calls=%fused_computation.7 | convolution fusion | flops 9065592832 | bytes 26920960 | tf_op jit(solution)/shard_map/dot_general | solution.py:1369
  521.0 16.3 %fusion.12.x_ref = f32[720,2304]{1,0:T(8,128)} fusion(bf16[2560,2304]{1,0:T(8,128)(2,1)} %bitcast.154, f32[2560,768]{0,1:T(8,128)} %get-tuple-element.125, f32[2560]{0:T(1024)S(1)} %mul.469), kind=kOutput, calls=%fused_computation.34 | convolution fusion | flops 8497152000 | bytes 25815040 | tf_op jit(solution)/shard_map/dot_general | solution.py:1369
  537.3 9.1 lined_up.1
  546.4 7.4 reshape.368
  553.8 9.9 multiply_convert_fusion.2
  563.7 24.2 %convolution_convert_fusion.1 = bf16[2560,2304]{1,0:T(8,128)(2,1)} fusion(bf16[2304,1536]{1,0:T(8,128)(2,1)} %bitcast.23, bf16[2560,768]{0,1:T(8,128)(2,1)S(1)} %get-tuple-element.132, bf16[2560,768]{0,1:T(8,128)(2,1)S(1)} %get-tuple-element.131), kind=kOutput, calls=%fused_computation.1 | convolution fusion | flops 18141020160 | bytes 26738688 | tf_op jit(solution)/shard_map/dot_general | solution.py:1369
  587.8 22.5 %convolution_convert_fusion.2 = bf16[2304,1536]{1,0:T(8,128)(2,1)} fusion(bf16[2560,2304]{1,0:T(8,128)(2,1)} %bitcast.152, bf16[2560,768]{0,1:T(8,128)(2,1)S(1)} %get-tuple-element.132, bf16[2560,768]{0,1:T(8,128)(2,1)S(1)} %get-tuple-element.131), kind=kOutput, calls=%fused_computation.2 | convolution fusion | flops 18138660864 | bytes 26738688 | tf_op jit(solution)/shard_map/dot_general | solution.py:1369
  611.1 99.3 %collect_rows.1 = (f32[128,2304]{1,0:T(8,128)}, f32[8,128]{1,0:T(8,128)}) custom-call(bf16[4,2,4,80,2304]{4,3,2,1,0:T(8,128)(2,1)} %bitcast.156, f32[4,2,4,8,128]{4,3,2,1,0:T(8,128)} %get-tuple-element.41.notes_ref, f32[4,2,4,8,128]{4,3,2,1,0:T(8,128)} %select_maximum_fusion.dots_ref), custom_call_target="tpu_custom_call" | custom-call | flops 1000000 | bytes 1000000 | tf_op jit(solution)/shard_map/collect_rows/pallas_call | solution.py:476
  716.5 10.1 copy.159
  730.6 29.0 %plane_gather.1 = bf16[4,128,2304]{2,1,0:T(8,128)(2,1)} custom-call(bf16[128,2304]{1,0:T(8,128)(2,1)} %multiply_convert_fusion.4.x_ref), custom_call_target="tpu_custom_call" | custom-call | flops 1000000 | bytes 1000000 | tf_op jit(solution)/shard_map/plane_gather/pallas_call | solution.py:911
  769.2 11.7 %fusion.76 = (bf16[512,2304]{1,0:T(8,128)(2,1)}, bf16[2304]{0:T(1024)(128)(2,1)S(1)}, bf16[512,2304]{1,0:T(8,128)(2,1)}) fusion(f32[512]{0:T(512)S(1)} %copy-done.80, bf16[4,128,2304]{2,1,0:T(8,128)(2,1)S(1)} %copy-done.1, f32[2304]{0:T(1024)S(1)} %copy-done.59, bf16[2304,1792]{1,0:T(8,128)(2,1)} %bitcast.196, bf16[512,576]{0,1:T(8,128)(2,1)S(1)} %bitcast.178, ...), kind=kOutput, calls=%fused_computation.180 | convolution fusion | flops 4244633344 | bytes 17124352 | tf_op jit(solution)/shard_map/dot_general | solution.py:1369
  788.0 10.2 convolution_convert_fusion.3
  798.2 205.3 %settle_weights.1 = (bf16[4,288,1792]{2,1,0:T(8,128)(2,1)}, bf16[4,288,128]{2,1,0:T(8,128)(2,1)}, bf16[288,2304]{1,0:T(8,128)(2,1)}, f32[128,2304]{1,0:T(8,128)}, bf16[4,80,2304]{2,1,0:T(8,128)(2,1)}) custom-call(bf16[4,2,288,1792]{3,2,1,0:T(8,128)(2,1)} %bitcast.158, bf16[4,2,288,128]{3,2,1,0:T(8,128)(2,1)} %bitcast.172, bf16[2,288,2304]{2,1,0:T(8,128)(2,1)} %bitcast.162, ...), custom_call_target="tpu_custom_call" | custom-call | flops 1000000 | bytes 1000000 | tf_op jit(solution)/shard_map/settle_weights/pallas_call | solution.py:1197
  1003.5 8.1 assemble_columns.1
  1022.3 14.5 %unpack_columns.1 = f32[25920,128]{1,0:T(8,128)} custom-call(bf16[8,288,1536]{2,1,0:T(8,128)(2,1)} %all-to-all-done.1.x_ref), custom_call_target="tpu_custom_call" | custom-call | tf_op jit(solution)/shard_map/unpack_columns/pallas_call | solution.py:562
  (286 shorter events, 103.8 us)
Async XLA Ops:
  173.6 31.4 %copy-start = (bf16[4,128,2304]{2,1,0:T(8,128)(2,1)}, bf16[4,128,2304]{2,1,0:T(8,128)(2,1)S(1)}, u32[]{:S(2)}) copy-start(bf16[4,128,2304]{2,1,0:T(8,128)(2,1)S(1)} %get-tuple-element.36) | copy-start | bytes 7077892
  173.6 97.8 %copy-start.2 = (bf16[4,2,288,128]{3,2,1,0:T(8,128)(2,1)}, bf16[4,2,288,128]{3,2,1,0:T(8,128)(2,1)S(1)}, u32[]{:S(2)}) copy-start(bf16[4,2,288,128]{3,2,1,0:T(8,128)(2,1)S(1)} %get-tuple-element.37) | copy-start | bytes 1769476
  173.6 272.4 %all-to-all-start = ((bf16[8,288,1536]{2,1,0:T(8,128)(2,1)}), bf16[8,288,1536]{2,1,0:T(8,128)(2,1)}, u32[]{:S(2)}, u32[]{:S(2)}) async-start(bf16[8,288,1536]{2,1,0:T(8,128)(2,1)} %copy-done.4), calls=%async_computation | async-start | bytes 14155776 | tf_op jit(solution)/shard_map/all_to_all | solution.py:1426
  199.8 510.6 %reduce-scatter.2.cloned.1.call-start = ((), (), s32[]{:S(2)}) async-start(), calls=%async_computation.3 | async-start | bytes 13271040 | tf_op jit(solution)/shard_map/reduce_scatter | solution.py:1511
  271.8 162.1 %copy-start.61 = (f32[128,2]{0,1:T(2,128)}, f32[128,2]{0,1:T(2,128)S(1)}, u32[]{:S(2)}) copy-start(f32[128,2]{0,1:T(2,128)S(1)} %select_reduce_fusion.1) | copy-start | bytes 3076
  271.9 162.1 %copy-start.65 = (f32[128]{0:T(128)}, f32[128]{0:T(128)S(1)}, u32[]{:S(2)}) copy-start(f32[128]{0:T(128)S(1)} %reduce_max.19) | copy-start | bytes 1540
  272.0 162.0 %copy-start.69 = (f32[128]{0:T(128)}, f32[128]{0:T(128)S(1)}, u32[]{:S(2)}) copy-start(f32[128]{0:T(128)S(1)} %fusion.64) | copy-start | bytes 1540
  272.0 162.0 %copy-start.67 = (f32[128,2]{0,1:T(2,128)}, f32[128,2]{0,1:T(2,128)S(1)}, u32[]{:S(2)}) copy-start(f32[128,2]{0,1:T(2,128)S(1)} %fusion.63) | copy-start | bytes 3076
  494.0 11.2 %copy-start.30 = (bf16[2560,768]{0,1:T(8,128)(2,1)S(1)}, bf16[2560,768]{0,1:T(8,128)(2,1)}, u32[]{:S(2)}) copy-start(bf16[2560,768]{0,1:T(8,128)(2,1)} %get-tuple-element.126) | copy-start | bytes 11796484
  710.5 311.8 %all-to-all-start.1 = ((bf16[8,288,1536]{2,1,0:T(8,128)(2,1)}), bf16[8,288,1536]{2,1,0:T(8,128)(2,1)}, u32[]{:S(2)}, u32[]{:S(2)}) async-start(bf16[8,288,1536]{2,1,0:T(8,128)(2,1)} %bitcast.159), calls=%async_computation.2 | async-start | bytes 14155776 | tf_op jit(solution)/shard_map/all_to_all | solution.py:1541
  715.3 53.6 %copy-start.73 = (bf16[1792]{0:T(1024)(128)(2,1)}, bf16[1792]{0:T(1024)(128)(2,1)S(1)}, u32[]{:S(2)}) copy-start(bf16[1792]{0:T(1024)(128)(2,1)S(1)} %pad.27.clone) | copy-start | bytes 10756
  716.5 10.2 copy-start.70
  716.5 10.2 copy-start.83
  716.5 10.2 copy-start.64
  716.5 10.3 copy-start.24
  716.5 10.6 %copy-start.3 = (bf16[4,2,288,128]{3,2,1,0:T(8,128)(2,1)S(1)}, bf16[4,2,288,128]{3,2,1,0:T(8,128)(2,1)}, u32[]{:S(2)}) copy-start(bf16[4,2,288,128]{3,2,1,0:T(8,128)(2,1)} %copy-done.2) | copy-start | bytes 1769476
  716.5 10.6 %copy-start.17 = (f32[128,2304]{1,0:T(8,128)S(1)}, f32[128,2304]{1,0:T(8,128)}, u32[]{:S(2)}) copy-start(f32[128,2304]{1,0:T(8,128)} %copy-done.16) | copy-start | bytes 3538948
  716.5 10.6 %copy-start.43 = (f32[128,2304]{1,0:T(8,128)S(1)}, f32[128,2304]{1,0:T(8,128)}, u32[]{:S(2)}) copy-start(f32[128,2304]{1,0:T(8,128)} %get-tuple-element.48) | copy-start | bytes 3538948
  716.5 10.6 %copy-start.55 = (f32[2304]{0:T(1024)S(1)}, f32[2304]{0:T(1024)}, u32[]{:S(2)}) copy-start(f32[2304]{0:T(1024)} %copy-done.54) | copy-start | bytes 27652
  716.5 10.6 %copy-start.72 = (f32[128]{0:T(128)S(1)}, f32[128]{0:T(128)}, u32[]{:S(2)}) copy-start(f32[128]{0:T(128)} %copy-done.71) | copy-start | bytes 1540
  728.2 31.3 %copy-start.81 = (f32[128]{0:T(128)}, f32[128]{0:T(128)S(1)}, u32[]{:S(2)}) copy-start(f32[128]{0:T(128)S(1)} %broadcast_multiply_fusion.3) | copy-start | bytes 1540
  730.6 29.0 %copy-start.8 = (bf16[2,288,2304]{2,1,0:T(8,128)(2,1)S(1)}, bf16[2,288,2304]{2,1,0:T(8,128)(2,1)}, u32[]{:S(2)}) copy-start(bf16[2,288,2304]{2,1,0:T(8,128)(2,1)} %copy-done.7) | copy-start | bytes 7962628
  768.9 12.0 %copy-start.50 = (bf16[72,8,4,128]{3,1,2,0:T(8,128)(2,1)}, bf16[72,8,4,128]{3,1,2,0:T(8,128)(2,1)S(1)}, u32[]{:S(2)}) copy-start(bf16[72,8,4,128]{3,1,2,0:T(8,128)(2,1)S(1)} %copy.200) | copy-start | bytes 1769476
  769.2 14.4 %copy-start.32 = (bf16[4,128,2304]{2,1,0:T(8,128)(2,1)S(1)}, bf16[4,128,2304]{2,1,0:T(8,128)(2,1)}, u32[]{:S(2)}) copy-start(bf16[4,128,2304]{2,1,0:T(8,128)(2,1)} %plane_gather.1) | copy-start | bytes 7077892
  (66 other events, 204.6 us)
Sparse Core Ops, SparseCore 0:
  494.1 120.2 reduce-scatter.1

commit v8 on v7

--- a/solution.py
+++ b/solution.py
@@ -206,48 +206,59 @@
 
 def spread_kernel(nz, splits, *refs):
     n = len(splits)
-    ins, outs, sems = refs[:n], refs[n : 2 * n], refs[2 * n :]
-    greet_cross(nz)
+    (gate_ref, up_ref), refs = refs[:2], refs[2:]
+    ins, refs = refs[:n], refs[n:]
+    pair, outs, sems = refs[0], refs[1 : n + 1], refs[n + 1 :]
+    v_sems, beside_sem, sems = sems[:3], sems[3], sems[4:]
+    width = gate_ref.shape[2]
+    greet_shard(nz)
     streams = [
         payload_stream(nz, ins[i], outs[i], sems[9 * i : 9 * i + 9], splits[i]) for i in range(n)
     ]
+    v_begin, v_end = scatter_stream(
+        nz, gate_ref, lambda i: pair.at[i, :, pl.ds(0, width)], *v_sems
+    )
+    beside = pltpu.make_async_copy(up_ref, pair.at[:, :, pl.ds(width, width)], beside_sem)
     for t in streams:
         t[0]()
+    beside.start()
     S = 2 * nz - 1
+    for s in range(1, S):
+        for t in streams:
+            t[1](s)
+    v_begin()
     for s in range(S):
         for t in streams:
-            t[1](s)
+            t[2](s)
         if s >= 1:
             for t in streams:
-                t[2](s - 1)
-        if s >= 2:
-            for t in streams:
-                t[3](s - 2)
+                t[3](s - 1)
     for t in streams:
-        t[2](S - 1)
-    for s in (S - 2, S - 1):
-        for t in streams:
-            t[3](s)
+        t[3](S - 1)
     for s in range(S):
         for t in streams:
             t[4](s)
-
-
-def spread_blocks(nz, blocks, collective):
+    beside.wait()
+    v_end()
+
+
+def spread_blocks(nz, blocks, gate, up, collective):
     sd = jax.ShapeDtypeStruct
     splits = tuple(b.shape[0] // 2 if b.shape[0] % 32 == 0 else 0 for b in blocks)
+    pair = sd(gate.shape[:2] + (2 * gate.shape[2],), gate.dtype)
     return pl.pallas_call(
         functools.partial(spread_kernel, nz, splits),
-        out_shape=tuple(sd((nz, 2, 4) + b.shape, b.dtype) for b in blocks),
-        in_specs=[ANY] * len(blocks),
-        out_specs=(ANY,) * len(blocks),
-        scratch_shapes=[s for _ in blocks for s in payload_sems(nz)],
+        out_shape=(pair,) + tuple(sd((nz, 2, 4) + b.shape, b.dtype) for b in blocks),
+        in_specs=[ANY] * (len(blocks) + 2),
+        out_specs=(ANY,) * (len(blocks) + 1),
+        scratch_shapes=[
+            *scatter_sems(nz), pltpu.SemaphoreType.DMA(()),
+            *[s for _ in blocks for s in payload_sems(nz)],
+        ],
         compiler_params=pltpu.CompilerParams(collective_id=collective, has_side_effects=True),
-        cost_estimate=pl.CostEstimate(
-            flops=10**6, bytes_accessed=10**6, transcendentals=0
-        ),
+        cost_estimate=pl.CostEstimate(flops=10**6, bytes_accessed=10**6, transcendentals=0),
         name="spread_blocks",
-    )(*blocks)
+    )(gate, up, *blocks)
 
 
 def line_order(nz, z):
@@ -518,7 +529,7 @@
     )(rows, notes, dots)
 
 
-def pack_rows(n, F, Fp, x_ref, o_ref):
+def pack_rows(n, F, Fp, x_ref, *o_refs):
     half = n * F
     rows = x_ref.shape[0]
     for i in range(n):
@@ -526,7 +537,7 @@
             cols = x_ref[:, part * half + i * F : part * half + (i + 1) * F]
             if Fp > F:
                 cols = jnp.concatenate([cols, jnp.zeros((rows, Fp - F), cols.dtype)], axis=1)
-            o_ref[i, :, part * Fp : (part + 1) * Fp] = cols
+            o_refs[part][i] = cols
 
 
 def pack_columns(w, n, F, Fp):
@@ -536,38 +547,38 @@
         functools.partial(pack_rows, n, F, Fp),
         grid=(rows // block,),
         in_specs=[pl.BlockSpec((block, w.shape[1]), lambda i: (i, 0))],
-        out_specs=pl.BlockSpec((n, block, 2 * Fp), lambda i: (0, i, 0)),
-        out_shape=jax.ShapeDtypeStruct((n, rows, 2 * Fp), w.dtype),
+        out_specs=(pl.BlockSpec((n, block, Fp), lambda i: (0, i, 0)),) * 2,
+        out_shape=(jax.ShapeDtypeStruct((n, rows, Fp), w.dtype),) * 2,
         name="pack_columns",
     )(w)
 
 
-def unpack_kernel(n, F, Fp, x_ref, o_ref, line):
+def unpack_kernel(n, F, gate_ref, up_ref, o_ref, line):
     half = n * F
     rows = line.shape[0]
     for i in range(n):
         for part in range(2):
-            cols = x_ref[i, :, part * Fp : part * Fp + F].astype(f32)
+            cols = (up_ref if part else gate_ref)[i, :, :F].astype(f32)
             line[:, part * half + i * F : part * half + (i + 1) * F] = cols
     tiles = 2 * half // 128
     for j in range(tiles):
         o_ref[pl.ds(j, rows, stride=tiles), :] = line[:, j * 128 : (j + 1) * 128]
 
 
-def unpack_columns(x, F):
-    n, rows, Fp2 = x.shape
+def unpack_columns(gate, up, F):
+    n, rows, Fp = gate.shape
     block = 16
     width = 2 * n * F
     tiles = width // 128
     flat = pl.pallas_call(
-        functools.partial(unpack_kernel, n, F, Fp2 // 2),
+        functools.partial(unpack_kernel, n, F),
         grid=(rows // block,),
-        in_specs=[pl.BlockSpec((n, block, Fp2), lambda i: (0, i, 0))],
+        in_specs=[pl.BlockSpec((n, block, Fp), lambda i: (0, i, 0))] * 2,
         out_specs=pl.BlockSpec((block * tiles, 128), lambda i: (i, 0)),
         out_shape=jax.ShapeDtypeStruct((rows * tiles, 128), f32),
         scratch_shapes=[pltpu.VMEM((block, width), f32)],
         name="unpack_columns",
-    )(x)
+    )(gate, up)
     return flat.reshape(rows, 1, width)
 
 
@@ -614,6 +625,50 @@
     pl.semaphore_wait(barrier, 4 + jnp.where(z > 0, 1, 0) + jnp.where(z < nz - 1, 1, 0))
 
 
+def greet_shard(nz):
+    e, z, c, ex, ey = place()
+    barrier = pltpu.get_barrier_semaphore()
+    n = 2 * nz
+    peers = [(te, z, c) for te in (ex, ey, (ex + 2) % 4)]
+    for d in range(1, n):
+        to = (2 * z + c + d) % n
+        peers.append((e, to // 2, to % 2))
+    for peer in peers:
+        pl.semaphore_signal(barrier, inc=1, device_id=peer, device_id_type=pl.DeviceIdType.MESH)
+    pl.semaphore_wait(barrier, n + 2)
+
+
+def scatter_stream(nz, ref, view, send, recv, own):
+    e, z, c, _, _ = place()
+    n = 2 * nz
+    me = 2 * z + c
+
+    def copy(d):
+        to = (me + d) % n
+        return remote(ref.at[to], view(me), send.at[d], recv.at[d], e, to // 2, to % 2)
+
+    kept = pltpu.make_async_copy(ref.at[me], view(me), own)
+
+    def begin():
+        for d in range(1, n):
+            copy(d).start()
+        kept.start()
+
+    def end():
+        kept.wait()
+        for d in range(1, n):
+            land = view((me + n - d) % n)
+            remote(land, land, send.at[d], recv.at[d], e, z, c).wait_recv()
+            copy(d).wait_send()
+
+    return begin, end
+
+
+def scatter_sems(nz):
+    dma = pltpu.SemaphoreType.DMA
+    return [dma((2 * nz,)), dma((2 * nz,)), dma(())]
+
+
 def line_stream(nz, ref, out, zrecv, zsend, sib_recv, sib_send, own):
     e, z, c, _, _ = place()
 
@@ -739,8 +794,8 @@
 def fetch_kernel(
     nz,
     F, w_ref, s_ref, o_ref, t_ref, l_ref, p_ref, x_ref,
-    w_out, s_out, o_out, t_out, l_out, p_out, x_out,
-    wide, packed, wide_sem, packed_sem,
+    w_out, s_out, o_out, t_out, l_out, p_out, gate_out, up_out,
+    wide, gate, up, wide_sem, packed_sem,
     *sems,
 ):
     e, z, c, ex, ey = place()
@@ -813,10 +868,16 @@
     @pl.loop(0, wide.shape[0] // 16)
     def _(b):
         rows = pl.ds(pl.multiple_of(b * 16, 16), 16)
-        pack_rows(packed.shape[0], F, packed.shape[2] // 2, wide.at[rows, :], packed.at[:, rows, :])
-
-    packed_copy = pltpu.make_async_copy(packed, x_out, packed_sem)
-    packed_copy.start()
+        pack_rows(
+            gate.shape[0], F, gate.shape[2], wide.at[rows, :], gate.at[:, rows, :], up.at[:, rows, :]
+        )
+
+    packed_copies = [
+        pltpu.make_async_copy(a, b, packed_sem.at[n])
+        for n, (a, b) in enumerate(((gate, gate_out), (up, up_out)))
+    ]
+    for copy in packed_copies:
+        copy.start()
 
     blocks = 2 * nz - 1
     for s in range(1, blocks):
@@ -854,12 +915,13 @@
     def _():
         pltpu.make_async_copy(o_ref, o_out.at[c], own).wait()
 
-    packed_copy.wait()
+    for copy in packed_copies:
+        copy.wait()
 
 
 def fetch_weights(nz, columns, small, rows, tokens, lengths, block, wide, F):
     dma = pltpu.SemaphoreType.DMA
-    packed = (2 * nz, wide.shape[0], 2 * (-(-F // 128) * 128))
+    packed = (2 * nz, wide.shape[0], -(-F // 128) * 128)
     sd = jax.ShapeDtypeStruct
     return pl.pallas_call(
         functools.partial(fetch_kernel, nz, F),
@@ -871,11 +933,13 @@
             sd((4,) + lengths.shape, lengths.dtype),
             sd((nz, 2, 4) + block.shape, block.dtype),
             sd(packed, wide.dtype),
+            sd(packed, wide.dtype),
         ),
         in_specs=[ANY] * 7,
-        out_specs=(ANY,) * 7,
+        out_specs=(ANY,) * 8,
         scratch_shapes=[
-            pltpu.VMEM(wide.shape, wide.dtype), pltpu.VMEM(packed, wide.dtype), dma(()), dma(()),
+            pltpu.VMEM(wide.shape, wide.dtype), pltpu.VMEM(packed, wide.dtype),
+            pltpu.VMEM(packed, wide.dtype), dma(()), dma((2,)),
             *line_sems(nz), *line_sems(nz), *plane_sems(), *plane_sems(), *payload_sems(nz),
             dma((6,)), dma((2, 6)), dma((6,)), dma((6,)), dma(()),
         ],
@@ -971,8 +1035,9 @@
 
 def settle_kernel(
     nz,
-    g_ref, s_ref, o_ref, x_ref, y_ref,
-    g_out, s_out, o_out, x_out, y_out,
+    g_ref, s_ref, o_ref, x_ref, y_ref, v_ref,
+    g_out, s_out, o_out, x_out, y_out, v_out,
+    v_send, v_recv, v_own,
     x_held, x_send, x_recv, x_own, y_send, y_recv, y_own,
     g_mine, g_sib, g_z, s_mine, s_sib, s_z, o_mine, o_sib, o_z,
     load, sib_send, sib_recv, zsend, zrecv,
@@ -983,7 +1048,8 @@
     e, z, c, ex, ey = place()
     peers = (ex, ey, (ex + 2) % 4)
     dest = line_order(nz, z)
-    greet_cross(nz)
+    greet_shard(nz)
+    v_begin, v_end = scatter_stream(nz, v_ref, lambda i: v_out.at[i], v_send, v_recv, v_own)
     W = g_ref.shape[3]
     first = W // 256 * 128
     groups = (
@@ -1154,6 +1220,8 @@
                 o_flow(m)
         if n == turn:
             x_total()
+        if (k, i) == (1, nz - 2):
+            v_begin()
 
     @pl.when(z == e)
     def _():
@@ -1185,9 +1253,10 @@
                 zcopy(k, i).wait_send()
     for _, end in streams:
         end()
-
-
-def settle_weights(nz, grads, small, rows, near, blocks):
+    v_end()
+
+
+def settle_weights(nz, grads, small, rows, near, blocks, columns):
     R, W = grads.shape[2:]
     D = rows.shape[2]
     dma = pltpu.SemaphoreType.DMA
@@ -1202,10 +1271,12 @@
             sd((R, D), bf16),
             sd(near.shape[1:], f32),
             sd(blocks.shape, bf16),
+            sd(columns.shape, bf16),
         ),
-        in_specs=[ANY] * 5,
-        out_specs=(ANY,) * 3 + (pl.BlockSpec(memory_space=vm), ANY),
+        in_specs=[ANY] * 6,
+        out_specs=(ANY,) * 3 + (pl.BlockSpec(memory_space=vm), ANY, ANY),
         scratch_shapes=[
+            *scatter_sems(nz),
             vm(near.shape, bf16), *plane_sems(), *plane_sems(),
             vm((nz, R, W), bf16), vm((nz, R, W), bf16), vm((2, nz, R, W), bf16),
             vm((nz, R, Ws), bf16), vm((nz, R, Ws), bf16), vm((2, nz, R, Ws), bf16),
@@ -1220,7 +1291,7 @@
         ),
         cost_estimate=pl.CostEstimate(flops=10**6, bytes_accessed=10**6, transcendentals=0),
         name="settle_weights",
-    )(grads, small, rows, near, blocks)
+    )(grads, small, rows, near, blocks, columns)
 
 
 def pick_kernel(width, q_ref, k_ref, v_ref, o_ref):
@@ -1276,7 +1347,7 @@
     D = tokens.shape[1]
     if fast:
         width = D // 4
-        columns, full_small, rows, tokens, lengths, blocks, packed = fetch_weights(
+        columns, full_small, rows, tokens, lengths, blocks, *packed = fetch_weights(
             nz, pick_columns(weights, width), small, w_output, tokens, lengths, block, wide, F
         )
         columns, rows = columns.reshape(D, -1), rows.reshape(width, D)
@@ -1288,21 +1359,22 @@
     return columns, full[3], full[4], tokens[None], lengths[None], blocks, packed
 
 
-def settle(nz, fast, columns, rows, small, near, blocks):
+def settle(nz, fast, columns, rows, small, near, blocks, term):
     D, width = rows.shape[1], rows.shape[0]
     if fast:
         R = D // (2 * nz)
         parts = [x.astype(bf16).reshape(nz, 2, R, -1) for x in (columns, small)]
         near = near.astype(bf16).reshape(4, -1, D)
         blocks = blocks.reshape(4, -1, D)
-        sums, small, out, near, blocks = settle_weights(
-            nz, *parts, rows.astype(bf16).reshape(2, R, D), near, blocks
+        sums, small, out, near, blocks, term = settle_weights(
+            nz, *parts, rows.astype(bf16).reshape(2, R, D), near, blocks, term
         )
         small, blocks = jnp.sum(small.astype(f32), axis=0), blocks.reshape(-1, D)
-        return *assemble_columns(sums, width), out.astype(f32), small, near, blocks
+        return *assemble_columns(sums, width), out.astype(f32), small, near, blocks, term
     parts = [columns[:, i * width : (i + 1) * width] for i in range(3)] + [rows, small]
     blocks = lax.all_to_all(blocks, "expert", split_axis=0, concat_axis=0, tiled=True)
-    return [sum_shard(x) for x in parts] + [near, blocks]
+    term = lax.all_to_all(term, SHARD, split_axis=0, concat_axis=0, tiled=True)
+    return [sum_shard(x) for x in parts] + [near, blocks, term]
 
 
 def spread_plain(nz, blocks, collective):
@@ -1312,6 +1384,11 @@
             block = lax.all_gather(block, axis, axis=0)
         out.append(block)
     return out
+
+
+def spread_pair(nz, blocks, gate, up, collective):
+    gate = lax.all_to_all(gate, SHARD, split_axis=0, concat_axis=0, tiled=True)
+    return jnp.concatenate([gate, up], axis=2), *spread_plain(nz, blocks, collective)
 
 
 def collect_plain(nz, rows, notes, dots, T):
@@ -1423,8 +1500,7 @@
     gain_ffn = full_small[:, experts + 1].astype(f32)
 
     Fp = -(-F // 128) * 128
-    moved = lax.all_to_all(packed, SHARD, split_axis=0, concat_axis=0, tiled=True)
-    w_pair = moved.reshape(n_shard * R, 2 * Fp)
+    moved_up = lax.all_to_all(packed[1], SHARD, split_axis=0, concat_axis=0, tiled=True)
     down = jnp.pad(w_down.reshape(F, D), ((0, Fp - F), (0, 0)))
 
     B, H = near_tokens.shape[0], full_output.shape[0]
@@ -1483,8 +1559,9 @@
 
     notes = jnp.concatenate([gate_probs, target.astype(f32), jnp.zeros((T, 4), f32)], axis=1)
     notes = jnp.pad(jnp.transpose(notes), ((0, 0), (0, -T % 128)))
-    spread = spread_blocks if fast else spread_plain
-    all_normed, all_notes = spread(nz, (normed_mid_half, notes), 2)
+    spread = spread_blocks if fast else spread_pair
+    w_pair, all_normed, all_notes = spread(nz, (normed_mid_half, notes), packed[0], moved_up, 2)
+    w_pair = w_pair.reshape(n_shard * R, 2 * Fp)
     devices = n_shard * n_exp
     flat_notes = all_notes.reshape(devices, 8, -1)[:, :, :T]
     wanted = (e_index * capacity + jnp.arange(capacity)).astype(f32)
@@ -1519,27 +1596,25 @@
     token_dots = jnp.stack(token_dots, axis=1).reshape(nz, 2, n_exp, 2, T)
     token_dots = jnp.pad(token_dots, ((0, 0),) * 3 + ((0, 6), (0, -T % 128)))
     act_grad = grad_scale * raw_grad
-    pre_grad = jnp.concatenate(
-        [
-            act_grad * up_part * sigmoid_gate * (1.0 + gate_part * (1.0 - sigmoid_gate)),
-            act_grad * silu_gate,
-        ],
-        axis=1,
-    ).astype(bf16)
+    gate_grads = act_grad * up_part * sigmoid_gate * (1.0 + gate_part * (1.0 - sigmoid_gate))
+    gate_grads, up_grads = gate_grads.astype(bf16), (act_grad * silu_gate).astype(bf16)
+    pre_grad = jnp.concatenate([gate_grads, up_grads], axis=1)
     in_rows = dot_dims(pre_grad, w_pair, 1, 1).astype(bf16)
     scaled = (grad_scale * activated.astype(f32)).astype(bf16)
     grad_w_down = lined_up(dot_dims(scaled[:, :F], cotangent_rows, 0, 0))
-    in_term = dot_dims(arrived, pre_grad, 0, 0).astype(bf16).reshape(n_shard, R, 2 * Fp)
-    in_rows, in_term, grad_w_down = lax.optimization_barrier((in_rows, in_term, grad_w_down))
+    gate_term, up_term = [
+        dot_dims(arrived, x, 0, 0).astype(bf16).reshape(n_shard, R, Fp)
+        for x in (gate_grads, up_grads)
+    ]
+    in_rows, up_term = lax.optimization_barrier((in_rows, up_term))
     in_rows = in_rows.reshape(nz, 2, n_exp, capacity, D)
     collect = collect_rows if fast else collect_plain
     normed_mid_grad, gate_grad = collect(nz, in_rows, all_notes, token_dots, T)
     gate_grad = jnp.transpose(gate_grad[:2, :T])
-    in_term, normed_mid_grad, out_sum = lax.optimization_barrier(
-        (in_term, normed_mid_grad, out_sum)
-    )
-    in_term = lax.all_to_all(in_term, SHARD, split_axis=0, concat_axis=0, tiled=True)
-    grad_w_in = unpack_columns(in_term, F)
+    up_term, normed_mid_grad, out_sum = lax.optimization_barrier(
+        (up_term, normed_mid_grad, out_sum)
+    )
+    up_term = lax.all_to_all(up_term, SHARD, split_axis=0, concat_axis=0, tiled=True)
 
     upstream = cotangent.astype(f32)
     chosen_grad = gate_probs * (gate_grad - jnp.sum(gate_probs * gate_grad, axis=-1, keepdims=True))
@@ -1586,9 +1661,11 @@
         [router_grad, gain_attn_grad[:, None], gain_ffn_grad[:, None]], axis=1
     )
     small_grad = jnp.pad(small_grad, ((0, 0), (0, 128 - small_grad.shape[1])))
-    sum_query, sum_key, sum_value, sum_output, small_sum, normed_in_grad, back = settle(
-        nz, fast, qkv_weight_grad, output_grad, small_grad, near_grad, out_sum
-    )
+    small_grad, up_term = lax.optimization_barrier((small_grad, up_term))
+    sum_query, sum_key, sum_value, sum_output, small_sum, normed_in_grad, back, gate_term = settle(
+        nz, fast, qkv_weight_grad, output_grad, small_grad, near_grad, out_sum, gate_term
+    )
+    grad_w_in = unpack_columns(gate_term, up_term, F)
     mixture = gate_probs[:, 0:1] * dot32(pick[0], back) + gate_probs[:, 1:2] * dot32(pick[1], back)
     activations = (residual_mid + branch_scale * mixture).astype(bf16)
     in_norm_grad = rms_backward(residual_in, inverse_in, gain_attn, normed_in_grad)[0]

time: 1050 us -> 1050 us (level)
  local copies, waits for them, and re-layouts: 67.1 us -> 48.5 us
  waiting for transfers between devices: 0.04 us -> 15.9 us
    all_to_all x2, waiting for transfers between devices: 0.01 us -> 15.9 us  [the longest x1 12.1 us: on_device(): lax.all_to_all(up_term, SHARD, split_axis=0, concat_axis=0, tiled=True)]
    pallas_call x2, Pallas kernels: 175 us -> 161 us  [the longest x1 146 us: spread_blocks(): pl.pallas_call(functools.partial(spread_kernel, nz, splits), out_shape=(p...]
    convert_element_type x1 -> x2, other arithmetic: 5.5 us -> 17.6 us  [the longest x1 12.1 us: on_device(): gate_grads.astype(bf16)]
    unnamed x183 -> x167, local copies, waits for them, and re-layouts: 34.3 us -> 22.2 us
    dot_general x8 -> x9, matrix products: 107 us -> 109 us  [dot_dims(): lax.dot_general(a, b, (((da,), (db,)), ((), ())), preferred_element_type=...]
  transfers between devices with their start and end apart: 3 -> 3, of which waited for: 0 -> 2; matrix products, arithmetic and copies ran while one was open for 21% -> 18% of each run, Pallas kernels for 52% -> 16%
where the time goes in v8:
time: 1050 us; the launch traced here: 1040 us
  Pallas kernels  697 us (66%)
  matrix products  194 us (18%)
  local copies, waits for them, and re-layouts  48.5 us (5%)
  other arithmetic  37 us (4%)
  starting transfers between devices  31 us (3%)
  waiting for transfers between devices  15.9 us (2%)
  between operations  15.6 us (1%)
    pallas_call x1, Pallas kernels, settle_weights(): pl.pallas_call(functools.partial(settle_kernel, nz), out_shape=(sd((4, R,...  212 us
    pallas_call x1, Pallas kernels, fetch_weights(): pl.pallas_call(functools.partial(fetch_kernel, nz, F), out_shape=(sd((nz,...  148 us
    pallas_call x1, Pallas kernels, spread_blocks(): pl.pallas_call(functools.partial(spread_kernel, nz, splits), out_shape=(p...  146 us
    dot_general x9, matrix products, dot_dims(): lax.dot_general(a, b, (((da,), (db,)), ((), ())), preferred_element_type=...  109 us
    pallas_call x1, Pallas kernels, collect_rows(): pl.pallas_call(functools.partial(collect_kernel, nz, cap), out_shape=(jax...  95.6 us
    dot_general x8, matrix products, dot32(): return jnp.dot(a, b, preferred_element_type=f32)  53.2 us
    pallas_call x1, Pallas kernels, plane_sum(): pl.pallas_call(plane_sum_kernel, out_shape=jax.ShapeDtypeStruct(x.shape[1...  29.7 us
    pallas_call x1, Pallas kernels, plane_gather(): pl.pallas_call(plane_gather_kernel, out_shape=jax.ShapeDtypeStruct((4,) +...  29.3 us
  transfers between devices with their start and end apart: 3, of which 2 were waited for; matrix products, arithmetic and copies ran while one was open for 18% of the time, Pallas kernels for 16%

profile of v8, /device:TPU:16, one launch (start us, length us, event | category | flops | bytes accessed | tf_op | source)
XLA Modules:
  0.0 1038.7 jit_solution(17138340063298655768)
XLA Ops:
  20.8 148.4 %fetch_weights.1 = (bf16[4,2,288,1792]{3,2,1,0:T(8,128)(2,1)}, bf16[4,2,288,128]{3,2,1,0:T(8,128)(2,1)S(1)}, bf16[2,288,2304]{2,1,0:T(8,128)(2,1)S(1)}, bf16[4,1...) custom-call(bf16[288,1792]{1,0:T(8,128)(2,1)S(1)} %copy-done.12, ...), custom_call_target="tpu_custom_call" | custom-call | flops 99999997952 | bytes 4128768 | tf_op jit(solution)/shard_map/fetch_weights/pallas_call | solution.py:926
  174.3 26.2 %all-to-all-start = ((bf16[8,288,768]{2,1,0:T(8,128)(2,1)}), bf16[8,288,768]{2,1,0:T(8,128)(2,1)}, u32[]{:S(2)}, u32[]{:S(2)}) async-start(bf16[8,288,768]{2,1,0:T(8,128)(2,1)} %copy-done.7), calls=%async_computation | async-start | bytes 7077888 | tf_op jit(solution)/shard_map/all_to_all | solution.py:1503
  206.3 7.8 fusion.85
  240.0 29.7 %plane_sum.1 = f32[128,2304]{1,0:T(8,128)} custom-call(bf16[4,128,2304]{2,1,0:T(8,128)(2,1)} %bitcast.165), custom_call_target="tpu_custom_call" | custom-call | flops 1000000 | bytes 1000000 | tf_op jit(solution)/shard_map/plane_sum/pallas_call | solution.py:1024
  277.2 145.6 %spread_blocks.1 = (bf16[8,288,1536]{2,1,0:T(8,128)(2,1)}, bf16[4,2,4,128,2304]{4,3,2,1,0:T(8,128)(2,1)}, f32[4,2,4,8,128]{4,3,2,1,0:T(8,128)}) custom-call(bf16[8,288,768]{2,1,0:T(8,128)(2,1)} %copy-done.6, bf16[8,288,768]{2,1,0:T(8,128)(2,1)} %all-to-all-done.refs_1_, bf16[128,2304]{1,0:T(8,128)(2,1)} %copy-done.24, f32[8,128]{1,0:T(8,128)} %maximum_bitcast_fusion.refs_3_), custom_call_target="tpu_custom_call" | custom-call | flops 1000000 | bytes 1000000 | tf_op jit(solution)/shard_map/spread_blocks/pallas_call | solution.py:249
  424.1 10.9 %convolution_convert_fusion.3 = bf16[32,80,2304]{2,1,0:T(8,128)(2,1)} fusion(bf16[32,128,2304]{2,1,0:T(8,128)(2,1)} %bitcast.155, f32[32,128]{1,0:T(8,128)S(1)} %bitcast.190, f32[32,128]{1,0:T(8,128)S(1)} %bitcast.193, f32[80]{0:T(128)S(1)} %add_convert_fusion.4), kind=kOutput, calls=%fused_computation.3 | convolution fusion | flops 1516830720 | bytes 30703936 | tf_op jit(solution)/shard_map/spt,std->spd/dot_general | solution.py:1450
  435.0 24.0 %fusion.86 = f32[2560,1536]{0,1:T(8,128)S(1)} fusion(bf16[2560,2304]{1,0:T(8,128)(2,1)} %bitcast.156, bf16[2304,1536]{1,0:T(8,128)(2,1)} %bitcast.203), kind=kOutput, calls=%fused_computation.191 | convolution fusion | flops 18119393280 | bytes 34603008 | tf_op jit(solution)/shard_map/dot_general | solution.py:1442
  468.9 13.9 %convolution_convert_fusion = bf16[2560,2304]{1,0:T(8,128)(2,1)} fusion(bf16[2560,768]{0,1:T(8,128)(2,1)} %get-tuple-element.134, bf16[720,2304]{1,0:T(8,128)(2,1)S(1)} %bitcast.205), kind=kOutput, calls=%fused_computation | convolution fusion | flops 9065594880 | bytes 19046400 | tf_op jit(solution)/shard_map/dot_general | solution.py:1442
  484.7 14.1 %convolution_convert_fusion.4 = bf16[32,80,2304]{2,1,0:T(8,128)(2,1)} fusion(bf16[32,128,2304]{2,1,0:T(8,128)(2,1)} %bitcast.154, f32[32,128]{1,0:T(8,128)S(1)} %bitcast.191, f32[32,128]{1,0:T(8,128)S(1)} %bitcast.194, f32[80]{0:T(128)S(1)} %add_convert_fusion.4), kind=kOutput, calls=%fused_computation.4 | convolution fusion | flops 1516830720 | bytes 30703936 | tf_op jit(solution)/shard_map/spt,std->spd/dot_general | solution.py:1450
  498.8 14.4 %multiply_reduce_fusion = (f32[2560]{0:T(1024)S(1)}, f32[2560,768]{0,1:T(8,128)}) fusion(bf16[2560,768]{0,1:T(8,128)(2,1)S(1)} %copy-done.31, bf16[2560,2304]{1,0:T(8,128)(2,1)} %bitcast.161, bf16[720,2304]{1,0:T(8,128)(2,1)S(1)} %bitcast.206), kind=kOutput, calls=%fused_computation.8 | convolution fusion | flops 9065592832 | bytes 26920960 | tf_op jit(solution)/shard_map/dot_general | solution.py:1446
  514.7 16.3 %fusion.15.x_ref = f32[720,2304]{1,0:T(8,128)} fusion(bf16[2560,2304]{1,0:T(8,128)(2,1)} %bitcast.162, f32[2560,768]{0,1:T(8,128)} %get-tuple-element.133, f32[2560]{0:T(1024)S(1)} %mul.469), kind=kOutput, calls=%fused_computation.37 | convolution fusion | flops 8497152000 | bytes 25815040 | tf_op jit(solution)/shard_map/dot_general | solution.py:1446
  531.0 9.4 lined_up.1
  540.4 12.1 %multiply_convert_fusion.2 = (bf16[2560,768]{0,1:T(8,128)(2,1)}, bf16[2560,768]{0,1:T(8,128)(2,1)S(1)}) fusion(f32[2560,1536]{0,1:T(8,128)} %copy-done.16, f32[2560,768]{0,1:T(8,128)} %get-tuple-element.180, f32[2560]{0:T(1024)S(1)} %mul.469), kind=kLoop, calls=%fused_computation.11 | loop fusion | flops 27525120 | bytes 31467520 | tf_op jit(solution)/shard_map/convert_element_type | solution.py:1600
  552.5 11.3 %convolution_convert_fusion.6 = bf16[2304,768]{1,0:T(8,128)(2,1)} fusion(bf16[2560,2304]{1,0:T(8,128)(2,1)S(1)} %bitcast.160, bf16[2560,768]{0,1:T(8,128)(2,1)S(1)} %get-tuple-element.140), kind=kOutput, calls=%fused_computation.17 | convolution fusion | flops 9061466112 | bytes 19267584 | tf_op jit(solution)/shard_map/dot_general | solution.py:1446
  563.9 25.3 %convolution_convert_fusion.1 = bf16[2560,2304]{1,0:T(8,128)(2,1)} fusion(bf16[2304,1536]{1,0:T(8,128)(2,1)} %bitcast.204, bf16[2560,768]{0,1:T(8,128)(2,1)} %copy-done.33, bf16[2560,768]{0,1:T(8,128)(2,1)} %get-tuple-element.139), kind=kOutput, calls=%fused_computation.1 | convolution fusion | flops 18141020160 | bytes 26738688 | tf_op jit(solution)/shard_map/dot_general | solution.py:1446
  590.0 95.6 %collect_rows.1 = (f32[128,2304]{1,0:T(8,128)}, f32[8,128]{1,0:T(8,128)}) custom-call(bf16[4,2,4,80,2304]{4,3,2,1,0:T(8,128)(2,1)} %bitcast.164, f32[4,2,4,8,128]{4,3,2,1,0:T(8,128)} %get-tuple-element.47.notes_ref, f32[4,2,4,8,128]{4,3,2,1,0:T(8,128)} %select_maximum_fusion.2.dots_ref), custom_call_target="tpu_custom_call" | custom-call | flops 1000000 | bytes 1000000 | tf_op jit(solution)/shard_map/collect_rows/pallas_call | solution.py:487
  687.5 13.7 %convolution_convert_fusion.5 = bf16[2304,768]{1,0:T(8,128)(2,1)} fusion(bf16[2560,2304]{1,0:T(8,128)(2,1)} %bitcast.157, bf16[2560,768]{0,1:T(8,128)(2,1)S(1)} %copy-done.32), kind=kOutput, calls=%fused_computation.16 | convolution fusion | flops 9061466112 | bytes 19267584 | tf_op jit(solution)/shard_map/dot_general | solution.py:1446
  709.6 29.3 %plane_gather.1 = bf16[4,128,2304]{2,1,0:T(8,128)(2,1)} custom-call(bf16[128,2304]{1,0:T(8,128)(2,1)} %multiply_convert_fusion.4.x_ref), custom_call_target="tpu_custom_call" | custom-call | flops 1000000 | bytes 1000000 | tf_op jit(solution)/shard_map/plane_gather/pallas_call | solution.py:975
  748.4 10.8 %fusion.78 = (bf16[512,2304]{1,0:T(8,128)(2,1)}, bf16[2304]{0:T(1024)(128)(2,1)S(1)}, bf16[512,2304]{1,0:T(8,128)(2,1)S(1)}) fusion(f32[512]{0:T(512)S(1)} %copy-done.73, bf16[4,128,2304]{2,1,0:T(8,128)(2,1)S(1)} %copy-done.1, f32[2304]{0:T(1024)S(1)} %copy-done.57, bf16[2304,1792]{1,0:T(8,128)(2,1)} %bitcast.208, bf16[512,576]{0,1:T(8,128)(2,1)S(1)} %bitcast.188, ...), kind=kOutput, calls=%fused_computation.183 | convolution fusion | flops 4244633344 | bytes 17124352 | tf_op jit(solution)/shard_map/dot_general | solution.py:1446
  762.6 10.0 convolution_convert_fusion.2
  772.6 12.1 %all-to-all-done.1.up_ref = bf16[8,288,768]{2,1,0:T(8,128)(2,1)} async-done(((bf16[8,288,768]{2,1,0:T(8,128)(2,1)}), bf16[8,288,768]{2,1,0:T(8,128)(2,1)}, u32[]{:S(2)}, u32[]{:S(2)}) %all-to-all-start.1) | async-done | bytes 3538976 | tf_op jit(solution)/shard_map/all_to_all | solution.py:1617
  785.7 212.3 %settle_weights.1 = (bf16[4,288,1792]{2,1,0:T(8,128)(2,1)}, bf16[4,288,128]{2,1,0:T(8,128)(2,1)}, bf16[288,2304]{1,0:T(8,128)(2,1)}, f32[128,2304]{1,0:T(8,128)}...) custom-call(bf16[4,2,288,1792]{3,2,1,0:T(8,128)(2,1)} %bitcast.166, bf16[4,2,288,128]{3,2,1,0:T(8,128)(2,1)} %bitcast.174, ...), custom_call_target="tpu_custom_call" | custom-call | flops 1000000 | bytes 1000000 | tf_op jit(solution)/shard_map/settle_weights/pallas_call | solution.py:1266
  998.0 8.2 assemble_columns.1
  1010.9 15.1 %unpack_columns.1 = f32[25920,128]{1,0:T(8,128)} custom-call(bf16[8,288,768]{2,1,0:T(8,128)(2,1)} %get-tuple-element.67.gate_ref, bf16[8,288,768]{2,1,0:T(8,128)(2,1)} %all-to-all-done.1.up_ref), custom_call_target="tpu_custom_call" | custom-call | tf_op jit(solution)/shard_map/unpack_columns/pallas_call | solution.py:573
  (271 shorter events, 106.7 us)
Async XLA Ops:
  174.3 31.4 %copy-start = (bf16[4,128,2304]{2,1,0:T(8,128)(2,1)}, bf16[4,128,2304]{2,1,0:T(8,128)(2,1)S(1)}, u32[]{:S(2)}) copy-start(bf16[4,128,2304]{2,1,0:T(8,128)(2,1)S(1)} %get-tuple-element.40) | copy-start | bytes 7077892
  174.3 97.8 %copy-start.2 = (bf16[4,2,288,128]{3,2,1,0:T(8,128)(2,1)}, bf16[4,2,288,128]{3,2,1,0:T(8,128)(2,1)S(1)}, u32[]{:S(2)}) copy-start(bf16[4,2,288,128]{3,2,1,0:T(8,128)(2,1)S(1)} %get-tuple-element.41) | copy-start | bytes 1769476
  174.3 102.9 %all-to-all-start = ((bf16[8,288,768]{2,1,0:T(8,128)(2,1)}), bf16[8,288,768]{2,1,0:T(8,128)(2,1)}, u32[]{:S(2)}, u32[]{:S(2)}) async-start(bf16[8,288,768]{2,1,0:T(8,128)(2,1)} %copy-done.7), calls=%async_computation | async-start | bytes 7077888 | tf_op jit(solution)/shard_map/all_to_all | solution.py:1503
  200.5 500.6 %reduce-scatter.2.cloned.1.call-start = ((), (), s32[]{:S(2)}) async-start(), calls=%async_computation.3 | async-start | bytes 13271040 | tf_op jit(solution)/shard_map/reduce_scatter | solution.py:1588
  272.5 150.3 %copy-start.58 = (f32[128,2]{0,1:T(2,128)}, f32[128,2]{0,1:T(2,128)S(1)}, u32[]{:S(2)}) copy-start(f32[128,2]{0,1:T(2,128)S(1)} %select_reduce_fusion.1) | copy-start | bytes 3076
  272.6 150.2 %copy-start.62 = (f32[128]{0:T(128)}, f32[128]{0:T(128)S(1)}, u32[]{:S(2)}) copy-start(f32[128]{0:T(128)S(1)} %reduce_max.19) | copy-start | bytes 1540
  272.7 150.1 %copy-start.64 = (f32[128]{0:T(128)}, f32[128]{0:T(128)S(1)}, u32[]{:S(2)}) copy-start(f32[128]{0:T(128)S(1)} %fusion.67) | copy-start | bytes 1540
  484.7 14.1 %copy-start.31 = (bf16[2560,768]{0,1:T(8,128)(2,1)S(1)}, bf16[2560,768]{0,1:T(8,128)(2,1)}, u32[]{:S(2)}) copy-start(bf16[2560,768]{0,1:T(8,128)(2,1)} %get-tuple-element.134) | copy-start | bytes 11796484
  531.0 21.5 %slice-start = ((s8[11796480]{0:T(1024)(128)(4,1)}), s8[3407872]{0:T(1024)(128)(4,1)S(1)}, s32[]{:S(2)}) async-start(s8[11796480]{0:T(1024)(128)(4,1)} %bitcast.158), calls=%async_computation.4 | async-start | bytes 6815744
  589.9 95.7 %copy-start.59 = (f32[128,2]{0,1:T(2,128)S(1)}, f32[128,2]{0,1:T(2,128)}, u32[]{:S(2)}) copy-start(f32[128,2]{0,1:T(2,128)} %copy-done.58) | copy-start | bytes 3076
  589.9 95.7 %copy-start.63 = (f32[128]{0:T(128)S(1)}, f32[128]{0:T(128)}, u32[]{:S(2)}) copy-start(f32[128]{0:T(128)} %copy-done.62) | copy-start | bytes 1540
  589.9 95.7 %copy-start.65 = (f32[128]{0:T(128)S(1)}, f32[128]{0:T(128)}, u32[]{:S(2)}) copy-start(f32[128]{0:T(128)} %copy-done.64) | copy-start | bytes 1540
  589.9 97.1 %copy-start.61 = (s32[128,2]{0,1:T(2,128)S(1)}, s32[128,2]{0,1:T(2,128)}, u32[]{:S(2)}) copy-start(s32[128,2]{0,1:T(2,128)} %param.15) | copy-start | bytes 3076
  589.9 97.1 %copy-start.25 = (bf16[128,2304]{1,0:T(8,128)(2,1)S(1)}, bf16[128,2304]{1,0:T(8,128)(2,1)}, u32[]{:S(2)}) copy-start(bf16[128,2304]{1,0:T(8,128)(2,1)} %copy-done.24) | copy-start | bytes 1769476
  589.9 97.5 %copy-start.32 = (bf16[2560,768]{0,1:T(8,128)(2,1)S(1)}, bf16[2560,768]{0,1:T(8,128)(2,1)}, u32[]{:S(2)}) copy-start(bf16[2560,768]{0,1:T(8,128)(2,1)} %get-tuple-element.139) | copy-start | bytes 11796484
  687.4 13.7 %copy-start.3 = (bf16[4,2,288,128]{3,2,1,0:T(8,128)(2,1)S(1)}, bf16[4,2,288,128]{3,2,1,0:T(8,128)(2,1)}, u32[]{:S(2)}) copy-start(bf16[4,2,288,128]{3,2,1,0:T(8,128)(2,1)} %copy-done.2) | copy-start | bytes 1769476
  687.4 13.7 %copy-start.18 = (f32[128,2304]{1,0:T(8,128)S(1)}, f32[128,2304]{1,0:T(8,128)}, u32[]{:S(2)}) copy-start(f32[128,2304]{1,0:T(8,128)} %copy-done.17) | copy-start | bytes 3538948
  687.5 13.7 %copy-start.53 = (f32[2304]{0:T(1024)S(1)}, f32[2304]{0:T(1024)}, u32[]{:S(2)}) copy-start(f32[2304]{0:T(1024)} %copy-done.52) | copy-start | bytes 27652
  687.5 13.7 %copy-start.67 = (f32[128]{0:T(128)S(1)}, f32[128]{0:T(128)}, u32[]{:S(2)}) copy-start(f32[128]{0:T(128)} %copy-done.66) | copy-start | bytes 1540
  703.5 81.2 %all-to-all-start.1 = ((bf16[8,288,768]{2,1,0:T(8,128)(2,1)}), bf16[8,288,768]{2,1,0:T(8,128)(2,1)}, u32[]{:S(2)}, u32[]{:S(2)}) async-start(bf16[8,288,768]{2,1,0:T(8,128)(2,1)} %bitcast.170), calls=%async_computation.2 | async-start | bytes 7077888 | tf_op jit(solution)/shard_map/all_to_all | solution.py:1617
  708.3 30.6 %copy-start.74 = (f32[128]{0:T(128)}, f32[128]{0:T(128)S(1)}, u32[]{:S(2)}) copy-start(f32[128]{0:T(128)S(1)} %broadcast_multiply_fusion.3) | copy-start | bytes 1540
  709.6 29.3 %copy-start.9 = (bf16[2,288,2304]{2,1,0:T(8,128)(2,1)S(1)}, bf16[2,288,2304]{2,1,0:T(8,128)(2,1)}, u32[]{:S(2)}) copy-start(bf16[2,288,2304]{2,1,0:T(8,128)(2,1)} %copy-done.8) | copy-start | bytes 7962628
  1010.9 15.2 %copy-start.19 = (f32[128,2304]{1,0:T(8,128)S(1)}, f32[128,2304]{1,0:T(8,128)}, u32[]{:S(2)}) copy-start(f32[128,2304]{1,0:T(8,128)} %copy-done.17) | copy-start | bytes 3538948
  1010.9 15.2 %copy-start.23 = (f32[128,2304]{1,0:T(8,128)S(1)}, f32[128,2304]{1,0:T(8,128)}, u32[]{:S(2)}) copy-start(f32[128,2304]{1,0:T(8,128)} %copy-done.22) | copy-start | bytes 3538948
  (59 other events, 202.6 us)
Sparse Core Ops, SparseCore 0:
  483.0 121.9 reduce-scatter.1

commit v9 on v8

--- a/solution.py
+++ b/solution.py
@@ -1035,9 +1035,8 @@
 
 def settle_kernel(
     nz,
-    g_ref, s_ref, o_ref, x_ref, y_ref, v_ref,
-    g_out, s_out, o_out, x_out, y_out, v_out,
-    v_send, v_recv, v_own,
+    g_ref, s_ref, o_ref, x_ref, y_ref,
+    g_out, s_out, o_out, x_out, y_out,
     x_held, x_send, x_recv, x_own, y_send, y_recv, y_own,
     g_mine, g_sib, g_z, s_mine, s_sib, s_z, o_mine, o_sib, o_z,
     load, sib_send, sib_recv, zsend, zrecv,
@@ -1048,8 +1047,7 @@
     e, z, c, ex, ey = place()
     peers = (ex, ey, (ex + 2) % 4)
     dest = line_order(nz, z)
-    greet_shard(nz)
-    v_begin, v_end = scatter_stream(nz, v_ref, lambda i: v_out.at[i], v_send, v_recv, v_own)
+    greet_cross(nz)
     W = g_ref.shape[3]
     first = W // 256 * 128
     groups = (
@@ -1220,8 +1218,6 @@
                 o_flow(m)
         if n == turn:
             x_total()
-        if (k, i) == (1, nz - 2):
-            v_begin()
 
     @pl.when(z == e)
     def _():
@@ -1253,10 +1249,9 @@
                 zcopy(k, i).wait_send()
     for _, end in streams:
         end()
-    v_end()
-
-
-def settle_weights(nz, grads, small, rows, near, blocks, columns):
+
+
+def settle_weights(nz, grads, small, rows, near, blocks):
     R, W = grads.shape[2:]
     D = rows.shape[2]
     dma = pltpu.SemaphoreType.DMA
@@ -1271,12 +1266,10 @@
             sd((R, D), bf16),
             sd(near.shape[1:], f32),
             sd(blocks.shape, bf16),
-            sd(columns.shape, bf16),
         ),
-        in_specs=[ANY] * 6,
-        out_specs=(ANY,) * 3 + (pl.BlockSpec(memory_space=vm), ANY, ANY),
+        in_specs=[ANY] * 5,
+        out_specs=(ANY,) * 3 + (pl.BlockSpec(memory_space=vm), ANY),
         scratch_shapes=[
-            *scatter_sems(nz),
             vm(near.shape, bf16), *plane_sems(), *plane_sems(),
             vm((nz, R, W), bf16), vm((nz, R, W), bf16), vm((2, nz, R, W), bf16),
             vm((nz, R, Ws), bf16), vm((nz, R, Ws), bf16), vm((2, nz, R, Ws), bf16),
@@ -1291,7 +1284,7 @@
         ),
         cost_estimate=pl.CostEstimate(flops=10**6, bytes_accessed=10**6, transcendentals=0),
         name="settle_weights",
-    )(grads, small, rows, near, blocks, columns)
+    )(grads, small, rows, near, blocks)
 
 
 def pick_kernel(width, q_ref, k_ref, v_ref, o_ref):
@@ -1359,22 +1352,21 @@
     return columns, full[3], full[4], tokens[None], lengths[None], blocks, packed
 
 
-def settle(nz, fast, columns, rows, small, near, blocks, term):
+def settle(nz, fast, columns, rows, small, near, blocks):
     D, width = rows.shape[1], rows.shape[0]
     if fast:
         R = D // (2 * nz)
         parts = [x.astype(bf16).reshape(nz, 2, R, -1) for x in (columns, small)]
         near = near.astype(bf16).reshape(4, -1, D)
         blocks = blocks.reshape(4, -1, D)
-        sums, small, out, near, blocks, term = settle_weights(
-            nz, *parts, rows.astype(bf16).reshape(2, R, D), near, blocks, term
+        sums, small, out, near, blocks = settle_weights(
+            nz, *parts, rows.astype(bf16).reshape(2, R, D), near, blocks
         )
         small, blocks = jnp.sum(small.astype(f32), axis=0), blocks.reshape(-1, D)
-        return *assemble_columns(sums, width), out.astype(f32), small, near, blocks, term
+        return *assemble_columns(sums, width), out.astype(f32), small, near, blocks
     parts = [columns[:, i * width : (i + 1) * width] for i in range(3)] + [rows, small]
     blocks = lax.all_to_all(blocks, "expert", split_axis=0, concat_axis=0, tiled=True)
-    term = lax.all_to_all(term, SHARD, split_axis=0, concat_axis=0, tiled=True)
-    return [sum_shard(x) for x in parts] + [near, blocks, term]
+    return [sum_shard(x) for x in parts] + [near, blocks]
 
 
 def spread_plain(nz, blocks, collective):
@@ -1606,15 +1598,16 @@
         dot_dims(arrived, x, 0, 0).astype(bf16).reshape(n_shard, R, Fp)
         for x in (gate_grads, up_grads)
     ]
-    in_rows, up_term = lax.optimization_barrier((in_rows, up_term))
+    gate_term, up_term = lax.optimization_barrier((gate_term, up_term))
+    up_term = lax.all_to_all(up_term, SHARD, split_axis=0, concat_axis=0, tiled=True)
     in_rows = in_rows.reshape(nz, 2, n_exp, capacity, D)
     collect = collect_rows if fast else collect_plain
     normed_mid_grad, gate_grad = collect(nz, in_rows, all_notes, token_dots, T)
     gate_grad = jnp.transpose(gate_grad[:2, :T])
-    up_term, normed_mid_grad, out_sum = lax.optimization_barrier(
-        (up_term, normed_mid_grad, out_sum)
-    )
-    up_term = lax.all_to_all(up_term, SHARD, split_axis=0, concat_axis=0, tiled=True)
+    up_term, normed_mid_grad, out_sum, gate_term = lax.optimization_barrier(
+        (up_term, normed_mid_grad, out_sum, gate_term)
+    )
+    gate_term = lax.all_to_all(gate_term, SHARD, split_axis=0, concat_axis=0, tiled=True)
 
     upstream = cotangent.astype(f32)
     chosen_grad = gate_probs * (gate_grad - jnp.sum(gate_probs * gate_grad, axis=-1, keepdims=True))
@@ -1661,9 +1654,9 @@
         [router_grad, gain_attn_grad[:, None], gain_ffn_grad[:, None]], axis=1
     )
     small_grad = jnp.pad(small_grad, ((0, 0), (0, 128 - small_grad.shape[1])))
-    small_grad, up_term = lax.optimization_barrier((small_grad, up_term))
-    sum_query, sum_key, sum_value, sum_output, small_sum, normed_in_grad, back, gate_term = settle(
-        nz, fast, qkv_weight_grad, output_grad, small_grad, near_grad, out_sum, gate_term
+    small_grad, gate_term = lax.optimization_barrier((small_grad, gate_term))
+    sum_query, sum_key, sum_value, sum_output, small_sum, normed_in_grad, back = settle(
+        nz, fast, qkv_weight_grad, output_grad, small_grad, near_grad, out_sum
     )
     grad_w_in = unpack_columns(gate_term, up_term, F)
     mixture = gate_probs[:, 0:1] * dot32(pick[0], back) + gate_probs[:, 1:2] * dot32(pick[1], back)

time: 1050 us -> 1010 us (0.962)
  Pallas kernels: 697 us -> 647 us
    pallas_call x1, Pallas kernels: 212 us -> 156 us  [settle_weights(): pl.pallas_call(functools.partial(settle_kernel, nz), out_shape=(sd((4, R,...]
    all_to_all x0 -> x1, waiting for transfers between devices: none -> 12.2 us  [on_device(): lax.all_to_all(gate_term, SHARD, split_axis=0, concat_axis=0, tiled=True)]
    all_to_all x1, waiting for transfers between devices: 12.1 us -> 0.01 us  [on_device(): lax.all_to_all(up_term, SHARD, split_axis=0, concat_axis=0, tiled=True)]
  transfers between devices with their start and end apart: 3 -> 4, of which waited for: 2 -> 2; matrix products, arithmetic and copies ran while one was open for 18% -> 19% of each run, Pallas kernels for 16% -> 17%
where the time goes in v9:
time: 1010 us; the launch traced here: 996 us
  Pallas kernels  647 us (64%)
  matrix products  197 us (20%)
  local copies, waits for them, and re-layouts  48.1 us (5%)
  starting transfers between devices  37.9 us (4%)
  other arithmetic  34.9 us (3%)
  waiting for transfers between devices  16.3 us (2%)
  between operations  15.4 us (2%)
    pallas_call x1, Pallas kernels, settle_weights(): pl.pallas_call(functools.partial(settle_kernel, nz), out_shape=(sd((4, R,...  156 us
    pallas_call x1, Pallas kernels, fetch_weights(): pl.pallas_call(functools.partial(fetch_kernel, nz, F), out_shape=(sd((nz,...  148 us
    pallas_call x1, Pallas kernels, spread_blocks(): pl.pallas_call(functools.partial(spread_kernel, nz, splits), out_shape=(p...  146 us
    dot_general x9, matrix products, dot_dims(): lax.dot_general(a, b, (((da,), (db,)), ((), ())), preferred_element_type=...  111 us
    pallas_call x1, Pallas kernels, collect_rows(): pl.pallas_call(functools.partial(collect_kernel, nz, cap), out_shape=(jax...  102 us
    dot_general x8, matrix products, dot32(): return jnp.dot(a, b, preferred_element_type=f32)  53.2 us
    pallas_call x1, Pallas kernels, plane_sum(): pl.pallas_call(plane_sum_kernel, out_shape=jax.ShapeDtypeStruct(x.shape[1...  29.7 us
    dot_general x8, matrix products, ein32(): return jnp.einsum(spec, a, b, preferred_element_type=f32)  29.5 us
  transfers between devices with their start and end apart: 4, of which 2 were waited for; matrix products, arithmetic and copies ran while one was open for 19% of the time, Pallas kernels for 17%

profile of v9, /device:TPU:16, one launch (start us, length us, event | category | flops | bytes accessed | tf_op | source)
XLA Modules:
  0.0 996.5 jit_solution(8622323916128914608)
XLA Ops:
  20.8 148.4 %fetch_weights.1 = (bf16[4,2,288,1792]{3,2,1,0:T(8,128)(2,1)}, bf16[4,2,288,128]{3,2,1,0:T(8,128)(2,1)S(1)}, bf16[2,288,2304]{2,1,0:T(8,128)(2,1)S(1)}, bf16[4,1...) custom-call(bf16[288,1792]{1,0:T(8,128)(2,1)S(1)} %copy-done.12, ...), custom_call_target="tpu_custom_call" | custom-call | flops 99999997952 | bytes 4128768 | tf_op jit(solution)/shard_map/fetch_weights/pallas_call | solution.py:926
  174.3 26.2 %all-to-all-start = ((bf16[8,288,768]{2,1,0:T(8,128)(2,1)}), bf16[8,288,768]{2,1,0:T(8,128)(2,1)}, u32[]{:S(2)}, u32[]{:S(2)}) async-start(bf16[8,288,768]{2,1,0:T(8,128)(2,1)} %copy-done.7), calls=%async_computation | async-start | bytes 7077888 | tf_op jit(solution)/shard_map/all_to_all | solution.py:1495
  206.3 7.8 fusion.85
  239.7 29.7 %plane_sum.1 = f32[128,2304]{1,0:T(8,128)} custom-call(bf16[4,128,2304]{2,1,0:T(8,128)(2,1)} %bitcast.165), custom_call_target="tpu_custom_call" | custom-call | flops 1000000 | bytes 1000000 | tf_op jit(solution)/shard_map/plane_sum/pallas_call | solution.py:1024
  277.2 145.6 %spread_blocks.1 = (bf16[8,288,1536]{2,1,0:T(8,128)(2,1)}, bf16[4,2,4,128,2304]{4,3,2,1,0:T(8,128)(2,1)}, f32[4,2,4,8,128]{4,3,2,1,0:T(8,128)}) custom-call(bf16[8,288,768]{2,1,0:T(8,128)(2,1)} %copy-done.6, bf16[8,288,768]{2,1,0:T(8,128)(2,1)} %all-to-all-done.refs_1_, bf16[128,2304]{1,0:T(8,128)(2,1)} %copy-done.24, f32[8,128]{1,0:T(8,128)} %maximum_bitcast_fusion.refs_3_), custom_call_target="tpu_custom_call" | custom-call | flops 1000000 | bytes 1000000 | tf_op jit(solution)/shard_map/spread_blocks/pallas_call | solution.py:249
  424.0 10.9 %convolution_convert_fusion.4 = bf16[32,80,2304]{2,1,0:T(8,128)(2,1)} fusion(bf16[32,128,2304]{2,1,0:T(8,128)(2,1)} %bitcast.155, f32[32,128]{1,0:T(8,128)S(1)} %bitcast.189, f32[32,128]{1,0:T(8,128)S(1)} %bitcast.192, f32[80]{0:T(128)S(1)} %add_convert_fusion.4), kind=kOutput, calls=%fused_computation.4 | convolution fusion | flops 1516830720 | bytes 30703936 | tf_op jit(solution)/shard_map/spt,std->spd/dot_general | solution.py:1442
  434.9 24.0 %fusion.86 = f32[2560,1536]{0,1:T(8,128)S(1)} fusion(bf16[2560,2304]{1,0:T(8,128)(2,1)} %bitcast.156, bf16[2304,1536]{1,0:T(8,128)(2,1)} %bitcast.202), kind=kOutput, calls=%fused_computation.191 | convolution fusion | flops 18119393280 | bytes 34603008 | tf_op jit(solution)/shard_map/dot_general | solution.py:1434
  468.8 13.9 %convolution_convert_fusion = bf16[2560,2304]{1,0:T(8,128)(2,1)} fusion(bf16[2560,768]{0,1:T(8,128)(2,1)} %get-tuple-element.134, bf16[720,2304]{1,0:T(8,128)(2,1)S(1)} %bitcast.204), kind=kOutput, calls=%fused_computation | convolution fusion | flops 9065594880 | bytes 19046400 | tf_op jit(solution)/shard_map/dot_general | solution.py:1434
  484.6 14.4 %convolution_convert_fusion.3 = bf16[32,80,2304]{2,1,0:T(8,128)(2,1)} fusion(bf16[32,128,2304]{2,1,0:T(8,128)(2,1)} %bitcast.154, f32[32,128]{1,0:T(8,128)S(1)} %bitcast.190, f32[32,128]{1,0:T(8,128)S(1)} %bitcast.193, f32[80]{0:T(128)S(1)} %add_convert_fusion.4), kind=kOutput, calls=%fused_computation.3 | convolution fusion | flops 1516830720 | bytes 30703936 | tf_op jit(solution)/shard_map/spt,std->spd/dot_general | solution.py:1442
  499.0 14.3 %multiply_reduce_fusion = (f32[2560]{0:T(1024)S(1)}, f32[2560,768]{0,1:T(8,128)}) fusion(bf16[2560,768]{0,1:T(8,128)(2,1)S(1)} %copy-done.31, bf16[2560,2304]{1,0:T(8,128)(2,1)} %bitcast.161, bf16[720,2304]{1,0:T(8,128)(2,1)S(1)} %bitcast.205), kind=kOutput, calls=%fused_computation.8 | convolution fusion | flops 9065592832 | bytes 26920960 | tf_op jit(solution)/shard_map/dot_general | solution.py:1438
  514.8 10.1 %multiply_convert_fusion.1 = (bf16[2560,768]{0,1:T(8,128)(2,1)S(1)}, bf16[2560,768]{0,1:T(8,128)(2,1)S(1)}) fusion(f32[2560,768]{0,1:T(8,128)} %get-tuple-element.180, f32[2560]{0:T(1024)S(1)} %mul.469, f32[2560,1536]{0,1:T(8,128)} %copy-done.16), kind=kLoop, calls=%fused_computation.10 | loop fusion | flops 27525120 | bytes 31467520 | tf_op jit(solution)/shard_map/convert_element_type | solution.py:1592
  524.9 16.9 %convolution_convert_fusion.5 = bf16[2304,768]{1,0:T(8,128)(2,1)} fusion(bf16[2560,2304]{1,0:T(8,128)(2,1)} %bitcast.157, bf16[2560,768]{0,1:T(8,128)(2,1)S(1)} %get-tuple-element.139), kind=kOutput, calls=%fused_computation.16 | convolution fusion | flops 9061466112 | bytes 19267584 | tf_op jit(solution)/shard_map/dot_general | solution.py:1438
  541.9 11.0 %convolution_convert_fusion.6 = bf16[2304,768]{1,0:T(8,128)(2,1)} fusion(bf16[2560,2304]{1,0:T(8,128)(2,1)S(1)} %bitcast.160, bf16[2560,768]{0,1:T(8,128)(2,1)S(1)} %get-tuple-element.140), kind=kOutput, calls=%fused_computation.17 | convolution fusion | flops 9061466112 | bytes 19267584 | tf_op jit(solution)/shard_map/dot_general | solution.py:1438
  558.4 16.2 %fusion.15.x_ref = f32[720,2304]{1,0:T(8,128)} fusion(bf16[2560,2304]{1,0:T(8,128)(2,1)} %bitcast.162, f32[2560,768]{0,1:T(8,128)} %get-tuple-element.133, f32[2560]{0:T(1024)S(1)} %mul.469), kind=kOutput, calls=%fused_computation.37 | convolution fusion | flops 8497152000 | bytes 25815040 | tf_op jit(solution)/shard_map/dot_general | solution.py:1438
  574.7 9.1 lined_up.1
  584.4 25.1 %convolution_convert_fusion.1 = bf16[2560,2304]{1,0:T(8,128)(2,1)} fusion(bf16[2304,1536]{1,0:T(8,128)(2,1)} %bitcast.203, bf16[2560,768]{0,1:T(8,128)(2,1)} %copy-done.32, bf16[2560,768]{0,1:T(8,128)(2,1)} %copy-done.33), kind=kOutput, calls=%fused_computation.1 | convolution fusion | flops 18141020160 | bytes 26738688 | tf_op jit(solution)/shard_map/dot_general | solution.py:1438
  609.6 102.3 %collect_rows.1 = (f32[128,2304]{1,0:T(8,128)}, f32[8,128]{1,0:T(8,128)}) custom-call(bf16[4,2,4,80,2304]{4,3,2,1,0:T(8,128)(2,1)} %bitcast.164, f32[4,2,4,8,128]{4,3,2,1,0:T(8,128)} %get-tuple-element.47.notes_ref, f32[4,2,4,8,128]{4,3,2,1,0:T(8,128)} %select_maximum_fusion.2.dots_ref), custom_call_target="tpu_custom_call" | custom-call | flops 1000000 | bytes 1000000 | tf_op jit(solution)/shard_map/collect_rows/pallas_call | solution.py:487
  723.5 29.4 %plane_gather.1 = bf16[4,128,2304]{2,1,0:T(8,128)(2,1)} custom-call(bf16[128,2304]{1,0:T(8,128)(2,1)} %multiply_convert_fusion.4.x_ref), custom_call_target="tpu_custom_call" | custom-call | flops 1000000 | bytes 1000000 | tf_op jit(solution)/shard_map/plane_gather/pallas_call | solution.py:975
  762.4 10.8 %fusion.78 = (bf16[512,2304]{1,0:T(8,128)(2,1)}, bf16[2304]{0:T(1024)(128)(2,1)S(1)}, bf16[512,2304]{1,0:T(8,128)(2,1)S(1)}) fusion(f32[512]{0:T(512)S(1)} %copy-done.73, bf16[4,128,2304]{2,1,0:T(8,128)(2,1)S(1)} %copy-done.1, f32[2304]{0:T(1024)S(1)} %copy-done.57, bf16[2304,1792]{1,0:T(8,128)(2,1)} %bitcast.207, bf16[512,576]{0,1:T(8,128)(2,1)S(1)} %bitcast.187, ...), kind=kOutput, calls=%fused_computation.183 | convolution fusion | flops 4244633344 | bytes 17124352 | tf_op jit(solution)/shard_map/dot_general | solution.py:1438
  776.6 10.0 %convolution_convert_fusion.2 = bf16[2304,1792]{1,0:T(8,128)(2,1)} fusion(bf16[512,2304]{1,0:T(8,128)(2,1)S(1)} %get-tuple-element.145, bf16[512,576]{0,1:T(8,128)(2,1)S(1)} %bitcast.188, bf16[512,576]{0,1:T(8,128)(2,1)S(1)} %bitcast.186, bf16[512,576]{0,1:T(8,128)(2,1)S(1)} %bitcast.184, bf16[1792]{0:T(1024)(128)(2,1)S(1)} %copy-done.68), kind=kOutput, calls=%fused_computation.2 | convolution fusion | flops 4239327232 | bytes 12389888 | tf_op jit(solution)/shard_map/dot_general | solution.py:1438
  786.6 12.2 %all-to-all-done.2.gate_ref = bf16[8,288,768]{2,1,0:T(8,128)(2,1)} async-done(((bf16[8,288,768]{2,1,0:T(8,128)(2,1)}), bf16[8,288,768]{2,1,0:T(8,128)(2,1)}, u32[]{:S(2)}, u32[]{:S(2)}) %all-to-all-start.2) | async-done | bytes 3538976 | tf_op jit(solution)/shard_map/all_to_all | solution.py:1610
  799.8 156.2 %settle_weights.1 = (bf16[4,288,1792]{2,1,0:T(8,128)(2,1)}, bf16[4,288,128]{2,1,0:T(8,128)(2,1)}, bf16[288,2304]{1,0:T(8,128)(2,1)}, f32[128,2304]{1,0:T(8,128)}, bf16[4,80,2304]{2,1,0:T(8,128)(2,1)}) custom-call(bf16[4,2,288,1792]{3,2,1,0:T(8,128)(2,1)} %bitcast.166, bf16[4,2,288,128]{3,2,1,0:T(8,128)(2,1)} %bitcast.181, bf16[2,288,2304]{2,1,0:T(8,128)(2,1)} %bitcast.171, ...), custom_call_target="tpu_custom_call" | custom-call | flops 1000000 | bytes 1000000 | tf_op jit(solution)/shard_map/settle_weights/pallas_call | solution.py:1261
  956.1 8.2 assemble_columns.1
  969.0 15.1 %unpack_columns.1 = f32[25920,128]{1,0:T(8,128)} custom-call(bf16[8,288,768]{2,1,0:T(8,128)(2,1)} %all-to-all-done.2.gate_ref, bf16[8,288,768]{2,1,0:T(8,128)(2,1)} %all-to-all-done.1.up_ref), custom_call_target="tpu_custom_call" | custom-call | tf_op jit(solution)/shard_map/unpack_columns/pallas_call | solution.py:573
  (273 shorter events, 113.4 us)
Async XLA Ops:
  174.3 31.4 %copy-start = (bf16[4,128,2304]{2,1,0:T(8,128)(2,1)}, bf16[4,128,2304]{2,1,0:T(8,128)(2,1)S(1)}, u32[]{:S(2)}) copy-start(bf16[4,128,2304]{2,1,0:T(8,128)(2,1)S(1)} %get-tuple-element.40) | copy-start | bytes 7077892
  174.3 97.5 %copy-start.2 = (bf16[4,2,288,128]{3,2,1,0:T(8,128)(2,1)}, bf16[4,2,288,128]{3,2,1,0:T(8,128)(2,1)S(1)}, u32[]{:S(2)}) copy-start(bf16[4,2,288,128]{3,2,1,0:T(8,128)(2,1)S(1)} %get-tuple-element.41) | copy-start | bytes 1769476
  174.3 102.9 %all-to-all-start = ((bf16[8,288,768]{2,1,0:T(8,128)(2,1)}), bf16[8,288,768]{2,1,0:T(8,128)(2,1)}, u32[]{:S(2)}, u32[]{:S(2)}) async-start(bf16[8,288,768]{2,1,0:T(8,128)(2,1)} %copy-done.7), calls=%async_computation | async-start | bytes 7077888 | tf_op jit(solution)/shard_map/all_to_all | solution.py:1495
  200.5 513.2 %reduce-scatter.2.cloned.1.call-start = ((), (), s32[]{:S(2)}) async-start(), calls=%async_computation.4 | async-start | bytes 13271040 | tf_op jit(solution)/shard_map/reduce_scatter | solution.py:1580
  272.3 150.5 %copy-start.58 = (f32[128,2]{0,1:T(2,128)}, f32[128,2]{0,1:T(2,128)S(1)}, u32[]{:S(2)}) copy-start(f32[128,2]{0,1:T(2,128)S(1)} %select_reduce_fusion.1) | copy-start | bytes 3076
  272.3 150.5 %copy-start.62 = (f32[128]{0:T(128)}, f32[128]{0:T(128)S(1)}, u32[]{:S(2)}) copy-start(f32[128]{0:T(128)S(1)} %reduce_max.19) | copy-start | bytes 1540
  272.4 150.4 %copy-start.64 = (f32[128]{0:T(128)}, f32[128]{0:T(128)S(1)}, u32[]{:S(2)}) copy-start(f32[128]{0:T(128)S(1)} %fusion.67) | copy-start | bytes 1540
  514.8 27.0 %slice-start = ((s8[11796480]{0:T(1024)(128)(4,1)}), s8[3407872]{0:T(1024)(128)(4,1)S(1)}, s32[]{:S(2)}) async-start(s8[11796480]{0:T(1024)(128)(4,1)} %bitcast.158), calls=%async_computation.5 | async-start | bytes 6815744
  524.9 16.9 %copy-start.32 = (bf16[2560,768]{0,1:T(8,128)(2,1)}, bf16[2560,768]{0,1:T(8,128)(2,1)S(1)}, u32[]{:S(2)}) copy-start(bf16[2560,768]{0,1:T(8,128)(2,1)S(1)} %get-tuple-element.139) | copy-start | bytes 11796484
  524.9 16.9 %copy-start.33 = (bf16[2560,768]{0,1:T(8,128)(2,1)}, bf16[2560,768]{0,1:T(8,128)(2,1)S(1)}, u32[]{:S(2)}) copy-start(bf16[2560,768]{0,1:T(8,128)(2,1)S(1)} %get-tuple-element.140) | copy-start | bytes 11796484
  524.9 16.9 %slice-start.1 = ((s8[11796480]{0:T(1024)(128)(4,1)}), s8[4194304]{0:T(1024)(128)(4,1)S(1)}, s32[]{:S(2)}) async-start(s8[11796480]{0:T(1024)(128)(4,1)} %bitcast.158), calls=%async_computation.6 | async-start | bytes 8388608
  552.8 160.9 %all-to-all-start.1 = ((bf16[8,288,768]{2,1,0:T(8,128)(2,1)}), bf16[8,288,768]{2,1,0:T(8,128)(2,1)}, u32[]{:S(2)}, u32[]{:S(2)}) async-start(bf16[8,288,768]{2,1,0:T(8,128)(2,1)} %bitcast.25), calls=%async_computation.1 | async-start | bytes 7077888 | tf_op jit(solution)/shard_map/all_to_all | solution.py:1602
  609.6 102.4 %copy-start.59 = (f32[128,2]{0,1:T(2,128)S(1)}, f32[128,2]{0,1:T(2,128)}, u32[]{:S(2)}) copy-start(f32[128,2]{0,1:T(2,128)} %copy-done.58) | copy-start | bytes 3076
  609.6 102.4 %copy-start.63 = (f32[128]{0:T(128)S(1)}, f32[128]{0:T(128)}, u32[]{:S(2)}) copy-start(f32[128]{0:T(128)} %copy-done.62) | copy-start | bytes 1540
  609.6 102.4 %copy-start.65 = (f32[128]{0:T(128)S(1)}, f32[128]{0:T(128)}, u32[]{:S(2)}) copy-start(f32[128]{0:T(128)} %copy-done.64) | copy-start | bytes 1540
  609.6 103.8 %copy-start.61 = (s32[128,2]{0,1:T(2,128)S(1)}, s32[128,2]{0,1:T(2,128)}, u32[]{:S(2)}) copy-start(s32[128,2]{0,1:T(2,128)} %param.15) | copy-start | bytes 3076
  609.6 103.8 %copy-start.25 = (bf16[128,2304]{1,0:T(8,128)(2,1)S(1)}, bf16[128,2304]{1,0:T(8,128)(2,1)}, u32[]{:S(2)}) copy-start(bf16[128,2304]{1,0:T(8,128)(2,1)} %copy-done.24) | copy-start | bytes 1769476
  609.6 104.2 %copy-start.3 = (bf16[4,2,288,128]{3,2,1,0:T(8,128)(2,1)S(1)}, bf16[4,2,288,128]{3,2,1,0:T(8,128)(2,1)}, u32[]{:S(2)}) copy-start(bf16[4,2,288,128]{3,2,1,0:T(8,128)(2,1)} %copy-done.2) | copy-start | bytes 1769476
  609.6 104.2 %copy-start.18 = (f32[128,2304]{1,0:T(8,128)S(1)}, f32[128,2304]{1,0:T(8,128)}, u32[]{:S(2)}) copy-start(f32[128,2304]{1,0:T(8,128)} %copy-done.17) | copy-start | bytes 3538948
  609.6 104.2 %copy-start.53 = (f32[2304]{0:T(1024)S(1)}, f32[2304]{0:T(1024)}, u32[]{:S(2)}) copy-start(f32[2304]{0:T(1024)} %copy-done.52) | copy-start | bytes 27652
  609.6 104.2 %copy-start.67 = (f32[128]{0:T(128)S(1)}, f32[128]{0:T(128)}, u32[]{:S(2)}) copy-start(f32[128]{0:T(128)} %copy-done.66) | copy-start | bytes 1540
  716.1 82.7 %all-to-all-start.2 = ((bf16[8,288,768]{2,1,0:T(8,128)(2,1)}), bf16[8,288,768]{2,1,0:T(8,128)(2,1)}, u32[]{:S(2)}, u32[]{:S(2)}) async-start(bf16[8,288,768]{2,1,0:T(8,128)(2,1)} %bitcast.170), calls=%async_computation.3 | async-start | bytes 7077888 | tf_op jit(solution)/shard_map/all_to_all | solution.py:1610
  722.2 30.7 %copy-start.74 = (f32[128]{0:T(128)}, f32[128]{0:T(128)S(1)}, u32[]{:S(2)}) copy-start(f32[128]{0:T(128)S(1)} %broadcast_multiply_fusion.3) | copy-start | bytes 1540
  723.5 29.4 %copy-start.9 = (bf16[2,288,2304]{2,1,0:T(8,128)(2,1)S(1)}, bf16[2,288,2304]{2,1,0:T(8,128)(2,1)}, u32[]{:S(2)}) copy-start(bf16[2,288,2304]{2,1,0:T(8,128)(2,1)} %copy-done.8) | copy-start | bytes 7962628
  (60 other events, 231.5 us)
Sparse Core Ops, SparseCore 0:
  482.9 198.9 reduce-scatter.1

commit v10 on v9

--- a/solution.py
+++ b/solution.py
@@ -567,7 +567,7 @@
 
 def unpack_columns(gate, up, F):
     n, rows, Fp = gate.shape
-    block = 16
+    block = 96 if rows % 96 == 0 else 16
     width = 2 * n * F
     tiles = width // 128
     flat = pl.pallas_call(
@@ -592,7 +592,7 @@
 def lined_up(x):
     rows, width = x.shape
     tiles = width // 128
-    block = 80 if rows % 80 == 0 else 8
+    block = 240 if rows % 240 == 0 else 8
     flat = pl.pallas_call(
         line_kernel,
         grid=(rows // block,),
@@ -944,7 +944,7 @@
             dma((6,)), dma((2, 6)), dma((6,)), dma((6,)), dma(()),
         ],
         compiler_params=pltpu.CompilerParams(
-            collective_id=0, has_side_effects=True, vmem_limit_bytes=32 << 20
+            collective_id=0, has_side_effects=True, vmem_limit_bytes=60 << 20
         ),
         cost_estimate=pl.CostEstimate(
             flops=10**11, bytes_accessed=8 * columns.size, transcendentals=0
@@ -1320,7 +1320,7 @@
 
 def assemble_columns(x, width):
     R = x.shape[1]
-    block = 32
+    block = 96 if R % 96 == 0 else 16
     return pl.pallas_call(
         functools.partial(assemble_kernel, width),
         grid=(R // block,),
@@ -1576,7 +1576,7 @@
     gate_part, up_part = pre[:, :Fp], pre[:, Fp:]
     sigmoid_gate = jax.nn.sigmoid(gate_part)
     silu_gate = gate_part * sigmoid_gate
-    activated = (silu_gate * up_part).astype(bf16)
+    activated = lax.optimization_barrier((silu_gate * up_part).astype(bf16))
     out_sum = lax.psum_scatter(
         dot32(activated, down).astype(bf16), SHARD, scatter_dimension=0, tiled=True
     )

time: 1010 us -> 998 us (0.988)
  Pallas kernels: 647 us -> 631 us
  other arithmetic: 34.9 us -> 46.4 us
    unnamed x167 -> x137, local copies, waits for them, and re-layouts: 22.3 us -> 14.2 us
  transfers between devices with their start and end apart: 4 -> 4, of which waited for: 2 -> 1; matrix products, arithmetic and copies ran while one was open for 19% -> 21% of each run, Pallas kernels for 17% -> 17%
where the time goes in v10:
time: 998 us; the launch traced here: 990 us
  Pallas kernels  631 us (63%)
  matrix products  195 us (20%)
  local copies, waits for them, and re-layouts  53.1 us (5%)
  other arithmetic  46.4 us (5%)
  starting transfers between devices  38.7 us (4%)
  between operations  15.3 us (2%)
  waiting for transfers between devices  10.4 us (1%)
    pallas_call x1, Pallas kernels, settle_weights(): pl.pallas_call(functools.partial(settle_kernel, nz), out_shape=(sd((4, R,...  156 us
    pallas_call x1, Pallas kernels, fetch_weights(): pl.pallas_call(functools.partial(fetch_kernel, nz, F), out_shape=(sd((nz,...  148 us
    pallas_call x1, Pallas kernels, spread_blocks(): pl.pallas_call(functools.partial(spread_kernel, nz, splits), out_shape=(p...  144 us
    dot_general x9, matrix products, dot_dims(): lax.dot_general(a, b, (((da,), (db,)), ((), ())), preferred_element_type=...  112 us
    pallas_call x1, Pallas kernels, collect_rows(): pl.pallas_call(functools.partial(collect_kernel, nz, cap), out_shape=(jax...  99.7 us
    dot_general x8, matrix products, dot32(): return jnp.dot(a, b, preferred_element_type=f32)  54.2 us
    pallas_call x1, Pallas kernels, plane_sum(): pl.pallas_call(plane_sum_kernel, out_shape=jax.ShapeDtypeStruct(x.shape[1...  29.7 us
    pallas_call x1, Pallas kernels, plane_gather(): pl.pallas_call(plane_gather_kernel, out_shape=jax.ShapeDtypeStruct((4,) +...  29.3 us
  transfers between devices with their start and end apart: 4, of which 1 were waited for; matrix products, arithmetic and copies ran while one was open for 21% of the time, Pallas kernels for 17%

profile of v10, /device:TPU:16, one launch (start us, length us, event | category | flops | bytes accessed | tf_op | source)
XLA Modules:
  0.0 990.2 jit_solution(10942010962902725481)
XLA Ops:
  14.0 148.3 %fetch_weights.1 = (bf16[4,2,288,1792]{3,2,1,0:T(8,128)(2,1)}, bf16[4,2,288,128]{3,2,1,0:T(8,128)(2,1)}, bf16[2,288,2304]{2,1,0:T(8,128)(2,1)}, bf16[4,128,2304]...) custom-call(bf16[288,1792]{1,0:T(8,128)(2,1)} %pick_columns.1.w_ref,, ...), custom_call_target="tpu_custom_call" | custom-call | flops 99999997952 | bytes 4128768 | tf_op jit(solution)/shard_map/fetch_weights/pallas_call | solution.py:926
  162.3 25.9 %all-to-all-start = ((bf16[8,288,768]{2,1,0:T(8,128)(2,1)}), bf16[8,288,768]{2,1,0:T(8,128)(2,1)S(1)}, u32[]{:S(2)}, u32[]{:S(2)}) async-start(bf16[8,288,768]{2,1,0:T(8,128)(2,1)} %get-tuple-element.46), calls=%async_computation | async-start | bytes 7077888 | tf_op jit(solution)/shard_map/all_to_all | solution.py:1495
  195.8 7.8 fusion.84
  242.5 29.7 %plane_sum.1 = f32[128,2304]{1,0:T(8,128)} custom-call(bf16[4,128,2304]{2,1,0:T(8,128)(2,1)} %bitcast.162), custom_call_target="tpu_custom_call" | custom-call | flops 1000000 | bytes 1000000 | tf_op jit(solution)/shard_map/plane_sum/pallas_call | solution.py:1024
  281.5 143.7 %spread_blocks.1 = (bf16[8,288,1536]{2,1,0:T(8,128)(2,1)}, bf16[4,2,4,128,2304]{4,3,2,1,0:T(8,128)(2,1)}, f32[4,2,4,8,128]{4,3,2,1,0:T(8,128)}) custom-call(bf16[8,288,768]{2,1,0:T(8,128)(2,1)} %get-tuple-element.45.refs_0_, bf16[8,288,768]{2,1,0:T(8,128)(2,1)} %copy-done.6, bf16[128,2304]{1,0:T(8,128)(2,1)} %copy-done.7, f32[8,128]{1,0:T(8,128)} %maximum_bitcast_fusion.refs_3_), custom_call_target="tpu_custom_call" | custom-call | flops 1000000 | bytes 1000000 | tf_op jit(solution)/shard_map/spread_blocks/pallas_call | solution.py:249
  426.4 10.9 %convolution_convert_fusion.4 = bf16[32,80,2304]{2,1,0:T(8,128)(2,1)} fusion(bf16[32,128,2304]{2,1,0:T(8,128)(2,1)} %bitcast.149, f32[32,128]{1,0:T(8,128)S(1)} %bitcast.188, f32[32,128]{1,0:T(8,128)S(1)} %bitcast.191, f32[80]{0:T(128)S(1)} %add_convert_fusion.4), kind=kOutput, calls=%fused_computation.4 | convolution fusion | flops 1516830720 | bytes 30703936 | tf_op jit(solution)/shard_map/spt,std->spd/dot_general | solution.py:1442
  437.3 24.0 %fusion.85 = f32[2560,1536]{0,1:T(8,128)S(1)} fusion(bf16[2560,2304]{1,0:T(8,128)(2,1)} %bitcast.150, bf16[2304,1536]{1,0:T(8,128)(2,1)} %bitcast.201), kind=kOutput, calls=%fused_computation.190 | convolution fusion | flops 18119393280 | bytes 34603008 | tf_op jit(solution)/shard_map/dot_general | solution.py:1434
  468.9 13.9 %convolution_convert_fusion = bf16[2560,2304]{1,0:T(8,128)(2,1)} fusion(bf16[2560,768]{0,1:T(8,128)(2,1)} %multiply_convert_fusion, bf16[720,2304]{1,0:T(8,128)(2,1)S(1)} %bitcast.204), kind=kOutput, calls=%fused_computation | convolution fusion | flops 9065594880 | bytes 19046400 | tf_op jit(solution)/shard_map/dot_general | solution.py:1434
  484.8 6.9 convert_element_type.243
  491.7 11.4 %convolution_convert_fusion.3 = bf16[32,80,2304]{2,1,0:T(8,128)(2,1)} fusion(bf16[32,128,2304]{2,1,0:T(8,128)(2,1)} %bitcast.148, f32[32,128]{1,0:T(8,128)S(1)} %bitcast.189, f32[32,128]{1,0:T(8,128)S(1)} %bitcast.192, f32[80]{0:T(128)S(1)} %add_convert_fusion.4), kind=kOutput, calls=%fused_computation.3 | convolution fusion | flops 1516830720 | bytes 30703936 | tf_op jit(solution)/shard_map/spt,std->spd/dot_general | solution.py:1442
  503.0 14.3 %multiply_reduce_fusion = (f32[2560]{0:T(1024)S(1)}, f32[2560,768]{0,1:T(8,128)}) fusion(bf16[2560,768]{0,1:T(8,128)(2,1)S(1)} %copy-done.5, bf16[2560,2304]{1,0:T(8,128)(2,1)} %bitcast.155, bf16[720,2304]{1,0:T(8,128)(2,1)S(1)} %bitcast.205), kind=kOutput, calls=%fused_computation.8 | convolution fusion | flops 9065592832 | bytes 26920960 | tf_op jit(solution)/shard_map/dot_general | solution.py:1438
  518.8 10.1 %multiply_convert_fusion.1 = (bf16[2560,768]{0,1:T(8,128)(2,1)S(1)}, bf16[2560,768]{0,1:T(8,128)(2,1)S(1)}) fusion(f32[2560,768]{0,1:T(8,128)} %get-tuple-element.178, f32[2560]{0:T(1024)S(1)} %mul.469, f32[2560,1536]{0,1:T(8,128)} %copy-done), kind=kLoop, calls=%fused_computation.10 | loop fusion | flops 27525120 | bytes 31467520 | tf_op jit(solution)/shard_map/convert_element_type | solution.py:1592
  528.9 16.9 %convolution_convert_fusion.6 = bf16[2304,768]{1,0:T(8,128)(2,1)} fusion(bf16[2560,2304]{1,0:T(8,128)(2,1)} %bitcast.151, bf16[2560,768]{0,1:T(8,128)(2,1)S(1)} %get-tuple-element.138), kind=kOutput, calls=%fused_computation.17 | convolution fusion | flops 9061466112 | bytes 19267584 | tf_op jit(solution)/shard_map/dot_general | solution.py:1438
  545.8 11.0 %convolution_convert_fusion.5 = bf16[2304,768]{1,0:T(8,128)(2,1)} fusion(bf16[2560,2304]{1,0:T(8,128)(2,1)S(1)} %bitcast.154, bf16[2560,768]{0,1:T(8,128)(2,1)S(1)} %get-tuple-element.137), kind=kOutput, calls=%fused_computation.16 | convolution fusion | flops 9061466112 | bytes 19267584 | tf_op jit(solution)/shard_map/dot_general | solution.py:1438
  556.9 6.7 all-to-all-start.1
  563.6 16.2 %fusion.15.x_ref = f32[720,2304]{1,0:T(8,128)} fusion(bf16[2560,2304]{1,0:T(8,128)(2,1)} %bitcast.156, f32[2560,768]{0,1:T(8,128)} %convert_element_type.243, f32[2560]{0:T(1024)S(1)} %mul.469), kind=kOutput, calls=%fused_computation.37 | convolution fusion | flops 8497152000 | bytes 25815040 | tf_op jit(solution)/shard_map/dot_general | solution.py:1438
  587.1 25.1 %convolution_convert_fusion.1 = bf16[2560,2304]{1,0:T(8,128)(2,1)} fusion(bf16[2304,1536]{1,0:T(8,128)(2,1)} %bitcast.202, bf16[2560,768]{0,1:T(8,128)(2,1)} %copy-done.17, bf16[2560,768]{0,1:T(8,128)(2,1)} %copy-done.18), kind=kOutput, calls=%fused_computation.1 | convolution fusion | flops 18141020160 | bytes 26738688 | tf_op jit(solution)/shard_map/dot_general | solution.py:1438
  612.3 99.7 %collect_rows.1 = (f32[128,2304]{1,0:T(8,128)}, f32[8,128]{1,0:T(8,128)}) custom-call(bf16[4,2,4,80,2304]{4,3,2,1,0:T(8,128)(2,1)} %bitcast.158, f32[4,2,4,8,128]{4,3,2,1,0:T(8,128)} %get-tuple-element.47.notes_ref, f32[4,2,4,8,128]{4,3,2,1,0:T(8,128)} %select_maximum_fusion.2.dots_ref), custom_call_target="tpu_custom_call" | custom-call | flops 1000000 | bytes 1000000 | tf_op jit(solution)/shard_map/collect_rows/pallas_call | solution.py:487
  723.6 29.3 %plane_gather.1 = bf16[4,128,2304]{2,1,0:T(8,128)(2,1)} custom-call(bf16[128,2304]{1,0:T(8,128)(2,1)} %multiply_convert_fusion.4.x_ref), custom_call_target="tpu_custom_call" | custom-call | flops 1000000 | bytes 1000000 | tf_op jit(solution)/shard_map/plane_gather/pallas_call | solution.py:975
  764.4 10.8 %fusion.77 = (bf16[512,2304]{1,0:T(8,128)(2,1)}, bf16[2304]{0:T(1024)(128)(2,1)S(1)}, bf16[512,2304]{1,0:T(8,128)(2,1)S(1)}) fusion(f32[512]{0:T(512)S(1)} %copy-done.59, bf16[4,128,2304]{2,1,0:T(8,128)(2,1)S(1)} %copy-done.10, f32[2304]{0:T(1024)S(1)} %copy-done.40, bf16[2304,1792]{1,0:T(8,128)(2,1)} %bitcast.207, bf16[512,576]{0,1:T(8,128)(2,1)S(1)} %bitcast.182, ...), kind=kOutput, calls=%fused_computation.182 | convolution fusion | flops 4244633344 | bytes 17124352 | tf_op jit(solution)/shard_map/dot_general | solution.py:1438
  778.5 10.0 %convolution_convert_fusion.2 = bf16[2304,1792]{1,0:T(8,128)(2,1)} fusion(bf16[512,2304]{1,0:T(8,128)(2,1)S(1)} %get-tuple-element.143, bf16[512,576]{0,1:T(8,128)(2,1)S(1)} %bitcast.183, bf16[512,576]{0,1:T(8,128)(2,1)S(1)} %bitcast.185, bf16[512,576]{0,1:T(8,128)(2,1)S(1)} %bitcast.187, bf16[1792]{0:T(1024)(128)(2,1)S(1)} %copy-done.53), kind=kOutput, calls=%fused_computation.2 | convolution fusion | flops 4239327232 | bytes 12389888 | tf_op jit(solution)/shard_map/dot_general | solution.py:1438
  788.5 10.3 %all-to-all-done.2.gate_ref = bf16[8,288,768]{2,1,0:T(8,128)(2,1)} async-done(((bf16[8,288,768]{2,1,0:T(8,128)(2,1)}), bf16[8,288,768]{2,1,0:T(8,128)(2,1)}, u32[]{:S(2)}, u32[]{:S(2)}) %all-to-all-start.2) | async-done | bytes 3538976 | tf_op jit(solution)/shard_map/all_to_all | solution.py:1610
  799.9 156.2 %settle_weights.1 = (bf16[4,288,1792]{2,1,0:T(8,128)(2,1)}, bf16[4,288,128]{2,1,0:T(8,128)(2,1)}, bf16[288,2304]{1,0:T(8,128)(2,1)}, f32[128,2304]{1,0:T(8,128)}, bf16[4,80,2304]{2,1,0:T(8,128)(2,1)}) custom-call(bf16[4,2,288,1792]{3,2,1,0:T(8,128)(2,1)} %bitcast.163, bf16[4,2,288,128]{3,2,1,0:T(8,128)(2,1)} %bitcast.180, bf16[2,288,2304]{2,1,0:T(8,128)(2,1)} %bitcast.170, ...), custom_call_target="tpu_custom_call" | custom-call | flops 1000000 | bytes 1000000 | tf_op jit(solution)/shard_map/settle_weights/pallas_call | solution.py:1261
  972.4 8.7 unpack_columns.1
  (244 shorter events, 127.1 us)
Async XLA Ops:
  162.3 117.4 %all-to-all-start = ((bf16[8,288,768]{2,1,0:T(8,128)(2,1)}), bf16[8,288,768]{2,1,0:T(8,128)(2,1)S(1)}, u32[]{:S(2)}, u32[]{:S(2)}) async-start(bf16[8,288,768]{2,1,0:T(8,128)(2,1)} %get-tuple-element.46), calls=%async_computation | async-start | bytes 7077888 | tf_op jit(solution)/shard_map/all_to_all | solution.py:1495
  188.2 525.7 %reduce-scatter.2.cloned.1.call-start = ((), (), s32[]{:S(2)}) async-start(), calls=%async_computation.4 | async-start | bytes 13271040 | tf_op jit(solution)/shard_map/reduce_scatter | solution.py:1580
  276.5 148.7 %copy-start.41 = (f32[128,2]{0,1:T(2,128)}, f32[128,2]{0,1:T(2,128)S(1)}, u32[]{:S(2)}) copy-start(f32[128,2]{0,1:T(2,128)S(1)} %select_reduce_fusion.1) | copy-start | bytes 3076
  276.5 148.7 %copy-start.45 = (f32[128]{0:T(128)}, f32[128]{0:T(128)S(1)}, u32[]{:S(2)}) copy-start(f32[128]{0:T(128)S(1)} %reduce_max.19) | copy-start | bytes 1540
  491.7 11.4 %copy-start.5 = (bf16[2560,768]{0,1:T(8,128)(2,1)S(1)}, bf16[2560,768]{0,1:T(8,128)(2,1)}, u32[]{:S(2)}) copy-start(bf16[2560,768]{0,1:T(8,128)(2,1)} %multiply_convert_fusion) | copy-start | bytes 11796484
  518.8 27.0 %slice-start = ((s8[11796480]{0:T(1024)(128)(4,1)}), s8[3407872]{0:T(1024)(128)(4,1)S(1)}, s32[]{:S(2)}) async-start(s8[11796480]{0:T(1024)(128)(4,1)} %bitcast.152), calls=%async_computation.5 | async-start | bytes 6815744
  528.9 16.9 %copy-start.18 = (bf16[2560,768]{0,1:T(8,128)(2,1)}, bf16[2560,768]{0,1:T(8,128)(2,1)S(1)}, u32[]{:S(2)}) copy-start(bf16[2560,768]{0,1:T(8,128)(2,1)S(1)} %get-tuple-element.138) | copy-start | bytes 11796484
  528.9 16.9 %copy-start.17 = (bf16[2560,768]{0,1:T(8,128)(2,1)}, bf16[2560,768]{0,1:T(8,128)(2,1)S(1)}, u32[]{:S(2)}) copy-start(bf16[2560,768]{0,1:T(8,128)(2,1)S(1)} %get-tuple-element.137) | copy-start | bytes 11796484
  528.9 16.9 %slice-start.1 = ((s8[11796480]{0:T(1024)(128)(4,1)}), s8[4194304]{0:T(1024)(128)(4,1)S(1)}, s32[]{:S(2)}) async-start(s8[11796480]{0:T(1024)(128)(4,1)} %bitcast.152), calls=%async_computation.6 | async-start | bytes 8388608
  528.9 16.9 %slice-start.2 = ((s8[11796480]{0:T(1024)(128)(4,1)}), s8[4194304]{0:T(1024)(128)(4,1)S(1)}, s32[]{:S(2)}) async-start(s8[11796480]{0:T(1024)(128)(4,1)} %bitcast.152), calls=%async_computation.7 | async-start | bytes 8388608
  556.9 157.0 %all-to-all-start.1 = ((bf16[8,288,768]{2,1,0:T(8,128)(2,1)}), bf16[8,288,768]{2,1,0:T(8,128)(2,1)}, u32[]{:S(2)}, u32[]{:S(2)}) async-start(bf16[8,288,768]{2,1,0:T(8,128)(2,1)} %bitcast.25), calls=%async_computation.1 | async-start | bytes 7077888 | tf_op jit(solution)/shard_map/all_to_all | solution.py:1602
  612.2 99.8 %copy-start.42 = (f32[128,2]{0,1:T(2,128)S(1)}, f32[128,2]{0,1:T(2,128)}, u32[]{:S(2)}) copy-start(f32[128,2]{0,1:T(2,128)} %copy-done.41) | copy-start | bytes 3076
  612.2 99.8 %copy-start.46 = (f32[128]{0:T(128)S(1)}, f32[128]{0:T(128)}, u32[]{:S(2)}) copy-start(f32[128]{0:T(128)} %copy-done.45) | copy-start | bytes 1540
  612.3 99.8 %copy-start.50 = (f32[128]{0:T(128)S(1)}, f32[128]{0:T(128)}, u32[]{:S(2)}) copy-start(f32[128]{0:T(128)} %copy-done.49) | copy-start | bytes 1540
  612.3 101.2 %copy-start.44 = (s32[128,2]{0,1:T(2,128)S(1)}, s32[128,2]{0,1:T(2,128)}, u32[]{:S(2)}) copy-start(s32[128,2]{0,1:T(2,128)} %param.15) | copy-start | bytes 3076
  612.3 101.2 %copy-start.8 = (bf16[128,2304]{1,0:T(8,128)(2,1)S(1)}, bf16[128,2304]{1,0:T(8,128)(2,1)}, u32[]{:S(2)}) copy-start(bf16[128,2304]{1,0:T(8,128)(2,1)} %copy-done.7) | copy-start | bytes 1769476
  612.3 101.6 %copy-start.2 = (f32[128,2304]{1,0:T(8,128)S(1)}, f32[128,2304]{1,0:T(8,128)}, u32[]{:S(2)}) copy-start(f32[128,2304]{1,0:T(8,128)} %copy-done.1) | copy-start | bytes 3538948
  612.3 101.6 %copy-start.12 = (bf16[4,2,288,128]{3,2,1,0:T(8,128)(2,1)S(1)}, bf16[4,2,288,128]{3,2,1,0:T(8,128)(2,1)}, u32[]{:S(2)}) copy-start(bf16[4,2,288,128]{3,2,1,0:T(8,128)(2,1)} %get-tuple-element.41) | copy-start | bytes 1769476
  612.3 101.6 %copy-start.37 = (f32[2304]{0:T(1024)S(1)}, f32[2304]{0:T(1024)}, u32[]{:S(2)}) copy-start(f32[2304]{0:T(1024)} %copy-done.36) | copy-start | bytes 27652
  612.3 101.6 %copy-start.52 = (f32[128]{0:T(128)S(1)}, f32[128]{0:T(128)}, u32[]{:S(2)}) copy-start(f32[128]{0:T(128)} %copy-done.51) | copy-start | bytes 1540
  716.2 82.6 %all-to-all-start.2 = ((bf16[8,288,768]{2,1,0:T(8,128)(2,1)}), bf16[8,288,768]{2,1,0:T(8,128)(2,1)}, u32[]{:S(2)}, u32[]{:S(2)}) async-start(bf16[8,288,768]{2,1,0:T(8,128)(2,1)} %bitcast.167), calls=%async_computation.3 | async-start | bytes 7077888 | tf_op jit(solution)/shard_map/all_to_all | solution.py:1610
  723.6 29.4 %copy-start.20 = (bf16[4,128,9,64]{1,3,2,0:T(8,128)(2,1)S(1)}, bf16[4,128,9,64]{1,3,2,0:T(8,128)(2,1)}, u32[]{:S(2)}) copy-start(bf16[4,128,9,64]{1,3,2,0:T(8,128)(2,1)} %copy-done.19) | copy-start | bytes 1769476
  764.4 10.9 %copy-start.23 = (bf16[4,128,9,64]{1,0,3,2:T(4,128)(2,1)S(1)}, bf16[4,128,9,64]{1,0,3,2:T(4,128)(2,1)}, u32[]{:S(2)}) copy-start(bf16[4,128,9,64]{1,0,3,2:T(4,128)(2,1)} %copy.144) | copy-start | bytes 1769476
  799.9 156.2 %copy-start.16 = (bf16[128,2304]{1,0:T(8,128)(2,1)S(1)}, bf16[128,2304]{1,0:T(8,128)(2,1)}, u32[]{:S(2)}) copy-start(bf16[128,2304]{1,0:T(8,128)(2,1)} %t_ref.1) | copy-start | bytes 1769476
  (45 other events, 125.9 us)
Sparse Core Ops, SparseCore 0:
  483.0 193.8 reduce-scatter.1

commit v11 on v10

--- a/solution.py
+++ b/solution.py
@@ -589,8 +589,8 @@
         o_ref[pl.ds(j, rows, stride=tiles), :] = x_ref[:, j * 128 : (j + 1) * 128]
 
 
-def lined_up(x):
-    rows, width = x.shape
+def lined_up(x, rows):
+    width = x.shape[1]
     tiles = width // 128
     block = 240 if rows % 240 == 0 else 8
     flat = pl.pallas_call(
@@ -953,11 +953,38 @@
     )(columns, small, rows, tokens, lengths, block, wide)
 
 
-def plane_gather_kernel(x_ref, out_ref, send, recv, own):
-    e, z, c, ex, ey = place()
+def plane_gather_kernel(
+    x_ref, a_ref, r_ref, out_ref, d_ref, left, right, prod, load, store, send, recv, own
+):
+    loads = [
+        pltpu.make_async_copy(a_ref, left, load.at[0]),
+        pltpu.make_async_copy(r_ref, right, load.at[1]),
+    ]
+    for copy in loads:
+        copy.start()
     greet_plane()
     begin, end = plane_stream(x_ref, lambda q: out_ref.at[q], send, recv, own)
     begin()
+    for copy in loads:
+        copy.wait()
+    tiles, step = store.shape[0], prod.shape[1] // store.shape[0]
+
+    def done(n):
+        cols = pl.ds(n * step, step)
+        return pltpu.make_async_copy(prod.at[:, cols], d_ref.at[:, cols], store.at[n])
+
+    for n in range(tiles):
+
+        @pl.loop(0, prod.shape[0] // 256)
+        def _(m):
+            rows = pl.ds(pl.multiple_of(m * 256, 256), 256)
+            prod[rows, n * step : (n + 1) * step] = jnp.dot(
+                left[rows, :], right[:, n * step : (n + 1) * step], preferred_element_type=f32
+            )
+
+        done(n).start()
+    for n in range(tiles):
+        done(n).wait()
     end()
 
 
@@ -971,17 +998,28 @@
     pl.semaphore_wait(barrier, 3)
 
 
-def plane_gather(x, collective):
+def plane_gather(x, left, right, collective):
+    M, N = left.shape[0], right.shape[1]
+    dma = pltpu.SemaphoreType.DMA
+    vm = pltpu.VMEM
     return pl.pallas_call(
         plane_gather_kernel,
-        out_shape=jax.ShapeDtypeStruct((4,) + x.shape, x.dtype),
-        in_specs=[ANY],
-        out_specs=ANY,
-        scratch_shapes=plane_sems(),
-        compiler_params=pltpu.CompilerParams(collective_id=collective, has_side_effects=True),
+        out_shape=(
+            jax.ShapeDtypeStruct((4,) + x.shape, x.dtype),
+            jax.ShapeDtypeStruct((M, N), f32),
+        ),
+        in_specs=[ANY] * 3,
+        out_specs=(ANY,) * 2,
+        scratch_shapes=[
+            vm(left.shape, bf16), vm(right.shape, bf16), vm((M, N), f32),
+            dma((2,)), dma((N // 256,)), *plane_sems(),
+        ],
+        compiler_params=pltpu.CompilerParams(
+            collective_id=collective, has_side_effects=True, vmem_limit_bytes=48 << 20
+        ),
         cost_estimate=pl.CostEstimate(flops=10**6, bytes_accessed=10**6, transcendentals=0),
         name="plane_gather",
-    )(x)
+    )(x, left, right)
 
 
 def plane_sum_parts(x_ref, out_ref, held, send, recv, own):
@@ -1576,7 +1614,7 @@
     gate_part, up_part = pre[:, :Fp], pre[:, Fp:]
     sigmoid_gate = jax.nn.sigmoid(gate_part)
     silu_gate = gate_part * sigmoid_gate
-    activated = lax.optimization_barrier((silu_gate * up_part).astype(bf16))
+    activated = (silu_gate * up_part).astype(bf16)
     out_sum = lax.psum_scatter(
         dot32(activated, down).astype(bf16), SHARD, scatter_dimension=0, tiled=True
     )
@@ -1593,7 +1631,6 @@
     pre_grad = jnp.concatenate([gate_grads, up_grads], axis=1)
     in_rows = dot_dims(pre_grad, w_pair, 1, 1).astype(bf16)
     scaled = (grad_scale * activated.astype(f32)).astype(bf16)
-    grad_w_down = lined_up(dot_dims(scaled[:, :F], cotangent_rows, 0, 0))
     gate_term, up_term = [
         dot_dims(arrived, x, 0, 0).astype(bf16).reshape(n_shard, R, Fp)
         for x in (gate_grads, up_grads)
@@ -1625,7 +1662,13 @@
     branch_grad = (branch_scale * residual_grad).astype(bf16)
 
     if fast:
-        branch_grad = plane_gather(branch_grad, 5).reshape(B * T, D)
+        branch_grad, down_term = plane_gather(
+            branch_grad, jnp.transpose(scaled), cotangent_rows, 5
+        )
+        branch_grad = branch_grad.reshape(B * T, D)
+    else:
+        down_term = dot_dims(scaled, cotangent_rows, 0, 0)
+    grad_w_down = lined_up(down_term, F)
     output_grad = dot_dims(context_flat, branch_grad, 0, 0)
     context_grad = dot_dims(branch_grad, full_output, 1, 1).reshape(head_shape)
     row_delta = jnp.sum(context_grad * context.astype(f32), axis=-1)

time: 998 us -> 1020 us (1.022)
  Pallas kernels: 631 us -> 687 us
  matrix products: 195 us -> 178 us
    pallas_call x1, Pallas kernels: 99.7 us -> 156 us  [collect_rows(): pl.pallas_call(functools.partial(collect_kernel, nz, cap), out_shape=(jax...]
    dot_general x9 -> x8, matrix products: 112 us -> 93.7 us  [dot_dims(): lax.dot_general(a, b, (((da,), (db,)), ((), ())), preferred_element_type=...]
    convert_element_type x2 -> x0, other arithmetic: 10.7 us -> none  [the longest x1 6.9 us: on_device(): row_dots = branch_scale * jnp.sum(raw_grad * activated.astype(f32), axis=1)]
  transfers between devices with their start and end apart: 4 -> 4, of which waited for: 1 -> 1; matrix products, arithmetic and copies ran while one was open for 21% -> 16% of each run, Pallas kernels for 17% -> 22%
where the time goes in v11:
time: 1020 us; the launch traced here: 1010 us
  Pallas kernels  687 us (67%)
  matrix products  178 us (17%)
  local copies, waits for them, and re-layouts  52.4 us (5%)
  other arithmetic  39.8 us (4%)
  starting transfers between devices  38.8 us (4%)
  between operations  15.3 us (2%)
    pallas_call x1, Pallas kernels, settle_weights(): pl.pallas_call(functools.partial(settle_kernel, nz), out_shape=(sd((4, R,...  156 us
    pallas_call x1, Pallas kernels, collect_rows(): pl.pallas_call(functools.partial(collect_kernel, nz, cap), out_shape=(jax...  156 us
    pallas_call x1, Pallas kernels, fetch_weights(): pl.pallas_call(functools.partial(fetch_kernel, nz, F), out_shape=(sd((nz,...  148 us
    pallas_call x1, Pallas kernels, spread_blocks(): pl.pallas_call(functools.partial(spread_kernel, nz, splits), out_shape=(p...  144 us
    dot_general x8, matrix products, dot_dims(): lax.dot_general(a, b, (((da,), (db,)), ((), ())), preferred_element_type=...  93.7 us
    dot_general x8, matrix products, dot32(): return jnp.dot(a, b, preferred_element_type=f32)  54.3 us
    pallas_call x1, Pallas kernels, plane_sum(): pl.pallas_call(plane_sum_kernel, out_shape=jax.ShapeDtypeStruct(x.shape[1...  29.7 us
    pallas_call x1, Pallas kernels, plane_gather(): pl.pallas_call(plane_gather_kernel, out_shape=(jax.ShapeDtypeStruct((4,)...  28.8 us
  transfers between devices with their start and end apart: 4, of which 1 were waited for; matrix products, arithmetic and copies ran while one was open for 16% of the time, Pallas kernels for 22%

profile of v11, /device:TPU:16, one launch (start us, length us, event | category | flops | bytes accessed | tf_op | source)
XLA Modules:
  0.0 1014.1 jit_solution(3033612873905441142)
XLA Ops:
  14.0 148.3 %fetch_weights.1 = (bf16[4,2,288,1792]{3,2,1,0:T(8,128)(2,1)}, bf16[4,2,288,128]{3,2,1,0:T(8,128)(2,1)}, bf16[2,288,2304]{2,1,0:T(8,128)(2,1)}, bf16[4,128,2304]...) custom-call(bf16[288,1792]{1,0:T(8,128)(2,1)} %pick_columns.1.w_ref,, ...), custom_call_target="tpu_custom_call" | custom-call | flops 99999997952 | bytes 4128768 | tf_op jit(solution)/shard_map/fetch_weights/pallas_call | solution.py:926
  162.3 25.9 %all-to-all-start = ((bf16[8,288,768]{2,1,0:T(8,128)(2,1)}), bf16[8,288,768]{2,1,0:T(8,128)(2,1)S(1)}, u32[]{:S(2)}, u32[]{:S(2)}) async-start(bf16[8,288,768]{2,1,0:T(8,128)(2,1)} %get-tuple-element.48), calls=%async_computation | async-start | bytes 7077888 | tf_op jit(solution)/shard_map/all_to_all | solution.py:1533
  195.8 7.8 fusion.83
  237.1 5.4 convolution_convert_fusion.8
  242.5 29.7 %plane_sum.1 = f32[128,2304]{1,0:T(8,128)} custom-call(bf16[4,128,2304]{2,1,0:T(8,128)(2,1)} %bitcast.164), custom_call_target="tpu_custom_call" | custom-call | flops 1000000 | bytes 1000000 | tf_op jit(solution)/shard_map/plane_sum/pallas_call | solution.py:1062
  281.5 143.7 %spread_blocks.1 = (bf16[8,288,1536]{2,1,0:T(8,128)(2,1)}, bf16[4,2,4,128,2304]{4,3,2,1,0:T(8,128)(2,1)}, f32[4,2,4,8,128]{4,3,2,1,0:T(8,128)}) custom-call(bf16[8,288,768]{2,1,0:T(8,128)(2,1)} %get-tuple-element.47.refs_0_, bf16[8,288,768]{2,1,0:T(8,128)(2,1)} %copy-done.4, bf16[128,2304]{1,0:T(8,128)(2,1)} %copy-done.7, f32[8,128]{1,0:T(8,128)} %maximum_bitcast_fusion.refs_3_), custom_call_target="tpu_custom_call" | custom-call | flops 1000000 | bytes 1000000 | tf_op jit(solution)/shard_map/spread_blocks/pallas_call | solution.py:249
  426.4 11.0 %convolution_convert_fusion.4 = bf16[32,80,2304]{2,1,0:T(8,128)(2,1)} fusion(bf16[32,128,2304]{2,1,0:T(8,128)(2,1)} %bitcast.153, f32[32,128]{1,0:T(8,128)S(1)} %bitcast.190, f32[32,128]{1,0:T(8,128)S(1)} %bitcast.193, f32[80]{0:T(128)S(1)} %add_convert_fusion.4), kind=kOutput, calls=%fused_computation.6 | convolution fusion | flops 1516830720 | bytes 30703936 | tf_op jit(solution)/shard_map/spt,std->spd/dot_general | solution.py:1480
  437.4 10.8 %convolution_convert_fusion.3 = bf16[32,80,2304]{2,1,0:T(8,128)(2,1)} fusion(bf16[32,128,2304]{2,1,0:T(8,128)(2,1)} %bitcast.152, f32[32,128]{1,0:T(8,128)S(1)} %bitcast.191, f32[32,128]{1,0:T(8,128)S(1)} %bitcast.194, f32[80]{0:T(128)S(1)} %add_convert_fusion.4), kind=kOutput, calls=%fused_computation.5 | convolution fusion | flops 1516830720 | bytes 30703936 | tf_op jit(solution)/shard_map/spt,std->spd/dot_general | solution.py:1480
  448.2 23.6 %fusion.84 = f32[2560,1536]{0,1:T(8,128)} fusion(bf16[2560,2304]{1,0:T(8,128)(2,1)} %bitcast.154, bf16[2304,1536]{1,0:T(8,128)(2,1)S(1)} %bitcast.206), kind=kOutput, calls=%fused_computation.190 | convolution fusion | flops 18119393280 | bytes 34603008 | tf_op jit(solution)/shard_map/dot_general | solution.py:1472
  471.8 19.3 %fusion = (f32[2560]{0:T(1024)S(1)}, bf16[2560,768]{0,1:T(8,128)(2,1)S(1)}, f32[2560,768]{0,1:T(8,128)}) fusion(f32[2560,1536]{0,1:T(8,128)} %fusion.84, bf16[2560,2304]{1,0:T(8,128)(2,1)} %bitcast.150, bf16[720,2304]{1,0:T(8,128)(2,1)} %bitcast.208), kind=kOutput, calls=%fused_computation.7 | convolution fusion | flops 9077389312 | bytes 42649600 | tf_op jit(solution)/shard_map/dot_general | solution.py:1476
  493.0 14.5 %convolution_convert_fusion = bf16[2560,2304]{1,0:T(8,128)(2,1)} fusion(bf16[2560,768]{0,1:T(8,128)(2,1)S(1)} %get-tuple-element.138, bf16[720,2304]{1,0:T(8,128)(2,1)} %bitcast.209), kind=kOutput, calls=%fused_computation | convolution fusion | flops 9065594880 | bytes 19046400 | tf_op jit(solution)/shard_map/dot_general | solution.py:1472
  509.1 13.3 %multiply_convert_fusion.1 = (bf16[2560,768]{0,1:T(8,128)(2,1)S(1)}, bf16[2560,768]{0,1:T(8,128)(2,1)S(1)}, bf16[768,2560]{1,0:T(8,128)(2,1)}) fusion(f32[2560,768]{0,1:T(8,128)} %get-tuple-element.184, f32[2560]{0:T(1024)S(1)} %mul.469, f32[2560,1536]{0,1:T(8,128)} %fusion.84, bf16[2560,768]{0,1:T(8,128)(2,1)} %copy-done.17), kind=kLoop, calls=%fused_computation.13 | loop fusion | flops 33423360 | bytes 39331840 | tf_op jit(solution)/shard_map/convert_element_type | solution.py:1630
  522.5 11.1 %convolution_convert_fusion.6 = bf16[2304,768]{1,0:T(8,128)(2,1)} fusion(bf16[2560,2304]{1,0:T(8,128)(2,1)S(1)} %bitcast.157, bf16[2560,768]{0,1:T(8,128)(2,1)S(1)} %get-tuple-element.144), kind=kOutput, calls=%fused_computation.18 | convolution fusion | flops 9061466112 | bytes 19267584 | tf_op jit(solution)/shard_map/dot_general | solution.py:1476
  533.6 10.9 %convolution_convert_fusion.5 = bf16[2304,768]{1,0:T(8,128)(2,1)} fusion(bf16[2560,2304]{1,0:T(8,128)(2,1)S(1)} %bitcast.158, bf16[2560,768]{0,1:T(8,128)(2,1)S(1)} %get-tuple-element.143), kind=kOutput, calls=%fused_computation.17 | convolution fusion | flops 9061466112 | bytes 19267584 | tf_op jit(solution)/shard_map/dot_general | solution.py:1476
  544.5 8.3 all-to-all-start.1
  555.4 25.0 %convolution_convert_fusion.1 = bf16[2560,2304]{1,0:T(8,128)(2,1)} fusion(bf16[2304,1536]{1,0:T(8,128)(2,1)} %bitcast.203, bf16[2560,768]{0,1:T(8,128)(2,1)} %copy-done.18, bf16[2560,768]{0,1:T(8,128)(2,1)} %copy-done.19), kind=kOutput, calls=%fused_computation.1 | convolution fusion | flops 18141020160 | bytes 26738688 | tf_op jit(solution)/shard_map/dot_general | solution.py:1476
  580.5 155.9 %collect_rows.1 = (f32[128,2304]{1,0:T(8,128)}, f32[8,128]{1,0:T(8,128)}) custom-call(bf16[4,2,4,80,2304]{4,3,2,1,0:T(8,128)(2,1)} %bitcast.160, f32[4,2,4,8,128]{4,3,2,1,0:T(8,128)} %get-tuple-element.49.notes_ref, f32[4,2,4,8,128]{4,3,2,1,0:T(8,128)} %select_maximum_fusion.2.dots_ref), custom_call_target="tpu_custom_call" | custom-call | flops 1000000 | bytes 1000000 | tf_op jit(solution)/shard_map/collect_rows/pallas_call | solution.py:487
  746.9 28.8 %plane_gather.1 = (bf16[4,128,2304]{2,1,0:T(8,128)(2,1)S(1)}, f32[768,2304]{1,0:T(8,128)}) custom-call(bf16[128,2304]{1,0:T(8,128)(2,1)S(1)} %multiply_convert_fusion.4.x_ref, bf16[768,2560]{1,0:T(8,128)(2,1)} %get-tuple-element.172.a_ref, bf16[2560,2304]{1,0:T(8,128)(2,1)} %bitcast.151), custom_call_target="tpu_custom_call" | custom-call | flops 1000000 | bytes 1000000 | tf_op jit(solution)/shard_map/plane_gather/pallas_call | solution.py:1005
  785.2 11.4 %fusion.76 = (bf16[512,2304]{1,0:T(8,128)(2,1)}, bf16[2304]{0:T(1024)(128)(2,1)S(1)}, bf16[512,2304]{1,0:T(8,128)(2,1)}) fusion(f32[512]{0:T(512)S(1)} %copy-done.69, bf16[4,128,2304]{2,1,0:T(8,128)(2,1)S(1)} %copy-done.10, f32[2304]{0:T(1024)S(1)} %copy-done.47, bf16[2304,1792]{1,0:T(8,128)(2,1)} %bitcast.211, bf16[512,576]{0,1:T(8,128)(2,1)S(1)} %bitcast.184, ...), kind=kOutput, calls=%fused_computation.182 | convolution fusion | flops 4244633344 | bytes 17124352 | tf_op jit(solution)/shard_map/dot_general | solution.py:1476
  797.2 6.8 lined_up.1
  810.0 10.1 convolution_convert_fusion.2
  823.8 156.2 %settle_weights.1 = (bf16[4,288,1792]{2,1,0:T(8,128)(2,1)}, bf16[4,288,128]{2,1,0:T(8,128)(2,1)}, bf16[288,2304]{1,0:T(8,128)(2,1)}, f32[128,2304]{1,0:T(8,128)}, bf16[4,80,2304]{2,1,0:T(8,128)(2,1)}) custom-call(bf16[4,2,288,1792]{3,2,1,0:T(8,128)(2,1)} %bitcast.165, bf16[4,2,288,128]{3,2,1,0:T(8,128)(2,1)} %bitcast.182, bf16[2,288,2304]{2,1,0:T(8,128)(2,1)} %bitcast.173, ...), custom_call_target="tpu_custom_call" | custom-call | flops 1000000 | bytes 1000000 | tf_op jit(solution)/shard_map/settle_weights/pallas_call | solution.py:1299
  983.5 5.8 assemble_columns.1
  996.3 8.7 unpack_columns.1
  (270 shorter events, 106.5 us)
Async XLA Ops:
  162.3 117.4 %all-to-all-start = ((bf16[8,288,768]{2,1,0:T(8,128)(2,1)}), bf16[8,288,768]{2,1,0:T(8,128)(2,1)S(1)}, u32[]{:S(2)}, u32[]{:S(2)}) async-start(bf16[8,288,768]{2,1,0:T(8,128)(2,1)} %get-tuple-element.48), calls=%async_computation | async-start | bytes 7077888 | tf_op jit(solution)/shard_map/all_to_all | solution.py:1533
  188.2 550.6 %reduce-scatter.2.cloned.1.call-start = ((), (), s32[]{:S(2)}) async-start(), calls=%async_computation.4 | async-start | bytes 13271040 | tf_op jit(solution)/shard_map/reduce_scatter | solution.py:1618
  276.4 148.7 %copy-start.49 = (f32[128,2]{0,1:T(2,128)}, f32[128,2]{0,1:T(2,128)S(1)}, u32[]{:S(2)}) copy-start(f32[128,2]{0,1:T(2,128)S(1)} %select_reduce_fusion.1) | copy-start | bytes 3076
  276.4 148.7 %copy-start.54 = (f32[128]{0:T(128)}, f32[128]{0:T(128)S(1)}, u32[]{:S(2)}) copy-start(f32[128]{0:T(128)S(1)} %reduce_max.19) | copy-start | bytes 1540
  426.3 21.9 %slice-start.3 = ((s8[7077888]{0:T(1024)(128)(4,1)}), s8[4194304]{0:T(1024)(128)(4,1)S(1)}, s32[]{:S(2)}) async-start(s8[7077888]{0:T(1024)(128)(4,1)} %bitcast.204), calls=%async_computation.8 | async-start | bytes 8388608
  507.5 14.9 %slice-start = ((s8[11796480]{0:T(1024)(128)(4,1)}), s8[3407872]{0:T(1024)(128)(4,1)S(1)}, s32[]{:S(2)}) async-start(s8[11796480]{0:T(1024)(128)(4,1)} %bitcast.155), calls=%async_computation.5 | async-start | bytes 6815744
  509.1 13.4 %slice-start.1 = ((s8[11796480]{0:T(1024)(128)(4,1)}), s8[4194304]{0:T(1024)(128)(4,1)S(1)}, s32[]{:S(2)}) async-start(s8[11796480]{0:T(1024)(128)(4,1)} %bitcast.155), calls=%async_computation.6 | async-start | bytes 8388608
  509.1 13.4 %slice-start.2 = ((s8[11796480]{0:T(1024)(128)(4,1)}), s8[4194304]{0:T(1024)(128)(4,1)S(1)}, s32[]{:S(2)}) async-start(s8[11796480]{0:T(1024)(128)(4,1)} %bitcast.155), calls=%async_computation.7 | async-start | bytes 8388608
  544.5 194.2 %all-to-all-start.1 = ((bf16[8,288,768]{2,1,0:T(8,128)(2,1)}), bf16[8,288,768]{2,1,0:T(8,128)(2,1)}, u32[]{:S(2)}, u32[]{:S(2)}) async-start(bf16[8,288,768]{2,1,0:T(8,128)(2,1)} %bitcast.170), calls=%async_computation.1 | async-start | bytes 7077888 | tf_op jit(solution)/shard_map/all_to_all | solution.py:1639
  580.4 155.9 %copy-start.50 = (f32[128,2]{0,1:T(2,128)S(1)}, f32[128,2]{0,1:T(2,128)}, u32[]{:S(2)}) copy-start(f32[128,2]{0,1:T(2,128)} %copy-done.49) | copy-start | bytes 3076
  580.4 156.0 %copy-start.55 = (f32[128]{0:T(128)S(1)}, f32[128]{0:T(128)}, u32[]{:S(2)}) copy-start(f32[128]{0:T(128)} %copy-done.54) | copy-start | bytes 1540
  580.4 156.0 %copy-start.59 = (f32[128]{0:T(128)S(1)}, f32[128]{0:T(128)}, u32[]{:S(2)}) copy-start(f32[128]{0:T(128)} %copy-done.58) | copy-start | bytes 1540
  580.4 157.4 %copy-start.53 = (s32[128,2]{0,1:T(2,128)S(1)}, s32[128,2]{0,1:T(2,128)}, u32[]{:S(2)}) copy-start(s32[128,2]{0,1:T(2,128)} %param.15) | copy-start | bytes 3076
  580.5 157.4 %copy-start.8 = (bf16[128,2304]{1,0:T(8,128)(2,1)S(1)}, bf16[128,2304]{1,0:T(8,128)(2,1)}, u32[]{:S(2)}) copy-start(bf16[128,2304]{1,0:T(8,128)(2,1)} %copy-done.7) | copy-start | bytes 1769476
  580.5 158.3 %copy-start.1 = (f32[128,2304]{1,0:T(8,128)S(1)}, f32[128,2304]{1,0:T(8,128)}, u32[]{:S(2)}) copy-start(f32[128,2304]{1,0:T(8,128)} %copy-done) | copy-start | bytes 3538948
  580.5 158.3 %copy-start.12 = (bf16[4,2,288,128]{3,2,1,0:T(8,128)(2,1)S(1)}, bf16[4,2,288,128]{3,2,1,0:T(8,128)(2,1)}, u32[]{:S(2)}) copy-start(bf16[4,2,288,128]{3,2,1,0:T(8,128)(2,1)} %get-tuple-element.43) | copy-start | bytes 1769476
  580.5 158.3 %copy-start.44 = (f32[2304]{0:T(1024)S(1)}, f32[2304]{0:T(1024)}, u32[]{:S(2)}) copy-start(f32[2304]{0:T(1024)} %copy-done.43) | copy-start | bytes 27652
  580.5 158.3 %copy-start.61 = (f32[128]{0:T(128)S(1)}, f32[128]{0:T(128)}, u32[]{:S(2)}) copy-start(f32[128]{0:T(128)} %copy-done.60) | copy-start | bytes 1540
  741.7 81.0 %all-to-all-start.2 = ((bf16[8,288,768]{2,1,0:T(8,128)(2,1)}), bf16[8,288,768]{2,1,0:T(8,128)(2,1)}, u32[]{:S(2)}, u32[]{:S(2)}) async-start(bf16[8,288,768]{2,1,0:T(8,128)(2,1)} %bitcast.169), calls=%async_computation.3 | async-start | bytes 7077888 | tf_op jit(solution)/shard_map/all_to_all | solution.py:1647
  746.9 28.8 %copy-start.20 = (bf16[2,288,2304]{2,1,0:T(8,128)(2,1)S(1)}, bf16[2,288,2304]{2,1,0:T(8,128)(2,1)}, u32[]{:S(2)}) copy-start(bf16[2,288,2304]{2,1,0:T(8,128)(2,1)} %get-tuple-element.46) | copy-start | bytes 7962628
  746.9 28.8 %copy-start.22 = (bf16[4,128,9,64]{1,3,2,0:T(8,128)(2,1)S(1)}, bf16[4,128,9,64]{1,3,2,0:T(8,128)(2,1)}, u32[]{:S(2)}) copy-start(bf16[4,128,9,64]{1,3,2,0:T(8,128)(2,1)} %copy-done.21) | copy-start | bytes 1769476
  783.2 13.3 %copy-start.37 = (bf16[72,8,4,128]{3,1,2,0:T(8,128)(2,1)}, bf16[72,8,4,128]{3,1,2,0:T(8,128)(2,1)S(1)}, u32[]{:S(2)}) copy-start(bf16[72,8,4,128]{3,1,2,0:T(8,128)(2,1)S(1)} %copy.200) | copy-start | bytes 1769476
  823.8 156.2 %copy-start.16 = (bf16[128,2304]{1,0:T(8,128)(2,1)S(1)}, bf16[128,2304]{1,0:T(8,128)(2,1)}, u32[]{:S(2)}) copy-start(bf16[128,2304]{1,0:T(8,128)(2,1)} %t_ref.1) | copy-start | bytes 1769476
  823.8 156.2 %copy-start.48 = (f32[2304]{0:T(1024)S(1)}, f32[2304]{0:T(1024)}, u32[]{:S(2)}) copy-start(f32[2304]{0:T(1024)} %copy-done.46) | copy-start | bytes 27652
  (59 other events, 213.1 us)
Sparse Core Ops, SparseCore 0:
  507.7 211.1 reduce-scatter.1

commit v12 on v11

--- a/solution.py
+++ b/solution.py
@@ -1608,16 +1608,17 @@
         return rows.astype(bf16).reshape(devices * capacity, D)
 
     arrived = take(all_normed)
-    cotangent_rows = take(all_cotangent)
     grad_scale = gate_rows * branch_scale
     pre = dot32(arrived, w_pair)
     gate_part, up_part = pre[:, :Fp], pre[:, Fp:]
     sigmoid_gate = jax.nn.sigmoid(gate_part)
     silu_gate = gate_part * sigmoid_gate
     activated = (silu_gate * up_part).astype(bf16)
-    out_sum = lax.psum_scatter(
-        dot32(activated, down).astype(bf16), SHARD, scatter_dimension=0, tiled=True
-    )
+    out_rows, all_cotangent = lax.optimization_barrier(
+        (dot32(activated, down).astype(bf16), all_cotangent)
+    )
+    out_sum = lax.psum_scatter(out_rows, SHARD, scatter_dimension=0, tiled=True)
+    cotangent_rows = take(all_cotangent)
 
     raw_grad = dot_dims(cotangent_rows, down, 1, 1)
     row_dots = branch_scale * jnp.sum(raw_grad * activated.astype(f32), axis=1)

time: 1020 us -> 1000 us (0.980)
  Pallas kernels: 687 us -> 654 us
    pallas_call x1, Pallas kernels: 156 us -> 122 us  [collect_rows(): pl.pallas_call(functools.partial(collect_kernel, nz, cap), out_shape=(jax...]
  transfers between devices with their start and end apart: 4 -> 4, of which waited for: 1 -> 1; matrix products, arithmetic and copies ran while one was open for 16% -> 20% of each run, Pallas kernels for 22% -> 19%
where the time goes in v12:
time: 1000 us; the launch traced here: 991 us
  Pallas kernels  654 us (65%)
  matrix products  180 us (18%)
  local copies, waits for them, and re-layouts  54.1 us (5%)
  other arithmetic  43.8 us (4%)
  starting transfers between devices  41.3 us (4%)
  between operations  15.3 us (2%)
    pallas_call x1, Pallas kernels, settle_weights(): pl.pallas_call(functools.partial(settle_kernel, nz), out_shape=(sd((4, R,...  156 us
    pallas_call x1, Pallas kernels, fetch_weights(): pl.pallas_call(functools.partial(fetch_kernel, nz, F), out_shape=(sd((nz,...  148 us
    pallas_call x1, Pallas kernels, spread_blocks(): pl.pallas_call(functools.partial(spread_kernel, nz, splits), out_shape=(p...  144 us
    pallas_call x1, Pallas kernels, collect_rows(): pl.pallas_call(functools.partial(collect_kernel, nz, cap), out_shape=(jax...  122 us
    dot_general x8, matrix products, dot_dims(): lax.dot_general(a, b, (((da,), (db,)), ((), ())), preferred_element_type=...  94.7 us
    dot_general x8, matrix products, dot32(): return jnp.dot(a, b, preferred_element_type=f32)  54.1 us
    pallas_call x1, Pallas kernels, plane_sum(): pl.pallas_call(plane_sum_kernel, out_shape=jax.ShapeDtypeStruct(x.shape[1...  29.7 us
    pallas_call x1, Pallas kernels, plane_gather(): pl.pallas_call(plane_gather_kernel, out_shape=(jax.ShapeDtypeStruct((4,)...  29.1 us
  transfers between devices with their start and end apart: 4, of which 1 were waited for; matrix products, arithmetic and copies ran while one was open for 20% of the time, Pallas kernels for 19%

profile of v12, /device:TPU:16, one launch (start us, length us, event | category | flops | bytes accessed | tf_op | source)
XLA Modules:
  0.0 991.2 jit_solution(1700358173813220053)
XLA Ops:
  14.0 148.3 %fetch_weights.1 = (bf16[4,2,288,1792]{3,2,1,0:T(8,128)(2,1)}, bf16[4,2,288,128]{3,2,1,0:T(8,128)(2,1)}, bf16[2,288,2304]{2,1,0:T(8,128)(2,1)}, bf16[4,128,2304]...) custom-call(bf16[288,1792]{1,0:T(8,128)(2,1)} %pick_columns.1.w_ref,, ...), custom_call_target="tpu_custom_call" | custom-call | flops 99999997952 | bytes 4128768 | tf_op jit(solution)/shard_map/fetch_weights/pallas_call | solution.py:926
  162.3 25.9 %all-to-all-start = ((bf16[8,288,768]{2,1,0:T(8,128)(2,1)}), bf16[8,288,768]{2,1,0:T(8,128)(2,1)S(1)}, u32[]{:S(2)}, u32[]{:S(2)}) async-start(bf16[8,288,768]{2,1,0:T(8,128)(2,1)} %get-tuple-element.50), calls=%async_computation | async-start | bytes 7077888 | tf_op jit(solution)/shard_map/all_to_all | solution.py:1533
  195.8 7.8 fusion.83
  242.5 29.7 %plane_sum.1 = f32[128,2304]{1,0:T(8,128)} custom-call(bf16[4,128,2304]{2,1,0:T(8,128)(2,1)} %bitcast.164), custom_call_target="tpu_custom_call" | custom-call | flops 1000000 | bytes 1000000 | tf_op jit(solution)/shard_map/plane_sum/pallas_call | solution.py:1062
  281.5 143.7 %spread_blocks.1 = (bf16[8,288,1536]{2,1,0:T(8,128)(2,1)}, bf16[4,2,4,128,2304]{4,3,2,1,0:T(8,128)(2,1)}, f32[4,2,4,8,128]{4,3,2,1,0:T(8,128)}) custom-call(bf16[8,288,768]{2,1,0:T(8,128)(2,1)} %get-tuple-element.49.refs_0_, bf16[8,288,768]{2,1,0:T(8,128)(2,1)} %copy-done.5, bf16[128,2304]{1,0:T(8,128)(2,1)} %copy-done.8, f32[8,128]{1,0:T(8,128)} %maximum_bitcast_fusion.refs_3_), custom_call_target="tpu_custom_call" | custom-call | flops 1000000 | bytes 1000000 | tf_op jit(solution)/shard_map/spread_blocks/pallas_call | solution.py:249
  426.4 10.9 %convolution_convert_fusion.4 = bf16[32,80,2304]{2,1,0:T(8,128)(2,1)} fusion(bf16[32,128,2304]{2,1,0:T(8,128)(2,1)} %bitcast.153, f32[32,128]{1,0:T(8,128)S(1)} %bitcast.189, f32[32,128]{1,0:T(8,128)S(1)} %bitcast.192, f32[80]{0:T(128)S(1)} %add_convert_fusion.4), kind=kOutput, calls=%fused_computation.6 | convolution fusion | flops 1516830720 | bytes 30703936 | tf_op jit(solution)/shard_map/spt,std->spd/dot_general | solution.py:1480
  437.3 24.0 %fusion.84 = f32[2560,1536]{0,1:T(8,128)S(1)} fusion(bf16[2560,2304]{1,0:T(8,128)(2,1)} %bitcast.154, bf16[2304,1536]{1,0:T(8,128)(2,1)} %bitcast.202), kind=kOutput, calls=%fused_computation.190 | convolution fusion | flops 18119393280 | bytes 34603008 | tf_op jit(solution)/shard_map/dot_general | solution.py:1472
  468.8 13.9 %convolution_convert_fusion.1 = bf16[2560,2304]{1,0:T(8,128)(2,1)} fusion(bf16[2560,768]{0,1:T(8,128)(2,1)} %multiply_convert_fusion.2, bf16[720,2304]{1,0:T(8,128)(2,1)S(1)} %bitcast.205), kind=kOutput, calls=%fused_computation.1 | convolution fusion | flops 9065594880 | bytes 19046400 | tf_op jit(solution)/shard_map/dot_general | solution.py:1472
  482.8 12.3 %convolution_convert_fusion.3 = bf16[32,80,2304]{2,1,0:T(8,128)(2,1)} fusion(bf16[32,128,2304]{2,1,0:T(8,128)(2,1)} %bitcast.152, f32[32,128]{1,0:T(8,128)S(1)} %bitcast.190, f32[32,128]{1,0:T(8,128)S(1)} %bitcast.193, f32[80]{0:T(128)S(1)} %add_convert_fusion.4), kind=kOutput, calls=%fused_computation.5 | convolution fusion | flops 1516830720 | bytes 30703936 | tf_op jit(solution)/shard_map/spt,std->spd/dot_general | solution.py:1480
  495.1 14.3 %fusion = (f32[2560]{0:T(1024)S(1)}, f32[2560,768]{0,1:T(8,128)}) fusion(bf16[2560,768]{0,1:T(8,128)(2,1)S(1)} %copy-done.18, bf16[2560,2304]{1,0:T(8,128)(2,1)} %bitcast.150, bf16[720,2304]{1,0:T(8,128)(2,1)S(1)} %bitcast.206), kind=kOutput, calls=%fused_computation.7 | convolution fusion | flops 9065592832 | bytes 26920960 | tf_op jit(solution)/shard_map/dot_general | solution.py:1476
  510.9 13.6 %multiply_convert_fusion = (bf16[2560,768]{0,1:T(8,128)(2,1)S(1)}, bf16[2560,768]{0,1:T(8,128)(2,1)S(1)}, bf16[768,2560]{1,0:T(8,128)(2,1)}) fusion(f32[2560,768]{0,1:T(8,128)} %get-tuple-element.187, f32[2560]{0:T(1024)S(1)} %mul.469, f32[2560,1536]{0,1:T(8,128)} %copy-done), kind=kLoop, calls=%fused_computation.12 | loop fusion | flops 37355520 | bytes 35399680 | tf_op jit(solution)/shard_map/convert_element_type | solution.py:1631
  524.5 16.9 %convolution_convert_fusion.6 = bf16[2304,768]{1,0:T(8,128)(2,1)} fusion(bf16[2560,2304]{1,0:T(8,128)(2,1)} %bitcast.155, bf16[2560,768]{0,1:T(8,128)(2,1)S(1)} %get-tuple-element.146), kind=kOutput, calls=%fused_computation.18 | convolution fusion | flops 9061466112 | bytes 19267584 | tf_op jit(solution)/shard_map/dot_general | solution.py:1476
  541.4 11.0 %convolution_convert_fusion.5 = bf16[2304,768]{1,0:T(8,128)(2,1)} fusion(bf16[2560,2304]{1,0:T(8,128)(2,1)S(1)} %bitcast.158, bf16[2560,768]{0,1:T(8,128)(2,1)S(1)} %get-tuple-element.145), kind=kOutput, calls=%fused_computation.17 | convolution fusion | flops 9061466112 | bytes 19267584 | tf_op jit(solution)/shard_map/dot_general | solution.py:1476
  552.5 9.5 all-to-all-start.1
  564.3 25.2 %convolution_convert_fusion = bf16[2560,2304]{1,0:T(8,128)(2,1)} fusion(bf16[2304,1536]{1,0:T(8,128)(2,1)} %bitcast.203, bf16[2560,768]{0,1:T(8,128)(2,1)} %copy-done.19, bf16[2560,768]{0,1:T(8,128)(2,1)} %copy-done.20), kind=kOutput, calls=%fused_computation | convolution fusion | flops 18141020160 | bytes 26738688 | tf_op jit(solution)/shard_map/dot_general | solution.py:1476
  589.6 122.3 %collect_rows.1 = (f32[128,2304]{1,0:T(8,128)}, f32[8,128]{1,0:T(8,128)}) custom-call(bf16[4,2,4,80,2304]{4,3,2,1,0:T(8,128)(2,1)} %bitcast.160, f32[4,2,4,8,128]{4,3,2,1,0:T(8,128)} %get-tuple-element.51.notes_ref, f32[4,2,4,8,128]{4,3,2,1,0:T(8,128)} %select_maximum_fusion.2.dots_ref), custom_call_target="tpu_custom_call" | custom-call | flops 1000000 | bytes 1000000 | tf_op jit(solution)/shard_map/collect_rows/pallas_call | solution.py:487
  717.2 6.0 all-to-all-start.2
  723.7 29.1 %plane_gather.1 = (bf16[4,128,2304]{2,1,0:T(8,128)(2,1)S(1)}, f32[768,2304]{1,0:T(8,128)}) custom-call(bf16[128,2304]{1,0:T(8,128)(2,1)S(1)} %multiply_convert_fusion.4.x_ref, bf16[768,2560]{1,0:T(8,128)(2,1)} %get-tuple-element.174.a_ref, bf16[2560,2304]{1,0:T(8,128)(2,1)} %bitcast.151), custom_call_target="tpu_custom_call" | custom-call | flops 1000000 | bytes 1000000 | tf_op jit(solution)/shard_map/plane_gather/pallas_call | solution.py:1005
  762.3 11.4 %fusion.76 = (bf16[512,2304]{1,0:T(8,128)(2,1)}, bf16[2304]{0:T(1024)(128)(2,1)S(1)}, bf16[512,2304]{1,0:T(8,128)(2,1)}) fusion(f32[512]{0:T(512)S(1)} %copy-done.70, bf16[4,128,2304]{2,1,0:T(8,128)(2,1)S(1)} %copy-done.11, f32[2304]{0:T(1024)S(1)} %copy-done.48, bf16[2304,1792]{1,0:T(8,128)(2,1)} %bitcast.208, bf16[512,576]{0,1:T(8,128)(2,1)S(1)} %bitcast.183, ...), kind=kOutput, calls=%fused_computation.182 | convolution fusion | flops 4244633344 | bytes 17124352 | tf_op jit(solution)/shard_map/dot_general | solution.py:1476
  774.3 6.8 lined_up.1
  787.1 10.1 %convolution_convert_fusion.2 = bf16[2304,1792]{1,0:T(8,128)(2,1)} fusion(bf16[512,2304]{1,0:T(8,128)(2,1)S(1)} %copy-done.75, bf16[512,576]{0,1:T(8,128)(2,1)S(1)} %bitcast.184, bf16[512,576]{0,1:T(8,128)(2,1)S(1)} %bitcast.186, bf16[512,576]{0,1:T(8,128)(2,1)S(1)} %bitcast.188, bf16[1792]{0:T(1024)(128)(2,1)S(1)} %copy-done.64), kind=kOutput, calls=%fused_computation.2 | convolution fusion | flops 4239327232 | bytes 12389888 | tf_op jit(solution)/shard_map/dot_general | solution.py:1476
  800.9 156.2 %settle_weights.1 = (bf16[4,288,1792]{2,1,0:T(8,128)(2,1)}, bf16[4,288,128]{2,1,0:T(8,128)(2,1)}, bf16[288,2304]{1,0:T(8,128)(2,1)}, f32[128,2304]{1,0:T(8,128)}, bf16[4,80,2304]{2,1,0:T(8,128)(2,1)}) custom-call(bf16[4,2,288,1792]{3,2,1,0:T(8,128)(2,1)} %bitcast.165, bf16[4,2,288,128]{3,2,1,0:T(8,128)(2,1)} %bitcast.181, bf16[2,288,2304]{2,1,0:T(8,128)(2,1)} %bitcast.172, ...), custom_call_target="tpu_custom_call" | custom-call | flops 1000000 | bytes 1000000 | tf_op jit(solution)/shard_map/settle_weights/pallas_call | solution.py:1299
  960.6 5.8 assemble_columns.1
  973.5 8.7 unpack_columns.1
  (270 shorter events, 112.7 us)
Async XLA Ops:
  162.3 117.4 %all-to-all-start = ((bf16[8,288,768]{2,1,0:T(8,128)(2,1)}), bf16[8,288,768]{2,1,0:T(8,128)(2,1)S(1)}, u32[]{:S(2)}, u32[]{:S(2)}) async-start(bf16[8,288,768]{2,1,0:T(8,128)(2,1)} %get-tuple-element.50), calls=%async_computation | async-start | bytes 7077888 | tf_op jit(solution)/shard_map/all_to_all | solution.py:1533
  188.2 526.1 %reduce-scatter.2.cloned.1.call-start = ((), (), s32[]{:S(2)}) async-start(), calls=%async_computation.4 | async-start | bytes 13271040 | tf_op jit(solution)/shard_map/reduce_scatter | solution.py:1620
  276.4 148.7 %copy-start.50 = (f32[128,2]{0,1:T(2,128)}, f32[128,2]{0,1:T(2,128)S(1)}, u32[]{:S(2)}) copy-start(f32[128,2]{0,1:T(2,128)S(1)} %select_reduce_fusion.1) | copy-start | bytes 3076
  276.5 148.7 %copy-start.55 = (f32[128]{0:T(128)}, f32[128]{0:T(128)S(1)}, u32[]{:S(2)}) copy-start(f32[128]{0:T(128)S(1)} %reduce_max.19) | copy-start | bytes 1540
  510.9 30.5 %slice-start = ((s8[11796480]{0:T(1024)(128)(4,1)}), s8[4194304]{0:T(1024)(128)(4,1)S(1)}, s32[]{:S(2)}) async-start(s8[11796480]{0:T(1024)(128)(4,1)} %bitcast.156), calls=%async_computation.5 | async-start | bytes 8388608
  510.9 30.5 %slice-start.1 = ((s8[11796480]{0:T(1024)(128)(4,1)}), s8[4194304]{0:T(1024)(128)(4,1)S(1)}, s32[]{:S(2)}) async-start(s8[11796480]{0:T(1024)(128)(4,1)} %bitcast.156), calls=%async_computation.6 | async-start | bytes 8388608
  524.5 16.9 %copy-start.20 = (bf16[2560,768]{0,1:T(8,128)(2,1)}, bf16[2560,768]{0,1:T(8,128)(2,1)S(1)}, u32[]{:S(2)}) copy-start(bf16[2560,768]{0,1:T(8,128)(2,1)S(1)} %get-tuple-element.146) | copy-start | bytes 11796484
  524.5 16.9 %copy-start.19 = (bf16[2560,768]{0,1:T(8,128)(2,1)}, bf16[2560,768]{0,1:T(8,128)(2,1)S(1)}, u32[]{:S(2)}) copy-start(bf16[2560,768]{0,1:T(8,128)(2,1)S(1)} %get-tuple-element.145) | copy-start | bytes 11796484
  524.5 16.9 %slice-start.2 = ((s8[11796480]{0:T(1024)(128)(4,1)}), s8[3407872]{0:T(1024)(128)(4,1)S(1)}, s32[]{:S(2)}) async-start(s8[11796480]{0:T(1024)(128)(4,1)} %bitcast.156), calls=%async_computation.7 | async-start | bytes 6815744
  552.5 161.8 %all-to-all-start.1 = ((bf16[8,288,768]{2,1,0:T(8,128)(2,1)}), bf16[8,288,768]{2,1,0:T(8,128)(2,1)}, u32[]{:S(2)}, u32[]{:S(2)}) async-start(bf16[8,288,768]{2,1,0:T(8,128)(2,1)} %bitcast.25), calls=%async_computation.1 | async-start | bytes 7077888 | tf_op jit(solution)/shard_map/all_to_all | solution.py:1640
  589.5 122.4 %copy-start.51 = (f32[128,2]{0,1:T(2,128)S(1)}, f32[128,2]{0,1:T(2,128)}, u32[]{:S(2)}) copy-start(f32[128,2]{0,1:T(2,128)} %copy-done.50) | copy-start | bytes 3076
  589.5 122.4 %copy-start.56 = (f32[128]{0:T(128)S(1)}, f32[128]{0:T(128)}, u32[]{:S(2)}) copy-start(f32[128]{0:T(128)} %copy-done.55) | copy-start | bytes 1540
  589.5 122.4 %copy-start.60 = (f32[128]{0:T(128)S(1)}, f32[128]{0:T(128)}, u32[]{:S(2)}) copy-start(f32[128]{0:T(128)} %copy-done.59) | copy-start | bytes 1540
  589.5 123.8 %copy-start.54 = (s32[128,2]{0,1:T(2,128)S(1)}, s32[128,2]{0,1:T(2,128)}, u32[]{:S(2)}) copy-start(s32[128,2]{0,1:T(2,128)} %param.15) | copy-start | bytes 3076
  589.5 123.8 %copy-start.9 = (bf16[128,2304]{1,0:T(8,128)(2,1)S(1)}, bf16[128,2304]{1,0:T(8,128)(2,1)}, u32[]{:S(2)}) copy-start(bf16[128,2304]{1,0:T(8,128)(2,1)} %copy-done.8) | copy-start | bytes 1769476
  589.5 124.8 %copy-start.2 = (f32[128,2304]{1,0:T(8,128)S(1)}, f32[128,2304]{1,0:T(8,128)}, u32[]{:S(2)}) copy-start(f32[128,2304]{1,0:T(8,128)} %copy-done.1) | copy-start | bytes 3538948
  589.5 124.8 %copy-start.13 = (bf16[4,2,288,128]{3,2,1,0:T(8,128)(2,1)S(1)}, bf16[4,2,288,128]{3,2,1,0:T(8,128)(2,1)}, u32[]{:S(2)}) copy-start(bf16[4,2,288,128]{3,2,1,0:T(8,128)(2,1)} %get-tuple-element.45) | copy-start | bytes 1769476
  589.5 124.8 %copy-start.45 = (f32[2304]{0:T(1024)S(1)}, f32[2304]{0:T(1024)}, u32[]{:S(2)}) copy-start(f32[2304]{0:T(1024)} %copy-done.44) | copy-start | bytes 27652
  589.6 124.8 %copy-start.62 = (f32[128]{0:T(128)S(1)}, f32[128]{0:T(128)}, u32[]{:S(2)}) copy-start(f32[128]{0:T(128)} %copy-done.61) | copy-start | bytes 1540
  717.2 82.7 %all-to-all-start.2 = ((bf16[8,288,768]{2,1,0:T(8,128)(2,1)}), bf16[8,288,768]{2,1,0:T(8,128)(2,1)}, u32[]{:S(2)}, u32[]{:S(2)}) async-start(bf16[8,288,768]{2,1,0:T(8,128)(2,1)} %bitcast.169), calls=%async_computation.3 | async-start | bytes 7077888 | tf_op jit(solution)/shard_map/all_to_all | solution.py:1648
  723.7 29.2 %copy-start.21 = (bf16[2,288,2304]{2,1,0:T(8,128)(2,1)S(1)}, bf16[2,288,2304]{2,1,0:T(8,128)(2,1)}, u32[]{:S(2)}) copy-start(bf16[2,288,2304]{2,1,0:T(8,128)(2,1)} %get-tuple-element.48) | copy-start | bytes 7962628
  723.7 29.2 %copy-start.23 = (bf16[4,128,9,64]{1,3,2,0:T(8,128)(2,1)S(1)}, bf16[4,128,9,64]{1,3,2,0:T(8,128)(2,1)}, u32[]{:S(2)}) copy-start(bf16[4,128,9,64]{1,3,2,0:T(8,128)(2,1)} %copy-done.22) | copy-start | bytes 1769476
  800.9 156.2 %copy-start.17 = (bf16[128,2304]{1,0:T(8,128)(2,1)S(1)}, bf16[128,2304]{1,0:T(8,128)(2,1)}, u32[]{:S(2)}) copy-start(bf16[128,2304]{1,0:T(8,128)(2,1)} %t_ref.1) | copy-start | bytes 1769476
  800.9 156.2 %copy-start.49 = (f32[2304]{0:T(1024)S(1)}, f32[2304]{0:T(1024)}, u32[]{:S(2)}) copy-start(f32[2304]{0:T(1024)} %copy-done.47) | copy-start | bytes 27652
  (59 other events, 223.7 us)
Sparse Core Ops, SparseCore 0:
  482.9 195.4 reduce-scatter.1

commit v13 on v12

--- a/solution.py
+++ b/solution.py
@@ -308,9 +308,6 @@
         )
 
     dot_kept = pltpu.make_async_copy(dots_ref.at[z, c, e], dots.at[0], dot_own)
-    dot_kept.start()
-    for d, te, tz, tc in others():
-        dot(d, te, tz, tc).start()
 
     note_copy = pltpu.make_async_copy(notes_ref, notes, note_sem)
     note_copy.start()
@@ -330,6 +327,9 @@
         for q in range(4):
             hand(i, q).start()
             fetch(i, q).start()
+    dot_kept.start()
+    for d, te, tz, tc in others():
+        dot(d, te, tz, tc).start()
     note_copy.wait()
 
     def open_out(i, q):
@@ -1087,10 +1087,11 @@
     dest = line_order(nz, z)
     greet_cross(nz)
     W = g_ref.shape[3]
-    first = W // 256 * 128
+    first = W // 384 * 128
     groups = (
         (g_ref, g_mine, g_sib, g_z, g_out, pl.ds(0, first)),
-        (g_ref, g_mine, g_sib, g_z, g_out, pl.ds(first, W - first)),
+        (g_ref, g_mine, g_sib, g_z, g_out, pl.ds(first, first)),
+        (g_ref, g_mine, g_sib, g_z, g_out, pl.ds(2 * first, W - 2 * first)),
         (s_ref, s_mine, s_sib, s_z, s_out, pl.ds(0, s_ref.shape[3])),
     )
     K = len(groups)
@@ -1312,10 +1313,10 @@
             vm((nz, R, W), bf16), vm((nz, R, W), bf16), vm((2, nz, R, W), bf16),
             vm((nz, R, Ws), bf16), vm((nz, R, Ws), bf16), vm((2, nz, R, Ws), bf16),
             vm((R, D), bf16), vm((R, D), bf16), vm((2, R, D), bf16),
-            dma((3, nz)), dma((3, nz)), dma((3, nz)), dma((3, nz)), dma((3, 2, nz)),
+            dma((4, nz)), dma((4, nz)), dma((4, nz)), dma((4, nz)), dma((4, 2, nz)),
             dma((6,)), dma((6,)), dma((6,)), dma((6,)), dma((2, 6)),
             dma((3, 6)), dma((6,)), dma(()),
-            *plane_sems(), *plane_sems(), *plane_sems(),
+            *plane_sems(), *plane_sems(), *plane_sems(), *plane_sems(),
         ],
         compiler_params=pltpu.CompilerParams(
             collective_id=1, has_side_effects=True, vmem_limit_bytes=56 << 20

time: 1000 us -> 998 us (level)
  no operation moved by 1% of the time
where the time goes in v13:
time: 998 us; the launch traced here: 982 us
  Pallas kernels  645 us (65%)
  matrix products  180 us (18%)
  local copies, waits for them, and re-layouts  54.1 us (5%)
  other arithmetic  43.8 us (4%)
  starting transfers between devices  41.3 us (4%)
  between operations  15.3 us (2%)
    pallas_call x1, Pallas kernels, fetch_weights(): pl.pallas_call(functools.partial(fetch_kernel, nz, F), out_shape=(sd((nz,...  148 us
    pallas_call x1, Pallas kernels, settle_weights(): pl.pallas_call(functools.partial(settle_kernel, nz), out_shape=(sd((4, R,...  147 us
    pallas_call x1, Pallas kernels, spread_blocks(): pl.pallas_call(functools.partial(spread_kernel, nz, splits), out_shape=(p...  144 us
    pallas_call x1, Pallas kernels, collect_rows(): pl.pallas_call(functools.partial(collect_kernel, nz, cap), out_shape=(jax...  122 us
    dot_general x8, matrix products, dot_dims(): lax.dot_general(a, b, (((da,), (db,)), ((), ())), preferred_element_type=...  94.7 us
    dot_general x8, matrix products, dot32(): return jnp.dot(a, b, preferred_element_type=f32)  54.1 us
    pallas_call x1, Pallas kernels, plane_sum(): pl.pallas_call(plane_sum_kernel, out_shape=jax.ShapeDtypeStruct(x.shape[1...  29.7 us
    pallas_call x1, Pallas kernels, plane_gather(): pl.pallas_call(plane_gather_kernel, out_shape=(jax.ShapeDtypeStruct((4,)...  29.1 us
  transfers between devices with their start and end apart: 4, of which 1 were waited for; matrix products, arithmetic and copies ran while one was open for 20% of the time, Pallas kernels for 19%

profile of v13, /device:TPU:16, one launch (start us, length us, event | category | flops | bytes accessed | tf_op | source)
XLA Modules:
  0.0 982.3 jit_solution(12951972576858569076)
XLA Ops:
  14.0 148.3 %fetch_weights.1 = (bf16[4,2,288,1792]{3,2,1,0:T(8,128)(2,1)}, bf16[4,2,288,128]{3,2,1,0:T(8,128)(2,1)}, bf16[2,288,2304]{2,1,0:T(8,128)(2,1)}, bf16[4,128,2304]...) custom-call(bf16[288,1792]{1,0:T(8,128)(2,1)} %pick_columns.1.w_ref,, ...), custom_call_target="tpu_custom_call" | custom-call | flops 99999997952 | bytes 4128768 | tf_op jit(solution)/shard_map/fetch_weights/pallas_call | solution.py:926
  162.3 25.9 %all-to-all-start = ((bf16[8,288,768]{2,1,0:T(8,128)(2,1)}), bf16[8,288,768]{2,1,0:T(8,128)(2,1)S(1)}, u32[]{:S(2)}, u32[]{:S(2)}) async-start(bf16[8,288,768]{2,1,0:T(8,128)(2,1)} %get-tuple-element.50), calls=%async_computation | async-start | bytes 7077888 | tf_op jit(solution)/shard_map/all_to_all | solution.py:1534
  195.8 7.8 fusion.83
  242.5 29.7 %plane_sum.1 = f32[128,2304]{1,0:T(8,128)} custom-call(bf16[4,128,2304]{2,1,0:T(8,128)(2,1)} %bitcast.164), custom_call_target="tpu_custom_call" | custom-call | flops 1000000 | bytes 1000000 | tf_op jit(solution)/shard_map/plane_sum/pallas_call | solution.py:1062
  281.5 143.7 %spread_blocks.1 = (bf16[8,288,1536]{2,1,0:T(8,128)(2,1)}, bf16[4,2,4,128,2304]{4,3,2,1,0:T(8,128)(2,1)}, f32[4,2,4,8,128]{4,3,2,1,0:T(8,128)}) custom-call(bf16[8,288,768]{2,1,0:T(8,128)(2,1)} %get-tuple-element.49.refs_0_, bf16[8,288,768]{2,1,0:T(8,128)(2,1)} %copy-done.5, bf16[128,2304]{1,0:T(8,128)(2,1)} %copy-done.8, f32[8,128]{1,0:T(8,128)} %maximum_bitcast_fusion.refs_3_), custom_call_target="tpu_custom_call" | custom-call | flops 1000000 | bytes 1000000 | tf_op jit(solution)/shard_map/spread_blocks/pallas_call | solution.py:249
  426.4 10.9 %convolution_convert_fusion.4 = bf16[32,80,2304]{2,1,0:T(8,128)(2,1)} fusion(bf16[32,128,2304]{2,1,0:T(8,128)(2,1)} %bitcast.153, f32[32,128]{1,0:T(8,128)S(1)} %bitcast.189, f32[32,128]{1,0:T(8,128)S(1)} %bitcast.192, f32[80]{0:T(128)S(1)} %add_convert_fusion.4), kind=kOutput, calls=%fused_computation.6 | convolution fusion | flops 1516830720 | bytes 30703936 | tf_op jit(solution)/shard_map/spt,std->spd/dot_general | solution.py:1481
  437.3 24.0 %fusion.84 = f32[2560,1536]{0,1:T(8,128)S(1)} fusion(bf16[2560,2304]{1,0:T(8,128)(2,1)} %bitcast.154, bf16[2304,1536]{1,0:T(8,128)(2,1)} %bitcast.202), kind=kOutput, calls=%fused_computation.190 | convolution fusion | flops 18119393280 | bytes 34603008 | tf_op jit(solution)/shard_map/dot_general | solution.py:1473
  468.8 13.9 %convolution_convert_fusion.1 = bf16[2560,2304]{1,0:T(8,128)(2,1)} fusion(bf16[2560,768]{0,1:T(8,128)(2,1)} %multiply_convert_fusion.2, bf16[720,2304]{1,0:T(8,128)(2,1)S(1)} %bitcast.205), kind=kOutput, calls=%fused_computation.1 | convolution fusion | flops 9065594880 | bytes 19046400 | tf_op jit(solution)/shard_map/dot_general | solution.py:1473
  482.8 12.3 %convolution_convert_fusion.3 = bf16[32,80,2304]{2,1,0:T(8,128)(2,1)} fusion(bf16[32,128,2304]{2,1,0:T(8,128)(2,1)} %bitcast.152, f32[32,128]{1,0:T(8,128)S(1)} %bitcast.190, f32[32,128]{1,0:T(8,128)S(1)} %bitcast.193, f32[80]{0:T(128)S(1)} %add_convert_fusion.4), kind=kOutput, calls=%fused_computation.5 | convolution fusion | flops 1516830720 | bytes 30703936 | tf_op jit(solution)/shard_map/spt,std->spd/dot_general | solution.py:1481
  495.1 14.3 %fusion = (f32[2560]{0:T(1024)S(1)}, f32[2560,768]{0,1:T(8,128)}) fusion(bf16[2560,768]{0,1:T(8,128)(2,1)S(1)} %copy-done.18, bf16[2560,2304]{1,0:T(8,128)(2,1)} %bitcast.150, bf16[720,2304]{1,0:T(8,128)(2,1)S(1)} %bitcast.206), kind=kOutput, calls=%fused_computation.7 | convolution fusion | flops 9065592832 | bytes 26920960 | tf_op jit(solution)/shard_map/dot_general | solution.py:1477
  510.9 13.6 %multiply_convert_fusion = (bf16[2560,768]{0,1:T(8,128)(2,1)S(1)}, bf16[2560,768]{0,1:T(8,128)(2,1)S(1)}, bf16[768,2560]{1,0:T(8,128)(2,1)}) fusion(f32[2560,768]{0,1:T(8,128)} %get-tuple-element.187, f32[2560]{0:T(1024)S(1)} %mul.469, f32[2560,1536]{0,1:T(8,128)} %copy-done), kind=kLoop, calls=%fused_computation.12 | loop fusion | flops 37355520 | bytes 35399680 | tf_op jit(solution)/shard_map/convert_element_type | solution.py:1632
  524.5 16.9 %convolution_convert_fusion.6 = bf16[2304,768]{1,0:T(8,128)(2,1)} fusion(bf16[2560,2304]{1,0:T(8,128)(2,1)} %bitcast.155, bf16[2560,768]{0,1:T(8,128)(2,1)S(1)} %get-tuple-element.146), kind=kOutput, calls=%fused_computation.18 | convolution fusion | flops 9061466112 | bytes 19267584 | tf_op jit(solution)/shard_map/dot_general | solution.py:1477
  541.4 11.0 %convolution_convert_fusion.5 = bf16[2304,768]{1,0:T(8,128)(2,1)} fusion(bf16[2560,2304]{1,0:T(8,128)(2,1)S(1)} %bitcast.158, bf16[2560,768]{0,1:T(8,128)(2,1)S(1)} %get-tuple-element.145), kind=kOutput, calls=%fused_computation.17 | convolution fusion | flops 9061466112 | bytes 19267584 | tf_op jit(solution)/shard_map/dot_general | solution.py:1477
  552.5 9.5 all-to-all-start.1
  564.3 25.1 %convolution_convert_fusion = bf16[2560,2304]{1,0:T(8,128)(2,1)} fusion(bf16[2304,1536]{1,0:T(8,128)(2,1)} %bitcast.203, bf16[2560,768]{0,1:T(8,128)(2,1)} %copy-done.19, bf16[2560,768]{0,1:T(8,128)(2,1)} %copy-done.20), kind=kOutput, calls=%fused_computation | convolution fusion | flops 18141020160 | bytes 26738688 | tf_op jit(solution)/shard_map/dot_general | solution.py:1477
  589.6 122.3 %collect_rows.1 = (f32[128,2304]{1,0:T(8,128)}, f32[8,128]{1,0:T(8,128)}) custom-call(bf16[4,2,4,80,2304]{4,3,2,1,0:T(8,128)(2,1)} %bitcast.160, f32[4,2,4,8,128]{4,3,2,1,0:T(8,128)} %get-tuple-element.51.notes_ref, f32[4,2,4,8,128]{4,3,2,1,0:T(8,128)} %select_maximum_fusion.2.dots_ref), custom_call_target="tpu_custom_call" | custom-call | flops 1000000 | bytes 1000000 | tf_op jit(solution)/shard_map/collect_rows/pallas_call | solution.py:487
  717.2 6.0 all-to-all-start.2
  723.7 29.1 %plane_gather.1 = (bf16[4,128,2304]{2,1,0:T(8,128)(2,1)S(1)}, f32[768,2304]{1,0:T(8,128)}) custom-call(bf16[128,2304]{1,0:T(8,128)(2,1)S(1)} %multiply_convert_fusion.4.x_ref, bf16[768,2560]{1,0:T(8,128)(2,1)} %get-tuple-element.174.a_ref, bf16[2560,2304]{1,0:T(8,128)(2,1)} %bitcast.151), custom_call_target="tpu_custom_call" | custom-call | flops 1000000 | bytes 1000000 | tf_op jit(solution)/shard_map/plane_gather/pallas_call | solution.py:1005
  762.3 11.4 %fusion.76 = (bf16[512,2304]{1,0:T(8,128)(2,1)}, bf16[2304]{0:T(1024)(128)(2,1)S(1)}, bf16[512,2304]{1,0:T(8,128)(2,1)}) fusion(f32[512]{0:T(512)S(1)} %copy-done.70, bf16[4,128,2304]{2,1,0:T(8,128)(2,1)S(1)} %copy-done.11, f32[2304]{0:T(1024)S(1)} %copy-done.48, bf16[2304,1792]{1,0:T(8,128)(2,1)} %bitcast.208, bf16[512,576]{0,1:T(8,128)(2,1)S(1)} %bitcast.183, ...), kind=kOutput, calls=%fused_computation.182 | convolution fusion | flops 4244633344 | bytes 17124352 | tf_op jit(solution)/shard_map/dot_general | solution.py:1477
  774.3 6.8 lined_up.1
  787.1 10.1 %convolution_convert_fusion.2 = bf16[2304,1792]{1,0:T(8,128)(2,1)} fusion(bf16[512,2304]{1,0:T(8,128)(2,1)S(1)} %copy-done.75, bf16[512,576]{0,1:T(8,128)(2,1)S(1)} %bitcast.184, bf16[512,576]{0,1:T(8,128)(2,1)S(1)} %bitcast.186, bf16[512,576]{0,1:T(8,128)(2,1)S(1)} %bitcast.188, bf16[1792]{0:T(1024)(128)(2,1)S(1)} %copy-done.64), kind=kOutput, calls=%fused_computation.2 | convolution fusion | flops 4239327232 | bytes 12389888 | tf_op jit(solution)/shard_map/dot_general | solution.py:1477
  800.9 147.2 %settle_weights.1 = (bf16[4,288,1792]{2,1,0:T(8,128)(2,1)}, bf16[4,288,128]{2,1,0:T(8,128)(2,1)}, bf16[288,2304]{1,0:T(8,128)(2,1)}, f32[128,2304]{1,0:T(8,128)}, bf16[4,80,2304]{2,1,0:T(8,128)(2,1)}) custom-call(bf16[4,2,288,1792]{3,2,1,0:T(8,128)(2,1)} %bitcast.165, bf16[4,2,288,128]{3,2,1,0:T(8,128)(2,1)} %bitcast.181, bf16[2,288,2304]{2,1,0:T(8,128)(2,1)} %bitcast.172, ...), custom_call_target="tpu_custom_call" | custom-call | flops 1000000 | bytes 1000000 | tf_op jit(solution)/shard_map/settle_weights/pallas_call | solution.py:1300
  951.6 5.8 assemble_columns.1
  964.5 8.7 unpack_columns.1
  (270 shorter events, 112.7 us)
Async XLA Ops:
  162.3 117.4 %all-to-all-start = ((bf16[8,288,768]{2,1,0:T(8,128)(2,1)}), bf16[8,288,768]{2,1,0:T(8,128)(2,1)S(1)}, u32[]{:S(2)}, u32[]{:S(2)}) async-start(bf16[8,288,768]{2,1,0:T(8,128)(2,1)} %get-tuple-element.50), calls=%async_computation | async-start | bytes 7077888 | tf_op jit(solution)/shard_map/all_to_all | solution.py:1534
  188.2 526.1 %reduce-scatter.2.cloned.1.call-start = ((), (), s32[]{:S(2)}) async-start(), calls=%async_computation.4 | async-start | bytes 13271040 | tf_op jit(solution)/shard_map/reduce_scatter | solution.py:1621
  276.4 148.7 %copy-start.50 = (f32[128,2]{0,1:T(2,128)}, f32[128,2]{0,1:T(2,128)S(1)}, u32[]{:S(2)}) copy-start(f32[128,2]{0,1:T(2,128)S(1)} %select_reduce_fusion.1) | copy-start | bytes 3076
  276.5 148.7 %copy-start.55 = (f32[128]{0:T(128)}, f32[128]{0:T(128)S(1)}, u32[]{:S(2)}) copy-start(f32[128]{0:T(128)S(1)} %reduce_max.19) | copy-start | bytes 1540
  510.9 30.5 %slice-start = ((s8[11796480]{0:T(1024)(128)(4,1)}), s8[4194304]{0:T(1024)(128)(4,1)S(1)}, s32[]{:S(2)}) async-start(s8[11796480]{0:T(1024)(128)(4,1)} %bitcast.156), calls=%async_computation.5 | async-start | bytes 8388608
  510.9 30.6 %slice-start.1 = ((s8[11796480]{0:T(1024)(128)(4,1)}), s8[4194304]{0:T(1024)(128)(4,1)S(1)}, s32[]{:S(2)}) async-start(s8[11796480]{0:T(1024)(128)(4,1)} %bitcast.156), calls=%async_computation.6 | async-start | bytes 8388608
  524.5 16.9 %copy-start.20 = (bf16[2560,768]{0,1:T(8,128)(2,1)}, bf16[2560,768]{0,1:T(8,128)(2,1)S(1)}, u32[]{:S(2)}) copy-start(bf16[2560,768]{0,1:T(8,128)(2,1)S(1)} %get-tuple-element.146) | copy-start | bytes 11796484
  524.5 16.9 %copy-start.19 = (bf16[2560,768]{0,1:T(8,128)(2,1)}, bf16[2560,768]{0,1:T(8,128)(2,1)S(1)}, u32[]{:S(2)}) copy-start(bf16[2560,768]{0,1:T(8,128)(2,1)S(1)} %get-tuple-element.145) | copy-start | bytes 11796484
  524.5 16.9 %slice-start.2 = ((s8[11796480]{0:T(1024)(128)(4,1)}), s8[3407872]{0:T(1024)(128)(4,1)S(1)}, s32[]{:S(2)}) async-start(s8[11796480]{0:T(1024)(128)(4,1)} %bitcast.156), calls=%async_computation.7 | async-start | bytes 6815744
  552.5 161.8 %all-to-all-start.1 = ((bf16[8,288,768]{2,1,0:T(8,128)(2,1)}), bf16[8,288,768]{2,1,0:T(8,128)(2,1)}, u32[]{:S(2)}, u32[]{:S(2)}) async-start(bf16[8,288,768]{2,1,0:T(8,128)(2,1)} %bitcast.25), calls=%async_computation.1 | async-start | bytes 7077888 | tf_op jit(solution)/shard_map/all_to_all | solution.py:1641
  589.5 122.4 %copy-start.51 = (f32[128,2]{0,1:T(2,128)S(1)}, f32[128,2]{0,1:T(2,128)}, u32[]{:S(2)}) copy-start(f32[128,2]{0,1:T(2,128)} %copy-done.50) | copy-start | bytes 3076
  589.5 122.4 %copy-start.56 = (f32[128]{0:T(128)S(1)}, f32[128]{0:T(128)}, u32[]{:S(2)}) copy-start(f32[128]{0:T(128)} %copy-done.55) | copy-start | bytes 1540
  589.5 122.4 %copy-start.60 = (f32[128]{0:T(128)S(1)}, f32[128]{0:T(128)}, u32[]{:S(2)}) copy-start(f32[128]{0:T(128)} %copy-done.59) | copy-start | bytes 1540
  589.5 123.8 %copy-start.54 = (s32[128,2]{0,1:T(2,128)S(1)}, s32[128,2]{0,1:T(2,128)}, u32[]{:S(2)}) copy-start(s32[128,2]{0,1:T(2,128)} %param.15) | copy-start | bytes 3076
  589.5 123.8 %copy-start.9 = (bf16[128,2304]{1,0:T(8,128)(2,1)S(1)}, bf16[128,2304]{1,0:T(8,128)(2,1)}, u32[]{:S(2)}) copy-start(bf16[128,2304]{1,0:T(8,128)(2,1)} %copy-done.8) | copy-start | bytes 1769476
  589.5 124.8 %copy-start.2 = (f32[128,2304]{1,0:T(8,128)S(1)}, f32[128,2304]{1,0:T(8,128)}, u32[]{:S(2)}) copy-start(f32[128,2304]{1,0:T(8,128)} %copy-done.1) | copy-start | bytes 3538948
  589.5 124.8 %copy-start.13 = (bf16[4,2,288,128]{3,2,1,0:T(8,128)(2,1)S(1)}, bf16[4,2,288,128]{3,2,1,0:T(8,128)(2,1)}, u32[]{:S(2)}) copy-start(bf16[4,2,288,128]{3,2,1,0:T(8,128)(2,1)} %get-tuple-element.45) | copy-start | bytes 1769476
  589.5 124.8 %copy-start.45 = (f32[2304]{0:T(1024)S(1)}, f32[2304]{0:T(1024)}, u32[]{:S(2)}) copy-start(f32[2304]{0:T(1024)} %copy-done.44) | copy-start | bytes 27652
  589.6 124.8 %copy-start.62 = (f32[128]{0:T(128)S(1)}, f32[128]{0:T(128)}, u32[]{:S(2)}) copy-start(f32[128]{0:T(128)} %copy-done.61) | copy-start | bytes 1540
  717.2 82.7 %all-to-all-start.2 = ((bf16[8,288,768]{2,1,0:T(8,128)(2,1)}), bf16[8,288,768]{2,1,0:T(8,128)(2,1)}, u32[]{:S(2)}, u32[]{:S(2)}) async-start(bf16[8,288,768]{2,1,0:T(8,128)(2,1)} %bitcast.169), calls=%async_computation.3 | async-start | bytes 7077888 | tf_op jit(solution)/shard_map/all_to_all | solution.py:1649
  723.7 29.2 %copy-start.21 = (bf16[2,288,2304]{2,1,0:T(8,128)(2,1)S(1)}, bf16[2,288,2304]{2,1,0:T(8,128)(2,1)}, u32[]{:S(2)}) copy-start(bf16[2,288,2304]{2,1,0:T(8,128)(2,1)} %get-tuple-element.48) | copy-start | bytes 7962628
  723.7 29.2 %copy-start.23 = (bf16[4,128,9,64]{1,3,2,0:T(8,128)(2,1)S(1)}, bf16[4,128,9,64]{1,3,2,0:T(8,128)(2,1)}, u32[]{:S(2)}) copy-start(bf16[4,128,9,64]{1,3,2,0:T(8,128)(2,1)} %copy-done.22) | copy-start | bytes 1769476
  800.9 147.2 %copy-start.17 = (bf16[128,2304]{1,0:T(8,128)(2,1)S(1)}, bf16[128,2304]{1,0:T(8,128)(2,1)}, u32[]{:S(2)}) copy-start(bf16[128,2304]{1,0:T(8,128)(2,1)} %t_ref.1) | copy-start | bytes 1769476
  800.9 147.2 %copy-start.49 = (f32[2304]{0:T(1024)S(1)}, f32[2304]{0:T(1024)}, u32[]{:S(2)}) copy-start(f32[2304]{0:T(1024)} %copy-done.47) | copy-start | bytes 27652
  (59 other events, 223.7 us)
Sparse Core Ops, SparseCore 0:
  482.9 195.4 reduce-scatter.1
